TPU v7x, 32 devices: a whole 2x2x4 slice. The times are simulated.
32 devices in a mesh: fsdp: 4 (over z), ctx: 4 (over y, x), tp: 2 (over core).
Axes of the slice: x: 2, y: 2, z: 4, core: 2. Of those that a mesh axis runs over, the one named last changes fastest.
Arguments:
- hidden_in: bfloat16 [16, 1024, 768], P('fsdp', 'ctx'), may hold values from -6 to 6
- valid_mask: int32 [16, 1024], P('fsdp', 'ctx'), may hold values from 0 to 1, as said below
- teacher: bfloat16 [16, 1024, 768], P('fsdp', 'ctx'), may hold values from -6 to 6
- qkv_weight: bfloat16 [768, 3, 768], P('fsdp', None, 'tp'), may hold values from -0.21875 to 0.21875
- qv_bias: float32 [2, 768], P(None, 'tp'), may hold values from -0.6 to 0.6
- out_weight: bfloat16 [768, 768], P('fsdp', 'tp'), may hold values from -1.75 to 1.75
- out_bias: float32 [768], replicated, may hold values from -1.2 to 1.2
- norm1_gain: float32 [768], replicated, may hold values from 0.5 to 1.5
- norm1_shift: float32 [768], replicated, may hold values from -1.2 to 1.2
- up_weight: bfloat16 [768, 3072], P('fsdp', 'tp'), may hold values from -0.21875 to 0.21875
- up_bias: float32 [3072], P('tp'), may hold values from -3 to 3
- down_weight: bfloat16 [768, 3072], P('fsdp', 'tp'), may hold values from -0.109375 to 0.109375
- down_bias: float32 [768], replicated, may hold values from -1.2 to 1.2
- norm2_gain: float32 [768], replicated, may hold values from 0.5 to 1.5
- norm2_shift: float32 [768], replicated, may hold values from -1.2 to 1.2
Outputs:
- layer_out: bfloat16 [16, 1024, 768], P('fsdp', 'ctx')
- input_grad: float32 [16, 1024, 768], P('fsdp', 'ctx')
- loss: float32 [], replicated
- qkv_weight_grad: float32 [768, 3, 768], P('fsdp', None, 'tp')
- qv_bias_grad: float32 [2, 768], P(None, 'tp')
- out_weight_grad: float32 [768, 768], P('fsdp', 'tp')
- out_bias_grad: float32 [768], replicated
- norm1_gain_grad: float32 [768], replicated
- norm1_shift_grad: float32 [768], replicated
- up_weight_grad: float32 [768, 3072], P('fsdp', 'tp')
- up_bias_grad: float32 [3072], P('tp')
- down_weight_grad: float32 [768, 3072], P('fsdp', 'tp')
- down_bias_grad: float32 [768], replicated
- norm2_gain_grad: float32 [768], replicated
- norm2_shift_grad: float32 [768], replicated
Inputs may be any that keep to these rules, and one draw needn't show every extreme that they name: `valid_mask`: in each sequence the valid tokens form a prefix that holds a quarter of its 1024 positions or more; the first sequence is valid throughout and the second holds exactly a quarter of them.
All inputs are finite; a program needn't handle non-finite values.
Results may differ from a plain program's by a relative error of at most 0.018.
Values may be sent and summed in bfloat16 or wider, within the bound.
No kernel may reach another device: no remote copies, remote signals or barrier semaphores. Data moves between devices by JAX's collectives and lax.ppermute only.
A program may use at most 320 MiB of HBM per device.

v0:
```python
import jax
import jax.numpy as jnp
from jax import lax
from jax.sharding import PartitionSpec as P

HEAD_DIM = 64


NORM_EPS = 1e-05
MASKED = -1e30


def layer_norm(values_in, gain_vec, shift_vec):
    row_mean = jnp.mean(values_in, axis=-1, keepdims=True)
    centered = values_in - row_mean
    row_var = jnp.mean(centered * centered, axis=-1, keepdims=True)
    return centered * lax.rsqrt(row_var + NORM_EPS) * gain_vec + shift_vec


def gelu_exact(pre_act):
    return jax.nn.gelu(pre_act, approximate=False)


def split_heads(packed):
    return packed.reshape(packed.shape[0], packed.shape[1], packed.shape[2] // HEAD_DIM, HEAD_DIM)


def scores_of(query_heads, key_heads, allowed, scaling):
    raw_scores = (
        jnp.einsum("sqhd,skhd->shqk", query_heads, key_heads, preferred_element_type=jnp.float32)
        * scaling
    )
    return jnp.where(allowed, raw_scores, MASKED)


def local(
    hidden_in,
    valid_mask,
    teacher,
    qkv_weight,
    qv_bias,
    out_weight,
    out_bias,
    norm1_gain,
    norm1_shift,
    up_weight,
    up_bias,
    down_weight,
    down_bias,
    norm2_gain,
    norm2_shift,
):
    seq_count, block_len, model_width = hidden_in.shape
    ctx_count = lax.axis_size("ctx")
    ctx_place = lax.axis_index("ctx")
    key_span = 2 * block_len
    seq_length = block_len * ctx_count
    row_count = seq_count * block_len
    scaling = HEAD_DIM ** (-0.5)
    full_qkv, full_out, full_up, full_down = (
        lax.all_gather(qkv_weight, "fsdp", axis=0, tiled=True),
        lax.all_gather(out_weight, "fsdp", axis=0, tiled=True),
        lax.all_gather(up_weight, "fsdp", axis=0, tiled=True),
        lax.all_gather(down_weight, "fsdp", axis=0, tiled=True),
    )
    inner_width = full_qkv.shape[2]
    head_count = inner_width // HEAD_DIM
    flat_in = hidden_in.reshape(row_count, model_width)
    full_bias = jnp.stack([qv_bias[0], jnp.zeros_like(qv_bias[0]), qv_bias[1]])
    projected = (
        jnp.einsum("td,dje->tje", flat_in, full_qkv, preferred_element_type=jnp.float32) + full_bias
    ).astype(jnp.bfloat16)
    queries = projected[:, 0].reshape(seq_count, block_len, inner_width)
    key_own = projected[:, 1].reshape(seq_count, block_len, inner_width)
    value_own = projected[:, 2].reshape(seq_count, block_len, inner_width)
    keep_own = valid_mask.astype(jnp.bfloat16)
    keys_all, values_all, keep_all = (
        lax.all_gather(key_own, "ctx", axis=1, tiled=True),
        lax.all_gather(value_own, "ctx", axis=1, tiled=True),
        lax.all_gather(keep_own, "ctx", axis=1, tiled=True),
    )
    query_heads = split_heads(queries)
    seen_limit = (ctx_place + 1) * block_len
    trip_count = ctx_place // 2 + 1
    offsets = jnp.arange(key_span, dtype=jnp.int32)

    def key_block(block_index):
        key_start = block_index * key_span
        key_heads = split_heads(lax.dynamic_slice_in_dim(keys_all, key_start, key_span, 1))
        value_heads = split_heads(lax.dynamic_slice_in_dim(values_all, key_start, key_span, 1))
        live_keys = lax.dynamic_slice_in_dim(keep_all, key_start, key_span, 1) > 0.5
        allowed = jnp.logical_and(live_keys, (key_start + offsets)[None, :] < seen_limit)
        return (key_heads, value_heads, allowed[:, None, None, :])

    def attend_step(block_index, carried):
        run_top, run_total, gathered = carried
        key_heads, value_heads, allowed = key_block(block_index)
        raw_scores = scores_of(query_heads, key_heads, allowed, scaling)
        new_top = jnp.maximum(run_top, jnp.max(raw_scores, axis=-1))
        shrink = jnp.exp(run_top - new_top)
        weights_now = jnp.exp(raw_scores - new_top[..., None])
        run_total = run_total * shrink + jnp.sum(weights_now, axis=-1)
        gathered = gathered * jnp.swapaxes(shrink, 1, 2)[..., None] + jnp.einsum(
            "shqk,skhd->sqhd",
            weights_now.astype(jnp.bfloat16),
            value_heads,
            preferred_element_type=jnp.float32,
        )
        return (new_top, run_total, gathered)

    start_top = jnp.full((seq_count, head_count, block_len), MASKED, jnp.float32)
    empty_heads = jnp.zeros((seq_count, block_len, head_count, HEAD_DIM), jnp.float32)
    run_top, run_total, gathered = lax.fori_loop(
        0, trip_count, attend_step, (start_top, jnp.zeros_like(start_top), empty_heads)
    )
    log_total = run_top + jnp.log(run_total)
    attended_exact = gathered / jnp.swapaxes(run_total, 1, 2)[..., None]
    attended = attended_exact.astype(jnp.bfloat16).reshape(row_count, inner_width)
    attn_branch = lax.psum(
        jnp.einsum("te,de->td", attended, full_out, preferred_element_type=jnp.float32).astype(
            jnp.bfloat16
        ),
        "tp",
    ).astype(jnp.float32)
    resid1 = flat_in.astype(jnp.float32) + attn_branch + out_bias
    normed1, norm1_back = jax.vjp(layer_norm, resid1, norm1_gain, norm1_shift)
    normed1_low = normed1.astype(jnp.bfloat16)
    pre_act = jnp.dot(normed1_low, full_up, preferred_element_type=jnp.float32) + up_bias
    active, gelu_back = jax.vjp(gelu_exact, pre_act)
    active = active.astype(jnp.bfloat16)
    ffn_branch = lax.psum(
        jnp.einsum("tf,df->td", active, full_down, preferred_element_type=jnp.float32).astype(
            jnp.bfloat16
        ),
        "tp",
    ).astype(jnp.float32)
    resid2 = normed1 + ffn_branch + down_bias
    output, norm2_back = jax.vjp(layer_norm, resid2, norm2_gain, norm2_shift)
    layer_out = output.astype(jnp.bfloat16).reshape(seq_count, block_len, model_width)
    keep_rows = valid_mask.reshape(row_count, 1).astype(jnp.float32)
    residue = (output - teacher.reshape(row_count, model_width).astype(jnp.float32)) * keep_rows
    squared = jnp.sum(residue * residue)
    counted = jnp.sum(keep_rows)
    grad_resid2, grad_gain2, grad_shift2 = norm2_back(residue)
    grad_down_bias = jnp.sum(grad_resid2, axis=0)
    grad_resid2_low = grad_resid2.astype(jnp.bfloat16)
    grad_active = jnp.dot(grad_resid2_low, full_down, preferred_element_type=jnp.float32)
    grad_down_weight = jnp.einsum(
        "td,tf->df", grad_resid2_low, active, preferred_element_type=jnp.float32
    )
    grad_pre = gelu_back(grad_active)[0].astype(jnp.bfloat16)
    grad_up_bias = jnp.sum(grad_pre.astype(jnp.float32), axis=0)
    grad_up_weight = jnp.einsum(
        "td,tf->df", normed1_low, grad_pre, preferred_element_type=jnp.float32
    )
    ffn_input_grad = lax.psum(
        jnp.einsum("tf,df->td", grad_pre, full_up, preferred_element_type=jnp.float32).astype(
            jnp.bfloat16
        ),
        "tp",
    ).astype(jnp.float32)
    grad_normed1 = grad_resid2 + ffn_input_grad
    grad_resid1, grad_gain1, grad_shift1 = norm1_back(grad_normed1)
    grad_out_bias = jnp.sum(grad_resid1, axis=0)
    grad_resid1_low = grad_resid1.astype(jnp.bfloat16)
    grad_mixed = jnp.dot(grad_resid1_low, full_out, preferred_element_type=jnp.float32)
    grad_out_weight = jnp.einsum(
        "td,te->de", grad_resid1_low, attended, preferred_element_type=jnp.float32
    )
    grad_attended = grad_mixed.astype(jnp.bfloat16).reshape(
        seq_count, block_len, head_count, HEAD_DIM
    )
    delta = jnp.swapaxes(jnp.sum(grad_attended.astype(jnp.float32) * attended_exact, axis=-1), 1, 2)

    def query_grads(block_index):
        key_heads, value_heads, allowed = key_block(block_index)
        prob_rows = jnp.exp(
            scores_of(query_heads, key_heads, allowed, scaling) - log_total[..., None]
        )
        push = jnp.einsum(
            "sqhd,skhd->shqk", grad_attended, value_heads, preferred_element_type=jnp.float32
        )
        slope = (prob_rows * (push - delta[..., None])).astype(jnp.bfloat16)
        grad_part = (
            jnp.einsum("shqk,skhd->sqhd", slope, key_heads, preferred_element_type=jnp.float32)
            * scaling
        )
        return (prob_rows, slope, grad_part)

    def back_step(block_index, carried):
        grad_query, spread = carried
        prob_rows, slope, grad_part = query_grads(block_index)
        grad_key = (
            jnp.einsum("shqk,sqhd->skhd", slope, query_heads, preferred_element_type=jnp.float32)
            * scaling
        )
        grad_value = jnp.einsum(
            "shqk,sqhd->skhd",
            prob_rows.astype(jnp.bfloat16),
            grad_attended,
            preferred_element_type=jnp.float32,
        )
        piece = jnp.stack(
            [
                grad_key.reshape(seq_count, key_span, inner_width),
                grad_value.reshape(seq_count, key_span, inner_width),
            ],
            axis=2,
        )
        spread = lax.dynamic_update_slice_in_dim(spread, piece, block_index * key_span, 1)
        return (grad_query + grad_part, spread)

    spread_start = jnp.zeros((seq_count, seq_length, 2, inner_width), jnp.float32)
    grad_query, spread = lax.fori_loop(0, trip_count, back_step, (empty_heads, spread_start))
    own_grads = lax.psum_scatter(
        spread.astype(jnp.bfloat16), "ctx", scatter_dimension=1, tiled=True
    ).astype(jnp.float32)
    grad_key_own = own_grads[:, :, 0]
    grad_value_own = own_grads[:, :, 1]
    grad_qkv = jnp.stack(
        [
            grad_query.reshape(row_count, inner_width),
            grad_key_own.reshape(row_count, inner_width),
            grad_value_own.reshape(row_count, inner_width),
        ],
        axis=1,
    ).astype(jnp.bfloat16)
    grad_qv_bias = jnp.sum(grad_qkv[:, 0::2].astype(jnp.float32), axis=0)
    grad_qkv_weight = jnp.einsum(
        "td,tje->dje", flat_in, grad_qkv, preferred_element_type=jnp.float32
    )
    input_part = lax.psum(
        jnp.einsum("tje,dje->td", grad_qkv, full_qkv, preferred_element_type=jnp.float32).astype(
            jnp.bfloat16
        ),
        "tp",
    ).astype(jnp.float32)
    grad_input = grad_resid1 + input_part
    vectors = jnp.stack(
        [grad_out_bias, grad_gain1, grad_shift1, grad_down_bias, grad_gain2, grad_shift2]
    )
    squared, counted, vectors, grad_qv_bias, grad_up_bias = lax.psum(
        (squared, counted, vectors, grad_qv_bias, grad_up_bias), ("fsdp", "ctx")
    )
    local_grads = (grad_qkv_weight, grad_out_weight, grad_up_weight, grad_down_weight)
    owned = (
        lax.psum_scatter(
            local_grads[0].astype(jnp.bfloat16), "fsdp", scatter_dimension=0, tiled=True
        ).astype(jnp.float32),
        lax.psum_scatter(
            local_grads[1].astype(jnp.bfloat16), "fsdp", scatter_dimension=0, tiled=True
        ).astype(jnp.float32),
        lax.psum_scatter(
            local_grads[2].astype(jnp.bfloat16), "fsdp", scatter_dimension=0, tiled=True
        ).astype(jnp.float32),
        lax.psum_scatter(
            local_grads[3].astype(jnp.bfloat16), "fsdp", scatter_dimension=0, tiled=True
        ).astype(jnp.float32),
    )
    owned = (
        lax.psum(owned[0].astype(jnp.bfloat16), "ctx").astype(jnp.float32),
        lax.psum(owned[1].astype(jnp.bfloat16), "ctx").astype(jnp.float32),
        lax.psum(owned[2].astype(jnp.bfloat16), "ctx").astype(jnp.float32),
        lax.psum(owned[3].astype(jnp.bfloat16), "ctx").astype(jnp.float32),
    )
    token_total = float(seq_count * seq_length * lax.axis_size("fsdp"))
    ratio = token_total / counted
    loss = squared / (counted * model_width)
    input_grad = (grad_input * ratio).reshape(seq_count, block_len, model_width)
    return (
        layer_out,
        input_grad,
        loss,
        owned[0] * ratio,
        grad_qv_bias * ratio,
        owned[1] * ratio,
        vectors[0] * ratio,
        vectors[1] * ratio,
        vectors[2] * ratio,
        owned[2] * ratio,
        grad_up_bias * ratio,
        owned[3] * ratio,
        vectors[3] * ratio,
        vectors[4] * ratio,
        vectors[5] * ratio,
    )


def solution(mesh):
    in_specs = (
        P("fsdp", "ctx", None),
        P("fsdp", "ctx"),
        P("fsdp", "ctx", None),
        P("fsdp", None, "tp"),
        P(None, "tp"),
        P("fsdp", "tp"),
        P(),
        P(),
        P(),
        P("fsdp", "tp"),
        P("tp"),
        P("fsdp", "tp"),
        P(),
        P(),
        P(),
    )
    out_specs = (
        P("fsdp", "ctx", None),
        P("fsdp", "ctx", None),
        P(),
        P("fsdp", None, "tp"),
        P(None, "tp"),
        P("fsdp", "tp"),
        P(),
        P(),
        P(),
        P("fsdp", "tp"),
        P("tp"),
        P("fsdp", "tp"),
        P(),
        P(),
        P(),
    )
    return jax.shard_map(local, mesh=mesh, in_specs=in_specs, out_specs=out_specs, check_vma=False)
```

profile of v0, /device:TPU:0, one launch (start us, length us, event | category | flops | bytes accessed | tf_op | source)
XLA Modules:
  0.0 789.0 jit_solution(12382844192823336021)
XLA Ops:
  8.9 43.8 %all-gather.6.cloned.1.call-done = bf16[768,3,384]{2,0,1:T(8,128)(2,1)} async-done(((bf16[192,3,384]{2,0,1:T(8,128)(2,1)}), bf16[768,3,384]{2,0,1:T(8,128)(2,1)}) %all-gather.6.cloned.1.call-update) | async-done | bytes 1769488 | tf_op jit(solution)/shard_map/all_gather | solution.py:61
  52.6 4.2 add_convert_fusion.1
  59.6 8.0 %all_gather.21 = bf16[4,1024]{1,0:T(4,128)(2,1)S(1)} all-gather(bf16[4,256]{1,0:T(4,128)(2,1)S(1)} %get-tuple-element.402), channel_id=1, replica_groups=mesh['fsdp'=4,'ctx'=4,'tp'=2] {'ctx'}, dimensions={1}, use_global_device_ids=true | all-gather | bytes 10240 | tf_op jit(solution)/shard_map/all_gather | solution.py:80
  67.6 15.8 %all_gather.25 = bf16[768,384]{1,0:T(8,128)(2,1)S(1)} all-gather(bf16[192,384]{1,0:T(8,128)(2,1)S(1)} %copy-done.17), channel_id=1, replica_groups=mesh['fsdp'=4,'ctx'=4,'tp'=2] {'fsdp'}, dimensions={0}, use_global_device_ids=true | all-gather | bytes 737280 | tf_op jit(solution)/shard_map/all_gather | solution.py:62
  84.4 16.7 %all-gather.10.cloned.1.call-done = bf16[4,1024,384]{1,2,0:T(8,128)(2,1)} async-done(((bf16[4,256,384]{1,2,0:T(8,128)(2,1)}), bf16[4,1024,384]{1,2,0:T(8,128)(2,1)}) %all-gather.10.cloned.1.call-update) | async-done | bytes 3145744 | tf_op jit(solution)/shard_map/all_gather | solution.py:79
  101.1 46.3 %all-gather.8.cloned.1.call-done = bf16[4,1024,384]{1,2,0:T(8,128)(2,1)} async-done(((bf16[4,256,384]{1,2,0:T(8,128)(2,1)}), bf16[4,1024,384]{1,2,0:T(8,128)(2,1)}) %all-gather.8.cloned.1.call-update) | async-done | bytes 3145744 | tf_op jit(solution)/shard_map/all_gather | solution.py:78
  147.6 12.4 %while.28 = (s32[]{:T(128)}, f32[4,6,256]{2,1,0:T(8,128)S(1)}, f32[4,6,256]{2,1,0:T(8,128)S(1)}, f32[4,256,6,64]{1,3,2,0:T(8,128)S(1)}, s32[]{:T(128)}, /*index=...) while((s32[]{:T(128)}, f32[4,6,256]{2,1,0:T(8,128)S(1)}, ...), condition=%wide.region_3.4_spmd.clone, body=%wide.region_0.3_spmd.clone.sunk | while | flops 840723456 | bytes 51524800 | solution.py:113
  149.7 3.1 bitcast_reduce_fusion.2
  152.8 3.5 bitcast_add_fusion.4
  156.4 3.5 fusion.115
  162.1 2.2 convolution_convert_fusion.3
  166.0 31.2 %all-reduce.8.cloned.1.call-done = bf16[1024,768]{1,0:T(8,128)(2,1)} async-done(((bf16[1024,768]{1,0:T(8,128)(2,1)}), bf16[1024,768]{1,0:T(8,128)(2,1)}) %all-reduce.8.cloned.1.call-update) | async-done | bytes 1572880 | tf_op jit(solution)/shard_map/psum | solution.py:119
  197.2 2.6 fusion.34
  200.0 2.5 multiply_reduce_fusion.6
  202.5 47.8 %all-gather.12.cloned.1.call-done = bf16[768,1536]{1,0:T(8,128)(2,1)} async-done(((bf16[192,1536]{1,0:T(8,128)(2,1)}), bf16[768,1536]{1,0:T(8,128)(2,1)}) %all-gather.12.cloned.1.call-update) | async-done | bytes 2359312 | tf_op jit(solution)/shard_map/all_gather | solution.py:63
  250.4 19.7 %multiply_convert_fusion.1 = (bf16[1024,1536]{1,0:T(8,128)(2,1)}, f32[1024,1536]{1,0:T(8,128)}, f32[1024,1536]{1,0:T(8,128)}) fusion(f32[1536]{0:T(1024)S(1)} %copy-done.42, bf16[768,1536]{1,0:T(8,128)(2,1)} %all-gather.12.cloned.1.call-done, f32[1024,768]{1,0:T(8,128)} %get-tuple-element.388, f32[768]{0:T(1024)S(1)} %copy-done.38, f32[768]{0:T(1024)S(1)} %copy-done.20, ...), kind=kOutput, calls=%fused_computation.43 | convolution fusion | flops 2522873856 | bytes 21250048 | tf_op jit(solution)/shard_map/dot_general | solution.py:128
  270.1 31.1 %all-gather.14.cloned.1.call-done = bf16[768,1536]{1,0:T(8,128)(2,1)} async-done(((bf16[192,1536]{1,0:T(8,128)(2,1)}), bf16[768,1536]{1,0:T(8,128)(2,1)}) %all-gather.14.cloned.1.call-update) | async-done | bytes 2359312 | tf_op jit(solution)/shard_map/all_gather | solution.py:64
  301.2 6.4 convolution_convert_fusion.5
  307.9 19.1 %all-reduce.10.cloned.1.call-done = bf16[1024,768]{1,0:T(8,128)(2,1)} async-done(((bf16[1024,768]{1,0:T(8,128)(2,1)}), bf16[1024,768]{1,0:T(8,128)(2,1)}) %all-reduce.10.cloned.1.call-update) | async-done | bytes 1572880 | tf_op jit(solution)/shard_map/psum | solution.py:131
  327.0 3.5 fusion.54
  331.9 3.3 fusion.51
  335.2 2.9 fusion.53
  338.1 8.5 %convert_reduce_fusion = (f32[1536]{0:T(1024)}, bf16[1024,1536]{1,0:T(8,128)(2,1)S(1)}) fusion(f32[1024,1536]{1,0:T(8,128)S(1)} %bitcast.183, bf16[768,1536]{1,0:T(8,128)(2,1)S(1)} %copy-done.41, f32[1024,768]{1,0:T(8,128)S(1)} %get-tuple-element.382, f32[1024]{0:T(1024)S(1)} %negate_multiply_fusion.2, f32[1024,1536]{1,0:T(8,128)} %get-tuple-element.405, ...), kind=kOutput, calls=%fused_computation.41 | convolution fusion | flops 2444229120 | bytes 21250048 | tf_op jit(solution)/shard_map/dot_general | solution.py:147
  348.3 3.7 convolution_convert_fusion.4
  352.3 21.4 %all-reduce.12.cloned.1.call-done = bf16[1024,768]{1,0:T(8,128)(2,1)} async-done(((bf16[1024,768]{1,0:T(8,128)(2,1)}), bf16[1024,768]{1,0:T(8,128)(2,1)}) %all-reduce.12.cloned.1.call-update) | async-done | bytes 1572880 | tf_op jit(solution)/shard_map/psum | solution.py:156
  373.8 4.9 multiply_reduce_fusion.1
  389.1 3.4 broadcast_in_dim.72
  392.5 19.5 %while.29 = (s32[]{:T(128)}, f32[4,256,6,64]{1,3,2,0:T(8,128)S(1)}, bf16[4,1024,2,384]{1,3,0,2:T(8,128)(2,1)}, s32[]{:T(128)}, bf16[4,1024,384]{1,2,0:T(8,128)(2...) while((s32[]{:T(128)}, f32[4,256,6,64]{1,3,2,0:T(8,128)S(1)}, ...), condition=%wide.region_17.18_spmd.clone, body=%wide.region_16.17_spmd.clone.sunk | while | flops 2053383168 | bytes 83447000 | solution.py:214
  392.8 3.4 constant_dynamic-slice_fusion.7
  398.1 3.0 fusion.128
  401.1 5.6 multiply_convert_fusion.3
  414.1 88.8 %reduce-scatter.8.cloned.1.call-done = bf16[4,256,2,384]{1,3,0,2:T(8,128)(2,1)} async-done(((bf16[4,1024,2,384]{1,3,0,2:T(8,128)(2,1)}), bf16[4,256,2,384]{1,3,0,2:T(8,128)(2,1)}) %reduce-scatter.8.cloned.1.call-update) | async-done | bytes 1572880 | tf_op jit(solution)/shard_map/reduce_scatter | solution.py:215
  502.8 2.6 fusion.58
  506.9 2.3 copy.71
  509.2 4.5 convolution_convert_fusion.2
  513.7 3.9 copy.79
  517.7 4.0 convolution_convert_fusion.7
  521.8 7.3 convolution_convert_fusion
  529.3 7.2 convolution_convert_fusion.1
  536.9 4.9 bitcast_convert_fusion
  541.9 14.3 %reduce-scatter.16.cloned.1.call-done = bf16[192,1152]{1,0:T(8,128)(2,1)} async-done(((bf16[768,1152]{1,0:T(8,128)(2,1)}), bf16[192,1152]{1,0:T(8,128)(2,1)}) %reduce-scatter.16.cloned.1.call-update) | async-done | bytes 442384
  558.2 21.9 %reduce-scatter.10.cloned.1.call-done = bf16[192,384]{1,0:T(8,128)(2,1)} async-done(((bf16[768,384]{1,0:T(8,128)(2,1)}), bf16[192,384]{1,0:T(8,128)(2,1)}) %reduce-scatter.10.cloned.1.call-update) | async-done | bytes 147472 | tf_op jit(solution)/shard_map/reduce_scatter | solution.py:250
  580.2 48.5 %reduce-scatter.14.cloned.1.call-done = bf16[192,1536]{1,0:T(8,128)(2,1)} async-done(((bf16[768,1536]{1,0:T(8,128)(2,1)}), bf16[192,1536]{1,0:T(8,128)(2,1)}) %reduce-scatter.14.cloned.1.call-update) | async-done | bytes 589840 | tf_op jit(solution)/shard_map/reduce_scatter | solution.py:256
  628.7 49.9 %reduce-scatter.12.cloned.1.call-done = bf16[192,1536]{1,0:T(8,128)(2,1)} async-done(((bf16[768,1536]{1,0:T(8,128)(2,1)}), bf16[192,1536]{1,0:T(8,128)(2,1)}) %reduce-scatter.12.cloned.1.call-update) | async-done | bytes 589840 | tf_op jit(solution)/shard_map/reduce_scatter | solution.py:253
  679.3 2.2 add_reduce_fusion
  682.2 77.0 %all-reduce = (f32[]{:T(128)}, f32[]{:T(128)}, f32[2,384]{1,0:T(2,128)S(1)}, f32[6,768]{1,0:T(8,128)S(1)}, f32[1536]{0:T(1024)S(1)}) all-reduce(f32[]{:T(128)} %convert_reduce_fusion.2, f32[]{:T(128)} %get-tuple-element.313, f32[2,384]{1,0:T(2,128)S(1)} %convert_reduce_fusion.1, ...), channel_id=1, replica_groups=mesh['fsdp'=4,'ctx'=4,'tp'=2] {'fsdp','ctx'}, use_global_device_ids=true, to_apply=%region_21.22 | all-reduce | flops 6914 | bytes 55312 | tf_op jit(solution)/shard_map/psum | solution.py:242
  763.0 4.7 add_multiply_fusion
  767.8 7.1 all-reduce.16.cloned.1.call-done
  (194 shorter events, 48.0 us)
Async XLA Ops:
  7.2 45.5 %all-gather.6.cloned.1.call-start = ((), (), s32[]{:S(2)}) async-start(), calls=%async_computation.5 | async-start | bytes 2211840 | tf_op jit(solution)/shard_map/all_gather | solution.py:61
  7.9 93.2 %all-gather.10.cloned.1.call-start = ((), (), s32[]{:S(2)}) async-start(), calls=%async_computation.7 | async-start | bytes 3932160 | tf_op jit(solution)/shard_map/all_gather | solution.py:79
  57.0 10.6 %copy-start.17 = (bf16[192,384]{1,0:T(8,128)(2,1)S(1)}, bf16[192,384]{1,0:T(8,128)(2,1)}, u32[]{:S(2)}) copy-start(bf16[192,384]{1,0:T(8,128)(2,1)} %param.24) | copy-start | bytes 442372
  58.2 89.1 %all-gather.8.cloned.1.call-start = ((), (), s32[]{:S(2)}) async-start(), calls=%async_computation.6 | async-start | bytes 3932160 | tf_op jit(solution)/shard_map/all_gather | solution.py:78
  59.5 137.7 %all-reduce.8.cloned.1.call-start = ((), (), s32[]{:S(2)}) async-start(), calls=%async_computation.8 | async-start | bytes 3145728 | tf_op jit(solution)/shard_map/psum | solution.py:119
  83.4 77.8 %copy-start.13 = (bf16[768,384]{1,0:T(8,128)(2,1)}, bf16[768,384]{1,0:T(8,128)(2,1)S(1)}, u32[]{:S(2)}) copy-start(bf16[768,384]{1,0:T(8,128)(2,1)S(1)} %all_gather.25) | copy-start | bytes 1769476
  161.2 36.0 %copy-start.35 = (f32[768]{0:T(1024)S(1)}, f32[768]{0:T(1024)}, u32[]{:S(2)}) copy-start(f32[768]{0:T(1024)} %param.25) | copy-start | bytes 9220
  164.2 86.1 %all-gather.12.cloned.1.call-start = ((), (), s32[]{:S(2)}) async-start(), calls=%async_computation.9 | async-start | bytes 2949120 | tf_op jit(solution)/shard_map/all_gather | solution.py:63
  164.8 136.4 %all-gather.14.cloned.1.call-start = ((), (), s32[]{:S(2)}) async-start(), calls=%async_computation.10 | async-start | bytes 2949120 | tf_op jit(solution)/shard_map/all_gather | solution.py:64
  165.4 161.6 %all-reduce.10.cloned.1.call-start = ((), (), s32[]{:S(2)}) async-start(), calls=%async_computation.11 | async-start | bytes 3145728 | tf_op jit(solution)/shard_map/psum | solution.py:131
  200.0 50.4 %copy-start.20 = (f32[768]{0:T(1024)S(1)}, f32[768]{0:T(1024)}, u32[]{:S(2)}) copy-start(f32[768]{0:T(1024)} %param.26) | copy-start | bytes 9220
  200.0 50.4 %copy-start.38 = (f32[768]{0:T(1024)S(1)}, f32[768]{0:T(1024)}, u32[]{:S(2)}) copy-start(f32[768]{0:T(1024)} %param.27) | copy-start | bytes 9220
  200.0 50.4 %copy-start.42 = (f32[1536]{0:T(1024)S(1)}, f32[1536]{0:T(1024)}, u32[]{:S(2)}) copy-start(f32[1536]{0:T(1024)} %param.29) | copy-start | bytes 18436
  202.5 176.1 %copy-start.18 = (f32[1024]{0:T(1024)}, f32[1024]{0:T(1024)S(1)}, u32[]{:S(2)}) copy-start(f32[1024]{0:T(1024)S(1)} %fusion.37) | copy-start | bytes 12292
  301.2 25.8 %copy-start.37 = (f32[768]{0:T(1024)S(1)}, f32[768]{0:T(1024)}, u32[]{:S(2)}) copy-start(f32[768]{0:T(1024)} %param.31) | copy-start | bytes 9220
  307.6 66.1 %all-reduce.12.cloned.1.call-start = ((), (), s32[]{:S(2)}) async-start(), calls=%async_computation.12 | async-start | bytes 3145728 | tf_op jit(solution)/shard_map/psum | solution.py:156
  327.0 11.1 %slice-start = ((s8[6291456]{0:T(1024)(128)(4,1)}), s8[4194304]{0:T(1024)(128)(4,1)S(1)}, s32[]{:S(2)}) async-start(s8[6291456]{0:T(1024)(128)(4,1)} %bitcast.182), calls=%async_computation.20 | async-start | bytes 8388608
  331.9 6.2 slice-start.1
  338.1 8.6 %copy-start.2 = (f32[1024,768]{1,0:T(8,128)}, f32[1024,768]{1,0:T(8,128)S(1)}, u32[]{:S(2)}) copy-start(f32[1024,768]{1,0:T(8,128)S(1)} %get-tuple-element.382) | copy-start | bytes 9437188
  338.1 40.6 %copy-start.24 = (f32[1024]{0:T(1024)}, f32[1024]{0:T(1024)S(1)}, u32[]{:S(2)}) copy-start(f32[1024]{0:T(1024)S(1)} %negate_multiply_fusion.2) | copy-start | bytes 12292
  338.1 10.1 %copy-start.40 = (bf16[768,1536]{1,0:T(8,128)(2,1)S(1)}, bf16[768,1536]{1,0:T(8,128)(2,1)}, u32[]{:S(2)}) copy-start(bf16[768,1536]{1,0:T(8,128)(2,1)} %all-gather.12.cloned.1.call-done) | copy-start | bytes 7077892
  352.0 150.8 %reduce-scatter.8.cloned.1.call-start = ((), (), s32[]{:S(2)}) async-start(), calls=%async_computation.13 | async-start | bytes 7864320 | tf_op jit(solution)/shard_map/reduce_scatter | solution.py:215
  373.8 4.9 copy-start
  373.8 5.2 copy-start.3
  373.8 5.6 copy-start.5
  389.1 3.5 copy-start.12
  412.0 144.1 %reduce-scatter.16.cloned.1.call-start = ((), (), s32[]{:S(2)}) async-start(), calls=%async_computation.18 | async-start | bytes 2211840
  414.0 95.2 %copy-start.7 = (bf16[4,256,768]{2,1,0:T(8,128)(2,1)S(1)}, bf16[4,256,768]{2,1,0:T(8,128)(2,1)}, u32[]{:S(2)}) copy-start(bf16[4,256,768]{2,1,0:T(8,128)(2,1)} %param.19) | copy-start | bytes 4718596
  513.7 4.0 copy-start.11
  513.7 4.0 copy-start.23
  517.6 4.2 copy-start.25
  517.7 62.5 %reduce-scatter.10.cloned.1.call-start = ((), (), s32[]{:S(2)}) async-start(), calls=%async_computation.15 | async-start | bytes 737280 | tf_op jit(solution)/shard_map/reduce_scatter | solution.py:250
  521.7 7.5 copy-start.19
  521.7 7.5 copy-start.21
  521.8 7.5 copy-start.39
  521.8 106.9 %reduce-scatter.14.cloned.1.call-start = ((), (), s32[]{:S(2)}) async-start(), calls=%async_computation.17 | async-start | bytes 2949120 | tf_op jit(solution)/shard_map/reduce_scatter | solution.py:256
  529.2 7.7 copy-start.9
  529.2 149.4 %reduce-scatter.12.cloned.1.call-start = ((), (), s32[]{:S(2)}) async-start(), calls=%async_computation.16 | async-start | bytes 2949120 | tf_op jit(solution)/shard_map/reduce_scatter | solution.py:253
  536.5 226.5 %all-reduce.14.cloned.1.call-start = ((), (), s32[]{:S(2)}) async-start(), calls=%async_computation.14 | async-start | bytes 3145728 | tf_op jit(solution)/shard_map/psum | solution.py:232
  541.7 136.8 %copy-start.34 = (s32[4,256]{1,0:T(4,128)S(1)}, s32[4,256]{1,0:T(4,128)}, u32[]{:S(2)}) copy-start(s32[4,256]{1,0:T(4,128)} %param.20) | copy-start | bytes 12292
  541.7 137.5 %copy-start.29 = (f32[768]{0:T(1024)S(1)}, f32[768]{0:T(1024)}, u32[]{:S(2)}) copy-start(f32[768]{0:T(1024)} %get-tuple-element.312) | copy-start | bytes 9220
  541.8 137.5 %copy-start.28 = (f32[768]{0:T(1024)S(1)}, f32[768]{0:T(1024)}, u32[]{:S(2)}) copy-start(f32[768]{0:T(1024)} %get-tuple-element.314) | copy-start | bytes 9220
  541.8 137.5 %copy-start.32 = (f32[768]{0:T(1024)S(1)}, f32[768]{0:T(1024)}, u32[]{:S(2)}) copy-start(f32[768]{0:T(1024)} %get-tuple-element.310) | copy-start | bytes 9220
  541.8 137.5 %copy-start.31 = (f32[768]{0:T(1024)S(1)}, f32[768]{0:T(1024)}, u32[]{:S(2)}) copy-start(f32[768]{0:T(1024)} %get-tuple-element.316) | copy-start | bytes 9220
  541.8 137.5 %copy-start.30 = (f32[768]{0:T(1024)S(1)}, f32[768]{0:T(1024)}, u32[]{:S(2)}) copy-start(f32[768]{0:T(1024)} %get-tuple-element.317) | copy-start | bytes 9220
  541.8 233.0 %all-reduce.16.cloned.1.call-start = ((), (), s32[]{:S(2)}) async-start(), calls=%async_computation.19 | async-start | bytes 3833856 | tf_op jit(solution)/shard_map/psum | solution.py:261
  774.9 4.2 copy-start.15
  774.9 4.2 copy-start.16
  (13 other events, 24.9 us)
Sparse Core Ops, SparseCore 0:
  9.6 43.0 all-gather.5
  58.4 42.6 all-gather.9
  103.5 43.8 all-gather.7
  164.4 32.7 all-reduce.7
  198.7 51.6 all-gather.11
  251.9 49.2 all-gather.13
  307.8 19.1 all-reduce.9
  352.1 21.5 all-reduce.11
  412.2 90.6 reduce-scatter.7
  517.8 38.3 reduce-scatter.15
  559.0 21.1 reduce-scatter.9
  582.3 46.3 reduce-scatter.13
  631.0 47.5 reduce-scatter.11
  681.3 19.8 all-reduce.13
  705.6 69.1 all-reduce.15
where the time goes:
time: 797 us; the launch traced here: 789 us
  waiting for transfers between devices  490 us (61%)
  blocking collectives  101 us (13%)
  matrix products  93.8 us (12%)
  other arithmetic  44.3 us (6%)
  local copies, waits for them, and re-layouts  39.4 us (5%)
  between operations  18.3 us (2%)
    reduce_scatter x1, waiting for transfers between devices, local(): lax.psum_scatter(spread.astype(jnp.bfloat16), 'ctx', scatter_dimension=1,...  88.8 us
    psum x1, blocking collectives, local(): lax.psum((squared, counted, vectors, grad_qv_bias, grad_up_bias), ('fsdp'...  77 us
    reduce_scatter x1, waiting for transfers between devices, local(): lax.psum_scatter(local_grads[2].astype(jnp.bfloat16), 'fsdp', scatter_dim...  49.9 us
    reduce_scatter x1, waiting for transfers between devices, local(): lax.psum_scatter(local_grads[3].astype(jnp.bfloat16), 'fsdp', scatter_dim...  48.5 us
    all_gather x1, waiting for transfers between devices, local(): lax.all_gather(up_weight, 'fsdp', axis=0, tiled=True)  47.8 us
    all_gather x1, waiting for transfers between devices, local(): lax.all_gather(key_own, 'ctx', axis=1, tiled=True)  46.3 us
    all_gather x1, waiting for transfers between devices, local(): lax.all_gather(qkv_weight, 'fsdp', axis=0, tiled=True)  43.8 us
    psum x1, waiting for transfers between devices, local(): lax.psum(jnp.einsum('te,de->td', attended, full_out, preferred_element_ty...  31.2 us
  transfers between devices with their start and end apart: 15, of which 14 were waited for; matrix products, arithmetic and copies ran while one was open for 8% of the time, Pallas kernels for 0%

commit v1 on v0

v1 whole, which is shorter than its diff:
```python
import jax
import jax.numpy as jnp
from jax import lax
from jax.experimental import pallas as pl
from jax.experimental.pallas import tpu as pltpu
from jax.sharding import PartitionSpec as P

HEAD_DIM = 64
NORM_EPS = 1e-05
MASKED = -1e30
LANES = 128


def layer_norm(values_in, gain_vec, shift_vec):
    row_mean = jnp.mean(values_in, axis=-1, keepdims=True)
    centered = values_in - row_mean
    row_var = jnp.mean(centered * centered, axis=-1, keepdims=True)
    return centered * lax.rsqrt(row_var + NORM_EPS) * gain_vec + shift_vec


def gelu_exact(pre_act):
    return jax.nn.gelu(pre_act, approximate=False)


def split_heads(packed):
    return packed.reshape(packed.shape[0], packed.shape[1], packed.shape[2] // HEAD_DIM, HEAD_DIM)


def scores_of(query_heads, key_heads, allowed, scaling):
    raw_scores = (
        jnp.einsum("sqhd,skhd->shqk", query_heads, key_heads, preferred_element_type=jnp.float32)
        * scaling
    )
    return jnp.where(allowed, raw_scores, MASKED)


def rows_by_rows(left, right):
    return lax.dot_general(left, right, (((1,), (1,)), ((), ())), preferred_element_type=jnp.float32)


def plain_dot(left, right):
    return jnp.dot(left, right, preferred_element_type=jnp.float32)


def lanes_of(head, lane):
    own = (lane < HEAD_DIM) if head == 0 else (lane >= HEAD_DIM)
    spare = HEAD_DIM if head == 0 else 0
    return own, lane == spare


def head_operands(query_ref, key_ref, slot, start, block, valid_count, head):
    lane = lax.broadcasted_iota(jnp.int32, (block, LANES), 1)
    own, spare = lanes_of(head, lane)
    position = start + lax.broadcasted_iota(jnp.int32, (block, LANES), 0)
    bias = jnp.where(position < valid_count, 0.0, MASKED)
    rows = pl.ds(slot * block, block)
    query = query_ref[rows, :].astype(jnp.float32) * (HEAD_DIM ** -0.5)
    key = key_ref[rows, :].astype(jnp.float32)
    query_side = jnp.where(spare, 1.0, query).astype(jnp.bfloat16)
    key_side = jnp.where(own, key, jnp.where(spare, bias, 0.0)).astype(jnp.bfloat16)
    return query_side, key_side


def attend_kernel(facts, query_ref, key_ref, value_ref, out_ref, log_ref, *, block):
    place, valid_count = facts[0], facts[1]
    blocks = query_ref.shape[0] // block
    slots = [lax.bitwise_xor(place, jnp.int32(i)) for i in range(blocks)]
    value_t = [
        value_ref[pl.ds(slots[j] * block, block), :].astype(jnp.float32).T.astype(jnp.bfloat16)
        for j in range(blocks)
    ]
    outs = [[] for _ in range(blocks)]
    for head in range(2):
        sides = [
            head_operands(query_ref, key_ref, slots[j], j * block, block, valid_count, head)
            for j in range(blocks)
        ]
        span = slice(head * HEAD_DIM, (head + 1) * HEAD_DIM)
        for i in range(blocks):
            scores = [rows_by_rows(sides[j][1], sides[i][0]) for j in range(i + 1)]
            top = scores[0].max(axis=0, keepdims=True)
            for j in range(1, i + 1):
                top = jnp.maximum(top, scores[j].max(axis=0, keepdims=True))
            total = jnp.zeros_like(top)
            mixed = jnp.zeros((HEAD_DIM, block), jnp.float32)
            for j in range(i + 1):
                weight = jnp.exp(scores[j] - top)
                total = total + weight.sum(axis=0, keepdims=True)
                mixed = mixed + plain_dot(value_t[j][span, :], weight.astype(jnp.bfloat16))
            outs[i].append(mixed / total)
            log_ref[0, head : head + 1, i * block : (i + 1) * block] = top + jnp.log(total)
    for i in range(blocks):
        both = jnp.concatenate(outs[i], axis=0)
        out_ref[pl.ds(slots[i] * block, block), :] = both.T.astype(out_ref.dtype)


def attend_back_kernel(
    facts, query_ref, key_ref, value_ref, grad_ref, log_ref, out_ref, grad_key, grad_value, *, block
):
    place, valid_count = facts[0], facts[1]
    blocks = query_ref.shape[0] // block
    slots = [lax.bitwise_xor(place, jnp.int32(i)) for i in range(blocks)]
    scaling = HEAD_DIM ** -0.5
    lane = lax.broadcasted_iota(jnp.int32, (block, LANES), 1)
    key_t, grads, queries, values = [], [], [], []
    for j in range(blocks):
        rows = pl.ds(slots[j] * block, block)
        key_t.append((key_ref[rows, :].astype(jnp.float32) * scaling).T.astype(jnp.bfloat16))
        grads.append(grad_ref[rows, :])
        queries.append(query_ref[rows, :].astype(jnp.float32) * scaling)
        values.append(value_ref[rows, :].astype(jnp.float32))
    grad_queries = [[] for _ in range(blocks)]
    for head in range(2):
        own, _ = lanes_of(head, lane)
        span = slice(head * HEAD_DIM, (head + 1) * HEAD_DIM)
        sides = [
            head_operands(query_ref, key_ref, slots[j], j * block, block, valid_count, head)
            for j in range(blocks)
        ]
        head_values = [jnp.where(own, item, 0.0).astype(jnp.bfloat16) for item in values]
        for i in range(blocks):
            log_row = log_ref[0, head : head + 1, i * block : (i + 1) * block]
            head_grad = jnp.where(own, grads[i].astype(jnp.float32), 0.0).astype(jnp.bfloat16)
            head_query = jnp.where(own, queries[i], 0.0).astype(jnp.bfloat16)
            probs, pushes = [], []
            delta = jnp.zeros((1, block), jnp.float32)
            for j in range(i + 1):
                prob = jnp.exp(rows_by_rows(sides[j][1], sides[i][0]) - log_row)
                push = rows_by_rows(head_values[j], grads[i])
                delta = delta + (prob * push).sum(axis=0, keepdims=True)
                probs.append(prob)
                pushes.append(push)
            grad_query = jnp.zeros((HEAD_DIM, block), jnp.float32)
            for j in range(i + 1):
                slope = (probs[j] * (pushes[j] - delta)).astype(jnp.bfloat16)
                part_value = plain_dot(probs[j].astype(jnp.bfloat16), head_grad)
                part_key = plain_dot(slope, head_query)
                span_rows = slice(j * block, (j + 1) * block)
                if head == 0 and i == j:
                    grad_value[span_rows, :] = part_value
                    grad_key[span_rows, :] = part_key
                else:
                    grad_value[span_rows, :] += part_value
                    grad_key[span_rows, :] += part_key
                grad_query = grad_query + plain_dot(key_t[j][span, :], slope)
            grad_queries[i].append(grad_query)
    for i in range(blocks):
        rows = pl.ds(slots[i] * block, block)
        both = jnp.concatenate(grad_queries[i], axis=0)
        out_ref[0, rows, :] = both.T.astype(out_ref.dtype)
        span_rows = slice(i * block, (i + 1) * block)
        out_ref[1, rows, :] = grad_key[span_rows, :].astype(out_ref.dtype)
        out_ref[2, rows, :] = grad_value[span_rows, :].astype(out_ref.dtype)


def attend(facts, projected, block):
    length, width = projected.shape
    width = width // 3
    pairs = width // LANES
    column = lambda kind: pl.BlockSpec((length, LANES), lambda pair, facts: (0, kind * pairs + pair))
    return pl.pallas_call(
        lambda *refs: attend_kernel(*refs, block=block),
        grid_spec=pltpu.PrefetchScalarGridSpec(
            num_scalar_prefetch=1,
            grid=(pairs,),
            in_specs=[column(0), column(1), column(2)],
            out_specs=[
                pl.BlockSpec((length, LANES), lambda pair, facts: (0, pair)),
                pl.BlockSpec((1, 2, length), lambda pair, facts: (pair, 0, 0)),
            ],
        ),
        out_shape=[
            jax.ShapeDtypeStruct((length, width), jnp.bfloat16),
            jax.ShapeDtypeStruct((pairs, 2, length), jnp.float32),
        ],
        name="attend",
    )(facts, projected, projected, projected)


def attend_back(facts, projected, grad_attended, log_total, block):
    length, width = grad_attended.shape
    pairs = width // LANES
    column = lambda kind: pl.BlockSpec((length, LANES), lambda pair, facts: (0, kind * pairs + pair))
    return pl.pallas_call(
        lambda *refs: attend_back_kernel(*refs, block=block),
        grid_spec=pltpu.PrefetchScalarGridSpec(
            num_scalar_prefetch=1,
            grid=(pairs,),
            in_specs=[
                column(0),
                column(1),
                column(2),
                pl.BlockSpec((length, LANES), lambda pair, facts: (0, pair)),
                pl.BlockSpec((1, 2, length), lambda pair, facts: (pair, 0, 0)),
            ],
            out_specs=pl.BlockSpec((3, length, LANES), lambda pair, facts: (0, 0, pair)),
            scratch_shapes=[
                pltpu.VMEM((length, LANES), jnp.float32),
                pltpu.VMEM((length, LANES), jnp.float32),
            ],
        ),
        out_shape=jax.ShapeDtypeStruct((3, length, width), jnp.bfloat16),
        name="attend_back",
    )(facts, projected, projected, projected, grad_attended, log_total)


def swaps(count, step):
    return [(place, place ^ step) for place in range(count)]


def swap(values, axis, step):
    return lax.ppermute(values, axis, swaps(lax.axis_size(axis), step))


def add_partner(values, axis="tp"):
    low = values.astype(jnp.bfloat16)
    if lax.axis_size(axis) != 2:
        return lax.psum(low, axis).astype(jnp.float32)
    return low.astype(jnp.float32) + swap(low, axis, 1).astype(jnp.float32)


def butterfly(values, axes):
    for axis in axes:
        count = lax.axis_size(axis)
        step = 1
        while step < count:
            values = values + swap(values, axis, step)
            step *= 2
    return values


def to_sequences(blocks, place):
    count = blocks.shape[0]
    pieces = [lax.dynamic_index_in_dim(blocks, place ^ s, 0, keepdims=False) for s in range(count)]
    pieces = [pieces[0]] + [swap(pieces[s], "ctx", s) for s in range(1, count)]
    return jnp.concatenate(pieces, axis=0)


def from_sequences(rows, place, count):
    pieces = jnp.split(rows, count, axis=0)
    pieces = [pieces[0]] + [swap(pieces[s], "ctx", s) for s in range(1, count)]
    result = jnp.zeros((count,) + pieces[0].shape, rows.dtype)
    for s in range(count):
        result = lax.dynamic_update_index_in_dim(result, pieces[s], place ^ s, 0)
    return result


def reduce_over_ctx(owned):
    count = lax.axis_size("ctx")
    rows = owned.shape[0] // count
    if owned.shape[0] % count or rows % 8 or count & (count - 1):
        return lax.psum(owned, "ctx").astype(jnp.float32)
    place = lax.axis_index("ctx")
    parts = owned.reshape((count, rows) + owned.shape[1:])
    total = lax.dynamic_index_in_dim(parts, place, 0, keepdims=False).astype(jnp.float32)
    for s in range(1, count):
        piece = lax.dynamic_index_in_dim(parts, place ^ s, 0, keepdims=False)
        total = total + swap(piece, "ctx", s).astype(jnp.float32)
    total = total.astype(jnp.bfloat16)
    result = jnp.zeros(parts.shape, jnp.bfloat16)
    result = lax.dynamic_update_index_in_dim(result, total, place, 0)
    for s in range(1, count):
        result = lax.dynamic_update_index_in_dim(result, swap(total, "ctx", s), place ^ s, 0)
    return result.reshape(owned.shape).astype(jnp.float32)


def key_blocks_over_ctx(projected, valid_mask, seq_count, block_len):
    inner_width = projected.shape[1] // 3
    ctx_place = lax.axis_index("ctx")
    key_span = 2 * block_len
    key_own = projected[:, inner_width : 2 * inner_width].reshape(seq_count, block_len, inner_width)
    value_own = projected[:, 2 * inner_width :].reshape(seq_count, block_len, inner_width)
    keep_own = valid_mask.astype(jnp.bfloat16)
    keys_all, values_all, keep_all = (
        lax.all_gather(key_own, "ctx", axis=1, tiled=True),
        lax.all_gather(value_own, "ctx", axis=1, tiled=True),
        lax.all_gather(keep_own, "ctx", axis=1, tiled=True),
    )
    seen_limit = (ctx_place + 1) * block_len
    offsets = jnp.arange(key_span, dtype=jnp.int32)

    def key_block(block_index):
        key_start = block_index * key_span
        key_heads = split_heads(lax.dynamic_slice_in_dim(keys_all, key_start, key_span, 1))
        value_heads = split_heads(lax.dynamic_slice_in_dim(values_all, key_start, key_span, 1))
        live_keys = lax.dynamic_slice_in_dim(keep_all, key_start, key_span, 1) > 0.5
        allowed = jnp.logical_and(live_keys, (key_start + offsets)[None, :] < seen_limit)
        return (key_heads, value_heads, allowed[:, None, None, :])

    return key_block


def spread_attend(projected, key_block, seq_count, block_len):
    inner_width = projected.shape[1] // 3
    head_count = inner_width // HEAD_DIM
    scaling = HEAD_DIM ** (-0.5)
    trip_count = lax.axis_index("ctx") // 2 + 1
    query_heads = split_heads(projected[:, :inner_width].reshape(seq_count, block_len, inner_width))

    def attend_step(block_index, carried):
        run_top, run_total, gathered = carried
        key_heads, value_heads, allowed = key_block(block_index)
        raw_scores = scores_of(query_heads, key_heads, allowed, scaling)
        new_top = jnp.maximum(run_top, jnp.max(raw_scores, axis=-1))
        shrink = jnp.exp(run_top - new_top)
        weights_now = jnp.exp(raw_scores - new_top[..., None])
        run_total = run_total * shrink + jnp.sum(weights_now, axis=-1)
        gathered = gathered * jnp.swapaxes(shrink, 1, 2)[..., None] + jnp.einsum(
            "shqk,skhd->sqhd",
            weights_now.astype(jnp.bfloat16),
            value_heads,
            preferred_element_type=jnp.float32,
        )
        return (new_top, run_total, gathered)

    start_top = jnp.full((seq_count, head_count, block_len), MASKED, jnp.float32)
    empty_heads = jnp.zeros((seq_count, block_len, head_count, HEAD_DIM), jnp.float32)
    run_top, run_total, gathered = lax.fori_loop(
        0, trip_count, attend_step, (start_top, jnp.zeros_like(start_top), empty_heads)
    )
    log_total = run_top + jnp.log(run_total)
    attended_exact = gathered / jnp.swapaxes(run_total, 1, 2)[..., None]
    attended = attended_exact.astype(jnp.bfloat16).reshape(seq_count * block_len, inner_width)
    return attended, (attended_exact, log_total)


def spread_attend_back(projected, grad_attended, kept, key_block, seq_count, block_len):
    attended_exact, log_total = kept
    inner_width = projected.shape[1] // 3
    head_count = inner_width // HEAD_DIM
    scaling = HEAD_DIM ** (-0.5)
    ctx_place = lax.axis_index("ctx")
    trip_count = ctx_place // 2 + 1
    key_span = 2 * block_len
    seq_length = block_len * lax.axis_size("ctx")
    row_count = seq_count * block_len
    query_heads = split_heads(projected[:, :inner_width].reshape(seq_count, block_len, inner_width))
    grad_attended = grad_attended.reshape(seq_count, block_len, head_count, HEAD_DIM)
    delta = jnp.swapaxes(jnp.sum(grad_attended.astype(jnp.float32) * attended_exact, axis=-1), 1, 2)
    empty_heads = jnp.zeros((seq_count, block_len, head_count, HEAD_DIM), jnp.float32)

    def back_step(block_index, carried):
        grad_query, spread = carried
        key_heads, value_heads, allowed = key_block(block_index)
        prob_rows = jnp.exp(
            scores_of(query_heads, key_heads, allowed, scaling) - log_total[..., None]
        )
        push = jnp.einsum(
            "sqhd,skhd->shqk", grad_attended, value_heads, preferred_element_type=jnp.float32
        )
        slope = (prob_rows * (push - delta[..., None])).astype(jnp.bfloat16)
        grad_part = (
            jnp.einsum("shqk,skhd->sqhd", slope, key_heads, preferred_element_type=jnp.float32)
            * scaling
        )
        grad_key = (
            jnp.einsum("shqk,sqhd->skhd", slope, query_heads, preferred_element_type=jnp.float32)
            * scaling
        )
        grad_value = jnp.einsum(
            "shqk,sqhd->skhd",
            prob_rows.astype(jnp.bfloat16),
            grad_attended,
            preferred_element_type=jnp.float32,
        )
        piece = jnp.stack(
            [
                grad_key.reshape(seq_count, key_span, inner_width),
                grad_value.reshape(seq_count, key_span, inner_width),
            ],
            axis=2,
        )
        spread = lax.dynamic_update_slice_in_dim(spread, piece, block_index * key_span, 1)
        return (grad_query + grad_part, spread)

    spread_start = jnp.zeros((seq_count, seq_length, 2, inner_width), jnp.float32)
    grad_query, spread = lax.fori_loop(0, trip_count, back_step, (empty_heads, spread_start))
    own_grads = lax.psum_scatter(
        spread.astype(jnp.bfloat16), "ctx", scatter_dimension=1, tiled=True
    ).reshape(row_count, 2, inner_width)
    return jnp.stack(
        [
            grad_query.reshape(row_count, inner_width).astype(jnp.bfloat16),
            own_grads[:, 0],
            own_grads[:, 1],
        ]
    )


def local(
    hidden_in,
    valid_mask,
    teacher,
    qkv_weight,
    qv_bias,
    out_weight,
    out_bias,
    norm1_gain,
    norm1_shift,
    up_weight,
    up_bias,
    down_weight,
    down_bias,
    norm2_gain,
    norm2_shift,
):
    seq_count, block_len, model_width = hidden_in.shape
    ctx_count = lax.axis_size("ctx")
    place = lax.axis_index("ctx")
    inner_width = qkv_weight.shape[2]
    row_count = seq_count * block_len
    whole = (
        seq_count == ctx_count
        and ctx_count & (ctx_count - 1) == 0
        and block_len % LANES == 0
        and inner_width % LANES == 0
    )
    full_qkv, full_out, full_up, full_down = (
        lax.all_gather(qkv_weight.reshape(-1, 3 * inner_width), "fsdp", axis=0, tiled=True),
        lax.all_gather(out_weight, "fsdp", axis=0, tiled=True),
        lax.all_gather(up_weight, "fsdp", axis=0, tiled=True),
        lax.all_gather(down_weight, "fsdp", axis=0, tiled=True),
    )
    local_counts = jnp.sum(valid_mask.astype(jnp.float32), axis=1)
    if whole:
        flat_in = to_sequences(hidden_in, place)
        teacher_rows = to_sequences(teacher, place)
        counts = butterfly(jnp.broadcast_to(local_counts[:, None], (seq_count, LANES)), ("ctx",))
        valid_count = lax.dynamic_slice(counts, (place, 0), (1, 1)).reshape(()).astype(jnp.int32)
        facts = jnp.stack([place, valid_count])
        row_index = jnp.arange(row_count, dtype=jnp.int32)
        positions = ((row_index // block_len) ^ place) * block_len + row_index % block_len
        keep_rows = (positions < valid_count).astype(jnp.float32)[:, None]
    else:
        flat_in = hidden_in.reshape(row_count, model_width)
        teacher_rows = teacher.reshape(row_count, model_width)
        keep_rows = valid_mask.reshape(row_count, 1).astype(jnp.float32)
    full_bias = jnp.concatenate([qv_bias[0], jnp.zeros_like(qv_bias[0]), qv_bias[1]])
    projected = (
        jnp.dot(flat_in, full_qkv, preferred_element_type=jnp.float32) + full_bias
    ).astype(jnp.bfloat16)
    if whole:
        attended, log_total = attend(facts, projected, block_len)
    else:
        key_block = key_blocks_over_ctx(projected, valid_mask, seq_count, block_len)
        attended, kept = spread_attend(projected, key_block, seq_count, block_len)
    attn_branch = add_partner(
        jnp.einsum("te,de->td", attended, full_out, preferred_element_type=jnp.float32)
    )
    resid1 = flat_in.astype(jnp.float32) + attn_branch + out_bias
    normed1, norm1_back = jax.vjp(layer_norm, resid1, norm1_gain, norm1_shift)
    normed1_low = normed1.astype(jnp.bfloat16)
    pre_act = jnp.dot(normed1_low, full_up, preferred_element_type=jnp.float32) + up_bias
    active, gelu_back = jax.vjp(gelu_exact, pre_act)
    active = active.astype(jnp.bfloat16)
    ffn_branch = add_partner(
        jnp.einsum("tf,df->td", active, full_down, preferred_element_type=jnp.float32)
    )
    resid2 = normed1 + ffn_branch + down_bias
    output, norm2_back = jax.vjp(layer_norm, resid2, norm2_gain, norm2_shift)
    layer_out = output.astype(jnp.bfloat16)
    residue = (output - teacher_rows.astype(jnp.float32)) * keep_rows
    squared = jnp.sum(residue * residue)
    grad_resid2, grad_gain2, grad_shift2 = norm2_back(residue)
    grad_down_bias = jnp.sum(grad_resid2, axis=0)
    grad_resid2_low = grad_resid2.astype(jnp.bfloat16)
    grad_active = jnp.dot(grad_resid2_low, full_down, preferred_element_type=jnp.float32)
    grad_down_weight = jnp.einsum(
        "td,tf->df", grad_resid2_low, active, preferred_element_type=jnp.float32
    )
    grad_pre = gelu_back(grad_active)[0].astype(jnp.bfloat16)
    grad_up_bias = jnp.sum(grad_pre.astype(jnp.float32), axis=0)
    grad_up_weight = jnp.einsum(
        "td,tf->df", normed1_low, grad_pre, preferred_element_type=jnp.float32
    )
    grad_normed1 = grad_resid2 + add_partner(
        jnp.einsum("tf,df->td", grad_pre, full_up, preferred_element_type=jnp.float32)
    )
    grad_resid1, grad_gain1, grad_shift1 = norm1_back(grad_normed1)
    grad_out_bias = jnp.sum(grad_resid1, axis=0)
    grad_resid1_low = grad_resid1.astype(jnp.bfloat16)
    grad_attended = jnp.dot(grad_resid1_low, full_out, preferred_element_type=jnp.float32).astype(
        jnp.bfloat16
    )
    grad_out_weight = jnp.einsum(
        "td,te->de", grad_resid1_low, attended, preferred_element_type=jnp.float32
    )
    if whole:
        grad_qkv = attend_back(facts, projected, grad_attended, log_total, block_len)
    else:
        grad_qkv = spread_attend_back(
            projected, grad_attended, kept, key_block, seq_count, block_len
        )
    grad_qv_bias = jnp.sum(grad_qkv[0::2].astype(jnp.float32), axis=1)
    grad_qkv_weight = jnp.concatenate(
        [
            jnp.einsum("td,te->de", flat_in, grad_qkv[kind], preferred_element_type=jnp.float32)
            for kind in range(3)
        ],
        axis=1,
    )
    grad_input = grad_resid1 + add_partner(
        sum(
            jnp.einsum(
                "te,de->td",
                grad_qkv[kind],
                full_qkv[:, kind * inner_width : (kind + 1) * inner_width],
                preferred_element_type=jnp.float32,
            )
            for kind in range(3)
        )
    )
    hidden_width = up_weight.shape[1]
    small = jnp.concatenate(
        [
            grad_out_bias,
            grad_gain1,
            grad_shift1,
            grad_down_bias,
            grad_gain2,
            grad_shift2,
            grad_qv_bias[0],
            grad_qv_bias[1],
            grad_up_bias,
            jnp.full((LANES,), squared),
            jnp.full((LANES,), jnp.sum(local_counts)),
        ]
    )
    small = butterfly(small.reshape(-1, LANES), ("ctx", "fsdp")).reshape(-1)
    vectors = small[: 6 * model_width].reshape(6, model_width)
    place_now = 6 * model_width
    grad_qv_bias = small[place_now : place_now + 2 * inner_width].reshape(2, inner_width)
    place_now += 2 * inner_width
    grad_up_bias = small[place_now : place_now + hidden_width]
    place_now += hidden_width
    squared = small[place_now]
    counted = small[place_now + LANES]
    local_grads = (grad_qkv_weight, grad_out_weight, grad_up_weight, grad_down_weight)
    owned = [
        lax.psum_scatter(item.astype(jnp.bfloat16), "fsdp", scatter_dimension=0, tiled=True)
        for item in local_grads
    ]
    owned = [reduce_over_ctx(item) for item in owned]
    token_total = float(row_count * ctx_count * lax.axis_size("fsdp"))
    ratio = token_total / counted
    loss = squared / (counted * model_width)
    input_grad = grad_input * ratio
    if whole:
        layer_out = from_sequences(layer_out, place, seq_count)
        input_grad = from_sequences(grad_input.astype(jnp.bfloat16), place, seq_count)
        input_grad = input_grad.astype(jnp.float32) * ratio
    else:
        layer_out = layer_out.reshape(seq_count, block_len, model_width)
        input_grad = input_grad.reshape(seq_count, block_len, model_width)
    return (
        layer_out,
        input_grad,
        loss,
        (owned[0] * ratio).reshape(-1, 3, inner_width),
        grad_qv_bias * ratio,
        owned[1] * ratio,
        vectors[0] * ratio,
        vectors[1] * ratio,
        vectors[2] * ratio,
        owned[2] * ratio,
        grad_up_bias * ratio,
        owned[3] * ratio,
        vectors[3] * ratio,
        vectors[4] * ratio,
        vectors[5] * ratio,
    )


def solution(mesh):
    in_specs = (
        P("fsdp", "ctx", None),
        P("fsdp", "ctx"),
        P("fsdp", "ctx", None),
        P("fsdp", None, "tp"),
        P(None, "tp"),
        P("fsdp", "tp"),
        P(),
        P(),
        P(),
        P("fsdp", "tp"),
        P("tp"),
        P("fsdp", "tp"),
        P(),
        P(),
        P(),
    )
    out_specs = (
        P("fsdp", "ctx", None),
        P("fsdp", "ctx", None),
        P(),
        P("fsdp", None, "tp"),
        P(None, "tp"),
        P("fsdp", "tp"),
        P(),
        P(),
        P(),
        P("fsdp", "tp"),
        P("tp"),
        P("fsdp", "tp"),
        P(),
        P(),
        P(),
    )
    return jax.shard_map(local, mesh=mesh, in_specs=in_specs, out_specs=out_specs, check_vma=False)
```

time: 797 us -> 419 us (0.53)
  waiting for transfers between devices: 490 us -> 134 us
  blocking collectives: 101 us -> 24.3 us
  starting transfers between devices: 2.15 us -> 50.8 us
  Pallas kernels: 0 us -> 28.9 us
  matrix products: 93.8 us -> 69.5 us
  local copies, waits for them, and re-layouts: 39.4 us -> 51.6 us
  other arithmetic: 44.3 us -> 34.3 us
    reduce_scatter x4, waiting for transfers between devices: 209 us -> 6.68 us  [local(): lax.psum_scatter(item.astype(jnp.bfloat16), 'fsdp', scatter_dimension=0,...]
    all_gather x3 -> x1, waiting for transfers between devices: 107 us -> 11.3 us  [local(): lax.all_gather(qkv_weight.reshape(-1, 3 * inner_width), 'fsdp', axis=0, t...]
    psum x5 -> x0, waiting for transfers between devices: 78.9 us -> none  [the longest x1 31.2 us: local(): lax.psum(jnp.einsum('te,de->td', attended, full_out, preferred_element_ty...]
    psum x1 -> x0, blocking collectives: 77 us -> none  [local(): lax.psum((squared, counted, vectors, grad_qv_bias, grad_up_bias), ('fsdp'...]
    ppermute x0 -> x46, waiting for transfers between devices: none -> 60.1 us  [swap(): return lax.ppermute(values, axis, swaps(lax.axis_size(axis), step))]
    ppermute x0 -> x46, starting transfers between devices: none -> 50.3 us  [swap(): return lax.ppermute(values, axis, swaps(lax.axis_size(axis), step))]
    pallas_call x0 -> x2, Pallas kernels: none -> 28.9 us  [the longest x1 16.8 us: attend_back(): pl.pallas_call(lambda *refs: attend_back_kernel(*refs, block=block), grid...]
    all_gather x1, waiting for transfers between devices: 47.8 us -> 24.7 us  [local(): lax.all_gather(up_weight, 'fsdp', axis=0, tiled=True)]
  transfers between devices with their start and end apart: 15 -> 53, of which waited for: 14 -> 30; matrix products, arithmetic and copies ran while one was open for 8% -> 29% of each run, Pallas kernels for 0% -> 7%
where the time goes in v1:
time: 419 us; the launch traced here: 412 us
  waiting for transfers between devices  134 us (32%)
  matrix products  69.5 us (17%)
  local copies, waits for them, and re-layouts  51.6 us (12%)
  starting transfers between devices  50.8 us (12%)
  other arithmetic  34.3 us (8%)
  Pallas kernels  28.9 us (7%)
  blocking collectives  24.3 us (6%)
  between operations  18.4 us (4%)
    ppermute x46, waiting for transfers between devices, swap(): return lax.ppermute(values, axis, swaps(lax.axis_size(axis), step))  60.1 us
    ppermute x46, starting transfers between devices, swap(): return lax.ppermute(values, axis, swaps(lax.axis_size(axis), step))  50.3 us
    all_gather x1, waiting for transfers between devices, local(): lax.all_gather(down_weight, 'fsdp', axis=0, tiled=True)  30.3 us
    all_gather x1, waiting for transfers between devices, local(): lax.all_gather(up_weight, 'fsdp', axis=0, tiled=True)  24.7 us
    all_gather x1, blocking collectives, local(): lax.all_gather(out_weight, 'fsdp', axis=0, tiled=True)  24.3 us
    dot_general x1, matrix products, local(): jnp.dot(normed1_low, full_up, preferred_element_type=jnp.float32) + up_bias  20.6 us
    pallas_call x1, Pallas kernels, attend_back(): pl.pallas_call(lambda *refs: attend_back_kernel(*refs, block=block), grid...  16.8 us
    dynamic_slice x9, local copies, waits for them, and re-layouts, to_sequences(): lax.dynamic_index_in_dim(blocks, place ^ s, 0, keepdims=False)  12.2 us
  transfers between devices with their start and end apart: 53, of which 30 were waited for; matrix products, arithmetic and copies ran while one was open for 29% of the time, Pallas kernels for 7%

profile of v1, /device:TPU:0, one launch (start us, length us, event | category | flops | bytes accessed | tf_op | source)
XLA Modules:
  0.0 411.6 jit_solution(12279334551411047914)
XLA Ops:
  9.9 3.1 constant_dynamic-slice_fusion.3
  13.2 3.0 collective-permute-start
  19.6 2.0 collective-permute-start.3
  21.6 24.3 %all_gather.13 = bf16[768,384]{1,0:T(8,128)(2,1)S(1)} all-gather(bf16[192,384]{1,0:T(8,128)(2,1)S(1)} %copy-done.16), channel_id=1, replica_groups=mesh['fsdp'=4,'ctx'=4,'tp'=2] {'fsdp'}, dimensions={0}, use_global_device_ids=true | all-gather | bytes 737280 | tf_op jit(solution)/shard_map/all_gather | solution.py:420
  51.4 11.3 %all-gather.4.cloned.1.call-done = bf16[768,1152]{1,0:T(8,128)(2,1)} async-done(((bf16[192,1152]{1,0:T(8,128)(2,1)}), bf16[768,1152]{1,0:T(8,128)(2,1)}) %all-gather.4.cloned.1.call-update) | async-done | bytes 1769488 | tf_op jit(solution)/shard_map/all_gather | solution.py:419
  62.7 5.2 %add_convert_fusion.1.refs_1_.refs_2_.refs_3_ = bf16[1024,1152]{1,0:T(8,128)(2,1)} fusion(bf16[768,1152]{1,0:T(8,128)(2,1)} %all-gather.4.cloned.1.call-done, f32[1152]{0:T(1024)S(1)} %pad_maximum_fusion.2, bf16[256,768]{0,1:T(8,128)(2,1)S(1)} %collective-permute-done.2, bf16[256,768]{0,1:T(8,128)(2,1)S(1)} %collective-permute-done.1, ...), kind=kOutput, calls=%fused_computation.20 | convolution fusion | flops 1820590080 | bytes 5706240 | tf_op jit(solution)/shard_map/dot_general | solution.py:440
  67.9 12.1 %attend.1 = (bf16[1024,384]{1,0:T(8,128)(2,1)}, f32[3,2,1024]{2,1,0:T(2,128)}) custom-call(s32[2]{0:T(128)} %pad_add_fusion.refs_0_, bf16[1024,1152]{1,0:T(8,128)(2,1)} %add_convert_fusion.1.refs_1_.refs_2_.refs_3_, bf16[1024,1152]{1,0:T(8,128)(2,1)} %add_convert_fusion.1.refs_1_.refs_2_.refs_3_, bf16[1024,1152]{1,0:T(8,128)(2,1)} %add_convert_fusion.1.refs_1_.refs_2_.refs_3_), custom_call_target="tpu_custom_call" | custom-call | tf_op jit(solution)/shard_map/attend/pallas_call | solution.py:161
  80.0 2.2 convolution_convert_fusion.2
  83.3 2.5 collective-permute-done.5
  85.7 2.7 fusion.58
  88.8 24.7 %all-gather.6.cloned.1.call-done = bf16[768,1536]{1,0:T(8,128)(2,1)} async-done(((bf16[192,1536]{1,0:T(8,128)(2,1)}), bf16[768,1536]{1,0:T(8,128)(2,1)}) %all-gather.6.cloned.1.call-update) | async-done | bytes 2359312 | tf_op jit(solution)/shard_map/all_gather | solution.py:421
  113.6 20.6 %multiply_convert_fusion = (bf16[1024,1536]{1,0:T(8,128)(2,1)}, f32[1024,1536]{1,0:T(8,128)}, f32[1024,1536]{1,0:T(8,128)}) fusion(f32[1536]{0:T(1024)} %param.25, bf16[768,1536]{1,0:T(8,128)(2,1)} %all-gather.6.cloned.1.call-done, f32[1024,768]{0,1:T(8,128)S(1)} %get-tuple-element.83, f32[768]{0:T(1024)} %param.23, f32[768]{0:T(1024)S(1)} %copy-done.18, ...), kind=kOutput, calls=%fused_computation.4 | convolution fusion | flops 2523660288 | bytes 21254144 | tf_op jit(solution)/shard_map/dot_general | solution.py:453
  134.2 30.3 %all-gather.8.cloned.1.call-done = bf16[768,1536]{1,0:T(8,128)(2,1)} async-done(((bf16[192,1536]{1,0:T(8,128)(2,1)}), bf16[768,1536]{1,0:T(8,128)(2,1)}) %all-gather.8.cloned.1.call-update) | async-done | bytes 2359312 | tf_op jit(solution)/shard_map/all_gather | solution.py:422
  164.5 6.4 %convolution_convert_fusion.4 = bf16[1024,768]{0,1:T(8,128)(2,1)} fusion(bf16[1024,1536]{1,0:T(8,128)(2,1)} %get-tuple-element.80, bf16[768,1536]{1,0:T(8,128)(2,1)} %all-gather.8.cloned.1.call-done), kind=kOutput, calls=%fused_computation.49 | convolution fusion | flops 2416705536 | bytes 7077888 | tf_op jit(solution)/shard_map/tf,df->td/dot_general | solution.py:457
  174.3 1.9 copy.87
  177.7 1.9 copy.88
  180.1 1.9 copy.85
  182.7 3.2 fusion.56
  186.4 9.8 %collective-permute-done.11 = bf16[256,768]{0,1:T(8,128)(2,1)} collective-permute-done((bf16[256,768]{0,1:T(8,128)(2,1)}, bf16[256,768]{0,1:T(8,128)(2,1)}, u32[]{:S(2)}, u32[]{:S(2)}) %collective-permute-start.11) | collective-permute-done | bytes 393248 | tf_op jit(solution)/shard_map/ppermute | solution.py:212
  196.2 5.4 %multiply_reduce_fusion = (f32[]{:T(128)}, f32[768]{0:T(1024)}, f32[1024]{0:T(1024)S(1)}, f32[768]{0:T(1024)}, f32[1024,768]{0,1:T(8,128)S(1)}, /*index=5*/bf16[1024,768]{0,1:T(8,128)(2,1)}) fusion(f32[768]{0:T(1024)S(1)} %copy-done.19, f32[1024,768]{0,1:T(8,128)S(1)} %get-tuple-element.79, f32[1024]{0:T(1024)S(1)} %broadcast_multiply_fusion, ...), kind=kLoop, calls=%fused_computation.23 | loop fusion | flops 18085376 | bytes 9465860 | tf_op jit(solution)/shard_map/reduce_sum | solution.py:463
  203.3 6.1 %convert_reduce_fusion = (f32[1536]{0:T(1024)}, bf16[1024,1536]{1,0:T(8,128)(2,1)S(1)}) fusion(f32[1024,1536]{1,0:T(8,128)S(1)} %bitcast.176, bf16[768,1536]{1,0:T(8,128)(2,1)S(1)} %copy-done.32, f32[1024,768]{0,1:T(8,128)S(1)} %get-tuple-element.76, f32[1024]{0:T(1024)S(1)} %negate_multiply_fusion.2, f32[1024,1536]{1,0:T(8,128)S(1)} %bitcast.178, ...), kind=kOutput, calls=%fused_computation.2 | convolution fusion | flops 2444229120 | bytes 21250048 | tf_op jit(solution)/shard_map/dot_general | solution.py:467
  209.4 2.6 convolution_convert_fusion.3
  212.1 3.4 collective-permute-done.13
  215.5 3.1 multiply_reduce_fusion.2
  223.0 6.9 %convolution_convert_fusion = bf16[768,1536]{1,0:T(8,128)(2,1)} fusion(bf16[1024,1536]{1,0:T(8,128)(2,1)} %get-tuple-element.80, f32[1024,768]{0,1:T(8,128)} %copy-done.4, f32[1024]{0:T(1024)} %copy-done.25), kind=kOutput, calls=%fused_computation.21 | convolution fusion | flops 2418671616 | bytes 8654848 | tf_op jit(solution)/shard_map/td,tf->df/dot_general | solution.py:468
  230.0 6.4 %convolution_convert_fusion.1 = bf16[768,1536]{1,0:T(8,128)(2,1)} fusion(bf16[1024,1536]{1,0:T(8,128)(2,1)} %copy-done.35, f32[1024,768]{0,1:T(8,128)S(1)} %get-tuple-element.83, f32[768]{0:T(1024)} %param.23, f32[768]{0:T(1024)S(1)} %copy-done.18, f32[1024]{0:T(1024)S(1)} %fusion.45, f32[1024]{0:T(1024)S(1)} %broadcast_multiply_fusion.1), kind=kOutput, calls=%fused_computation.22 | convolution fusion | flops 2421030912 | bytes 8665088 | tf_op jit(solution)/shard_map/td,tf->df/dot_general | solution.py:473
  244.6 1.9 constant_dynamic-update-slice_fusion.7
  246.5 4.7 %collective-permute-done.7 = bf16[256,768]{0,1:T(8,128)(2,1)} collective-permute-done((bf16[256,768]{0,1:T(8,128)(2,1)}, bf16[256,768]{0,1:T(8,128)(2,1)}, u32[]{:S(2)}, u32[]{:S(2)}) %collective-permute-start.7) | collective-permute-done | bytes 393248 | tf_op jit(solution)/shard_map/ppermute | solution.py:212
  251.2 1.9 copy.82
  253.2 5.0 %collective-permute-done.8 = bf16[256,768]{0,1:T(8,128)(2,1)} collective-permute-done((bf16[256,768]{0,1:T(8,128)(2,1)}, bf16[256,768]{0,1:T(8,128)(2,1)}, u32[]{:S(2)}, u32[]{:S(2)}) %collective-permute-start.8) | collective-permute-done | bytes 393248 | tf_op jit(solution)/shard_map/ppermute | solution.py:212
  260.1 1.9 copy.84
  267.3 3.0 convolution_convert_fusion.5.refs_4_
  270.3 16.8 %attend_back.1 = bf16[3,1024,384]{2,1,0:T(8,128)(2,1)} custom-call(s32[2]{0:T(128)} %pad_add_fusion.refs_0_, bf16[1024,1152]{1,0:T(8,128)(2,1)} %add_convert_fusion.1.refs_1_.refs_2_.refs_3_, bf16[1024,1152]{1,0:T(8,128)(2,1)} %add_convert_fusion.1.refs_1_.refs_2_.refs_3_, bf16[1024,1152]{1,0:T(8,128)(2,1)} %add_convert_fusion.1.refs_1_.refs_2_.refs_3_, ...), custom_call_target="tpu_custom_call" | custom-call | tf_op jit(solution)/shard_map/attend_back/pallas_call | solution.py:184
  287.1 2.5 fusion.9
  290.8 2.3 add_convert_fusion.3
  297.7 2.5 collective-permute-start.28
  304.2 2.4 collective-permute-done.30
  308.0 4.1 copy.104
  312.2 2.9 collective-permute-start.33
  315.2 2.7 add_reduce_fusion
  320.0 3.3 collective-permute-done.18
  323.9 3.4 collective-permute-done.19
  328.3 2.9 collective-permute-start.17
  333.6 5.5 %collective-permute-done.21 = f32[56,128]{1,0:T(8,128)S(1)} collective-permute-done((f32[56,128]{1,0:T(8,128)S(1)}, f32[56,128]{1,0:T(8,128)S(1)}, u32[]{:S(2)}, u32[]{:S(2)}) %collective-permute-start.21) | collective-permute-done | bytes 28704 | tf_op jit(solution)/shard_map/ppermute | solution.py:212
  347.8 1.9 convert_multiply_fusion
  375.9 6.7 %reduce-scatter.13.cloned.1.call-done = bf16[192,1152]{1,0:T(8,128)(2,1)} async-done(((bf16[768,1152]{1,0:T(8,128)(2,1)}), bf16[192,1152]{1,0:T(8,128)(2,1)}) %reduce-scatter.13.cloned.1.call-update) | async-done | bytes 442384 | tf_op jit(solution)/shard_map/reduce_scatter | solution.py:540
  388.5 2.6 collective-permute-done.23
  398.2 2.6 collective-permute-done.26
  (278 shorter events, 107.1 us)
Async XLA Ops:
  7.2 55.5 %all-gather.4.cloned.1.call-start = ((), (), s32[]{:S(2)}) async-start(), calls=%async_computation.4 | async-start | bytes 2211840 | tf_op jit(solution)/shard_map/all_gather | solution.py:419
  9.1 104.5 %all-gather.6.cloned.1.call-start = ((), (), s32[]{:S(2)}) async-start(), calls=%async_computation.5 | async-start | bytes 2949120 | tf_op jit(solution)/shard_map/all_gather | solution.py:421
  9.8 154.7 %all-gather.8.cloned.1.call-start = ((), (), s32[]{:S(2)}) async-start(), calls=%async_computation.6 | async-start | bytes 2949120 | tf_op jit(solution)/shard_map/all_gather | solution.py:422
  13.2 38.2 %collective-permute-start = (bf16[256,768]{0,1:T(8,128)(2,1)S(1)}, bf16[256,768]{0,1:T(8,128)(2,1)S(1)}, u32[]{:S(2)}, u32[]{:S(2)}) collective-permute-start(bf16[256,768]{0,1:T(8,128)(2,1)S(1)} %bitcast.165), channel_id=1, source_target_pairs={{0,2},{2,0},{4,6},{6,4},{1,3},{3,1},{5,7},{7,5},{8,10},{10,8},{12,... | collective-permute-start | bytes 1179656 | tf_op jit(solution)/shard_map/ppermute | solution.py:212
  16.4 35.0 %collective-permute-start.1 = (bf16[256,768]{0,1:T(8,128)(2,1)S(1)}, bf16[256,768]{0,1:T(8,128)(2,1)S(1)}, u32[]{:S(2)}, u32[]{:S(2)}) collective-permute-start(bf16[256,768]{0,1:T(8,128)(2,1)S(1)} %bitcast.166), channel_id=1, source_target_pairs={{0,4},{2,6},{4,0},{6,2},{1,5},{3,7},{5,1},{7,3},{8,12},{10,14},{12... | collective-permute-start | bytes 1179656 | tf_op jit(solution)/shard_map/ppermute | solution.py:212
  18.9 32.5 %collective-permute-start.2 = (bf16[256,768]{0,1:T(8,128)(2,1)}, bf16[256,768]{0,1:T(8,128)(2,1)S(1)}, u32[]{:S(2)}, u32[]{:S(2)}) collective-permute-start(bf16[256,768]{0,1:T(8,128)(2,1)} %bitcast.3), channel_id=1, source_target_pairs={{0,6},{2,4},{4,2},{6,0},{1,7},{3,5},{5,3},{7,1},{8,14},{10,12},{12... | collective-permute-start | bytes 1179656 | tf_op jit(solution)/shard_map/ppermute | solution.py:212
  19.6 26.3 %collective-permute-start.3 = (f32[4,128]{1,0:T(4,128)S(1)}, f32[4,128]{1,0:T(4,128)S(1)}, u32[]{:S(2)}, u32[]{:S(2)}) collective-permute-start(f32[4,128]{1,0:T(4,128)S(1)} %broadcast_in_dim.122), channel_id=1, source_target_pairs={{0,2},{2,0},{4,6},{6,4},{1,3},{3,1},{5,7},{7,5},{8,10},{10,8},{12,... | collective-permute-start | bytes 6152 | tf_op jit(solution)/shard_map/ppermute | solution.py:212
  82.2 214.7 %reduce-scatter.7.cloned.1.call-start = ((), (), s32[]{:S(2)}) async-start(), calls=%async_computation.7 | async-start | bytes 737280 | tf_op jit(solution)/shard_map/reduce_scatter | solution.py:540
  170.9 11.8 %collective-permute-start.6 = (bf16[1024,768]{0,1:T(8,128)(2,1)}, bf16[1024,768]{0,1:T(8,128)(2,1)}, u32[]{:S(2)}, u32[]{:S(2)}) collective-permute-start(bf16[1024,768]{0,1:T(8,128)(2,1)} %convolution_convert_fusion.4), channel_id=1, source_target_pairs={{0,1},{1,0},{2,3},{3,2},{4,5},{5,4},{6,7},{7,6},{8,9},{9,8},{10,11... | collective-permute-start | bytes 4718600 | tf_op jit(solution)/shard_map/ppermute | solution.py:212
  172.8 13.6 %collective-permute-start.10 = (bf16[256,768]{0,1:T(8,128)(2,1)}, bf16[256,768]{0,1:T(8,128)(2,1)}, u32[]{:S(2)}, u32[]{:S(2)}) collective-permute-start(bf16[256,768]{0,1:T(8,128)(2,1)} %bitcast.167), channel_id=1, source_target_pairs={{0,2},{2,0},{4,6},{6,4},{1,3},{3,1},{5,7},{7,5},{8,10},{10,8},{12,... | collective-permute-start | bytes 1179656 | tf_op jit(solution)/shard_map/ppermute | solution.py:212
  176.2 20.0 %collective-permute-start.11 = (bf16[256,768]{0,1:T(8,128)(2,1)}, bf16[256,768]{0,1:T(8,128)(2,1)}, u32[]{:S(2)}, u32[]{:S(2)}) collective-permute-start(bf16[256,768]{0,1:T(8,128)(2,1)} %bitcast.168), channel_id=1, source_target_pairs={{0,4},{2,6},{4,0},{6,2},{1,5},{3,7},{5,1},{7,3},{8,12},{10,14},{12... | collective-permute-start | bytes 1179656 | tf_op jit(solution)/shard_map/ppermute | solution.py:212
  179.6 16.6 %collective-permute-start.12 = (bf16[256,768]{0,1:T(8,128)(2,1)}, bf16[256,768]{0,1:T(8,128)(2,1)}, u32[]{:S(2)}, u32[]{:S(2)}) collective-permute-start(bf16[256,768]{0,1:T(8,128)(2,1)} %bitcast.169), channel_id=1, source_target_pairs={{0,6},{2,4},{4,2},{6,0},{1,7},{3,5},{5,3},{7,1},{8,14},{10,12},{12... | collective-permute-start | bytes 1179656 | tf_op jit(solution)/shard_map/ppermute | solution.py:212
  223.0 126.8 %reduce-scatter.11.cloned.1.call-start = ((), (), s32[]{:S(2)}) async-start(), calls=%async_computation.9 | async-start | bytes 2949120 | tf_op jit(solution)/shard_map/reduce_scatter | solution.py:540
  230.0 124.5 %reduce-scatter.9.cloned.1.call-start = ((), (), s32[]{:S(2)}) async-start(), calls=%async_computation.8 | async-start | bytes 2949120 | tf_op jit(solution)/shard_map/reduce_scatter | solution.py:540
  236.5 146.1 %reduce-scatter.13.cloned.1.call-start = ((), (), s32[]{:S(2)}) async-start(), calls=%async_computation.10 | async-start | bytes 2211840 | tf_op jit(solution)/shard_map/reduce_scatter | solution.py:540
  238.9 12.3 %collective-permute-start.7 = (bf16[256,768]{0,1:T(8,128)(2,1)}, bf16[256,768]{0,1:T(8,128)(2,1)}, u32[]{:S(2)}, u32[]{:S(2)}) collective-permute-start(bf16[256,768]{0,1:T(8,128)(2,1)} %get-tuple-element.98), channel_id=1, source_target_pairs={{0,2},{2,0},{4,6},{6,4},{1,3},{3,1},{5,7},{7,5},{8,10},{10,8},{12,... | collective-permute-start | bytes 1179656 | tf_op jit(solution)/shard_map/ppermute | solution.py:212
  239.5 18.6 %collective-permute-start.8 = (bf16[256,768]{0,1:T(8,128)(2,1)}, bf16[256,768]{0,1:T(8,128)(2,1)}, u32[]{:S(2)}, u32[]{:S(2)}) collective-permute-start(bf16[256,768]{0,1:T(8,128)(2,1)} %get-tuple-element.97), channel_id=1, source_target_pairs={{0,4},{2,6},{4,0},{6,2},{1,5},{3,7},{5,1},{7,3},{8,12},{10,14},{12... | collective-permute-start | bytes 1179656 | tf_op jit(solution)/shard_map/ppermute | solution.py:212
  241.0 19.1 %collective-permute-start.9 = (bf16[256,768]{0,1:T(8,128)(2,1)}, bf16[256,768]{0,1:T(8,128)(2,1)}, u32[]{:S(2)}, u32[]{:S(2)}) collective-permute-start(bf16[256,768]{0,1:T(8,128)(2,1)} %get-tuple-element.96), channel_id=1, source_target_pairs={{0,6},{2,4},{4,2},{6,0},{1,7},{3,5},{5,3},{7,1},{8,14},{10,12},{12... | collective-permute-start | bytes 1179656 | tf_op jit(solution)/shard_map/ppermute | solution.py:212
  293.0 22.2 %collective-permute-start.14 = (bf16[1024,768]{0,1:T(8,128)(2,1)}, bf16[1024,768]{0,1:T(8,128)(2,1)}, u32[]{:S(2)}, u32[]{:S(2)}) collective-permute-start(bf16[1024,768]{0,1:T(8,128)(2,1)} %add_convert_fusion.3), channel_id=1, source_target_pairs={{0,1},{1,0},{2,3},{3,2},{4,5},{5,4},{6,7},{7,6},{8,9},{9,8},{10,11... | collective-permute-start | bytes 4718600 | tf_op jit(solution)/shard_map/ppermute | solution.py:212
  297.7 4.6 %collective-permute-start.28 = (bf16[48,384]{1,0:T(8,128)(2,1)S(1)}, bf16[48,384]{1,0:T(8,128)(2,1)S(1)}, u32[]{:S(2)}, u32[]{:S(2)}) collective-permute-start(bf16[48,384]{1,0:T(8,128)(2,1)S(1)} %get-tuple-element.113), channel_id=1, source_target_pairs={{0,2},{2,0},{4,6},{6,4},{1,3},{3,1},{5,7},{7,5},{8,10},{10,8},{12,... | collective-permute-start | bytes 110600 | tf_op jit(solution)/shard_map/ppermute | solution.py:212
  300.2 4.0 collective-permute-start.29
  301.7 4.9 %collective-permute-start.30 = (bf16[48,384]{1,0:T(8,128)(2,1)S(1)}, bf16[48,384]{1,0:T(8,128)(2,1)S(1)}, u32[]{:S(2)}, u32[]{:S(2)}) collective-permute-start(bf16[48,384]{1,0:T(8,128)(2,1)S(1)} %get-tuple-element.114), channel_id=1, source_target_pairs={{0,6},{2,4},{4,2},{6,0},{1,7},{3,5},{5,3},{7,1},{8,14},{10,12},{12... | collective-permute-start | bytes 110600 | tf_op jit(solution)/shard_map/ppermute | solution.py:212
  307.4 7.7 %collective-permute-start.31 = (bf16[48,384]{1,0:T(8,128)(2,1)S(1)}, bf16[48,384]{1,0:T(8,128)(2,1)S(1)}, u32[]{:S(2)}, u32[]{:S(2)}) collective-permute-start(bf16[48,384]{1,0:T(8,128)(2,1)S(1)} %get-tuple-element.69), channel_id=1, source_target_pairs={{0,2},{2,0},{4,6},{6,4},{1,3},{3,1},{5,7},{7,5},{8,10},{10,8},{12,... | collective-permute-start | bytes 110600 | tf_op jit(solution)/shard_map/ppermute | solution.py:212
  312.1 7.9 %collective-permute-start.32 = (bf16[48,384]{1,0:T(8,128)(2,1)S(1)}, bf16[48,384]{1,0:T(8,128)(2,1)S(1)}, u32[]{:S(2)}, u32[]{:S(2)}) collective-permute-start(bf16[48,384]{1,0:T(8,128)(2,1)S(1)} %get-tuple-element.69), channel_id=1, source_target_pairs={{0,4},{2,6},{4,0},{6,2},{1,5},{3,7},{5,1},{7,3},{8,12},{10,14},{12... | collective-permute-start | bytes 110600 | tf_op jit(solution)/shard_map/ppermute | solution.py:212
  312.2 11.6 %collective-permute-start.33 = (bf16[48,384]{1,0:T(8,128)(2,1)S(1)}, bf16[48,384]{1,0:T(8,128)(2,1)S(1)}, u32[]{:S(2)}, u32[]{:S(2)}) collective-permute-start(bf16[48,384]{1,0:T(8,128)(2,1)S(1)} %get-tuple-element.69), channel_id=1, source_target_pairs={{0,6},{2,4},{4,2},{6,0},{1,7},{3,5},{5,3},{7,1},{8,14},{10,12},{12... | collective-permute-start | bytes 110600 | tf_op jit(solution)/shard_map/ppermute | solution.py:212
  327.2 4.7 %collective-permute-start.20 = (f32[56,128]{1,0:T(8,128)S(1)}, f32[56,128]{1,0:T(8,128)S(1)}, u32[]{:S(2)}, u32[]{:S(2)}) collective-permute-start(f32[56,128]{1,0:T(8,128)S(1)} %fusion.76), channel_id=1, source_target_pairs={{0,8},{8,0},{16,24},{24,16},{1,9},{9,1},{17,25},{25,17},{2,10},{10... | collective-permute-start | bytes 86024 | tf_op jit(solution)/shard_map/ppermute | solution.py:212
  327.6 16.5 %collective-permute-start.15 = (bf16[256,768]{0,1:T(8,128)(2,1)S(1)}, bf16[256,768]{0,1:T(8,128)(2,1)}, u32[]{:S(2)}, u32[]{:S(2)}) collective-permute-start(bf16[256,768]{0,1:T(8,128)(2,1)S(1)} %get-tuple-element.90), channel_id=1, source_target_pairs={{0,2},{2,0},{4,6},{6,4},{1,3},{3,1},{5,7},{7,5},{8,10},{10,8},{12,... | collective-permute-start | bytes 1179656 | tf_op jit(solution)/shard_map/ppermute | solution.py:212
  328.2 17.1 %collective-permute-start.16 = (bf16[256,768]{0,1:T(8,128)(2,1)S(1)}, bf16[256,768]{0,1:T(8,128)(2,1)}, u32[]{:S(2)}, u32[]{:S(2)}) collective-permute-start(bf16[256,768]{0,1:T(8,128)(2,1)S(1)} %get-tuple-element.89), channel_id=1, source_target_pairs={{0,4},{2,6},{4,0},{6,2},{1,5},{3,7},{5,1},{7,3},{8,12},{10,14},{12... | collective-permute-start | bytes 1179656 | tf_op jit(solution)/shard_map/ppermute | solution.py:212
  328.3 18.2 %collective-permute-start.17 = (bf16[256,768]{0,1:T(8,128)(2,1)S(1)}, bf16[256,768]{0,1:T(8,128)(2,1)}, u32[]{:S(2)}, u32[]{:S(2)}) collective-permute-start(bf16[256,768]{0,1:T(8,128)(2,1)S(1)} %get-tuple-element.88), channel_id=1, source_target_pairs={{0,6},{2,4},{4,2},{6,0},{1,7},{3,5},{5,3},{7,1},{8,14},{10,12},{12... | collective-permute-start | bytes 1179656 | tf_op jit(solution)/shard_map/ppermute | solution.py:212
  331.9 7.1 %collective-permute-start.21 = (f32[56,128]{1,0:T(8,128)S(1)}, f32[56,128]{1,0:T(8,128)S(1)}, u32[]{:S(2)}, u32[]{:S(2)}) collective-permute-start(f32[56,128]{1,0:T(8,128)S(1)} %add.281), channel_id=1, source_target_pairs={{0,16},{8,24},{16,0},{24,8},{1,17},{9,25},{17,1},{25,9},{2,18},{10... | collective-permute-start | bytes 86024 | tf_op jit(solution)/shard_map/ppermute | solution.py:212
  350.9 6.8 %collective-permute-start.40 = (bf16[48,1536]{1,0:T(8,128)(2,1)S(1)}, bf16[48,1536]{1,0:T(8,128)(2,1)S(1)}, u32[]{:S(2)}, u32[]{:S(2)}) collective-permute-start(bf16[48,1536]{1,0:T(8,128)(2,1)S(1)} %get-tuple-element.104), channel_id=1, source_target_pairs={{0,2},{2,0},{4,6},{6,4},{1,3},{3,1},{5,7},{7,5},{8,10},{10,8},{12,... | collective-permute-start | bytes 442376 | tf_op jit(solution)/shard_map/ppermute | solution.py:212
  352.4 7.9 %collective-permute-start.41 = (bf16[48,1536]{1,0:T(8,128)(2,1)S(1)}, bf16[48,1536]{1,0:T(8,128)(2,1)S(1)}, u32[]{:S(2)}, u32[]{:S(2)}) collective-permute-start(bf16[48,1536]{1,0:T(8,128)(2,1)S(1)} %get-tuple-element.106), channel_id=1, source_target_pairs={{0,4},{2,6},{4,0},{6,2},{1,5},{3,7},{5,1},{7,3},{8,12},{10,14},{12... | collective-permute-start | bytes 442376 | tf_op jit(solution)/shard_map/ppermute | solution.py:212
  353.1 8.7 %collective-permute-start.42 = (bf16[48,1536]{1,0:T(8,128)(2,1)S(1)}, bf16[48,1536]{1,0:T(8,128)(2,1)S(1)}, u32[]{:S(2)}, u32[]{:S(2)}) collective-permute-start(bf16[48,1536]{1,0:T(8,128)(2,1)S(1)} %get-tuple-element.105), channel_id=1, source_target_pairs={{0,6},{2,4},{4,2},{6,0},{1,7},{3,5},{5,3},{7,1},{8,14},{10,12},{12... | collective-permute-start | bytes 442376 | tf_op jit(solution)/shard_map/ppermute | solution.py:212
  355.5 9.4 %collective-permute-start.34 = (bf16[48,1536]{1,0:T(8,128)(2,1)S(1)}, bf16[48,1536]{1,0:T(8,128)(2,1)S(1)}, u32[]{:S(2)}, u32[]{:S(2)}) collective-permute-start(bf16[48,1536]{1,0:T(8,128)(2,1)S(1)} %get-tuple-element.107), channel_id=1, source_target_pairs={{0,2},{2,0},{4,6},{6,4},{1,3},{3,1},{5,7},{7,5},{8,10},{10,8},{12,... | collective-permute-start | bytes 442376 | tf_op jit(solution)/shard_map/ppermute | solution.py:212
  357.0 10.0 %collective-permute-start.35 = (bf16[48,1536]{1,0:T(8,128)(2,1)S(1)}, bf16[48,1536]{1,0:T(8,128)(2,1)S(1)}, u32[]{:S(2)}, u32[]{:S(2)}) collective-permute-start(bf16[48,1536]{1,0:T(8,128)(2,1)S(1)} %get-tuple-element.109), channel_id=1, source_target_pairs={{0,4},{2,6},{4,0},{6,2},{1,5},{3,7},{5,1},{7,3},{8,12},{10,14},{12... | collective-permute-start | bytes 442376 | tf_op jit(solution)/shard_map/ppermute | solution.py:212
  357.7 10.3 %collective-permute-start.36 = (bf16[48,1536]{1,0:T(8,128)(2,1)S(1)}, bf16[48,1536]{1,0:T(8,128)(2,1)S(1)}, u32[]{:S(2)}, u32[]{:S(2)}) collective-permute-start(bf16[48,1536]{1,0:T(8,128)(2,1)S(1)} %get-tuple-element.108), channel_id=1, source_target_pairs={{0,6},{2,4},{4,2},{6,0},{1,7},{3,5},{5,3},{7,1},{8,14},{10,12},{12... | collective-permute-start | bytes 442376 | tf_op jit(solution)/shard_map/ppermute | solution.py:212
  362.8 8.4 %collective-permute-start.43 = (bf16[48,1536]{1,0:T(8,128)(2,1)S(1)}, bf16[48,1536]{1,0:T(8,128)(2,1)S(1)}, u32[]{:S(2)}, u32[]{:S(2)}) collective-permute-start(bf16[48,1536]{1,0:T(8,128)(2,1)S(1)} %get-tuple-element.65), channel_id=1, source_target_pairs={{0,2},{2,0},{4,6},{6,4},{1,3},{3,1},{5,7},{7,5},{8,10},{10,8},{12,... | collective-permute-start | bytes 442376 | tf_op jit(solution)/shard_map/ppermute | solution.py:212
  363.2 10.0 %collective-permute-start.44 = (bf16[48,1536]{1,0:T(8,128)(2,1)S(1)}, bf16[48,1536]{1,0:T(8,128)(2,1)S(1)}, u32[]{:S(2)}, u32[]{:S(2)}) collective-permute-start(bf16[48,1536]{1,0:T(8,128)(2,1)S(1)} %get-tuple-element.65), channel_id=1, source_target_pairs={{0,4},{2,6},{4,0},{6,2},{1,5},{3,7},{5,1},{7,3},{8,12},{10,14},{12... | collective-permute-start | bytes 442376 | tf_op jit(solution)/shard_map/ppermute | solution.py:212
  364.9 8.3 %collective-permute-start.45 = (bf16[48,1536]{1,0:T(8,128)(2,1)S(1)}, bf16[48,1536]{1,0:T(8,128)(2,1)S(1)}, u32[]{:S(2)}, u32[]{:S(2)}) collective-permute-start(bf16[48,1536]{1,0:T(8,128)(2,1)S(1)} %get-tuple-element.65), channel_id=1, source_target_pairs={{0,6},{2,4},{4,2},{6,0},{1,7},{3,5},{5,3},{7,1},{8,14},{10,12},{12... | collective-permute-start | bytes 442376 | tf_op jit(solution)/shard_map/ppermute | solution.py:212
  369.1 5.2 %collective-permute-start.37 = (bf16[48,1536]{1,0:T(8,128)(2,1)S(1)}, bf16[48,1536]{1,0:T(8,128)(2,1)S(1)}, u32[]{:S(2)}, u32[]{:S(2)}) collective-permute-start(bf16[48,1536]{1,0:T(8,128)(2,1)S(1)} %get-tuple-element.67), channel_id=1, source_target_pairs={{0,2},{2,0},{4,6},{6,4},{1,3},{3,1},{5,7},{7,5},{8,10},{10,8},{12,... | collective-permute-start | bytes 442376 | tf_op jit(solution)/shard_map/ppermute | solution.py:212
  369.5 5.2 %collective-permute-start.38 = (bf16[48,1536]{1,0:T(8,128)(2,1)S(1)}, bf16[48,1536]{1,0:T(8,128)(2,1)S(1)}, u32[]{:S(2)}, u32[]{:S(2)}) collective-permute-start(bf16[48,1536]{1,0:T(8,128)(2,1)S(1)} %get-tuple-element.67), channel_id=1, source_target_pairs={{0,4},{2,6},{4,0},{6,2},{1,5},{3,7},{5,1},{7,3},{8,12},{10,14},{12... | collective-permute-start | bytes 442376 | tf_op jit(solution)/shard_map/ppermute | solution.py:212
  371.2 16.0 %collective-permute-start.39 = (bf16[48,1536]{1,0:T(8,128)(2,1)S(1)}, bf16[48,1536]{1,0:T(8,128)(2,1)S(1)}, u32[]{:S(2)}, u32[]{:S(2)}) collective-permute-start(bf16[48,1536]{1,0:T(8,128)(2,1)S(1)} %get-tuple-element.67), channel_id=1, source_target_pairs={{0,6},{2,4},{4,2},{6,0},{1,7},{3,5},{5,3},{7,1},{8,14},{10,12},{12... | collective-permute-start | bytes 442376 | tf_op jit(solution)/shard_map/ppermute | solution.py:212
  383.6 4.9 %collective-permute-start.22 = (bf16[48,1152]{1,0:T(8,128)(2,1)S(1)}, bf16[48,1152]{1,0:T(8,128)(2,1)S(1)}, u32[]{:S(2)}, u32[]{:S(2)}) collective-permute-start(bf16[48,1152]{1,0:T(8,128)(2,1)S(1)} %get-tuple-element.110), channel_id=1, source_target_pairs={{0,2},{2,0},{4,6},{6,4},{1,3},{3,1},{5,7},{7,5},{8,10},{10,8},{12,... | collective-permute-start | bytes 331784 | tf_op jit(solution)/shard_map/ppermute | solution.py:212
  385.2 5.9 %collective-permute-start.23 = (bf16[48,1152]{1,0:T(8,128)(2,1)S(1)}, bf16[48,1152]{1,0:T(8,128)(2,1)S(1)}, u32[]{:S(2)}, u32[]{:S(2)}) collective-permute-start(bf16[48,1152]{1,0:T(8,128)(2,1)S(1)} %get-tuple-element.112), channel_id=1, source_target_pairs={{0,4},{2,6},{4,0},{6,2},{1,5},{3,7},{5,1},{7,3},{8,12},{10,14},{12... | collective-permute-start | bytes 331784 | tf_op jit(solution)/shard_map/ppermute | solution.py:212
  386.6 5.7 %collective-permute-start.24 = (bf16[48,1152]{1,0:T(8,128)(2,1)S(1)}, bf16[48,1152]{1,0:T(8,128)(2,1)S(1)}, u32[]{:S(2)}, u32[]{:S(2)}) collective-permute-start(bf16[48,1152]{1,0:T(8,128)(2,1)S(1)} %get-tuple-element.111), channel_id=1, source_target_pairs={{0,6},{2,4},{4,2},{6,0},{1,7},{3,5},{5,3},{7,1},{8,14},{10,12},{12... | collective-permute-start | bytes 331784 | tf_op jit(solution)/shard_map/ppermute | solution.py:212
  393.3 4.9 %collective-permute-start.25 = (bf16[48,1152]{1,0:T(8,128)(2,1)S(1)}, bf16[48,1152]{1,0:T(8,128)(2,1)S(1)}, u32[]{:S(2)}, u32[]{:S(2)}) collective-permute-start(bf16[48,1152]{1,0:T(8,128)(2,1)S(1)} %get-tuple-element.71), channel_id=1, source_target_pairs={{0,2},{2,0},{4,6},{6,4},{1,3},{3,1},{5,7},{7,5},{8,10},{10,8},{12,... | collective-permute-start | bytes 331784 | tf_op jit(solution)/shard_map/ppermute | solution.py:212
  395.4 5.4 %collective-permute-start.26 = (bf16[48,1152]{1,0:T(8,128)(2,1)S(1)}, bf16[48,1152]{1,0:T(8,128)(2,1)S(1)}, u32[]{:S(2)}, u32[]{:S(2)}) collective-permute-start(bf16[48,1152]{1,0:T(8,128)(2,1)S(1)} %get-tuple-element.71), channel_id=1, source_target_pairs={{0,4},{2,6},{4,0},{6,2},{1,5},{3,7},{5,1},{7,3},{8,12},{10,14},{12... | collective-permute-start | bytes 331784 | tf_op jit(solution)/shard_map/ppermute | solution.py:212
  396.3 5.7 %collective-permute-start.27 = (bf16[48,1152]{1,0:T(8,128)(2,1)S(1)}, bf16[48,1152]{1,0:T(8,128)(2,1)S(1)}, u32[]{:S(2)}, u32[]{:S(2)}) collective-permute-start(bf16[48,1152]{1,0:T(8,128)(2,1)S(1)} %get-tuple-element.71), channel_id=1, source_target_pairs={{0,6},{2,4},{4,2},{6,0},{1,7},{3,5},{5,3},{7,1},{8,14},{10,12},{12... | collective-permute-start | bytes 331784 | tf_op jit(solution)/shard_map/ppermute | solution.py:212
  (45 other events, 378.4 us)
Sparse Core Ops, SparseCore 0:
  10.2 52.4 all-gather.3
  64.2 49.2 all-gather.5
  115.2 49.2 all-gather.7
  223.1 19.8 reduce-scatter.6
  245.1 46.3 reduce-scatter.10
  293.7 48.7 reduce-scatter.8
  344.8 37.7 reduce-scatter.12

commit v2 on v0

--- a/solution.py
+++ b/solution.py
@@ -1,13 +1,14 @@
 import jax
 import jax.numpy as jnp
 from jax import lax
+from jax.experimental import pallas as pl
+from jax.experimental.pallas import tpu as pltpu
 from jax.sharding import PartitionSpec as P
 
 HEAD_DIM = 64
-
-
 NORM_EPS = 1e-05
 MASKED = -1e30
+LANES = 128
 
 
 def layer_norm(values_in, gain_vec, shift_vec):
@@ -33,7 +34,770 @@
     return jnp.where(allowed, raw_scores, MASKED)
 
 
-def local(
+def rows_by_rows(left, right):
+    return lax.dot_general(left, right, (((1,), (1,)), ((), ())), preferred_element_type=jnp.float32)
+
+
+def plain_dot(left, right):
+    return jnp.dot(left, right, preferred_element_type=jnp.float32)
+
+
+def lanes_of(head, lane):
+    own = (lane < HEAD_DIM) if head == 0 else (lane >= HEAD_DIM)
+    spare = HEAD_DIM if head == 0 else 0
+    return own, lane == spare
+
+
+def head_operands(query_ref, key_ref, slot, start, block, valid_count, head):
+    lane = lax.broadcasted_iota(jnp.int32, (block, LANES), 1)
+    own, spare = lanes_of(head, lane)
+    position = start + lax.broadcasted_iota(jnp.int32, (block, LANES), 0)
+    bias = jnp.where(position < valid_count, 0.0, MASKED)
+    rows = pl.ds(slot * block, block)
+    query = query_ref[rows, :].astype(jnp.float32) * (HEAD_DIM ** -0.5)
+    key = key_ref[rows, :].astype(jnp.float32)
+    query_side = jnp.where(spare, 1.0, query).astype(jnp.bfloat16)
+    key_side = jnp.where(own, key, jnp.where(spare, bias, 0.0)).astype(jnp.bfloat16)
+    return query_side, key_side
+
+
+def attend_kernel(facts, query_ref, key_ref, value_ref, out_ref, log_ref, *, block):
+    valid_count = facts[0]
+    blocks = query_ref.shape[0] // block
+    slots = list(range(blocks))
+    value_t = [
+        value_ref[pl.ds(slots[j] * block, block), :].astype(jnp.float32).T.astype(jnp.bfloat16)
+        for j in range(blocks)
+    ]
+    outs = [[] for _ in range(blocks)]
+    for head in range(2):
+        sides = [
+            head_operands(query_ref, key_ref, slots[j], j * block, block, valid_count, head)
+            for j in range(blocks)
+        ]
+        span = slice(head * HEAD_DIM, (head + 1) * HEAD_DIM)
+        for i in range(blocks):
+            scores = [rows_by_rows(sides[j][1], sides[i][0]) for j in range(i + 1)]
+            top = scores[0].max(axis=0, keepdims=True)
+            for j in range(1, i + 1):
+                top = jnp.maximum(top, scores[j].max(axis=0, keepdims=True))
+            total = jnp.zeros_like(top)
+            mixed = jnp.zeros((HEAD_DIM, block), jnp.float32)
+            for j in range(i + 1):
+                weight = jnp.exp(scores[j] - top)
+                total = total + weight.sum(axis=0, keepdims=True)
+                mixed = mixed + plain_dot(value_t[j][span, :], weight.astype(jnp.bfloat16))
+            outs[i].append(mixed / total)
+            log_ref[0, head : head + 1, i * block : (i + 1) * block] = top + jnp.log(total)
+    for i in range(blocks):
+        both = jnp.concatenate(outs[i], axis=0)
+        out_ref[pl.ds(slots[i] * block, block), :] = both.T.astype(out_ref.dtype)
+
+
+def attend_back_kernel(
+    facts,
+    query_ref,
+    key_ref,
+    value_ref,
+    grad_ref,
+    log_ref,
+    out_ref,
+    stats_ref,
+    grad_key,
+    grad_value,
+    *,
+    block,
+):
+    valid_count = facts[0]
+    blocks = query_ref.shape[0] // block
+    slots = list(range(blocks))
+    scaling = HEAD_DIM ** -0.5
+    lane = lax.broadcasted_iota(jnp.int32, (block, LANES), 1)
+    key_t, grads, queries, values = [], [], [], []
+    for j in range(blocks):
+        rows = pl.ds(slots[j] * block, block)
+        key_t.append((key_ref[rows, :].astype(jnp.float32) * scaling).T.astype(jnp.bfloat16))
+        grads.append(grad_ref[rows, :])
+        queries.append(query_ref[rows, :].astype(jnp.float32) * scaling)
+        values.append(value_ref[rows, :].astype(jnp.float32))
+    grad_queries = [[] for _ in range(blocks)]
+    for head in range(2):
+        own, _ = lanes_of(head, lane)
+        span = slice(head * HEAD_DIM, (head + 1) * HEAD_DIM)
+        sides = [
+            head_operands(query_ref, key_ref, slots[j], j * block, block, valid_count, head)
+            for j in range(blocks)
+        ]
+        head_values = [jnp.where(own, item, 0.0).astype(jnp.bfloat16) for item in values]
+        for i in range(blocks):
+            log_row = log_ref[0, head : head + 1, i * block : (i + 1) * block]
+            head_grad = jnp.where(own, grads[i].astype(jnp.float32), 0.0).astype(jnp.bfloat16)
+            head_query = jnp.where(own, queries[i], 0.0).astype(jnp.bfloat16)
+            probs, pushes = [], []
+            delta = jnp.zeros((1, block), jnp.float32)
+            for j in range(i + 1):
+                prob = jnp.exp(rows_by_rows(sides[j][1], sides[i][0]) - log_row)
+                push = rows_by_rows(head_values[j], grads[i])
+                delta = delta + (prob * push).sum(axis=0, keepdims=True)
+                probs.append(prob)
+                pushes.append(push)
+            grad_query = jnp.zeros((HEAD_DIM, block), jnp.float32)
+            for j in range(i + 1):
+                slope = (probs[j] * (pushes[j] - delta)).astype(jnp.bfloat16)
+                part_value = plain_dot(probs[j].astype(jnp.bfloat16), head_grad)
+                part_key = plain_dot(slope, head_query)
+                span_rows = slice(j * block, (j + 1) * block)
+                if head == 0 and i == j:
+                    grad_value[span_rows, :] = part_value
+                    grad_key[span_rows, :] = part_key
+                else:
+                    grad_value[span_rows, :] += part_value
+                    grad_key[span_rows, :] += part_key
+                grad_query = grad_query + plain_dot(key_t[j][span, :], slope)
+            grad_queries[i].append(grad_query)
+    totals = jnp.zeros((1, 3 * LANES), jnp.float32)
+    for i in range(blocks):
+        rows = pl.ds(slots[i] * block, block)
+        both = jnp.concatenate(grad_queries[i], axis=0)
+        out_ref[rows, :LANES] = both.T.astype(out_ref.dtype)
+        span_rows = slice(i * block, (i + 1) * block)
+        out_ref[rows, LANES : 2 * LANES] = grad_key[span_rows, :].astype(out_ref.dtype)
+        out_ref[rows, 2 * LANES :] = grad_value[span_rows, :].astype(out_ref.dtype)
+        totals += jnp.sum(out_ref[rows, :].astype(jnp.float32), axis=0, keepdims=True)
+    stats_ref[...] = jnp.broadcast_to(totals, stats_ref.shape)
+
+
+def attend(facts, projected, block):
+    length, width = projected.shape
+    pairs = width // (3 * LANES)
+    column = lambda kind: pl.BlockSpec((length, LANES), lambda pair, facts: (0, 3 * pair + kind))
+    return pl.pallas_call(
+        lambda *refs: attend_kernel(*refs, block=block),
+        grid_spec=pltpu.PrefetchScalarGridSpec(
+            num_scalar_prefetch=1,
+            grid=(pairs,),
+            in_specs=[column(0), column(1), column(2)],
+            out_specs=[
+                pl.BlockSpec((length, LANES), lambda pair, facts: (0, pair)),
+                pl.BlockSpec((1, 2, length), lambda pair, facts: (pair, 0, 0)),
+            ],
+        ),
+        out_shape=[
+            jax.ShapeDtypeStruct((length, pairs * LANES), jnp.bfloat16),
+            jax.ShapeDtypeStruct((pairs, 2, length), jnp.float32),
+        ],
+        name="attend",
+    )(facts, projected, projected, projected)
+
+
+def attend_back(facts, projected, grad_attended, log_total, block):
+    length, width = grad_attended.shape
+    pairs = width // LANES
+    column = lambda kind: pl.BlockSpec((length, LANES), lambda pair, facts: (0, 3 * pair + kind))
+    return pl.pallas_call(
+        lambda *refs: attend_back_kernel(*refs, block=block),
+        grid_spec=pltpu.PrefetchScalarGridSpec(
+            num_scalar_prefetch=1,
+            grid=(pairs,),
+            in_specs=[
+                column(0),
+                column(1),
+                column(2),
+                pl.BlockSpec((length, LANES), lambda pair, facts: (0, pair)),
+                pl.BlockSpec((1, 2, length), lambda pair, facts: (pair, 0, 0)),
+            ],
+            out_specs=[
+                pl.BlockSpec((length, 3 * LANES), lambda pair, facts: (0, pair)),
+                pl.BlockSpec((8, 3 * LANES), lambda pair, facts: (0, pair)),
+            ],
+            scratch_shapes=[
+                pltpu.VMEM((length, LANES), jnp.float32),
+                pltpu.VMEM((length, LANES), jnp.float32),
+            ],
+        ),
+        out_shape=[
+            jax.ShapeDtypeStruct((length, 3 * width), jnp.bfloat16),
+            jax.ShapeDtypeStruct((8, 3 * width), jnp.float32),
+        ],
+        name="attend_back",
+    )(facts, projected, projected, projected, grad_attended, log_total)
+
+
+def by_pairs(values):
+    kinds, width = values.shape[-2:]
+    cut = values.reshape(values.shape[:-1] + (width // LANES, LANES))
+    return jnp.swapaxes(cut, -3, -2).reshape(values.shape[:-2] + (kinds * width,))
+
+
+def by_kinds(values, kinds=3):
+    width = values.shape[-1] // kinds
+    cut = values.reshape(values.shape[:-1] + (width // LANES, kinds, LANES))
+    return jnp.swapaxes(cut, -3, -2).reshape(values.shape[:-1] + (kinds, width))
+
+
+def assemble_kernel(facts, own_ref, *refs, fsdp, count, rows):
+    part_refs, out_ref = refs[:count], refs[count]
+    place, depth = facts[0], facts[1]
+    out_ref[pl.ds(depth * (rows * count), rows * count), :] = own_ref[...]
+    for s in range(count):
+        for d in range(1, fsdp):
+            start = lax.bitwise_xor(depth, jnp.int32(d)) * (rows * count)
+            start = start + lax.bitwise_xor(place, jnp.int32(s)) * rows
+            out_ref[pl.ds(pl.multiple_of(start, rows), rows), :] = part_refs[s][
+                (d - 1) * rows : d * rows, :
+            ]
+
+
+def assemble(places, own, parts):
+    fsdp, count = lax.axis_size("fsdp"), len(parts)
+    rows = own.shape[0] // count
+    width = 3 * LANES if own.shape[1] % (3 * LANES) == 0 else own.shape[1]
+    whole_block = lambda shape: pl.BlockSpec((shape[0], width), lambda step, facts: (0, step))
+    out_shape = (fsdp * own.shape[0], own.shape[1])
+    return pl.pallas_call(
+        lambda *refs: assemble_kernel(*refs, fsdp=fsdp, count=count, rows=rows),
+        grid_spec=pltpu.PrefetchScalarGridSpec(
+            num_scalar_prefetch=1,
+            grid=(own.shape[1] // width,),
+            in_specs=[whole_block(own.shape)] + [whole_block(item.shape) for item in parts],
+            out_specs=whole_block(out_shape),
+        ),
+        out_shape=jax.ShapeDtypeStruct(out_shape, own.dtype),
+        name="assemble",
+    )(places, own, *parts)
+
+
+def swap(values, axis, step):
+    pairs = [(place, place ^ step) for place in range(lax.axis_size(axis))]
+    return lax.ppermute(values, axis, pairs)
+
+
+def swap_all(values, axis):
+    return [swap(values, axis, step) for step in range(1, lax.axis_size(axis))]
+
+
+def relay_all(values, axis):
+    if lax.axis_size(axis) != 4:
+        return swap_all(values, axis)
+    first, second = swap(values, axis, 1), swap(values, axis, 2)
+    return [first, second, swap(first, axis, 2)]
+
+
+def swap_each(pieces, axis):
+    return [swap(pieces[step], axis, step) for step in range(1, len(pieces))]
+
+
+def together(*values):
+    return lax.optimization_barrier(values)
+
+
+def wide(values):
+    return values.astype(jnp.float32)
+
+
+def low(values):
+    return values.astype(jnp.bfloat16)
+
+
+def add_partner(values):
+    mine = low(values)
+    return wide(mine) + wide(swap(mine, "tp", 1))
+
+
+def add_up(pieces):
+    pieces = [wide(item) for item in pieces]
+    while len(pieces) > 1:
+        pieces = [pieces[i] + pieces[i + 1] for i in range(0, len(pieces), 2)]
+    return pieces[0]
+
+
+def sum_over(values, axis):
+    step = 1
+    while step < lax.axis_size(axis):
+        values = values + swap(values, axis, step)
+        step *= 2
+    return values
+
+
+def deal(pieces, axis):
+    return lax.all_to_all(pieces, axis, 0, 0)
+
+
+def own_half(blocks):
+    rows = blocks.shape[1] // 2
+    return lax.dynamic_slice_in_dim(blocks, lax.axis_index("tp") * rows, rows, 1)
+
+
+def row_kernel_stats(stats_ref, step, rows):
+    @pl.when(step == 0)
+    def _():
+        stats_ref[...] = jnp.zeros_like(stats_ref)
+
+    for index, row in enumerate(rows):
+        stats_ref[index : index + 1, :] += jnp.sum(row, axis=0, keepdims=True)
+
+
+def normalize(values):
+    mean = jnp.mean(values, axis=-1, keepdims=True)
+    centered = values - mean
+    scale = lax.rsqrt(jnp.mean(centered * centered, axis=-1, keepdims=True) + NORM_EPS)
+    return centered * scale, scale
+
+
+def normalize_back(grads, normal, scale, gain):
+    pushed = grads * gain
+    mean = jnp.mean(pushed, axis=-1, keepdims=True)
+    along = jnp.mean(pushed * normal, axis=-1, keepdims=True)
+    return (pushed - mean - normal * along) * scale
+
+
+def first_norm_kernel(
+    hidden_ref, mine_ref, other_ref, bias_ref, gain_ref, shift_ref, normal_ref, scale_ref, low_ref
+):
+    branch = mine_ref[...].astype(jnp.float32) + other_ref[...].astype(jnp.float32)
+    normal, scale = normalize(hidden_ref[...].astype(jnp.float32) + branch + bias_ref[...])
+    normal_ref[...] = normal
+    scale_ref[...] = scale
+    low_ref[...] = (normal * gain_ref[...] + shift_ref[...]).astype(low_ref.dtype)
+
+
+def second_norm_kernel(
+    facts,
+    normal_ref,
+    gain1_ref,
+    shift1_ref,
+    mine_ref,
+    other_ref,
+    bias_ref,
+    gain_ref,
+    shift_ref,
+    own_teacher_ref,
+    other_teacher_ref,
+    half_ref,
+    grad_ref,
+    low_ref,
+    stats_ref,
+):
+    step = pl.program_id(0)
+    block = normal_ref.shape[0]
+    rows = block // 2
+    branch = mine_ref[...].astype(jnp.float32) + other_ref[...].astype(jnp.float32)
+    normed1 = normal_ref[...] * gain1_ref[...] + shift1_ref[...]
+    normal, scale = normalize(normed1 + branch + bias_ref[...])
+    output = normal * gain_ref[...] + shift_ref[...]
+    first = facts[1] == 0
+    half_ref[0] = jnp.where(first, output[:rows], output[rows:]).astype(half_ref.dtype)
+    own, other = own_teacher_ref[0], other_teacher_ref[0]
+    own, other = own.astype(jnp.float32), other.astype(jnp.float32)
+    teacher = jnp.concatenate(
+        [jnp.where(first, own, other), jnp.where(first, other, own)], axis=0
+    )
+    position = step * block + lax.broadcasted_iota(jnp.int32, (block, 1), 0)
+    residue = jnp.where(position < facts[0], output - teacher, 0.0)
+    grads = normalize_back(residue, normal, scale, gain_ref[...])
+    grad_ref[...] = grads
+    low_ref[...] = grads.astype(low_ref.dtype)
+    row_kernel_stats(stats_ref, step, [grads, residue * normal, residue, residue * residue])
+
+
+def first_norm_back_kernel(
+    facts,
+    grad_ref,
+    mine_ref,
+    other_ref,
+    normal_ref,
+    scale_ref,
+    gain_ref,
+    low_ref,
+    half_ref,
+    stats_ref,
+):
+    rows = grad_ref.shape[0] // 2
+    branch = mine_ref[...].astype(jnp.float32) + other_ref[...].astype(jnp.float32)
+    pushed = grad_ref[...] + branch
+    normal = normal_ref[...]
+    grads = normalize_back(pushed, normal, scale_ref[...], gain_ref[...])
+    low_ref[...] = grads.astype(low_ref.dtype)
+    half_ref[0] = jnp.where(facts[1] == 0, grads[:rows], grads[rows:])
+    row_kernel_stats(stats_ref, pl.program_id(0), [grads, pushed * normal, pushed])
+
+
+def by_rows(kernel, name, block, operands, results, facts=None, stats=0):
+    def spec(shape):
+        if len(shape) == 3:
+            return pl.BlockSpec((1,) + shape[1:], lambda step, *_: (step, 0, 0))
+        if shape[0] == 1:
+            return pl.BlockSpec(shape, lambda step, *_: (0, 0))
+        return pl.BlockSpec((block, shape[1]), lambda step, *_: (step, 0))
+
+    length = next(item.shape[0] for item in operands if item.ndim == 2 and item.shape[0] > 1)
+    out_specs = [spec(item.shape) for item in results]
+    if stats:
+        results = results + [jax.ShapeDtypeStruct((8, stats), jnp.float32)]
+        out_specs.append(pl.BlockSpec((8, stats), lambda step, *_: (0, 0)))
+    return pl.pallas_call(
+        kernel,
+        grid_spec=pltpu.PrefetchScalarGridSpec(
+            num_scalar_prefetch=0 if facts is None else 1,
+            grid=(length // block,),
+            in_specs=[spec(item.shape) for item in operands],
+            out_specs=out_specs,
+        ),
+        out_shape=results,
+        name=name,
+    )(*([] if facts is None else [facts]), *operands)
+
+
+def up_kernel(low_ref, weight_ref, bias_ref, active_ref, slope_ref):
+    pre = plain_dot(low_ref[...], weight_ref[...]) + bias_ref[...]
+    below = 0.5 * (1.0 + lax.erf(pre * (0.5**0.5)))
+    active_ref[...] = (pre * below).astype(active_ref.dtype)
+    bell = jnp.exp(-0.5 * pre * pre) * 0.3989422804014327
+    slope_ref[...] = (below + pre * bell).astype(slope_ref.dtype)
+
+
+def grad_pre_kernel(low_ref, weight_ref, slope_ref, out_ref, stats_ref):
+    grads = plain_dot(low_ref[...], weight_ref[...]) * slope_ref[...].astype(jnp.float32)
+    grads = grads.astype(out_ref.dtype)
+    out_ref[...] = grads
+    row_kernel_stats(stats_ref, pl.program_id(0), [grads.astype(jnp.float32)])
+
+
+def wide_layer(kernel, name, block, low, weight, operands, count, stats=0):
+    length, width = low.shape[0], weight.shape[1]
+
+    def spec(shape):
+        if shape[0] == 1:
+            return pl.BlockSpec(shape, lambda step: (0, 0))
+        return pl.BlockSpec((block, shape[1]), lambda step: (step, 0))
+
+    out_specs = [pl.BlockSpec((block, width), lambda step: (step, 0))] * count
+    out_shape = [jax.ShapeDtypeStruct((length, width), jnp.bfloat16)] * count
+    if stats:
+        out_specs = out_specs + [pl.BlockSpec((8, width), lambda step: (0, 0))]
+        out_shape = out_shape + [jax.ShapeDtypeStruct((8, width), jnp.float32)]
+    return pl.pallas_call(
+        kernel,
+        grid=(length // block,),
+        in_specs=[spec(low.shape), pl.BlockSpec(weight.shape, lambda step: (0, 0))]
+        + [spec(item.shape) for item in operands],
+        out_specs=out_specs,
+        out_shape=out_shape,
+        name=name,
+    )(low, weight, *operands)
+
+
+def pack_kernel(second_ref, first_ref, up_ref, qkv_ref, count_ref, out_ref):
+    width = out_ref.shape[1]
+    out_ref[...] = jnp.zeros_like(out_ref)
+    out_ref[0:4, :] = second_ref[0:4, :]
+    out_ref[4:7, :] = first_ref[0:3, :]
+    row = 7
+    for ref in (up_ref, qkv_ref, count_ref):
+        for start in range(0, ref.shape[1], width):
+            span = min(width, ref.shape[1] - start)
+            out_ref[row : row + 1, :span] = ref[0:1, start : start + span]
+            row += 1
+
+
+def pack(second, first, up, qkv, count):
+    width = second.shape[1]
+    rows = 7 + sum(-(-item.shape[1] // width) for item in (up, qkv, count))
+    return pl.pallas_call(
+        pack_kernel,
+        out_shape=jax.ShapeDtypeStruct((-(-rows // 8) * 8, width), jnp.float32),
+        name="pack",
+    )(second, first, up, qkv, count)
+
+
+def join_kernel(facts, ratio_ref, own_ref, other_ref, out_ref):
+    rows = own_ref.shape[1]
+    for ref, half in ((own_ref, facts[0]), (other_ref, 1 - facts[0])):
+        values = ref[0].astype(jnp.float32) * ratio_ref[0]
+        out_ref[0, pl.ds(pl.multiple_of(half * rows, rows), rows), :] = values.astype(out_ref.dtype)
+
+
+def join_halves(half, ratio=None, dtype=jnp.bfloat16):
+    count, rows, width = half.shape
+    ratio = jnp.ones((1,), jnp.float32) if ratio is None else ratio.reshape(1)
+    return pl.pallas_call(
+        join_kernel,
+        grid_spec=pltpu.PrefetchScalarGridSpec(
+            num_scalar_prefetch=1,
+            grid=(count,),
+            in_specs=[pl.BlockSpec(memory_space=pltpu.SMEM)]
+            + [pl.BlockSpec((1, rows, width), lambda step, facts: (step, 0, 0))] * 2,
+            out_specs=pl.BlockSpec((1, 2 * rows, width), lambda step, facts: (step, 0, 0)),
+        ),
+        out_shape=jax.ShapeDtypeStruct((count, 2 * rows, width), dtype),
+        name="join_halves",
+    )(lax.axis_index("tp").reshape(1), ratio, half, swap(half, "tp", 1))
+
+
+def weight_grad_kernel(places, left_ref, right_ref, *refs, fsdp, count):
+    total = lax.dot_general(
+        left_ref[...],
+        right_ref[...],
+        (((0,), (0,)), ((), ())),
+        preferred_element_type=jnp.float32,
+    )
+    out_refs, held = refs[:-1], refs[-1]
+    held[...] = total.astype(held.dtype)
+    rows = held.shape[0] // (fsdp * count)
+    for s in range(count):
+        for d in range(fsdp):
+            start = d * rows * count + lax.bitwise_xor(places[0], jnp.int32(s)) * rows
+            out_refs[s][d * rows : (d + 1) * rows, :] = held[
+                pl.ds(pl.multiple_of(start, rows), rows), :
+            ]
+
+
+def weight_grad(places, left, right):
+    fsdp, count = lax.axis_size("fsdp"), lax.axis_size("ctx")
+    tokens, rows = left.shape
+    columns = right.shape[1]
+    width = max(item for item in range(LANES, 6 * LANES + 1, LANES) if columns % item == 0)
+    return pl.pallas_call(
+        lambda *refs: weight_grad_kernel(*refs, fsdp=fsdp, count=count),
+        grid_spec=pltpu.PrefetchScalarGridSpec(
+            num_scalar_prefetch=1,
+            grid=(columns // width,),
+            in_specs=[
+                pl.BlockSpec((tokens, rows), lambda step, places: (0, 0)),
+                pl.BlockSpec((tokens, width), lambda step, places: (0, step)),
+            ],
+            out_specs=[pl.BlockSpec((rows // count, width), lambda step, places: (0, step))]
+            * count,
+            scratch_shapes=[pltpu.VMEM((rows, width), jnp.bfloat16)],
+        ),
+        out_shape=[jax.ShapeDtypeStruct((rows // count, columns), jnp.bfloat16)] * count,
+        name="weight_grad",
+    )(places, left, right)
+
+
+def place_kernel(places, ratio_ref, *refs):
+    part_refs, out_ref = refs[:-1], refs[-1]
+    rows = part_refs[0].shape[0]
+    ratio = ratio_ref[0]
+    for s in range(len(part_refs)):
+        start = lax.bitwise_xor(places[0], jnp.int32(s)) * rows
+        out_ref[pl.ds(pl.multiple_of(start, rows), rows), :] = (
+            part_refs[s][...].astype(jnp.float32) * ratio
+        )
+
+
+def place_rows(places, parts, ratio):
+    rows, columns = parts[0].shape
+    width = 3 * LANES if columns % (3 * LANES) == 0 else columns
+    block = pl.BlockSpec((rows, width), lambda step, places: (0, step))
+    return pl.pallas_call(
+        place_kernel,
+        grid_spec=pltpu.PrefetchScalarGridSpec(
+            num_scalar_prefetch=1,
+            grid=(columns // width,),
+            in_specs=[pl.BlockSpec(memory_space=pltpu.SMEM)] + [block] * len(parts),
+            out_specs=pl.BlockSpec((rows * len(parts), width), lambda step, places: (0, step)),
+        ),
+        out_shape=jax.ShapeDtypeStruct((rows * len(parts), columns), jnp.float32),
+        name="place_rows",
+    )(places, ratio.reshape(1), *parts)
+
+
+def whole_local(
+    hidden_in,
+    valid_mask,
+    teacher,
+    qkv_weight,
+    qv_bias,
+    out_weight,
+    out_bias,
+    norm1_gain,
+    norm1_shift,
+    up_weight,
+    up_bias,
+    down_weight,
+    down_bias,
+    norm2_gain,
+    norm2_shift,
+):
+    seq_count, block_len, model_width = hidden_in.shape
+    ctx_count = lax.axis_size("ctx")
+    place, depth, core = lax.axis_index("ctx"), lax.axis_index("fsdp"), lax.axis_index("tp")
+    inner_width = qkv_weight.shape[2]
+    hidden_width = up_weight.shape[1]
+    row_count = seq_count * block_len
+    shape = hidden_in.shape
+    places = jnp.stack([place, depth])
+    fsdp_count = lax.axis_size("fsdp")
+    row = lambda values: values.reshape(1, -1)
+    struct = jax.ShapeDtypeStruct
+    part_rows = qkv_weight.shape[0] // ctx_count
+    qkv_out = jnp.concatenate([by_pairs(qkv_weight), out_weight], axis=1)
+    local_counts = jnp.sum(wide(valid_mask), axis=1)
+    weight_rows = swap_all(
+        lax.dynamic_slice_in_dim(qkv_out, place * part_rows, part_rows, 0), "fsdp"
+    )
+    hidden_half = deal(own_half(hidden_in), "ctx")
+    full_up = lax.all_gather(up_weight, "fsdp", axis=0, tiled=True)
+    full_down = lax.all_gather(down_weight, "fsdp", axis=0, tiled=True)
+    weight_rows, hidden_half = together(weight_rows, hidden_half)
+    count_rows = jnp.broadcast_to(
+        jnp.pad(low(local_counts), (0, qkv_out.shape[1] - seq_count)), (16, qkv_out.shape[1])
+    )
+    weight_part = jnp.concatenate(weight_rows + [count_rows], axis=0)
+    weight_parts = [weight_part] + relay_all(weight_part, "ctx")
+    flat_in = join_halves(hidden_half).reshape(row_count, model_width)
+    full_bias = by_pairs(jnp.stack([qv_bias[0], jnp.zeros_like(qv_bias[0]), qv_bias[1]]))
+    weight_parts, flat_in, teacher_own = together(weight_parts, flat_in, own_half(teacher))
+    full_qkv_out = assemble(places, qkv_out, weight_parts)
+    full_qkv, full_out = full_qkv_out[:, : 3 * inner_width], full_qkv_out[:, 3 * inner_width :]
+    counts = sum(wide(item[-16, :LANES]) for item in weight_parts)
+    valid_count = lax.dynamic_index_in_dim(counts, place, 0, keepdims=False).astype(jnp.int32)
+    facts = jnp.stack([valid_count, core])
+    teacher_half = deal(teacher_own, "ctx")
+    projected = low(jnp.dot(flat_in, full_qkv, preferred_element_type=jnp.float32) + full_bias)
+    attended, log_total = attend(facts, projected, block_len)
+    branch = low(jnp.einsum("te,de->td", attended, full_out, preferred_element_type=jnp.float32))
+    normal1, scale1, normed1_low = by_rows(
+        first_norm_kernel,
+        "first_norm",
+        block_len,
+        [flat_in, branch, swap(branch, "tp", 1), row(out_bias), row(norm1_gain), row(norm1_shift)],
+        [
+            struct((row_count, model_width), jnp.float32),
+            struct((row_count, 1), jnp.float32),
+            struct((row_count, model_width), jnp.bfloat16),
+        ],
+    )
+    normed1_low, teacher_half = together(normed1_low, teacher_half)
+    active, slope = wide_layer(
+        up_kernel, "up", block_len, normed1_low, full_up, [row(up_bias)], 2
+    )
+    branch = low(jnp.einsum("tf,df->td", active, full_down, preferred_element_type=jnp.float32))
+    layer_half, grad_resid2, grad_resid2_low, stats2 = by_rows(
+        second_norm_kernel,
+        "second_norm",
+        block_len,
+        [
+            normal1,
+            row(norm1_gain),
+            row(norm1_shift),
+            branch,
+            swap(branch, "tp", 1),
+            row(down_bias),
+            row(norm2_gain),
+            row(norm2_shift),
+            teacher_half,
+            swap(teacher_half, "tp", 1),
+        ],
+        [
+            struct(teacher_half.shape, jnp.bfloat16),
+            struct((row_count, model_width), jnp.float32),
+            struct((row_count, model_width), jnp.bfloat16),
+        ],
+        facts=facts,
+        stats=model_width,
+    )
+    grad_down = low(
+        jnp.einsum("td,tf->df", grad_resid2_low, active, preferred_element_type=jnp.float32)
+    )
+    grad_down, grad_resid2_low, layer_half = together(grad_down, grad_resid2_low, layer_half)
+    owned_down = lax.psum_scatter(grad_down, "fsdp", scatter_dimension=0, tiled=True)
+    grad_pre, stats_up = wide_layer(
+        grad_pre_kernel, "grad_pre", block_len, grad_resid2_low, full_down, [slope], 1, hidden_width
+    )
+    grad_up = low(
+        jnp.einsum("td,tf->df", normed1_low, grad_pre, preferred_element_type=jnp.float32)
+    )
+    grad_pre, grad_up, layer_half = together(grad_pre, grad_up, layer_half)
+    owned_up = lax.psum_scatter(grad_up, "fsdp", scatter_dimension=0, tiled=True)
+    layer_half = deal(layer_half, "ctx")
+    branch = low(jnp.einsum("tf,df->td", grad_pre, full_up, preferred_element_type=jnp.float32))
+    grad_resid1_low, grad_half, stats1 = by_rows(
+        first_norm_back_kernel,
+        "first_norm_back",
+        block_len,
+        [grad_resid2, branch, swap(branch, "tp", 1), normal1, scale1, row(norm1_gain)],
+        [
+            struct((row_count, model_width), jnp.bfloat16),
+            struct(layer_half.shape, jnp.float32),
+        ],
+        facts=facts,
+        stats=model_width,
+    )
+    out_pieces = weight_grad(places, grad_resid1_low, attended)
+    grad_attended = low(jnp.dot(grad_resid1_low, full_out, preferred_element_type=jnp.float32))
+    grad_attended, out_pieces, owned_down, layer_half = together(
+        grad_attended, out_pieces, owned_down, layer_half
+    )
+    down_other = swap(owned_down, "ctx", 1)
+    out_sums = swap_each(out_pieces, "ctx")
+    grad_qkv, stats_qkv = attend_back(facts, projected, grad_attended, log_total, block_len)
+    grad_qkv, down_other, out_sums = together(grad_qkv, down_other, out_sums)
+    qkv_pieces = weight_grad(places, flat_in, grad_qkv)
+    qkv_pieces, grad_qkv, down_other, out_sums, layer_half = together(
+        qkv_pieces, grad_qkv, down_other, out_sums, layer_half
+    )
+    qkv_sums = swap_each(qkv_pieces, "ctx")
+    layer_out = join_halves(layer_half)
+    input_part = jnp.einsum("te,de->td", grad_qkv, full_qkv, preferred_element_type=jnp.float32)
+    parts = low(input_part).reshape(seq_count, 2, block_len // 2, model_width)
+    mine = lax.dynamic_index_in_dim(parts, core, 1, keepdims=False)
+    other = swap(lax.dynamic_index_in_dim(parts, 1 - core, 1, keepdims=False), "tp", 1)
+    half = low(grad_half + (wide(mine) + wide(other)))
+    owned_down = low(wide(owned_down) + wide(down_other))
+    down_other = swap(owned_down, "ctx", 2)
+    local_count = jnp.broadcast_to(jnp.sum(local_counts), (1, LANES))
+    small = pack(stats2, stats1, stats_up, stats_qkv, local_count)
+    out_part = add_up([out_pieces[0]] + out_sums)
+    qkv_sums, down_other, half, small, out_part, owned_up = together(
+        qkv_sums, down_other, half, small, out_part, owned_up
+    )
+    part = low(jnp.concatenate([add_up([qkv_pieces[0]] + qkv_sums), out_part], axis=1))
+    pieces = deal(part.reshape(fsdp_count, -1, part.shape[1]), "fsdp")
+    up_other = swap(owned_up, "ctx", 1)
+    small = sum_over(small, "ctx")
+    pieces, half, small, up_other = together(pieces, half, small, up_other)
+    part = low(add_up([pieces[d] for d in range(fsdp_count)]))
+    qkv_out_owned = [part] + relay_all(part, "ctx")
+    owned_up = low(wide(owned_up) + wide(up_other))
+    up_other = swap(owned_up, "ctx", 2)
+    input_half = deal(half, "ctx")
+    small = sum_over(small, "fsdp")
+    at = 7 + -(-hidden_width // model_width)
+    counted = small[at + -(-3 * inner_width // model_width), 0]
+    ratio = float(row_count * ctx_count * fsdp_count) / counted
+    loss = jnp.sum(small[3]) / (counted * model_width)
+    scaled = small * ratio
+    grad_up_bias = scaled[7:at].reshape(-1)[:hidden_width]
+    grad_qv_bias = by_kinds(
+        scaled[at : at + -(-3 * inner_width // model_width)].reshape(-1)[: 3 * inner_width]
+    )[0::2]
+    owned_up = (wide(owned_up) + wide(up_other)) * ratio
+    owned_down = (wide(owned_down) + wide(down_other)) * ratio
+    owned_qkv_out = place_rows(places, qkv_out_owned, ratio)
+    owned_qkv = by_kinds(owned_qkv_out[:, : 3 * inner_width])
+    input_grad = join_halves(input_half, ratio, jnp.float32)
+    return (
+        layer_out,
+        input_grad,
+        loss,
+        owned_qkv,
+        grad_qv_bias,
+        owned_qkv_out[:, 3 * inner_width :],
+        scaled[4],
+        scaled[5],
+        scaled[6],
+        owned_up,
+        grad_up_bias,
+        owned_down,
+        scaled[0],
+        scaled[1],
+        scaled[2],
+    )
+
+
+def spread_local(
     hidden_in,
     valid_mask,
     teacher,
@@ -286,6 +1050,23 @@
     )
 
 
+def local(hidden_in, *others):
+    seq_count, block_len, model_width = hidden_in.shape
+    ctx_count, fsdp_count = lax.axis_size("ctx"), lax.axis_size("fsdp")
+    rows, inner_width = others[2].shape[0], others[2].shape[2]
+    whole = (
+        seq_count == ctx_count
+        and ctx_count & (ctx_count - 1) == 0
+        and fsdp_count & (fsdp_count - 1) == 0
+        and lax.axis_size("tp") == 2
+        and block_len % LANES == 0
+        and others[5].shape[0] >= inner_width
+        and inner_width % LANES == 0
+        and rows % (16 * ctx_count) == 0
+    )
+    return (whole_local if whole else spread_local)(hidden_in, *others)
+
+
 def solution(mesh):
     in_specs = (
         P("fsdp", "ctx", None),

time: 797 us -> 363 us (0.46)
  waiting for transfers between devices: 490 us -> 111 us
  blocking collectives: 101 us -> 0 us
  Pallas kernels: 0 us -> 98.2 us
  matrix products: 93.8 us -> 40.6 us
  starting transfers between devices: 2.15 us -> 51.8 us
  other arithmetic: 44.3 us -> 18.5 us
  local copies, waits for them, and re-layouts: 39.4 us -> 23.5 us
    reduce_scatter x4 -> x2, waiting for transfers between devices: 209 us -> 14 us  [the longest x1 11.4 us: whole_local(): lax.psum_scatter(grad_down, 'fsdp', scatter_dimension=0, tiled=True)]
    all_gather x5 -> x2, waiting for transfers between devices: 186 us -> 7.4 us  [the longest x1 7.4 us: whole_local(): full_down = lax.all_gather(down_weight, 'fsdp', axis=0, tiled=True)]
    pallas_call x0 -> x15, Pallas kernels: none -> 98.2 us  [the longest x3 21.7 us: by_rows(): pl.pallas_call(kernel, grid_spec=pltpu.PrefetchScalarGridSpec(num_scalar_...]
    psum x5 -> x0, waiting for transfers between devices: 78.9 us -> none  [the longest x1 31.2 us: local(): lax.psum(jnp.einsum('te,de->td', attended, full_out, preferred_element_ty...]
    psum x1 -> x0, blocking collectives: 77 us -> none  [local(): lax.psum((squared, counted, vectors, grad_qv_bias, grad_up_bias), ('fsdp'...]
    ppermute x0 -> x31, waiting for transfers between devices: none -> 70.4 us  [swap(): return lax.ppermute(values, axis, pairs)]
    dot_general x19 -> x8, matrix products: 93.8 us -> 40.6 us  [the longest x1 6.88 us: whole_local(): jnp.einsum('td,tf->df', normed1_low, grad_pre, preferred_element_type=jnp...]
    ppermute x0 -> x31, starting transfers between devices: none -> 32.2 us  [swap(): return lax.ppermute(values, axis, pairs)]
  transfers between devices with their start and end apart: 15 -> 40, of which waited for: 14 -> 15; matrix products, arithmetic and copies ran while one was open for 8% -> 17% of each run, Pallas kernels for 0% -> 24%
where the time goes in v2:
time: 363 us; the launch traced here: 361 us
  waiting for transfers between devices  111 us (31%)
  Pallas kernels  98.2 us (27%)
  starting transfers between devices  51.8 us (14%)
  matrix products  40.6 us (11%)
  local copies, waits for them, and re-layouts  23.5 us (6%)
  other arithmetic  18.5 us (5%)
  between operations  17.5 us (5%)
    ppermute x31, waiting for transfers between devices, swap(): return lax.ppermute(values, axis, pairs)  70.4 us
    ppermute x31, starting transfers between devices, swap(): return lax.ppermute(values, axis, pairs)  32.2 us
    pallas_call x3, Pallas kernels, by_rows(): pl.pallas_call(kernel, grid_spec=pltpu.PrefetchScalarGridSpec(num_scalar_...  21.7 us
    all_to_all x5, starting transfers between devices, deal(): return lax.all_to_all(pieces, axis, 0, 0)  19.3 us
    all_to_all x5, waiting for transfers between devices, deal(): return lax.all_to_all(pieces, axis, 0, 0)  18.6 us
    pallas_call x1, Pallas kernels, attend_back(): pl.pallas_call(lambda *refs: attend_back_kernel(*refs, block=block), grid...  16.8 us
    pallas_call x2, Pallas kernels, wide_layer(): pl.pallas_call(kernel, grid=(length // block,), in_specs=[spec(low.shape)...  15.3 us
    pallas_call x1, Pallas kernels, attend(): pl.pallas_call(lambda *refs: attend_kernel(*refs, block=block), grid_spec...  12.2 us
  transfers between devices with their start and end apart: 40, of which 15 were waited for; matrix products, arithmetic and copies ran while one was open for 17% of the time, Pallas kernels for 24%

profile of v2, /device:TPU:0, one launch (start us, length us, event | category | flops | bytes accessed | tf_op | source)
XLA Modules:
  0.0 361.2 jit_solution(14977341155904603888)
XLA Ops:
  9.5 5.2 %all-to-all-start = ((bf16[4,128,768]{2,1,0:T(8,128)(2,1)}), bf16[4,128,768]{2,1,0:T(8,128)(2,1)S(1)}, u32[]{:S(2)}, u32[]{:S(2)}) async-start(bf16[4,128,768]{2,1,0:T(8,128)(2,1)} %constant_dynamic-slice_fusion.2), calls=%async_computation | async-start | bytes 1572864 | tf_op jit(solution)/shard_map/all_to_all | solution.py:323
  17.6 2.6 collective-permute-start.1
  21.1 2.7 collective-permute-done
  23.8 14.6 %collective-permute-done.1 = bf16[48,1536]{1,0:T(8,128)(2,1)S(1)} collective-permute-done((bf16[48,1536]{1,0:T(8,128)(2,1)S(1)}, bf16[48,1536]{1,0:T(8,128)(2,1)S(1)}, u32[]{:S(2)}, u32[]{:S(2)}) %collective-permute-start.1) | collective-permute-done | bytes 147488 | tf_op jit(solution)/shard_map/ppermute | solution.py:272
  38.6 2.1 collective-permute-start.3
  42.3 5.2 %collective-permute-done.3.refs_3_ = bf16[160,1536]{1,0:T(8,128)(2,1)S(1)} collective-permute-done((bf16[160,1536]{1,0:T(8,128)(2,1)S(1)}, bf16[160,1536]{1,0:T(8,128)(2,1)S(1)}, u32[]{:S(2)}, u32[]{:S(2)}) %collective-permute-start.3) | collective-permute-done | bytes 491552 | tf_op jit(solution)/shard_map/ppermute | solution.py:272
  47.5 2.0 collective-permute-start.5
  50.3 2.1 constant_dynamic-slice_fusion.1
  53.3 3.7 %join_halves.3 = bf16[4,256,768]{2,1,0:T(8,128)(2,1)} custom-call(s32[1]{0:T(128)} %bitcast.facts, f32[1]{0:T(128)} %constant.19.clone.1.ratio_ref, bf16[4,128,768]{2,1,0:T(8,128)(2,1)} %copy-done.6, bf16[4,128,768]{2,1,0:T(8,128)(2,1)} %copy-done.15), custom_call_target="tpu_custom_call" | custom-call | tf_op jit(solution)/shard_map/join_halves/pallas_call | solution.py:523
  57.0 8.0 %collective-permute-done.5.refs_5_ = bf16[160,1536]{1,0:T(8,128)(2,1)} collective-permute-done((bf16[160,1536]{1,0:T(8,128)(2,1)S(1)}, bf16[160,1536]{1,0:T(8,128)(2,1)}, u32[]{:S(2)}, u32[]{:S(2)}) %collective-permute-start.5) | collective-permute-done | bytes 491552 | tf_op jit(solution)/shard_map/ppermute | solution.py:272
  65.0 4.8 %assemble.1 = bf16[768,1536]{1,0:T(8,128)(2,1)} custom-call(s32[2]{0:T(128)} %pad_add_fusion.refs_0_.places, bf16[192,1536]{1,0:T(8,128)(2,1)} %copy-done.8, bf16[160,1536]{1,0:T(8,128)(2,1)} %copy-done.10, bf16[160,1536]{1,0:T(8,128)(2,1)} %copy-done.24, bf16[160,1536]{1,0:T(8,128)(2,1)} %collective-permute-done.4.refs_4_, ...), custom_call_target="tpu_custom_call" | custom-call | tf_op jit(solution)/shard_map/assemble/pallas_call | solution.py:257
  72.4 5.1 %add_convert_fusion.refs_1_.refs_2_.refs_3_ = bf16[1024,1152]{1,0:T(8,128)(2,1)} fusion(bf16[1024,768]{1,0:T(8,128)(2,1)S(1)} %bitcast.49, f32[1152]{0:T(1024)S(1)} %add.113, bf16[768,1536]{1,0:T(8,128)(2,1)} %assemble.1), kind=kOutput, calls=%fused_computation | convolution fusion | flops 1814298624 | bytes 5706240 | tf_op jit(solution)/shard_map/dot_general | solution.py:658
  77.5 12.2 %attend.1 = (bf16[1024,384]{1,0:T(8,128)(2,1)}, f32[3,2,1024]{2,1,0:T(2,128)}) custom-call(s32[2]{0:T(128)} %pad_add_fusion.1.refs_0_.facts, bf16[1024,1152]{1,0:T(8,128)(2,1)} %add_convert_fusion.refs_1_.refs_2_.refs_3_, bf16[1024,1152]{1,0:T(8,128)(2,1)} %add_convert_fusion.refs_1_.refs_2_.refs_3_, bf16[1024,1152]{1,0:T(8,128)(2,1)} %add_convert_fusion.refs_1_.refs_2_.refs_3_), custom_call_target="tpu_custom_call" | custom-call | tf_op jit(solution)/shard_map/attend/pallas_call | solution.py:174
  89.7 3.3 convolution_convert_fusion.2.mine_ref
  93.1 3.5 all-to-all-start.1
  99.1 5.7 %first_norm.1 = (f32[1024,768]{1,0:T(8,128)}, f32[1024,1]{1,0:T(8,128)}, bf16[1024,768]{1,0:T(8,128)(2,1)}) custom-call(bf16[1024,768]{1,0:T(8,128)(2,1)} %bitcast.47, bf16[1024,768]{1,0:T(8,128)(2,1)} %convolution_convert_fusion.2.mine_ref, bf16[1024,768]{1,0:T(8,128)(2,1)} %collective-permute-done.7.other_ref, f32[1,768]{1,0:T(1,128)} %reshape.130.bias_ref, ...), custom_call_target="tpu_custom_call" | custom-call | tf_op jit(solution)/shard_map/first_norm/pallas_call | solution.py:438
  104.8 3.5 all-to-all-done.1.own_teacher_ref
  108.3 8.2 %up.1 = (bf16[1024,1536]{1,0:T(8,128)(2,1)}, bf16[1024,1536]{1,0:T(8,128)(2,1)}) custom-call(bf16[1024,768]{1,0:T(8,128)(2,1)} %get-tuple-element.106.low_ref, bf16[768,1536]{1,0:T(8,128)(2,1)} %all-gather.3.cloned.1.call-done.weight_ref, f32[1,1536]{1,0:T(1,128)} %reshape.133.bias_ref), custom_call_target="tpu_custom_call" | custom-call | tf_op jit(solution)/shard_map/up/pallas_call | solution.py:479
  116.5 7.4 %all-gather.5.cloned.1.call-done.weight_ref = bf16[768,1536]{1,0:T(8,128)(2,1)} async-done(((bf16[192,1536]{1,0:T(8,128)(2,1)}), bf16[768,1536]{1,0:T(8,128)(2,1)}) %all-gather.5.cloned.1.call-update) | async-done | bytes 2359312 | tf_op jit(solution)/shard_map/all_gather | solution.py:642
  123.9 5.3 %convolution_convert_fusion.5.mine_ref = bf16[1024,768]{1,0:T(8,128)(2,1)S(1)} fusion(bf16[1024,1536]{1,0:T(8,128)(2,1)} %get-tuple-element.107, bf16[768,1536]{1,0:T(8,128)(2,1)} %all-gather.5.cloned.1.call-done.weight_ref), kind=kOutput, calls=%fused_computation.6 | convolution fusion | flops 2416705536 | bytes 7077888 | tf_op jit(solution)/shard_map/tf,df->td/dot_general | solution.py:676
  131.5 2.3 collective-permute-done.9.other_teacher_ref
  135.8 8.5 %second_norm.1 = (bf16[4,128,768]{2,1,0:T(8,128)(2,1)}, f32[1024,768]{1,0:T(8,128)}, bf16[1024,768]{1,0:T(8,128)(2,1)}, f32[8,768]{1,0:T(8,128)}) custom-call(s32[2]{0:T(128)} %pad_add_fusion.1.refs_0_.facts, f32[1024,768]{1,0:T(8,128)} %get-tuple-element.103.normal_ref, f32[1,768]{1,0:T(1,128)} %reshape.131.gain_ref.gain1_ref, ...), custom_call_target="tpu_custom_call" | custom-call | tf_op jit(solution)/shard_map/second_norm/pallas_call | solution.py:438
  144.3 6.4 %convolution_convert_fusion.1 = bf16[768,1536]{1,0:T(8,128)(2,1)} fusion(bf16[1024,768]{1,0:T(8,128)(2,1)} %get-tuple-element.112.low_ref, bf16[1024,1536]{1,0:T(8,128)(2,1)} %get-tuple-element.107), kind=kOutput, calls=%fused_computation.2 | convolution fusion | flops 2417098752 | bytes 7077888 | tf_op jit(solution)/shard_map/td,tf->df/dot_general | solution.py:702
  150.8 7.1 %grad_pre.1 = (bf16[1024,1536]{1,0:T(8,128)(2,1)}, f32[8,1536]{1,0:T(8,128)}) custom-call(bf16[1024,768]{1,0:T(8,128)(2,1)} %get-tuple-element.112.low_ref, bf16[768,1536]{1,0:T(8,128)(2,1)} %all-gather.5.cloned.1.call-done.weight_ref, bf16[1024,1536]{1,0:T(8,128)(2,1)} %get-tuple-element.113.slope_ref), custom_call_target="tpu_custom_call" | custom-call | tf_op jit(solution)/shard_map/grad_pre/pallas_call | solution.py:479
  157.9 6.9 %convolution_convert_fusion = bf16[768,1536]{1,0:T(8,128)(2,1)} fusion(bf16[1024,768]{1,0:T(8,128)(2,1)} %get-tuple-element.106.low_ref, bf16[1024,1536]{1,0:T(8,128)(2,1)} %get-tuple-element.116), kind=kOutput, calls=%fused_computation.1 | convolution fusion | flops 2417098752 | bytes 7077888 | tf_op jit(solution)/shard_map/td,tf->df/dot_general | solution.py:710
  164.8 6.5 %convolution_convert_fusion.4.mine_ref = bf16[1024,768]{1,0:T(8,128)(2,1)} fusion(bf16[1024,1536]{1,0:T(8,128)(2,1)} %get-tuple-element.116, bf16[768,1536]{1,0:T(8,128)(2,1)} %all-gather.3.cloned.1.call-done.weight_ref), kind=kOutput, calls=%fused_computation.5 | convolution fusion | flops 2416705536 | bytes 7077888 | tf_op jit(solution)/shard_map/tf,df->td/dot_general | solution.py:715
  171.4 3.7 %all-to-all-start.2 = ((bf16[4,128,768]{2,1,0:T(8,128)(2,1)}), bf16[4,128,768]{2,1,0:T(8,128)(2,1)S(1)}, u32[]{:S(2)}, u32[]{:S(2)}) async-start(bf16[4,128,768]{2,1,0:T(8,128)(2,1)} %get-tuple-element.124), calls=%async_computation.3 | async-start | bytes 1572864 | tf_op jit(solution)/shard_map/all_to_all | solution.py:323
  175.1 7.5 %first_norm_back.1 = (bf16[1024,768]{1,0:T(8,128)(2,1)}, f32[4,128,768]{2,1,0:T(8,128)}, f32[8,768]{1,0:T(8,128)}) custom-call(s32[2]{0:T(128)} %pad_add_fusion.1.refs_0_.facts, f32[1024,768]{1,0:T(8,128)} %get-tuple-element.109.grad_ref, bf16[1024,768]{1,0:T(8,128)(2,1)} %convolution_convert_fusion.4.mine_ref, ...), custom_call_target="tpu_custom_call" | custom-call | tf_op jit(solution)/shard_map/first_norm_back/pallas_call | solution.py:438
  182.6 4.1 %weight_grad.2 = (bf16[192,384]{1,0:T(8,128)(2,1)}, bf16[192,384]{1,0:T(8,128)(2,1)}, bf16[192,384]{1,0:T(8,128)(2,1)}, bf16[192,384]{1,0:T(8,128)(2,1)}) custom-call(s32[2]{0:T(128)} %pad_add_fusion.refs_0_.places, bf16[1024,768]{1,0:T(8,128)(2,1)} %get-tuple-element.118.refs_1_, bf16[1024,384]{1,0:T(8,128)(2,1)} %get-tuple-element.102.refs_2_), custom_call_target="tpu_custom_call" | custom-call | tf_op jit(solution)/shard_map/weight_grad/pallas_call | solution.py:560
  186.7 3.3 convolution_convert_fusion.6.refs_4_
  190.0 11.4 %reduce-scatter.3.cloned.1.call-done = bf16[192,1536]{1,0:T(8,128)(2,1)} async-done(((bf16[768,1536]{1,0:T(8,128)(2,1)}), bf16[192,1536]{1,0:T(8,128)(2,1)}) %reduce-scatter.3.cloned.1.call-update) | async-done | bytes 589840 | tf_op jit(solution)/shard_map/reduce_scatter | solution.py:705
  206.4 16.8 %attend_back.1 = (bf16[1024,1152]{1,0:T(8,128)(2,1)}, f32[8,1152]{1,0:T(8,128)}) custom-call(s32[2]{0:T(128)} %pad_add_fusion.1.refs_0_.facts, bf16[1024,1152]{1,0:T(8,128)(2,1)} %add_convert_fusion.refs_1_.refs_2_.refs_3_, bf16[1024,1152]{1,0:T(8,128)(2,1)} %add_convert_fusion.refs_1_.refs_2_.refs_3_, ...), custom_call_target="tpu_custom_call" | custom-call | tf_op jit(solution)/shard_map/attend_back/pallas_call | solution.py:197
  223.9 6.7 %weight_grad.3 = (bf16[192,1152]{1,0:T(8,128)(2,1)}, bf16[192,1152]{1,0:T(8,128)(2,1)}, bf16[192,1152]{1,0:T(8,128)(2,1)}, bf16[192,1152]{1,0:T(8,128)(2,1)}) custom-call(s32[2]{0:T(128)} %pad_add_fusion.refs_0_.places, bf16[1024,768]{1,0:T(8,128)(2,1)} %bitcast.48, bf16[1024,1152]{1,0:T(8,128)(2,1)} %get-tuple-element.149.refs_2_), custom_call_target="tpu_custom_call" | custom-call | tf_op jit(solution)/shard_map/weight_grad/pallas_call | solution.py:560
  230.5 3.9 %convolution_convert_fusion.3 = bf16[1024,768]{1,0:T(8,128)(2,1)S(1)} fusion(bf16[1024,1152]{1,0:T(8,128)(2,1)} %get-tuple-element.149.refs_2_, bf16[768,1536]{1,0:T(8,128)(2,1)S(1)} %copy-done.9), kind=kOutput, calls=%fused_computation.4 | convolution fusion | flops 1812725760 | bytes 5701632 | tf_op jit(solution)/shard_map/te,de->td/dot_general | solution.py:743
  246.1 2.5 fusion.1
  248.6 2.6 reduce-scatter.5.cloned.1.call-done
  251.1 3.0 collective-permute-done.16
  254.1 17.4 %collective-permute-done.17 = bf16[192,1152]{1,0:T(8,128)(2,1)} collective-permute-done((bf16[192,1152]{1,0:T(8,128)(2,1)}, bf16[192,1152]{1,0:T(8,128)(2,1)}, u32[]{:S(2)}, u32[]{:S(2)}) %collective-permute-start.17) | collective-permute-done | bytes 442400 | tf_op jit(solution)/shard_map/ppermute | solution.py:272
  274.9 3.5 all-to-all-start.3
  280.5 14.7 %collective-permute-done.21 = f32[16,768]{1,0:T(8,128)S(1)} collective-permute-done((f32[16,768]{1,0:T(8,128)S(1)}, f32[16,768]{1,0:T(8,128)S(1)}, u32[]{:S(2)}, u32[]{:S(2)}) %collective-permute-start.21) | collective-permute-done | bytes 49184 | tf_op jit(solution)/shard_map/ppermute | solution.py:272
  297.0 3.7 %join_halves.4 = bf16[4,256,768]{2,1,0:T(8,128)(2,1)} custom-call(s32[1]{0:T(128)} %bitcast.facts, f32[1]{0:T(128)} %constant.19.clone.1.ratio_ref, bf16[4,128,768]{2,1,0:T(8,128)(2,1)} %copy-done.5, bf16[4,128,768]{2,1,0:T(8,128)(2,1)} %copy-done.16), custom_call_target="tpu_custom_call" | custom-call | tf_op jit(solution)/shard_map/join_halves/pallas_call | solution.py:523
  305.6 2.4 collective-permute-start.25
  308.0 2.0 add_convert_fusion.1
  311.0 3.5 all-to-all-start.4
  317.0 15.2 %all-to-all-done.4.own_ref = bf16[4,128,768]{2,1,0:T(8,128)(2,1)S(1)} async-done(((bf16[4,128,768]{2,1,0:T(8,128)(2,1)}), bf16[4,128,768]{2,1,0:T(8,128)(2,1)S(1)}, u32[]{:S(2)}, u32[]{:S(2)}) %all-to-all-start.4) | async-done | bytes 786464 | tf_op jit(solution)/shard_map/all_to_all | solution.py:323
  339.1 3.8 %place_rows.1 = f32[192,1536]{1,0:T(8,128)} custom-call(s32[2]{0:T(128)} %pad_add_fusion.refs_0_.places, f32[1]{0:T(128)} %bitcast.13.ratio_ref, bf16[48,1536]{1,0:T(8,128)(2,1)} %copy-done.22, bf16[48,1536]{1,0:T(8,128)(2,1)} %copy-done.27, bf16[48,1536]{1,0:T(8,128)(2,1)} %copy-done.28, bf16[48,1536]{1,0:T(8,128)(2,1)} %copy-done.29), custom_call_target="tpu_custom_call" | custom-call | tf_op jit(solution)/shard_map/place_rows/pallas_call | solution.py:593
  347.0 2.5 add_multiply_fusion.1
  349.5 4.0 %join_halves.5 = f32[4,256,768]{2,1,0:T(8,128)} custom-call(s32[1]{0:T(128)} %bitcast.facts, f32[1]{0:T(128)} %bitcast.13.ratio_ref, bf16[4,128,768]{2,1,0:T(8,128)(2,1)} %copy-done.4, bf16[4,128,768]{2,1,0:T(8,128)(2,1)} %collective-permute-done.26.other_ref), custom_call_target="tpu_custom_call" | custom-call | tf_op jit(solution)/shard_map/join_halves/pallas_call | solution.py:523
  (200 shorter events, 60.9 us)
Async XLA Ops:
  7.2 101.1 %all-gather.3.cloned.1.call-start = ((), (), s32[]{:S(2)}) async-start(), calls=%async_computation.7 | async-start | bytes 2949120 | tf_op jit(solution)/shard_map/all_gather | solution.py:641
  9.5 29.0 %all-to-all-start = ((bf16[4,128,768]{2,1,0:T(8,128)(2,1)}), bf16[4,128,768]{2,1,0:T(8,128)(2,1)S(1)}, u32[]{:S(2)}, u32[]{:S(2)}) async-start(bf16[4,128,768]{2,1,0:T(8,128)(2,1)} %constant_dynamic-slice_fusion.2), calls=%async_computation | async-start | bytes 1572864 | tf_op jit(solution)/shard_map/all_to_all | solution.py:323
  14.7 109.2 %all-gather.5.cloned.1.call-start = ((), (), s32[]{:S(2)}) async-start(), calls=%async_computation.8 | async-start | bytes 2949120 | tf_op jit(solution)/shard_map/all_gather | solution.py:642
  15.8 33.7 %copy-start.41 = (f32[2,384]{1,0:T(2,128)S(1)}, f32[2,384]{1,0:T(2,128)}, u32[]{:S(2)}) copy-start(f32[2,384]{1,0:T(2,128)} %param.19) | copy-start | bytes 9220
  15.9 36.4 %copy-start.8 = (bf16[192,1536]{1,0:T(8,128)(2,1)}, bf16[192,1536]{1,0:T(8,128)(2,1)S(1)}, u32[]{:S(2)}) copy-start(bf16[192,1536]{1,0:T(8,128)(2,1)S(1)} %constant_dynamic-update-slice_fusion.refs_1_) | copy-start | bytes 1769476
  16.0 7.8 %collective-permute-start = (bf16[48,1536]{1,0:T(8,128)(2,1)S(1)}, bf16[48,1536]{1,0:T(8,128)(2,1)S(1)}, u32[]{:S(2)}, u32[]{:S(2)}) collective-permute-start(bf16[48,1536]{1,0:T(8,128)(2,1)S(1)} %constant_dynamic-slice_fusion.3), channel_id=1, source_target_pairs={{0,8},{8,0},{16,24},{24,16},{1,9},{9,1},{17,25},{25,17},{2,10},{10... | collective-permute-start | bytes 442376 | tf_op jit(solution)/shard_map/ppermute | solution.py:272
  17.6 20.8 %collective-permute-start.1 = (bf16[48,1536]{1,0:T(8,128)(2,1)S(1)}, bf16[48,1536]{1,0:T(8,128)(2,1)S(1)}, u32[]{:S(2)}, u32[]{:S(2)}) collective-permute-start(bf16[48,1536]{1,0:T(8,128)(2,1)S(1)} %constant_dynamic-slice_fusion.3), channel_id=1, source_target_pairs={{0,16},{8,24},{16,0},{24,8},{1,17},{9,25},{17,1},{25,9},{2,18},{10... | collective-permute-start | bytes 442376 | tf_op jit(solution)/shard_map/ppermute | solution.py:272
  20.2 18.3 %collective-permute-start.2 = (bf16[48,1536]{1,0:T(8,128)(2,1)S(1)}, bf16[48,1536]{1,0:T(8,128)(2,1)S(1)}, u32[]{:S(2)}, u32[]{:S(2)}) collective-permute-start(bf16[48,1536]{1,0:T(8,128)(2,1)S(1)} %constant_dynamic-slice_fusion.3), channel_id=1, source_target_pairs={{0,24},{8,16},{16,8},{24,0},{1,25},{9,17},{17,9},{25,1},{2,26},{10... | collective-permute-start | bytes 442376 | tf_op jit(solution)/shard_map/ppermute | solution.py:272
  38.5 13.9 %copy-start.6 = (bf16[4,128,768]{2,1,0:T(8,128)(2,1)}, bf16[4,128,768]{2,1,0:T(8,128)(2,1)S(1)}, u32[]{:S(2)}) copy-start(bf16[4,128,768]{2,1,0:T(8,128)(2,1)S(1)} %all-to-all-done.own_ref) | copy-start | bytes 2359300
  38.5 18.4 %copy-start.10 = (bf16[160,1536]{1,0:T(8,128)(2,1)}, bf16[160,1536]{1,0:T(8,128)(2,1)S(1)}, u32[]{:S(2)}) copy-start(bf16[160,1536]{1,0:T(8,128)(2,1)S(1)} %pad_maximum_fusion.1.refs_2_) | copy-start | bytes 1474564
  38.6 8.9 %collective-permute-start.3 = (bf16[160,1536]{1,0:T(8,128)(2,1)S(1)}, bf16[160,1536]{1,0:T(8,128)(2,1)S(1)}, u32[]{:S(2)}, u32[]{:S(2)}) collective-permute-start(bf16[160,1536]{1,0:T(8,128)(2,1)S(1)} %pad_maximum_fusion.1.refs_2_), channel_id=1, source_target_pairs={{0,2},{2,0},{4,6},{6,4},{1,3},{3,1},{5,7},{7,5},{8,10},{10,8},{12,... | collective-permute-start | bytes 1474568 | tf_op jit(solution)/shard_map/ppermute | solution.py:272
  40.7 11.7 %collective-permute-start.6 = (bf16[4,128,768]{2,1,0:T(8,128)(2,1)S(1)}, bf16[4,128,768]{2,1,0:T(8,128)(2,1)S(1)}, u32[]{:S(2)}, u32[]{:S(2)}) collective-permute-start(bf16[4,128,768]{2,1,0:T(8,128)(2,1)S(1)} %all-to-all-done.own_ref), channel_id=1, source_target_pairs={{0,1},{1,0},{2,3},{3,2},{4,5},{5,4},{6,7},{7,6},{8,9},{9,8},{10,11... | collective-permute-start | bytes 2359304 | tf_op jit(solution)/shard_map/ppermute | solution.py:272
  40.8 16.2 %collective-permute-start.4 = (bf16[160,1536]{1,0:T(8,128)(2,1)S(1)}, bf16[160,1536]{1,0:T(8,128)(2,1)}, u32[]{:S(2)}, u32[]{:S(2)}) collective-permute-start(bf16[160,1536]{1,0:T(8,128)(2,1)S(1)} %pad_maximum_fusion.1.refs_2_), channel_id=1, source_target_pairs={{0,4},{2,6},{4,0},{6,2},{1,5},{3,7},{5,1},{7,3},{8,12},{10,14},{12... | collective-permute-start | bytes 1474568 | tf_op jit(solution)/shard_map/ppermute | solution.py:272
  47.5 17.6 %collective-permute-start.5 = (bf16[160,1536]{1,0:T(8,128)(2,1)S(1)}, bf16[160,1536]{1,0:T(8,128)(2,1)}, u32[]{:S(2)}, u32[]{:S(2)}) collective-permute-start(bf16[160,1536]{1,0:T(8,128)(2,1)S(1)} %collective-permute-done.3.refs_3_), channel_id=1, source_target_pairs={{0,4},{2,6},{4,0},{6,2},{1,5},{3,7},{5,1},{7,3},{8,12},{10,14},{12... | collective-permute-start | bytes 1474568 | tf_op jit(solution)/shard_map/ppermute | solution.py:272
  77.5 12.2 %copy-start.9 = (bf16[768,1536]{1,0:T(8,128)(2,1)S(1)}, bf16[768,1536]{1,0:T(8,128)(2,1)}, u32[]{:S(2)}) copy-start(bf16[768,1536]{1,0:T(8,128)(2,1)} %assemble.1) | copy-start | bytes 7077892
  93.0 6.1 %collective-permute-start.7 = (bf16[1024,768]{1,0:T(8,128)(2,1)}, bf16[1024,768]{1,0:T(8,128)(2,1)}, u32[]{:S(2)}, u32[]{:S(2)}) collective-permute-start(bf16[1024,768]{1,0:T(8,128)(2,1)} %convolution_convert_fusion.2.mine_ref), channel_id=1, source_target_pairs={{0,1},{1,0},{2,3},{3,2},{4,5},{5,4},{6,7},{7,6},{8,9},{9,8},{10,11... | collective-permute-start | bytes 4718600 | tf_op jit(solution)/shard_map/ppermute | solution.py:272
  93.1 15.3 %all-to-all-start.1 = ((bf16[4,128,768]{2,1,0:T(8,128)(2,1)}), bf16[4,128,768]{2,1,0:T(8,128)(2,1)S(1)}, u32[]{:S(2)}, u32[]{:S(2)}) async-start(bf16[4,128,768]{2,1,0:T(8,128)(2,1)} %constant_dynamic-slice_fusion.1), calls=%async_computation.1 | async-start | bytes 1572864 | tf_op jit(solution)/shard_map/all_to_all | solution.py:323
  96.6 104.8 %reduce-scatter.3.cloned.1.call-start = ((), (), s32[]{:S(2)}) async-start(), calls=%async_computation.9 | async-start | bytes 2949120 | tf_op jit(solution)/shard_map/reduce_scatter | solution.py:705
  108.3 21.0 %copy-start.7 = (bf16[4,128,768]{2,1,0:T(8,128)(2,1)}, bf16[4,128,768]{2,1,0:T(8,128)(2,1)S(1)}, u32[]{:S(2)}) copy-start(bf16[4,128,768]{2,1,0:T(8,128)(2,1)S(1)} %all-to-all-done.1.own_teacher_ref) | copy-start | bytes 2359300
  129.2 4.6 %collective-permute-start.8 = (bf16[1024,768]{1,0:T(8,128)(2,1)S(1)}, bf16[1024,768]{1,0:T(8,128)(2,1)S(1)}, u32[]{:S(2)}, u32[]{:S(2)}) collective-permute-start(bf16[1024,768]{1,0:T(8,128)(2,1)S(1)} %convolution_convert_fusion.5.mine_ref), channel_id=1, source_target_pairs={{0,1},{1,0},{2,3},{3,2},{4,5},{5,4},{6,7},{7,6},{8,9},{9,8},{10,11... | collective-permute-start | bytes 4718600 | tf_op jit(solution)/shard_map/ppermute | solution.py:272
  129.3 4.5 %collective-permute-start.9 = (bf16[4,128,768]{2,1,0:T(8,128)(2,1)S(1)}, bf16[4,128,768]{2,1,0:T(8,128)(2,1)S(1)}, u32[]{:S(2)}, u32[]{:S(2)}) collective-permute-start(bf16[4,128,768]{2,1,0:T(8,128)(2,1)S(1)} %all-to-all-done.1.own_teacher_ref), channel_id=1, source_target_pairs={{0,1},{1,0},{2,3},{3,2},{4,5},{5,4},{6,7},{7,6},{8,9},{9,8},{10,11... | collective-permute-start | bytes 2359304 | tf_op jit(solution)/shard_map/ppermute | solution.py:272
  150.8 100.4 %reduce-scatter.5.cloned.1.call-start = ((), (), s32[]{:S(2)}) async-start(), calls=%async_computation.10 | async-start | bytes 2949120 | tf_op jit(solution)/shard_map/reduce_scatter | solution.py:713
  171.3 3.8 %collective-permute-start.10 = (bf16[1024,768]{1,0:T(8,128)(2,1)}, bf16[1024,768]{1,0:T(8,128)(2,1)}, u32[]{:S(2)}, u32[]{:S(2)}) collective-permute-start(bf16[1024,768]{1,0:T(8,128)(2,1)} %convolution_convert_fusion.4.mine_ref), channel_id=1, source_target_pairs={{0,1},{1,0},{2,3},{3,2},{4,5},{5,4},{6,7},{7,6},{8,9},{9,8},{10,11... | collective-permute-start | bytes 4718600 | tf_op jit(solution)/shard_map/ppermute | solution.py:272
  171.4 18.6 %all-to-all-start.2 = ((bf16[4,128,768]{2,1,0:T(8,128)(2,1)}), bf16[4,128,768]{2,1,0:T(8,128)(2,1)S(1)}, u32[]{:S(2)}, u32[]{:S(2)}) async-start(bf16[4,128,768]{2,1,0:T(8,128)(2,1)} %get-tuple-element.124), calls=%async_computation.3 | async-start | bytes 1572864 | tf_op jit(solution)/shard_map/all_to_all | solution.py:323
  190.0 88.4 %copy-start.5 = (bf16[4,128,768]{2,1,0:T(8,128)(2,1)}, bf16[4,128,768]{2,1,0:T(8,128)(2,1)S(1)}, u32[]{:S(2)}) copy-start(bf16[4,128,768]{2,1,0:T(8,128)(2,1)S(1)} %all-to-all-done.2.own_ref) | copy-start | bytes 2359300
  201.4 22.5 %collective-permute-start.11 = (bf16[192,1536]{1,0:T(8,128)(2,1)}, bf16[192,1536]{1,0:T(8,128)(2,1)}, u32[]{:S(2)}, u32[]{:S(2)}) collective-permute-start(bf16[192,1536]{1,0:T(8,128)(2,1)} %reduce-scatter.3.cloned.1.call-done), channel_id=1, source_target_pairs={{0,2},{2,0},{4,6},{6,4},{1,3},{3,1},{5,7},{7,5},{8,10},{10,8},{12,... | collective-permute-start | bytes 1769480 | tf_op jit(solution)/shard_map/ppermute | solution.py:272
  202.9 20.3 %collective-permute-start.12 = (bf16[192,384]{1,0:T(8,128)(2,1)}, bf16[192,384]{1,0:T(8,128)(2,1)S(1)}, u32[]{:S(2)}, u32[]{:S(2)}) collective-permute-start(bf16[192,384]{1,0:T(8,128)(2,1)} %get-tuple-element.129), channel_id=1, source_target_pairs={{0,2},{2,0},{4,6},{6,4},{1,3},{3,1},{5,7},{7,5},{8,10},{10,8},{12,... | collective-permute-start | bytes 442376 | tf_op jit(solution)/shard_map/ppermute | solution.py:272
  203.4 19.8 %collective-permute-start.13 = (bf16[192,384]{1,0:T(8,128)(2,1)}, bf16[192,384]{1,0:T(8,128)(2,1)S(1)}, u32[]{:S(2)}, u32[]{:S(2)}) collective-permute-start(bf16[192,384]{1,0:T(8,128)(2,1)} %get-tuple-element.130), channel_id=1, source_target_pairs={{0,4},{2,6},{4,0},{6,2},{1,5},{3,7},{5,1},{7,3},{8,12},{10,14},{12... | collective-permute-start | bytes 442376 | tf_op jit(solution)/shard_map/ppermute | solution.py:272
  204.9 18.9 %collective-permute-start.14 = (bf16[192,384]{1,0:T(8,128)(2,1)}, bf16[192,384]{1,0:T(8,128)(2,1)}, u32[]{:S(2)}, u32[]{:S(2)}) collective-permute-start(bf16[192,384]{1,0:T(8,128)(2,1)} %get-tuple-element.131), channel_id=1, source_target_pairs={{0,6},{2,4},{4,2},{6,0},{1,7},{3,5},{5,3},{7,1},{8,14},{10,12},{12... | collective-permute-start | bytes 442376 | tf_op jit(solution)/shard_map/ppermute | solution.py:272
  235.4 10.7 %collective-permute-start.20 = (bf16[4,128,768]{2,1,0:T(8,128)(2,1)}, bf16[4,128,768]{2,1,0:T(8,128)(2,1)}, u32[]{:S(2)}, u32[]{:S(2)}) collective-permute-start(bf16[4,128,768]{2,1,0:T(8,128)(2,1)} %dynamic-slice_bitcast_fusion), channel_id=1, source_target_pairs={{0,1},{1,0},{2,3},{3,2},{4,5},{5,4},{6,7},{7,6},{8,9},{9,8},{10,11... | collective-permute-start | bytes 2359304 | tf_op jit(solution)/shard_map/ppermute | solution.py:272
  237.1 34.3 %collective-permute-start.19 = (bf16[192,1536]{1,0:T(8,128)(2,1)S(1)}, bf16[192,1536]{1,0:T(8,128)(2,1)S(1)}, u32[]{:S(2)}, u32[]{:S(2)}) collective-permute-start(bf16[192,1536]{1,0:T(8,128)(2,1)S(1)} %add_convert_fusion.2), channel_id=1, source_target_pairs={{0,4},{2,6},{4,0},{6,2},{1,5},{3,7},{5,1},{7,3},{8,12},{10,14},{12... | collective-permute-start | bytes 1769480 | tf_op jit(solution)/shard_map/ppermute | solution.py:272
  240.7 13.4 %collective-permute-start.16 = (bf16[192,1152]{1,0:T(8,128)(2,1)}, bf16[192,1152]{1,0:T(8,128)(2,1)}, u32[]{:S(2)}, u32[]{:S(2)}) collective-permute-start(bf16[192,1152]{1,0:T(8,128)(2,1)} %get-tuple-element.144), channel_id=1, source_target_pairs={{0,2},{2,0},{4,6},{6,4},{1,3},{3,1},{5,7},{7,5},{8,10},{10,8},{12,... | collective-permute-start | bytes 1327112 | tf_op jit(solution)/shard_map/ppermute | solution.py:272
  241.8 29.6 %collective-permute-start.17 = (bf16[192,1152]{1,0:T(8,128)(2,1)}, bf16[192,1152]{1,0:T(8,128)(2,1)}, u32[]{:S(2)}, u32[]{:S(2)}) collective-permute-start(bf16[192,1152]{1,0:T(8,128)(2,1)} %get-tuple-element.145), channel_id=1, source_target_pairs={{0,4},{2,6},{4,0},{6,2},{1,5},{3,7},{5,1},{7,3},{8,12},{10,14},{12... | collective-permute-start | bytes 1327112 | tf_op jit(solution)/shard_map/ppermute | solution.py:272
  243.4 28.1 %collective-permute-start.18 = (bf16[192,1152]{1,0:T(8,128)(2,1)}, bf16[192,1152]{1,0:T(8,128)(2,1)}, u32[]{:S(2)}, u32[]{:S(2)}) collective-permute-start(bf16[192,1152]{1,0:T(8,128)(2,1)} %get-tuple-element.146), channel_id=1, source_target_pairs={{0,6},{2,4},{4,2},{6,0},{1,7},{3,5},{5,3},{7,1},{8,14},{10,12},{12... | collective-permute-start | bytes 1327112 | tf_op jit(solution)/shard_map/ppermute | solution.py:272
  248.6 25.4 %copy-start.23 = (bf16[192,384]{1,0:T(8,128)(2,1)S(1)}, bf16[192,384]{1,0:T(8,128)(2,1)}, u32[]{:S(2)}) copy-start(bf16[192,384]{1,0:T(8,128)(2,1)} %add_add_fusion) | copy-start | bytes 442372
  274.9 25.9 %all-to-all-start.3 = ((bf16[4,48,1536]{2,1,0:T(8,128)(2,1)}), bf16[4,48,1536]{2,1,0:T(8,128)(2,1)S(1)}, u32[]{:S(2)}, u32[]{:S(2)}) async-start(bf16[4,48,1536]{2,1,0:T(8,128)(2,1)} %pad_maximum_fusion), calls=%async_computation.5 | async-start | bytes 1179648 | tf_op jit(solution)/shard_map/all_to_all | solution.py:323
  278.3 17.8 %collective-permute-start.15 = (bf16[4,128,768]{2,1,0:T(8,128)(2,1)S(1)}, bf16[4,128,768]{2,1,0:T(8,128)(2,1)S(1)}, u32[]{:S(2)}, u32[]{:S(2)}) collective-permute-start(bf16[4,128,768]{2,1,0:T(8,128)(2,1)S(1)} %all-to-all-done.2.own_ref), channel_id=1, source_target_pairs={{0,1},{1,0},{2,3},{3,2},{4,5},{5,4},{6,7},{7,6},{8,9},{9,8},{10,11... | collective-permute-start | bytes 2359304 | tf_op jit(solution)/shard_map/ppermute | solution.py:272
  278.4 22.3 %collective-permute-start.23 = (bf16[192,1536]{1,0:T(8,128)(2,1)S(1)}, bf16[192,1536]{1,0:T(8,128)(2,1)}, u32[]{:S(2)}, u32[]{:S(2)}) collective-permute-start(bf16[192,1536]{1,0:T(8,128)(2,1)S(1)} %copy-done.18), channel_id=1, source_target_pairs={{0,2},{2,0},{4,6},{6,4},{1,3},{3,1},{5,7},{7,5},{8,10},{10,8},{12,... | collective-permute-start | bytes 1769480 | tf_op jit(solution)/shard_map/ppermute | solution.py:272
  280.0 15.3 %collective-permute-start.21 = (f32[16,768]{1,0:T(8,128)S(1)}, f32[16,768]{1,0:T(8,128)S(1)}, u32[]{:S(2)}, u32[]{:S(2)}) collective-permute-start(f32[16,768]{1,0:T(8,128)S(1)} %copy-done.26), channel_id=1, source_target_pairs={{0,2},{2,0},{4,6},{6,4},{1,3},{3,1},{5,7},{7,5},{8,10},{10,8},{12,... | collective-permute-start | bytes 147464 | tf_op jit(solution)/shard_map/ppermute | solution.py:272
  295.2 5.5 %collective-permute-start.22 = (f32[16,768]{1,0:T(8,128)S(1)}, f32[16,768]{1,0:T(8,128)S(1)}, u32[]{:S(2)}, u32[]{:S(2)}) collective-permute-start(f32[16,768]{1,0:T(8,128)S(1)} %add.127), channel_id=1, source_target_pairs={{0,4},{2,6},{4,0},{6,2},{1,5},{3,7},{5,1},{7,3},{8,12},{10,14},{12... | collective-permute-start | bytes 147464 | tf_op jit(solution)/shard_map/ppermute | solution.py:272
  300.8 4.8 %collective-permute-start.24 = (f32[16,768]{1,0:T(8,128)S(1)}, f32[16,768]{1,0:T(8,128)S(1)}, u32[]{:S(2)}, u32[]{:S(2)}) collective-permute-start(f32[16,768]{1,0:T(8,128)S(1)} %add.128), channel_id=1, source_target_pairs={{0,8},{8,0},{16,24},{24,16},{1,9},{9,1},{17,25},{25,17},{2,10},{10... | collective-permute-start | bytes 147464 | tf_op jit(solution)/shard_map/ppermute | solution.py:272
  302.8 29.3 %collective-permute-start.27 = (bf16[48,1536]{1,0:T(8,128)(2,1)S(1)}, bf16[48,1536]{1,0:T(8,128)(2,1)S(1)}, u32[]{:S(2)}, u32[]{:S(2)}) collective-permute-start(bf16[48,1536]{1,0:T(8,128)(2,1)S(1)} %fusion.6.refs_0_), channel_id=1, source_target_pairs={{0,2},{2,0},{4,6},{6,4},{1,3},{3,1},{5,7},{7,5},{8,10},{10,8},{12,... | collective-permute-start | bytes 442376 | tf_op jit(solution)/shard_map/ppermute | solution.py:272
  304.1 32.6 %collective-permute-start.28 = (bf16[48,1536]{1,0:T(8,128)(2,1)S(1)}, bf16[48,1536]{1,0:T(8,128)(2,1)S(1)}, u32[]{:S(2)}, u32[]{:S(2)}) collective-permute-start(bf16[48,1536]{1,0:T(8,128)(2,1)S(1)} %fusion.6.refs_0_), channel_id=1, source_target_pairs={{0,4},{2,6},{4,0},{6,2},{1,5},{3,7},{5,1},{7,3},{8,12},{10,14},{12... | collective-permute-start | bytes 442376 | tf_op jit(solution)/shard_map/ppermute | solution.py:272
  305.6 8.9 %collective-permute-start.25 = (f32[16,768]{1,0:T(8,128)S(1)}, f32[16,768]{1,0:T(8,128)S(1)}, u32[]{:S(2)}, u32[]{:S(2)}) collective-permute-start(f32[16,768]{1,0:T(8,128)S(1)} %add.129), channel_id=1, source_target_pairs={{0,16},{8,24},{16,0},{24,8},{1,17},{9,25},{17,1},{25,9},{2,18},{10... | collective-permute-start | bytes 147464 | tf_op jit(solution)/shard_map/ppermute | solution.py:272
  310.0 37.0 %collective-permute-start.30 = (bf16[192,1536]{1,0:T(8,128)(2,1)}, bf16[192,1536]{1,0:T(8,128)(2,1)}, u32[]{:S(2)}, u32[]{:S(2)}) collective-permute-start(bf16[192,1536]{1,0:T(8,128)(2,1)} %add_convert_fusion.1), channel_id=1, source_target_pairs={{0,4},{2,6},{4,0},{6,2},{1,5},{3,7},{5,1},{7,3},{8,12},{10,14},{12... | collective-permute-start | bytes 1769480 | tf_op jit(solution)/shard_map/ppermute | solution.py:272
  311.0 21.1 %all-to-all-start.4 = ((bf16[4,128,768]{2,1,0:T(8,128)(2,1)}), bf16[4,128,768]{2,1,0:T(8,128)(2,1)S(1)}, u32[]{:S(2)}, u32[]{:S(2)}) async-start(bf16[4,128,768]{2,1,0:T(8,128)(2,1)} %fusion.1), calls=%async_computation.6 | async-start | bytes 1572864 | tf_op jit(solution)/shard_map/all_to_all | solution.py:323
  332.1 17.4 %collective-permute-start.26 = (bf16[4,128,768]{2,1,0:T(8,128)(2,1)S(1)}, bf16[4,128,768]{2,1,0:T(8,128)(2,1)}, u32[]{:S(2)}, u32[]{:S(2)}) collective-permute-start(bf16[4,128,768]{2,1,0:T(8,128)(2,1)S(1)} %all-to-all-done.4.own_ref), channel_id=1, source_target_pairs={{0,1},{1,0},{2,3},{3,2},{4,5},{5,4},{6,7},{7,6},{8,9},{9,8},{10,11... | collective-permute-start | bytes 2359304 | tf_op jit(solution)/shard_map/ppermute | solution.py:272
  332.2 6.3 %collective-permute-start.29 = (bf16[48,1536]{1,0:T(8,128)(2,1)S(1)}, bf16[48,1536]{1,0:T(8,128)(2,1)S(1)}, u32[]{:S(2)}, u32[]{:S(2)}) collective-permute-start(bf16[48,1536]{1,0:T(8,128)(2,1)S(1)} %collective-permute-done.27.refs_1_), channel_id=1, source_target_pairs={{0,4},{2,6},{4,0},{6,2},{1,5},{3,7},{5,1},{7,3},{8,12},{10,14},{12... | collective-permute-start | bytes 442376 | tf_op jit(solution)/shard_map/ppermute | solution.py:272
  (35 other events, 179.4 us)
Sparse Core Ops, SparseCore 0:
  9.6 61.9 all-gather.2
  73.2 50.6 all-gather.4
  150.9 50.4 reduce-scatter.2
  203.6 47.5 reduce-scatter.4

commit v3 on v2

--- a/solution.py
+++ b/solution.py
@@ -187,6 +187,7 @@
             jax.ShapeDtypeStruct((pairs, 2, length), jnp.float32),
         ],
         name="attend",
+        compiler_params=pltpu.CompilerParams(vmem_limit_bytes=9 << 20),
     )(facts, projected, projected, projected)
 
 
@@ -220,6 +221,7 @@
             jax.ShapeDtypeStruct((8, 3 * width), jnp.float32),
         ],
         name="attend_back",
+        compiler_params=pltpu.CompilerParams(vmem_limit_bytes=12 << 20),
     )(facts, projected, projected, projected, grad_attended, log_total)
 
 
@@ -235,10 +237,13 @@
     return jnp.swapaxes(cut, -3, -2).reshape(values.shape[:-1] + (kinds, width))
 
 
-def assemble_kernel(facts, own_ref, *refs, fsdp, count, rows):
-    part_refs, out_ref = refs[:count], refs[count]
-    place, depth = facts[0], facts[1]
-    out_ref[pl.ds(depth * (rows * count), rows * count), :] = own_ref[...]
+def fill_rows(places, own_ref, part_refs, out_ref):
+    count = len(part_refs)
+    rows = own_ref.shape[0] // count
+    fsdp = out_ref.shape[0] // own_ref.shape[0]
+    place, depth = places[0], places[1]
+    start = pl.multiple_of(depth * (rows * count), rows)
+    out_ref[pl.ds(start, rows * count), :] = own_ref[...]
     for s in range(count):
         for d in range(1, fsdp):
             start = lax.bitwise_xor(depth, jnp.int32(d)) * (rows * count)
@@ -248,23 +253,86 @@
             ]
 
 
-def assemble(places, own, parts):
-    fsdp, count = lax.axis_size("fsdp"), len(parts)
-    rows = own.shape[0] // count
-    width = 3 * LANES if own.shape[1] % (3 * LANES) == 0 else own.shape[1]
-    whole_block = lambda shape: pl.BlockSpec((shape[0], width), lambda step, facts: (0, step))
-    out_shape = (fsdp * own.shape[0], own.shape[1])
+def project_kernel(places, left_ref, bias_ref, own_ref, *refs):
+    part_refs, (out_ref, full_ref) = refs[:-2], refs[-2:]
+
+    @pl.when(pl.program_id(0) == 0)
+    def _():
+        fill_rows(places, own_ref, part_refs, full_ref)
+
+    total = plain_dot(left_ref[...], full_ref[:, : out_ref.shape[1]]) + bias_ref[...]
+    out_ref[...] = total.astype(out_ref.dtype)
+
+
+def up_kernel(places, left_ref, bias_ref, own_ref, *refs):
+    part_refs, (active_ref, slope_ref, full_ref) = refs[:-3], refs[-3:]
+
+    @pl.when(pl.program_id(0) == 0)
+    def _():
+        fill_rows(places, own_ref, part_refs, full_ref)
+
+    pre = plain_dot(left_ref[...], full_ref[...]) + bias_ref[...]
+    below = 0.5 * (1.0 + lax.erf(pre * (0.5**0.5)))
+    active_ref[...] = (pre * below).astype(active_ref.dtype)
+    bell = jnp.exp(-0.5 * pre * pre) * 0.3989422804014327
+    slope_ref[...] = (below + pre * bell).astype(slope_ref.dtype)
+
+
+def down_kernel(places, left_ref, own_ref, part_ref, *refs):
+    part_refs, (out_ref, full_ref) = refs[:-2], refs[-2:]
+    count = len(part_refs) // 2
+    cut = part_refs[0].shape[1]
+
+    @pl.when(pl.program_id(0) == 0)
+    def _():
+        for index in range(2):
+            span = slice(index * cut, (index + 1) * cut)
+            fill_rows(
+                places,
+                own_ref.at[:, span],
+                [part_ref.at[:, span]] + list(part_refs[index * count : (index + 1) * count]),
+                full_ref.at[:, span],
+            )
+
+    out_ref[...] = rows_by_rows(left_ref[...], full_ref[...]).astype(out_ref.dtype)
+
+
+def gathered_layer(kernel, name, block, places, left, vectors, own, parts, widths, fsdp):
+    length = left.shape[0]
+    full = (fsdp * own.shape[0], own.shape[1])
+    whole = lambda shape: pl.BlockSpec(shape, lambda step, places: (0, 0))
+    by_block = lambda width: pl.BlockSpec((block, width), lambda step, places: (step, 0))
     return pl.pallas_call(
-        lambda *refs: assemble_kernel(*refs, fsdp=fsdp, count=count, rows=rows),
+        kernel,
         grid_spec=pltpu.PrefetchScalarGridSpec(
             num_scalar_prefetch=1,
-            grid=(own.shape[1] // width,),
-            in_specs=[whole_block(own.shape)] + [whole_block(item.shape) for item in parts],
-            out_specs=whole_block(out_shape),
+            grid=(length // block,),
+            in_specs=[by_block(left.shape[1])]
+            + [whole(item.shape) for item in vectors + [own] + parts],
+            out_specs=[by_block(width) for width in widths] + [whole(full)],
         ),
-        out_shape=jax.ShapeDtypeStruct(out_shape, own.dtype),
-        name="assemble",
-    )(places, own, *parts)
+        out_shape=[jax.ShapeDtypeStruct((length, width), jnp.bfloat16) for width in widths]
+        + [jax.ShapeDtypeStruct(full, jnp.bfloat16)],
+        name=name,
+        compiler_params=pltpu.CompilerParams(vmem_limit_bytes=20 << 20),
+    )(places, left, *vectors, own, *parts)
+
+
+def stack_kernel(*refs):
+    row = 0
+    for ref in refs[:-1]:
+        refs[-1][row : row + ref.shape[0], :] = ref[...]
+        row += ref.shape[0]
+
+
+def stack_rows(pieces):
+    rows = sum(item.shape[0] for item in pieces)
+    return pl.pallas_call(
+        stack_kernel,
+        out_shape=jax.ShapeDtypeStruct((rows, pieces[0].shape[1]), pieces[0].dtype),
+        name="stack_rows",
+        compiler_params=pltpu.CompilerParams(vmem_limit_bytes=4 << 20),
+    )(*pieces)
 
 
 def swap(values, axis, step):
@@ -423,15 +491,15 @@
 
 
 def by_rows(kernel, name, block, operands, results, facts=None, stats=0):
-    def spec(shape):
-        if len(shape) == 3:
-            return pl.BlockSpec((1,) + shape[1:], lambda step, *_: (step, 0, 0))
+    def spec(shape, dealt=False):
+        if dealt:
+            return pl.BlockSpec((1,) + shape[1:], lambda step, facts: (step ^ facts[2], 0, 0))
         if shape[0] == 1:
             return pl.BlockSpec(shape, lambda step, *_: (0, 0))
         return pl.BlockSpec((block, shape[1]), lambda step, *_: (step, 0))
 
     length = next(item.shape[0] for item in operands if item.ndim == 2 and item.shape[0] > 1)
-    out_specs = [spec(item.shape) for item in results]
+    out_specs = [spec(item.shape, item.ndim == 3) for item in results]
     if stats:
         results = results + [jax.ShapeDtypeStruct((8, stats), jnp.float32)]
         out_specs.append(pl.BlockSpec((8, stats), lambda step, *_: (0, 0)))
@@ -440,20 +508,13 @@
         grid_spec=pltpu.PrefetchScalarGridSpec(
             num_scalar_prefetch=0 if facts is None else 1,
             grid=(length // block,),
-            in_specs=[spec(item.shape) for item in operands],
+            in_specs=[spec(item.shape, item.ndim == 3) for item in operands],
             out_specs=out_specs,
         ),
         out_shape=results,
         name=name,
+        compiler_params=pltpu.CompilerParams(vmem_limit_bytes=20 << 20),
     )(*([] if facts is None else [facts]), *operands)
-
-
-def up_kernel(low_ref, weight_ref, bias_ref, active_ref, slope_ref):
-    pre = plain_dot(low_ref[...], weight_ref[...]) + bias_ref[...]
-    below = 0.5 * (1.0 + lax.erf(pre * (0.5**0.5)))
-    active_ref[...] = (pre * below).astype(active_ref.dtype)
-    bell = jnp.exp(-0.5 * pre * pre) * 0.3989422804014327
-    slope_ref[...] = (below + pre * bell).astype(slope_ref.dtype)
 
 
 def grad_pre_kernel(low_ref, weight_ref, slope_ref, out_ref, stats_ref):
@@ -484,7 +545,58 @@
         out_specs=out_specs,
         out_shape=out_shape,
         name=name,
+        compiler_params=pltpu.CompilerParams(vmem_limit_bytes=20 << 20),
     )(low, weight, *operands)
+
+
+def rows_kernel(left_ref, right_ref, out_ref, *, transposed):
+    product = (rows_by_rows if transposed else plain_dot)(left_ref[...], right_ref[...])
+    out_ref[...] = product.astype(out_ref.dtype)
+
+
+def rows_times(left, right, block, transposed):
+    length, depth = left.shape
+    width = right.shape[0] if transposed else right.shape[1]
+    return pl.pallas_call(
+        lambda *refs: rows_kernel(*refs, transposed=transposed),
+        grid=(length // block,),
+        in_specs=[
+            pl.BlockSpec((block, depth), lambda step: (step, 0)),
+            pl.BlockSpec(right.shape, lambda step: (0, 0)),
+        ],
+        out_specs=pl.BlockSpec((block, width), lambda step: (step, 0)),
+        out_shape=jax.ShapeDtypeStruct((length, width), jnp.bfloat16),
+        name="rows_times",
+        compiler_params=pltpu.CompilerParams(vmem_limit_bytes=14 << 20),
+    )(left, right)
+
+
+def input_back_kernel(facts, grad_ref, weight_ref, mine_ref, other_ref):
+    total = rows_by_rows(grad_ref[...], weight_ref[...]).astype(mine_ref.dtype)
+    rows = mine_ref.shape[1]
+    first = facts[1] == 0
+    mine_ref[0] = jnp.where(first, total[:rows], total[rows:])
+    other_ref[0] = jnp.where(first, total[rows:], total[:rows])
+
+
+def input_back(facts, grads, weight, block):
+    length, width = grads.shape
+    half = (1, block // 2, weight.shape[0])
+    return pl.pallas_call(
+        input_back_kernel,
+        grid_spec=pltpu.PrefetchScalarGridSpec(
+            num_scalar_prefetch=1,
+            grid=(length // block,),
+            in_specs=[
+                pl.BlockSpec((block, width), lambda step, facts: (step, 0)),
+                pl.BlockSpec((weight.shape[0], width), lambda step, facts: (0, 0)),
+            ],
+            out_specs=[pl.BlockSpec(half, lambda step, facts: (step ^ facts[2], 0, 0))] * 2,
+        ),
+        out_shape=[jax.ShapeDtypeStruct((length // block,) + half[1:], jnp.bfloat16)] * 2,
+        name="input_back",
+        compiler_params=pltpu.CompilerParams(vmem_limit_bytes=10 << 20),
+    )(facts, grads, weight)
 
 
 def pack_kernel(second_ref, first_ref, up_ref, qkv_ref, count_ref, out_ref):
@@ -507,6 +619,7 @@
         pack_kernel,
         out_shape=jax.ShapeDtypeStruct((-(-rows // 8) * 8, width), jnp.float32),
         name="pack",
+        compiler_params=pltpu.CompilerParams(vmem_limit_bytes=2 << 20),
     )(second, first, up, qkv, count)
 
 
@@ -517,7 +630,7 @@
         out_ref[0, pl.ds(pl.multiple_of(half * rows, rows), rows), :] = values.astype(out_ref.dtype)
 
 
-def join_halves(half, ratio=None, dtype=jnp.bfloat16):
+def join_halves(half, ratio=None, dtype=jnp.bfloat16, place=0):
     count, rows, width = half.shape
     ratio = jnp.ones((1,), jnp.float32) if ratio is None else ratio.reshape(1)
     return pl.pallas_call(
@@ -527,80 +640,172 @@
             grid=(count,),
             in_specs=[pl.BlockSpec(memory_space=pltpu.SMEM)]
             + [pl.BlockSpec((1, rows, width), lambda step, facts: (step, 0, 0))] * 2,
-            out_specs=pl.BlockSpec((1, 2 * rows, width), lambda step, facts: (step, 0, 0)),
+            out_specs=pl.BlockSpec(
+                (1, 2 * rows, width), lambda step, facts: (step ^ facts[1], 0, 0)
+            ),
         ),
         out_shape=jax.ShapeDtypeStruct((count, 2 * rows, width), dtype),
         name="join_halves",
-    )(lax.axis_index("tp").reshape(1), ratio, half, swap(half, "tp", 1))
-
-
-def weight_grad_kernel(places, left_ref, right_ref, *refs, fsdp, count):
-    total = lax.dot_general(
-        left_ref[...],
-        right_ref[...],
-        (((0,), (0,)), ((), ())),
-        preferred_element_type=jnp.float32,
-    )
-    out_refs, held = refs[:-1], refs[-1]
-    held[...] = total.astype(held.dtype)
+        compiler_params=pltpu.CompilerParams(vmem_limit_bytes=4 << 20),
+    )(
+        jnp.stack([lax.axis_index("tp"), jnp.asarray(place, jnp.int32)]),
+        ratio,
+        half,
+        swap(half, "tp", 1),
+    )
+
+
+def weight_grad_kernel(places, *refs, chunks, fsdp, count, order):
+    kinds = len(chunks)
+    left_refs, right_refs = refs[:kinds], refs[kinds : 2 * kinds]
+    out_refs, held = refs[2 * kinds : -1], refs[-1]
+    step = pl.program_id(0)
+    first = 0
+    for left_ref, right_ref, chunk in zip(left_refs, right_refs, chunks):
+
+        @pl.when(jnp.logical_and(step >= first, step < first + chunk))
+        def _():
+            total = lax.dot_general(
+                left_ref[...],
+                right_ref[...],
+                (((0,), (0,)), ((), ())),
+                preferred_element_type=jnp.float32,
+            )
+            held[...] = total.astype(held.dtype)
+
+        first += chunk
     rows = held.shape[0] // (fsdp * count)
-    for s in range(count):
-        for d in range(fsdp):
-            start = d * rows * count + lax.bitwise_xor(places[0], jnp.int32(s)) * rows
-            out_refs[s][d * rows : (d + 1) * rows, :] = held[
-                pl.ds(pl.multiple_of(start, rows), rows), :
-            ]
-
-
-def weight_grad(places, left, right):
+    if order == "fsdp":
+        own = rows * count
+        for half in range(2):
+            for index in range(fsdp // 2):
+                start = lax.bitwise_xor(places[1], jnp.int32(half + 2 * index)) * own
+                out_refs[half][index * own : (index + 1) * own, :] = held[
+                    pl.ds(pl.multiple_of(start, own), own), :
+                ]
+    else:
+        steps = list(range(0, fsdp, 2)) + list(range(1, fsdp, 2))
+        for s in range(count):
+            for index, d in enumerate(steps):
+                start = lax.bitwise_xor(places[1], jnp.int32(d)) * (rows * count)
+                start = start + lax.bitwise_xor(places[0], jnp.int32(s)) * rows
+                out_refs[s][index * rows : (index + 1) * rows, :] = held[
+                    pl.ds(pl.multiple_of(start, rows), rows), :
+                ]
+
+
+def weight_grad(places, pairs, order="ctx"):
     fsdp, count = lax.axis_size("fsdp"), lax.axis_size("ctx")
-    tokens, rows = left.shape
-    columns = right.shape[1]
-    width = max(item for item in range(LANES, 6 * LANES + 1, LANES) if columns % item == 0)
+    tokens, rows = pairs[0][0].shape
+    columns = [right.shape[1] for _, right in pairs]
+    width = max(
+        item for item in range(LANES, 6 * LANES + 1, LANES) if not any(c % item for c in columns)
+    )
+    chunks = [item // width for item in columns]
+    firsts = [sum(chunks[:index]) for index in range(len(chunks))]
+    pieces = count if order == "ctx" else 2
+    right_spec = lambda first, chunk: pl.BlockSpec(
+        (tokens, width), lambda step, places: (0, jnp.clip(step - first, 0, chunk - 1))
+    )
     return pl.pallas_call(
-        lambda *refs: weight_grad_kernel(*refs, fsdp=fsdp, count=count),
+        lambda *refs: weight_grad_kernel(
+            *refs, chunks=chunks, fsdp=fsdp, count=count, order=order
+        ),
         grid_spec=pltpu.PrefetchScalarGridSpec(
             num_scalar_prefetch=1,
-            grid=(columns // width,),
-            in_specs=[
-                pl.BlockSpec((tokens, rows), lambda step, places: (0, 0)),
-                pl.BlockSpec((tokens, width), lambda step, places: (0, step)),
-            ],
-            out_specs=[pl.BlockSpec((rows // count, width), lambda step, places: (0, step))]
-            * count,
+            grid=(sum(chunks),),
+            in_specs=[pl.BlockSpec((tokens, rows), lambda step, places: (0, 0))] * len(pairs)
+            + [right_spec(first, chunk) for first, chunk in zip(firsts, chunks)],
+            out_specs=[pl.BlockSpec((rows // pieces, width), lambda step, places: (0, step))]
+            * pieces,
             scratch_shapes=[pltpu.VMEM((rows, width), jnp.bfloat16)],
         ),
-        out_shape=[jax.ShapeDtypeStruct((rows // count, columns), jnp.bfloat16)] * count,
+        out_shape=[jax.ShapeDtypeStruct((rows // pieces, sum(columns)), jnp.bfloat16)] * pieces,
         name="weight_grad",
-    )(places, left, right)
-
-
-def place_kernel(places, ratio_ref, *refs):
-    part_refs, out_ref = refs[:-1], refs[-1]
+        compiler_params=pltpu.CompilerParams(vmem_limit_bytes=14 << 20),
+    )(places, *[left for left, _ in pairs], *[right for _, right in pairs])
+
+
+def halve(kept, brought):
+    rows = kept.shape[0] // 2
+    return [
+        low(wide(kept[cut]) + wide(brought[cut]))
+        for cut in (slice(0, rows), slice(rows, 2 * rows))
+    ]
+
+
+def sum_kernel(*refs):
+    part_refs, (kept_ref, sent_ref) = refs[:-2], refs[-2:]
+    total = part_refs[0][...].astype(jnp.float32) + part_refs[1][...].astype(jnp.float32)
+    for first, second in zip(part_refs[2::2], part_refs[3::2]):
+        total = total + (first[...].astype(jnp.float32) + second[...].astype(jnp.float32))
+    rows = kept_ref.shape[0]
+    kept_ref[...] = total[:rows].astype(kept_ref.dtype)
+    sent_ref[...] = total[rows:].astype(sent_ref.dtype)
+
+
+def sum_and_cut(parts):
+    rows, columns = parts[0].shape
+    return pl.pallas_call(
+        sum_kernel,
+        out_shape=[jax.ShapeDtypeStruct((rows // 2, columns), jnp.bfloat16)] * 2,
+        name="sum_and_cut",
+        compiler_params=pltpu.CompilerParams(vmem_limit_bytes=8 << 20),
+    )(*parts)
+
+
+def place_kernel(places, ratio_ref, *refs, kinds):
+    part_refs, (first_ref, second_ref) = refs[:-2], refs[-2:]
     rows = part_refs[0].shape[0]
+    width = first_ref.shape[1]
+    pairs = width // (kinds * LANES)
     ratio = ratio_ref[0]
     for s in range(len(part_refs)):
         start = lax.bitwise_xor(places[0], jnp.int32(s)) * rows
-        out_ref[pl.ds(pl.multiple_of(start, rows), rows), :] = (
-            part_refs[s][...].astype(jnp.float32) * ratio
-        )
-
-
-def place_rows(places, parts, ratio):
+        start = pl.multiple_of(start, rows)
+        second_ref[pl.ds(start, rows), :] = part_refs[s][:, width:].astype(jnp.float32) * ratio
+        for kind in range(kinds):
+            for pair in range(pairs):
+                source = (pair * kinds + kind) * LANES
+                target = (kind * pairs + pair) * LANES
+                out = part_refs[s][:, source : source + LANES].astype(jnp.float32) * ratio
+                first_ref[pl.ds(start, rows), target : target + LANES] = out
+
+
+def place_rows(places, parts, ratio, width, kinds):
     rows, columns = parts[0].shape
-    width = 3 * LANES if columns % (3 * LANES) == 0 else columns
-    block = pl.BlockSpec((rows, width), lambda step, places: (0, step))
+    whole = lambda shape: pl.BlockSpec(shape, lambda step, places: (0, 0))
+    shapes = [(rows * len(parts), width), (rows * len(parts), columns - width)]
     return pl.pallas_call(
-        place_kernel,
+        lambda *refs: place_kernel(*refs, kinds=kinds),
         grid_spec=pltpu.PrefetchScalarGridSpec(
             num_scalar_prefetch=1,
-            grid=(columns // width,),
-            in_specs=[pl.BlockSpec(memory_space=pltpu.SMEM)] + [block] * len(parts),
-            out_specs=pl.BlockSpec((rows * len(parts), width), lambda step, places: (0, step)),
+            grid=(1,),
+            in_specs=[pl.BlockSpec(memory_space=pltpu.SMEM)]
+            + [whole(item.shape) for item in parts],
+            out_specs=[whole(shape) for shape in shapes],
         ),
-        out_shape=jax.ShapeDtypeStruct((rows * len(parts), columns), jnp.float32),
+        out_shape=[jax.ShapeDtypeStruct(shape, jnp.float32) for shape in shapes],
         name="place_rows",
+        compiler_params=pltpu.CompilerParams(vmem_limit_bytes=10 << 20),
     )(places, ratio.reshape(1), *parts)
+
+
+def columns_kernel(first_ref, second_ref, out_ref):
+    width = first_ref.shape[1]
+    out_ref[:, :width] = first_ref[...]
+    out_ref[:, width:] = second_ref[...]
+
+
+def stack_columns(first, second):
+    return pl.pallas_call(
+        columns_kernel,
+        out_shape=jax.ShapeDtypeStruct(
+            (first.shape[0], first.shape[1] + second.shape[1]), first.dtype
+        ),
+        name="stack_columns",
+        compiler_params=pltpu.CompilerParams(vmem_limit_bytes=4 << 20),
+    )(first, second)
 
 
 def whole_local(
@@ -632,32 +837,66 @@
     row = lambda values: values.reshape(1, -1)
     struct = jax.ShapeDtypeStruct
     part_rows = qkv_weight.shape[0] // ctx_count
+    own_part = lambda weight: lax.dynamic_slice_in_dim(weight, place * part_rows, part_rows, 0)
     qkv_out = jnp.concatenate([by_pairs(qkv_weight), out_weight], axis=1)
     local_counts = jnp.sum(wide(valid_mask), axis=1)
-    weight_rows = swap_all(
-        lax.dynamic_slice_in_dim(qkv_out, place * part_rows, part_rows, 0), "fsdp"
-    )
-    hidden_half = deal(own_half(hidden_in), "ctx")
-    full_up = lax.all_gather(up_weight, "fsdp", axis=0, tiled=True)
-    full_down = lax.all_gather(down_weight, "fsdp", axis=0, tiled=True)
-    weight_rows, hidden_half = together(weight_rows, hidden_half)
+    hidden_own, weight_own = together(own_half(hidden_in), own_part(qkv_out))
+    weight_rows = swap_all(weight_own, "fsdp")
+    hidden_half = deal(hidden_own, "ctx")
     count_rows = jnp.broadcast_to(
         jnp.pad(low(local_counts), (0, qkv_out.shape[1] - seq_count)), (16, qkv_out.shape[1])
     )
-    weight_part = jnp.concatenate(weight_rows + [count_rows], axis=0)
-    weight_parts = [weight_part] + relay_all(weight_part, "ctx")
+    full_bias = row(by_pairs(jnp.stack([qv_bias[0], jnp.zeros_like(qv_bias[0]), qv_bias[1]])))
+    teacher_own = own_half(teacher)
+    teacher_own = [
+        lax.dynamic_index_in_dim(teacher_own, place ^ s, 0, keepdims=False)
+        for s in range(ctx_count)
+    ]
+    weight_rows, hidden_half, count_rows, up_own, down_own, teacher_own, full_bias = together(
+        weight_rows,
+        hidden_half,
+        count_rows,
+        own_part(up_weight),
+        own_part(down_weight),
+        teacher_own,
+        full_bias,
+    )
+    weight_part = stack_rows(weight_rows + [count_rows])
+    weight_parts = [weight_part, swap(weight_part, "ctx", 1), swap(weight_part, "ctx", 2)]
+    up_rows = [swap(up_own, "fsdp", 1), swap(up_own, "fsdp", 2)]
+    weight_parts, up_rows = together(weight_parts, up_rows)
+    weight_parts = weight_parts + [swap(weight_parts[1], "ctx", 2)]
+    up_rows = up_rows + [swap(up_rows[0], "fsdp", 2)]
+    down_rows = [swap(down_own, "fsdp", 1), swap(down_own, "fsdp", 2)]
     flat_in = join_halves(hidden_half).reshape(row_count, model_width)
-    full_bias = by_pairs(jnp.stack([qv_bias[0], jnp.zeros_like(qv_bias[0]), qv_bias[1]]))
-    weight_parts, flat_in, teacher_own = together(weight_parts, flat_in, own_half(teacher))
-    full_qkv_out = assemble(places, qkv_out, weight_parts)
-    full_qkv, full_out = full_qkv_out[:, : 3 * inner_width], full_qkv_out[:, 3 * inner_width :]
+    weight_parts, flat_in, up_rows, down_rows = together(
+        weight_parts, flat_in, up_rows, down_rows
+    )
+    up_part = stack_rows(up_rows)
+    up_parts = [up_part] + swap_all(up_part, "ctx")
+    down_rows = down_rows + [swap(down_rows[0], "fsdp", 2)]
     counts = sum(wide(item[-16, :LANES]) for item in weight_parts)
     valid_count = lax.dynamic_index_in_dim(counts, place, 0, keepdims=False).astype(jnp.int32)
-    facts = jnp.stack([valid_count, core])
-    teacher_half = deal(teacher_own, "ctx")
-    projected = low(jnp.dot(flat_in, full_qkv, preferred_element_type=jnp.float32) + full_bias)
+    facts = jnp.stack([valid_count, core, place])
+    projected, full_qkv_out = gathered_layer(
+        project_kernel,
+        "project",
+        block_len,
+        places,
+        flat_in,
+        [full_bias],
+        qkv_out,
+        weight_parts,
+        [3 * inner_width],
+        fsdp_count,
+    )
+    full_out = full_qkv_out[:, 3 * inner_width :]
     attended, log_total = attend(facts, projected, block_len)
-    branch = low(jnp.einsum("te,de->td", attended, full_out, preferred_element_type=jnp.float32))
+    attended, up_parts, down_rows = together(attended, up_parts, down_rows)
+    down_part = stack_rows(down_rows)
+    cut = hidden_width // 2
+    down_parts = [down_part] + swap_all(down_part[:, :cut], "ctx")
+    branch = rows_times(attended, full_out, block_len, True)
     normal1, scale1, normed1_low = by_rows(
         first_norm_kernel,
         "first_norm",
@@ -669,11 +908,36 @@
             struct((row_count, model_width), jnp.bfloat16),
         ],
     )
-    normed1_low, teacher_half = together(normed1_low, teacher_half)
-    active, slope = wide_layer(
-        up_kernel, "up", block_len, normed1_low, full_up, [row(up_bias)], 2
-    )
-    branch = low(jnp.einsum("tf,df->td", active, full_down, preferred_element_type=jnp.float32))
+    normed1_low, down_parts = together(normed1_low, down_parts)
+    down_others = swap_all(down_parts[0][:, cut:], "ctx")
+    active, slope, full_up = gathered_layer(
+        up_kernel,
+        "up",
+        block_len,
+        places,
+        normed1_low,
+        [row(up_bias)],
+        up_weight,
+        up_parts,
+        [hidden_width, hidden_width],
+        fsdp_count,
+    )
+    active, down_parts, down_others = together(active, down_parts, down_others)
+    teacher_half = stack_rows(
+        [teacher_own[0]] + swap_each(teacher_own, "ctx")
+    ).reshape(ctx_count, block_len // 2, model_width)
+    branch, full_down = gathered_layer(
+        down_kernel,
+        "down",
+        block_len,
+        places,
+        active,
+        [],
+        down_weight,
+        down_parts[:1] + down_parts[1:] + down_others,
+        [model_width],
+        fsdp_count,
+    )
     layer_half, grad_resid2, grad_resid2_low, stats2 = by_rows(
         second_norm_kernel,
         "second_norm",
@@ -698,21 +962,18 @@
         facts=facts,
         stats=model_width,
     )
-    grad_down = low(
-        jnp.einsum("td,tf->df", grad_resid2_low, active, preferred_element_type=jnp.float32)
-    )
-    grad_down, grad_resid2_low, layer_half = together(grad_down, grad_resid2_low, layer_half)
-    owned_down = lax.psum_scatter(grad_down, "fsdp", scatter_dimension=0, tiled=True)
+    down_kept, down_sent = weight_grad(places, [(grad_resid2_low, active)], "fsdp")
+    down_kept, down_sent, grad_resid2_low = together(down_kept, down_sent, grad_resid2_low)
+    down_brought = swap(down_sent, "fsdp", 1)
+    layer_pieces = [layer_half[s] for s in range(ctx_count)]
+    layer_pieces = layer_pieces[:1] + swap_each(layer_pieces, "ctx")
     grad_pre, stats_up = wide_layer(
         grad_pre_kernel, "grad_pre", block_len, grad_resid2_low, full_down, [slope], 1, hidden_width
     )
-    grad_up = low(
-        jnp.einsum("td,tf->df", normed1_low, grad_pre, preferred_element_type=jnp.float32)
-    )
-    grad_pre, grad_up, layer_half = together(grad_pre, grad_up, layer_half)
-    owned_up = lax.psum_scatter(grad_up, "fsdp", scatter_dimension=0, tiled=True)
-    layer_half = deal(layer_half, "ctx")
-    branch = low(jnp.einsum("tf,df->td", grad_pre, full_up, preferred_element_type=jnp.float32))
+    branch = rows_times(grad_pre, full_up, block_len, True)
+    branch, grad_pre, layer_pieces = together(branch, grad_pre, layer_pieces)
+    up_pieces = weight_grad(places, [(normed1_low, grad_pre)])
+    up_brought = swap_each(up_pieces, "ctx")
     grad_resid1_low, grad_half, stats1 = by_rows(
         first_norm_back_kernel,
         "first_norm_back",
@@ -725,66 +986,100 @@
         facts=facts,
         stats=model_width,
     )
-    out_pieces = weight_grad(places, grad_resid1_low, attended)
-    grad_attended = low(jnp.dot(grad_resid1_low, full_out, preferred_element_type=jnp.float32))
-    grad_attended, out_pieces, owned_down, layer_half = together(
-        grad_attended, out_pieces, owned_down, layer_half
-    )
-    down_other = swap(owned_down, "ctx", 1)
-    out_sums = swap_each(out_pieces, "ctx")
+    out_kept, out_sent = weight_grad(places, [(grad_resid1_low, attended)], "fsdp")
+    grad_attended = rows_times(grad_resid1_low, full_out, block_len, False)
+    out_kept, out_sent, grad_attended = together(out_kept, out_sent, grad_attended)
+    out_brought = swap(out_sent, "fsdp", 1)
     grad_qkv, stats_qkv = attend_back(facts, projected, grad_attended, log_total, block_len)
-    grad_qkv, down_other, out_sums = together(grad_qkv, down_other, out_sums)
-    qkv_pieces = weight_grad(places, flat_in, grad_qkv)
-    qkv_pieces, grad_qkv, down_other, out_sums, layer_half = together(
-        qkv_pieces, grad_qkv, down_other, out_sums, layer_half
-    )
-    qkv_sums = swap_each(qkv_pieces, "ctx")
-    layer_out = join_halves(layer_half)
-    input_part = jnp.einsum("te,de->td", grad_qkv, full_qkv, preferred_element_type=jnp.float32)
-    parts = low(input_part).reshape(seq_count, 2, block_len // 2, model_width)
-    mine = lax.dynamic_index_in_dim(parts, core, 1, keepdims=False)
-    other = swap(lax.dynamic_index_in_dim(parts, 1 - core, 1, keepdims=False), "tp", 1)
-    half = low(grad_half + (wide(mine) + wide(other)))
-    owned_down = low(wide(owned_down) + wide(down_other))
-    down_other = swap(owned_down, "ctx", 2)
+    grad_qkv, up_brought, down_brought, out_brought = together(
+        grad_qkv, up_brought, down_brought, out_brought
+    )
+    last_pieces = weight_grad(places, [(flat_in, grad_qkv)])
+    down_kept, down_sent = sum_and_cut([down_kept, down_brought])
+    out_kept, out_sent = sum_and_cut([out_kept, out_brought])
+    last_pieces, grad_qkv, up_brought, down_sent, out_sent, layer_pieces, stats_qkv = together(
+        last_pieces, grad_qkv, up_brought, down_sent, out_sent, layer_pieces, stats_qkv
+    )
+    last_brought = swap_each(last_pieces, "ctx")
+    down_brought = swap(down_sent, "fsdp", 2)
+    out_brought = swap(out_sent, "fsdp", 2)
+    mine, other = input_back(facts, grad_qkv, full_qkv_out, block_len)
+    up_kept, up_sent = sum_and_cut([up_pieces[0]] + up_brought)
     local_count = jnp.broadcast_to(jnp.sum(local_counts), (1, LANES))
     small = pack(stats2, stats1, stats_up, stats_qkv, local_count)
-    out_part = add_up([out_pieces[0]] + out_sums)
-    qkv_sums, down_other, half, small, out_part, owned_up = together(
-        qkv_sums, down_other, half, small, out_part, owned_up
-    )
-    part = low(jnp.concatenate([add_up([qkv_pieces[0]] + qkv_sums), out_part], axis=1))
-    pieces = deal(part.reshape(fsdp_count, -1, part.shape[1]), "fsdp")
-    up_other = swap(owned_up, "ctx", 1)
+    last_brought, mine, other, down_brought, out_brought, up_sent, small, layer_pieces = together(
+        last_brought, mine, other, down_brought, out_brought, up_sent, small, layer_pieces
+    )
+    last_kept, last_sent = sum_and_cut([last_pieces[0]] + last_brought)
+    last_sent, other, down_brought, out_brought, up_sent, small, layer_pieces = together(
+        last_sent, other, down_brought, out_brought, up_sent, small, layer_pieces
+    )
+    last_brought = swap(last_sent, "fsdp", 1)
+    up_brought = swap(up_sent, "fsdp", 1)
+    other = swap(other, "tp", 1)
+    owned_down = low(wide(down_kept) + wide(down_brought))
+    down_other = swap(owned_down, "ctx", 1)
+    layer_stack = stack_rows(layer_pieces).reshape(layer_half.shape)
+    layer_out = join_halves(layer_stack, place=place)
+    last_brought, up_brought, other, small, layer_out, out_brought = together(
+        last_brought, up_brought, other, small, layer_out, out_brought
+    )
+    last_kept, last_sent = sum_and_cut([last_kept, last_brought])
+    last_sent, up_brought, other, small, out_brought = together(
+        last_sent, up_brought, other, small, out_brought
+    )
+    last_brought = swap(last_sent, "fsdp", 2)
+    up_kept, up_sent = sum_and_cut([up_kept, up_brought])
+    up_brought = swap(up_sent, "fsdp", 2)
+    owned_out = low(wide(out_kept) + wide(out_brought))
+    out_other = swap(owned_out, "ctx", 1)
+    half = low(grad_half + (wide(mine) + wide(other)))
     small = sum_over(small, "ctx")
-    pieces, half, small, up_other = together(pieces, half, small, up_other)
-    part = low(add_up([pieces[d] for d in range(fsdp_count)]))
-    qkv_out_owned = [part] + relay_all(part, "ctx")
-    owned_up = low(wide(owned_up) + wide(up_other))
-    up_other = swap(owned_up, "ctx", 2)
-    input_half = deal(half, "ctx")
+    last_brought, up_brought, half, down_other, out_other, small = together(
+        last_brought, up_brought, half, down_other, out_other, small
+    )
+    part = low(wide(last_kept) + wide(last_brought))
+    up_part = low(wide(up_kept) + wide(up_brought))
+    shared = stack_columns(part, up_part)
+    shared, half, down_other, out_other, small = together(
+        shared, half, down_other, out_other, small
+    )
+    shared = [shared, swap(shared, "ctx", 1), swap(shared, "ctx", 2)]
+    half_pieces = [half[s] for s in range(ctx_count)]
+    half_brought = swap_each(half_pieces, "ctx")
+    shared, half_brought, down_other, out_other, small = together(
+        shared, half_brought, down_other, out_other, small
+    )
+    shared = shared + [swap(shared[1], "ctx", 2)]
+    owned_down = low(wide(owned_down) + wide(down_other))
+    owned_out = low(wide(owned_out) + wide(out_other))
+    down_other, out_other = swap(owned_down, "ctx", 2), swap(owned_out, "ctx", 2)
     small = sum_over(small, "fsdp")
+    input_half = stack_rows(half_pieces[:1] + half_brought).reshape(half.shape)
     at = 7 + -(-hidden_width // model_width)
     counted = small[at + -(-3 * inner_width // model_width), 0]
     ratio = float(row_count * ctx_count * fsdp_count) / counted
     loss = jnp.sum(small[3]) / (counted * model_width)
     scaled = small * ratio
+    input_grad = join_halves(input_half, ratio, jnp.float32, place)
+    shared, down_other, out_other, input_grad, scaled = together(
+        shared, down_other, out_other, input_grad, scaled
+    )
+    owned_qkv, owned_up = place_rows(places, shared, ratio, 3 * inner_width, 3)
+    owned_qkv = owned_qkv.reshape(qkv_weight.shape)
+    owned_down = (wide(owned_down) + wide(down_other)) * ratio
+    owned_out = (wide(owned_out) + wide(out_other)) * ratio
     grad_up_bias = scaled[7:at].reshape(-1)[:hidden_width]
     grad_qv_bias = by_kinds(
         scaled[at : at + -(-3 * inner_width // model_width)].reshape(-1)[: 3 * inner_width]
     )[0::2]
-    owned_up = (wide(owned_up) + wide(up_other)) * ratio
-    owned_down = (wide(owned_down) + wide(down_other)) * ratio
-    owned_qkv_out = place_rows(places, qkv_out_owned, ratio)
-    owned_qkv = by_kinds(owned_qkv_out[:, : 3 * inner_width])
-    input_grad = join_halves(input_half, ratio, jnp.float32)
     return (
         layer_out,
         input_grad,
         loss,
         owned_qkv,
         grad_qv_bias,
-        owned_qkv_out[:, 3 * inner_width :],
+        owned_out,
         scaled[4],
         scaled[5],
         scaled[6],
@@ -1057,7 +1352,7 @@
     whole = (
         seq_count == ctx_count
         and ctx_count & (ctx_count - 1) == 0
-        and fsdp_count & (fsdp_count - 1) == 0
+        and fsdp_count == 4
         and lax.axis_size("tp") == 2
         and block_len % LANES == 0
         and others[5].shape[0] >= inner_width

time: 363 us -> 304 us (0.84)
  matrix products: 40.6 us -> 0 us
  starting transfers between devices: 51.8 us -> 71.9 us
  between operations: 17.5 us -> 4.52 us
  other arithmetic: 18.5 us -> 8.39 us
  local copies, waits for them, and re-layouts: 23.5 us -> 16.1 us
  Pallas kernels: 98.2 us -> 91 us
    ppermute x31 -> x63, waiting for transfers between devices: 70.4 us -> 111 us  [swap(): return lax.ppermute(values, axis, pairs)]
    dot_general x8 -> x0, matrix products: 40.6 us -> none  [the longest x1 6.88 us: whole_local(): jnp.einsum('td,tf->df', normed1_low, grad_pre, preferred_element_type=jnp...]
    ppermute x31 -> x63, starting transfers between devices: 32.2 us -> 68 us  [swap(): return lax.ppermute(values, axis, pairs)]
    pallas_call x4 -> x25, Pallas kernels: 19.4 us -> 43.3 us  [the longest x3 14.3 us: gathered_layer(): pl.pallas_call(kernel, grid_spec=pltpu.PrefetchScalarGridSpec(num_scalar_...]
    all_to_all x5 -> x1, waiting for transfers between devices: 18.6 us -> 0.56 us  [deal(): return lax.all_to_all(pieces, axis, 0, 0)]
    all_to_all x5 -> x1, starting transfers between devices: 19.3 us -> 3.94 us  [deal(): return lax.all_to_all(pieces, axis, 0, 0)]
    reduce_scatter x2 -> x0, waiting for transfers between devices: 14 us -> none  [the longest x1 11.4 us: whole_local(): lax.psum_scatter(grad_down, 'fsdp', scatter_dimension=0, tiled=True)]
    pallas_call x3, Pallas kernels: 21.7 us -> 9.86 us  [by_rows(): pl.pallas_call(kernel, grid_spec=pltpu.PrefetchScalarGridSpec(num_scalar_...]
  transfers between devices with their start and end apart: 40 -> 64, of which waited for: 15 -> 29; matrix products, arithmetic and copies ran while one was open for 17% -> 3% of each run, Pallas kernels for 24% -> 24%
where the time goes in v3:
time: 304 us
  waiting for transfers between devices  112 us (37%)
  Pallas kernels  91 us (30%)
  starting transfers between devices  71.9 us (24%)
  local copies, waits for them, and re-layouts  16.1 us (5%)
  other arithmetic  8.39 us (3%)
  between operations  4.52 us (1%)
    ppermute x63, waiting for transfers between devices, swap(): return lax.ppermute(values, axis, pairs)  111 us
    ppermute x63, starting transfers between devices, swap(): return lax.ppermute(values, axis, pairs)  68 us
    pallas_call x1, Pallas kernels, attend_back(): pl.pallas_call(lambda *refs: attend_back_kernel(*refs, block=block), grid...  15.5 us
    pallas_call x3, Pallas kernels, gathered_layer(): pl.pallas_call(kernel, grid_spec=pltpu.PrefetchScalarGridSpec(num_scalar_...  14.3 us
    pallas_call x4, Pallas kernels, weight_grad(): pl.pallas_call(lambda *refs: weight_grad_kernel(*refs, chunks=chunks, fsd...  13.9 us
    pallas_call x1, Pallas kernels, attend(): pl.pallas_call(lambda *refs: attend_kernel(*refs, block=block), grid_spec...  10.8 us
    pallas_call x3, Pallas kernels, by_rows(): pl.pallas_call(kernel, grid_spec=pltpu.PrefetchScalarGridSpec(num_scalar_...  9.86 us
    pallas_call x3, Pallas kernels, join_halves(): pl.pallas_call(join_kernel, grid_spec=pltpu.PrefetchScalarGridSpec(num_sc...  7.69 us
  transfers between devices with their start and end apart: 64, of which 29 were waited for; matrix products, arithmetic and copies ran while one was open for 3% of the time, Pallas kernels for 24%

profile of v3, /device:TPU:0, one launch (start us, length us, event | category | flops | bytes accessed | tf_op | source)
XLA Modules:
  0.0 303.8 jit_solution(6077199720068956814)
XLA Ops:
  5.0 5.0 %collective-permute-start.2 = (bf16[48,1536]{1,0:T(8,128)(2,1)}, bf16[48,1536]{1,0:T(8,128)(2,1)S(1)}, u32[]{:S(2)}, u32[]{:S(2)}) collective-permute-start(bf16[48,1536]{1,0:T(8,128)(2,1)} %constant_dynamic-slice_fusion.3), channel_id=1, source_target_pairs={{0,24},{8,16},{16,8},{24,0},{1,25},{9,17},{17,9},{25,1},{2,26},{10... | collective-permute-start | bytes 442376 | tf_op jit(solution)/shard_map/ppermute | solution.py:340
  10.6 3.9 %all-to-all-start = ((bf16[4,128,768]{2,1,0:T(8,128)(2,1)}), bf16[4,128,768]{2,1,0:T(8,128)(2,1)S(1)}, u32[]{:S(2)}, u32[]{:S(2)}) async-start(bf16[4,128,768]{2,1,0:T(8,128)(2,1)} %constant_dynamic-slice_fusion.4), calls=%async_computation | async-start | bytes 1572864 | tf_op jit(solution)/shard_map/all_to_all | solution.py:391
  16.1 2.2 dynamic-slice_bitcast_fusion
  18.3 4.4 %collective-permute-done.1.refs_1_ = bf16[48,1536]{1,0:T(8,128)(2,1)S(1)} collective-permute-done((bf16[48,1536]{1,0:T(8,128)(2,1)}, bf16[48,1536]{1,0:T(8,128)(2,1)S(1)}, u32[]{:S(2)}, u32[]{:S(2)}) %collective-permute-start.1) | collective-permute-done | bytes 147488 | tf_op jit(solution)/shard_map/ppermute | solution.py:340
  29.0 1.9 collective-permute-start.6
  32.6 7.0 %collective-permute-done.6.refs_1_ = bf16[48,1536]{1,0:T(8,128)(2,1)S(1)} collective-permute-done((bf16[48,1536]{1,0:T(8,128)(2,1)}, bf16[48,1536]{1,0:T(8,128)(2,1)S(1)}, u32[]{:S(2)}, u32[]{:S(2)}) %collective-permute-start.6) | collective-permute-done | bytes 147488 | tf_op jit(solution)/shard_map/ppermute | solution.py:340
  42.9 2.9 collective-permute-start.10
  45.9 2.7 join_halves.3
  48.6 7.2 %collective-permute-done.11.refs_1_ = bf16[48,1536]{1,0:T(8,128)(2,1)S(1)} collective-permute-done((bf16[48,1536]{1,0:T(8,128)(2,1)}, bf16[48,1536]{1,0:T(8,128)(2,1)S(1)}, u32[]{:S(2)}, u32[]{:S(2)}) %collective-permute-start.11) | collective-permute-done | bytes 147488 | tf_op jit(solution)/shard_map/ppermute | solution.py:340
  55.8 2.2 collective-permute-done.9.refs_2_
  63.3 4.7 %project.1 = (bf16[1024,1152]{1,0:T(8,128)(2,1)S(1)}, bf16[768,1536]{1,0:T(8,128)(2,1)S(1)}) custom-call(s32[2]{0:T(128)S(1)} %pad_add_fusion.places.refs_0_, bf16[1024,768]{1,0:T(8,128)(2,1)S(1)} %bitcast.51, f32[1,1152]{1,0:T(1,128)S(1)} %reshape_reshape.3.bias_ref, bf16[192,1536]{1,0:T(8,128)(2,1)S(1)} %constant_dynamic-update-slice_fusion.own_ref, ...), custom_call_target="tpu_custom_call" | custom-call | tf_op jit(solution)/shard_map/project/pallas_call | solution.py:305
  69.4 10.8 %attend.1 = (bf16[1024,384]{1,0:T(8,128)(2,1)S(1)}, f32[3,2,1024]{2,1,0:T(2,128)S(1)}) custom-call(s32[3]{0:T(128)S(1)} %pad_add_fusion.2.refs_0_.facts, bf16[1024,1152]{1,0:T(8,128)(2,1)S(1)} %get-tuple-element.231.refs_1_.refs_2_.refs_3_, bf16[1024,1152]{1,0:T(8,128)(2,1)S(1)} %get-tuple-element.231.refs_1_.refs_2_.refs_3_, ...), custom_call_target="tpu_custom_call" | custom-call | tf_op jit(solution)/shard_map/attend/pallas_call | solution.py:174
  88.6 4.0 %collective-permute-done.19.refs_2_ = bf16[144,768]{1,0:T(8,128)(2,1)S(1)} collective-permute-done((bf16[144,768]{1,0:T(8,128)(2,1)S(1)}, bf16[144,768]{1,0:T(8,128)(2,1)S(1)}, u32[]{:S(2)}, u32[]{:S(2)}) %collective-permute-start.19) | collective-permute-done | bytes 221216 | tf_op jit(solution)/shard_map/ppermute | solution.py:340
  92.5 4.3 %collective-permute-done.18.refs_1_ = bf16[144,768]{1,0:T(8,128)(2,1)S(1)} collective-permute-done((bf16[144,768]{1,0:T(8,128)(2,1)S(1)}, bf16[144,768]{1,0:T(8,128)(2,1)S(1)}, u32[]{:S(2)}, u32[]{:S(2)}) %collective-permute-start.18) | collective-permute-done | bytes 221216 | tf_op jit(solution)/shard_map/ppermute | solution.py:340
  100.4 5.5 %up.1 = (bf16[1024,1536]{1,0:T(8,128)(2,1)S(1)}, bf16[1024,1536]{1,0:T(8,128)(2,1)S(1)}, bf16[768,1536]{1,0:T(8,128)(2,1)S(1)}) custom-call(s32[2]{0:T(128)S(1)} %pad_add_fusion.places.refs_0_, bf16[1024,768]{1,0:T(8,128)(2,1)S(1)} %get-tuple-element.245.left_ref.refs_1_, f32[1,1536]{1,0:T(1,128)S(1)} %reshape.114.bias_ref, bf16[192,1536]{1,0:T(8,128)(2,1)S(1)} %copy-done.2, ...), custom_call_target="tpu_custom_call" | custom-call | tf_op jit(solution)/shard_map/up/pallas_call | solution.py:305
  106.1 3.8 %collective-permute-done.21.refs_4_ = bf16[144,768]{1,0:T(8,128)(2,1)S(1)} collective-permute-done((bf16[144,768]{1,0:T(8,128)(2,1)S(1)}, bf16[144,768]{1,0:T(8,128)(2,1)S(1)}, u32[]{:S(2)}, u32[]{:S(2)}) %collective-permute-start.21) | collective-permute-done | bytes 221216 | tf_op jit(solution)/shard_map/ppermute | solution.py:340
  109.9 4.1 %down.1 = (bf16[1024,768]{1,0:T(8,128)(2,1)S(1)}, bf16[768,1536]{1,0:T(8,128)(2,1)S(1)}) custom-call(s32[2]{0:T(128)S(1)} %pad_add_fusion.places.refs_0_, bf16[1024,1536]{1,0:T(8,128)(2,1)S(1)} %get-tuple-element.255.left_ref.refs_2_, bf16[192,1536]{1,0:T(8,128)(2,1)S(1)} %copy-done.3, bf16[144,1536]{1,0:T(8,128)(2,1)S(1)} %stack_rows.8.part_ref, ...), custom_call_target="tpu_custom_call" | custom-call | tf_op jit(solution)/shard_map/down/pallas_call | solution.py:305
  117.7 4.2 %collective-permute-done.24.refs_1_ = bf16[128,768]{1,0:T(8,128)(2,1)S(1)} collective-permute-done((bf16[128,768]{1,0:T(8,128)(2,1)S(1)}, bf16[128,768]{1,0:T(8,128)(2,1)S(1)}, u32[]{:S(2)}, u32[]{:S(2)}) %collective-permute-start.24) | collective-permute-done | bytes 196640 | tf_op jit(solution)/shard_map/ppermute | solution.py:340
  122.2 3.7 %collective-permute-done.26.refs_3_ = bf16[128,768]{1,0:T(8,128)(2,1)S(1)} collective-permute-done((bf16[128,768]{1,0:T(8,128)(2,1)S(1)}, bf16[128,768]{1,0:T(8,128)(2,1)S(1)}, u32[]{:S(2)}, u32[]{:S(2)}) %collective-permute-start.26) | collective-permute-done | bytes 196640 | tf_op jit(solution)/shard_map/ppermute | solution.py:340
  126.1 2.2 collective-permute-done.27.other_teacher_ref
  128.3 5.1 %second_norm.1 = (bf16[4,128,768]{2,1,0:T(8,128)(2,1)S(1)}, f32[1024,768]{1,0:T(8,128)S(1)}, bf16[1024,768]{1,0:T(8,128)(2,1)S(1)}, f32[8,768]{1,0:T(8,128)S(1)}) custom-call(s32[3]{0:T(128)S(1)} %pad_add_fusion.2.refs_0_.facts, f32[1024,768]{1,0:T(8,128)S(1)} %get-tuple-element.240.normal_ref, f32[1,768]{1,0:T(1,128)S(1)} %reshape.112.gain_ref.gain1_ref, ...), custom_call_target="tpu_custom_call" | custom-call | tf_op jit(solution)/shard_map/second_norm/pallas_call | solution.py:506
  137.0 4.0 %weight_grad.4 = (bf16[384,1536]{1,0:T(8,128)(2,1)S(1)}, bf16[384,1536]{1,0:T(8,128)(2,1)S(1)}) custom-call(s32[2]{0:T(128)S(1)} %pad_add_fusion.places.refs_0_, bf16[1024,768]{1,0:T(8,128)(2,1)S(1)} %get-tuple-element.272.refs_1_.low_ref, bf16[1024,1536]{1,0:T(8,128)(2,1)S(1)} %get-tuple-element.255.left_ref.refs_2_), custom_call_target="tpu_custom_call" | custom-call | tf_op jit(solution)/shard_map/weight_grad/pallas_call | solution.py:710
  141.1 3.9 %grad_pre.1 = (bf16[1024,1536]{1,0:T(8,128)(2,1)S(1)}, f32[8,1536]{1,0:T(8,128)S(1)}) custom-call(bf16[1024,768]{1,0:T(8,128)(2,1)S(1)} %get-tuple-element.272.refs_1_.low_ref, bf16[768,1536]{1,0:T(8,128)(2,1)S(1)} %get-tuple-element.273.weight_ref, bf16[1024,1536]{1,0:T(8,128)(2,1)S(1)} %get-tuple-element.274.slope_ref), custom_call_target="tpu_custom_call" | custom-call | tf_op jit(solution)/shard_map/grad_pre/pallas_call | solution.py:540
  145.0 3.3 %rows_times.4.mine_ref = bf16[1024,768]{1,0:T(8,128)(2,1)S(1)} custom-call(bf16[1024,1536]{1,0:T(8,128)(2,1)S(1)} %get-tuple-element.286.refs_0_.refs_2_, bf16[768,1536]{1,0:T(8,128)(2,1)S(1)} %get-tuple-element.276.refs_1_), custom_call_target="tpu_custom_call" | custom-call | tf_op jit(solution)/shard_map/rows_times/pallas_call | solution.py:560
  148.3 2.2 collective-permute-start.35
  150.5 4.0 %weight_grad.6 = (bf16[192,1536]{1,0:T(8,128)(2,1)S(1)}, bf16[192,1536]{1,0:T(8,128)(2,1)S(1)}, bf16[192,1536]{1,0:T(8,128)(2,1)S(1)}, bf16[192,1536]{1,0:T(8,128)(2,1)S(1)}) custom-call(s32[2]{0:T(128)S(1)} %pad_add_fusion.places.refs_0_, bf16[1024,768]{1,0:T(8,128)(2,1)S(1)} %get-tuple-element.245.left_ref.refs_1_, ...), custom_call_target="tpu_custom_call" | custom-call | tf_op jit(solution)/shard_map/weight_grad/pallas_call | solution.py:710
  158.1 3.2 %first_norm_back.1 = (bf16[1024,768]{1,0:T(8,128)(2,1)S(1)}, f32[4,128,768]{2,1,0:T(8,128)S(1)}, f32[8,768]{1,0:T(8,128)S(1)}) custom-call(s32[3]{0:T(128)S(1)} %pad_add_fusion.2.refs_0_.facts, f32[1024,768]{1,0:T(8,128)S(1)} %get-tuple-element.268.grad_ref, bf16[1024,768]{1,0:T(8,128)(2,1)S(1)} %rows_times.4.mine_ref, ...), custom_call_target="tpu_custom_call" | custom-call | tf_op jit(solution)/shard_map/first_norm_back/pallas_call | solution.py:506
  164.5 15.5 %attend_back.1 = (bf16[1024,1152]{1,0:T(8,128)(2,1)S(1)}, f32[8,1152]{1,0:T(8,128)S(1)}) custom-call(s32[3]{0:T(128)S(1)} %pad_add_fusion.2.refs_0_.facts, bf16[1024,1152]{1,0:T(8,128)(2,1)S(1)} %get-tuple-element.231.refs_1_.refs_2_.refs_3_, bf16[1024,1152]{1,0:T(8,128)(2,1)S(1)} %get-tuple-element.231.refs_1_.refs_2_.refs_3_, ...), custom_call_target="tpu_custom_call" | custom-call | tf_op jit(solution)/shard_map/attend_back/pallas_call | solution.py:198
  180.0 3.8 %collective-permute-done.33.refs_2_ = bf16[192,1536]{1,0:T(8,128)(2,1)S(1)} collective-permute-done((bf16[192,1536]{1,0:T(8,128)(2,1)S(1)}, bf16[192,1536]{1,0:T(8,128)(2,1)S(1)}, u32[]{:S(2)}, u32[]{:S(2)}) %collective-permute-start.33) | collective-permute-done | bytes 589856 | tf_op jit(solution)/shard_map/ppermute | solution.py:340
  183.8 4.3 %weight_grad.7 = (bf16[192,1152]{1,0:T(8,128)(2,1)S(1)}, bf16[192,1152]{1,0:T(8,128)(2,1)S(1)}, bf16[192,1152]{1,0:T(8,128)(2,1)S(1)}, bf16[192,1152]{1,0:T(8,128)(2,1)S(1)}) custom-call(s32[2]{0:T(128)S(1)} %pad_add_fusion.places.refs_0_, bf16[1024,768]{1,0:T(8,128)(2,1)S(1)} %bitcast.53, bf16[1024,1152]{1,0:T(8,128)(2,1)S(1)} %get-tuple-element.315.refs_2_.grad_ref), custom_call_target="tpu_custom_call" | custom-call | tf_op jit(solution)/shard_map/weight_grad/pallas_call | solution.py:710
  188.4 2.0 collective-permute-start.40
  194.9 3.9 %input_back.1 = (bf16[4,128,768]{2,1,0:T(8,128)(2,1)S(1)}, bf16[4,128,768]{2,1,0:T(8,128)(2,1)S(1)}) custom-call(s32[3]{0:T(128)S(1)} %pad_add_fusion.2.refs_0_.facts, bf16[1024,1152]{1,0:T(8,128)(2,1)S(1)} %get-tuple-element.315.refs_2_.grad_ref, bf16[768,1536]{1,0:T(8,128)(2,1)S(1)} %get-tuple-element.239.weight_ref), custom_call_target="tpu_custom_call" | custom-call | tf_op jit(solution)/shard_map/input_back/pallas_call | solution.py:585
  199.7 23.3 %collective-permute-done.41 = bf16[192,384]{1,0:T(8,128)(2,1)S(1)} collective-permute-done((bf16[192,384]{1,0:T(8,128)(2,1)S(1)}, bf16[192,384]{1,0:T(8,128)(2,1)S(1)}, u32[]{:S(2)}, u32[]{:S(2)}) %collective-permute-start.41) | collective-permute-done | bytes 147488 | tf_op jit(solution)/shard_map/ppermute | solution.py:340
  223.9 2.0 collective-permute-start.43
  227.6 2.3 join_halves.4
  230.0 2.2 collective-permute-done.42.refs_1_
  232.2 5.4 %collective-permute-done.43.refs_1_ = bf16[96,1536]{1,0:T(8,128)(2,1)S(1)} collective-permute-done((bf16[96,1536]{1,0:T(8,128)(2,1)S(1)}, bf16[96,1536]{1,0:T(8,128)(2,1)S(1)}, u32[]{:S(2)}, u32[]{:S(2)}) %collective-permute-start.43) | collective-permute-done | bytes 294944 | tf_op jit(solution)/shard_map/ppermute | solution.py:340
  240.3 1.9 collective-permute-start.47
  244.8 2.4 collective-permute-done.51
  247.2 2.9 collective-permute-done.46
  250.1 2.6 collective-permute-done.47
  258.5 9.1 %collective-permute-done.56.refs_3_ = bf16[128,768]{1,0:T(8,128)(2,1)S(1)} collective-permute-done((bf16[128,768]{1,0:T(8,128)(2,1)S(1)}, bf16[128,768]{1,0:T(8,128)(2,1)S(1)}, u32[]{:S(2)}, u32[]{:S(2)}) %collective-permute-start.56) | collective-permute-done | bytes 196640 | tf_op jit(solution)/shard_map/ppermute | solution.py:340
  271.0 2.4 collective-permute-done.60
  276.7 1.9 collective-permute-done.61
  281.8 2.7 join_halves.5
  284.5 4.6 %collective-permute-done.59 = bf16[192,384]{1,0:T(8,128)(2,1)} collective-permute-done((bf16[192,384]{1,0:T(8,128)(2,1)S(1)}, bf16[192,384]{1,0:T(8,128)(2,1)}, u32[]{:S(2)}, u32[]{:S(2)}) %collective-permute-start.59) | collective-permute-done | bytes 147488 | tf_op jit(solution)/shard_map/ppermute | solution.py:340
  289.0 5.0 %collective-permute-done.57.refs_5_ = bf16[48,2688]{1,0:T(8,128)(2,1)S(1)} collective-permute-done((bf16[48,2688]{1,0:T(8,128)(2,1)S(1)}, bf16[48,2688]{1,0:T(8,128)(2,1)S(1)}, u32[]{:S(2)}, u32[]{:S(2)}) %collective-permute-start.57) | collective-permute-done | bytes 258080 | tf_op jit(solution)/shard_map/ppermute | solution.py:340
  297.6 2.4 add_multiply_fusion
  (223 shorter events, 84.5 us)
Async XLA Ops:
  5.0 13.3 %collective-permute-start.2 = (bf16[48,1536]{1,0:T(8,128)(2,1)}, bf16[48,1536]{1,0:T(8,128)(2,1)S(1)}, u32[]{:S(2)}, u32[]{:S(2)}) collective-permute-start(bf16[48,1536]{1,0:T(8,128)(2,1)} %constant_dynamic-slice_fusion.3), channel_id=1, source_target_pairs={{0,24},{8,16},{16,8},{24,0},{1,25},{9,17},{17,9},{25,1},{2,26},{10... | collective-permute-start | bytes 442376 | tf_op jit(solution)/shard_map/ppermute | solution.py:340
  10.0 12.7 %collective-permute-start.1 = (bf16[48,1536]{1,0:T(8,128)(2,1)}, bf16[48,1536]{1,0:T(8,128)(2,1)S(1)}, u32[]{:S(2)}, u32[]{:S(2)}) collective-permute-start(bf16[48,1536]{1,0:T(8,128)(2,1)} %constant_dynamic-slice_fusion.3), channel_id=1, source_target_pairs={{0,16},{8,24},{16,0},{24,8},{1,17},{9,25},{17,1},{25,9},{2,18},{10... | collective-permute-start | bytes 442376 | tf_op jit(solution)/shard_map/ppermute | solution.py:340
  10.0 13.4 %collective-permute-start = (bf16[48,1536]{1,0:T(8,128)(2,1)}, bf16[48,1536]{1,0:T(8,128)(2,1)S(1)}, u32[]{:S(2)}, u32[]{:S(2)}) collective-permute-start(bf16[48,1536]{1,0:T(8,128)(2,1)} %constant_dynamic-slice_fusion.3), channel_id=1, source_target_pairs={{0,8},{8,0},{16,24},{24,16},{1,9},{9,1},{17,25},{25,17},{2,10},{10... | collective-permute-start | bytes 442376 | tf_op jit(solution)/shard_map/ppermute | solution.py:340
  10.6 14.0 %all-to-all-start = ((bf16[4,128,768]{2,1,0:T(8,128)(2,1)}), bf16[4,128,768]{2,1,0:T(8,128)(2,1)S(1)}, u32[]{:S(2)}, u32[]{:S(2)}) async-start(bf16[4,128,768]{2,1,0:T(8,128)(2,1)} %constant_dynamic-slice_fusion.4), calls=%async_computation | async-start | bytes 1572864 | tf_op jit(solution)/shard_map/all_to_all | solution.py:391
  26.5 13.8 %collective-permute-start.4 = (bf16[160,1536]{1,0:T(8,128)(2,1)S(1)}, bf16[160,1536]{1,0:T(8,128)(2,1)S(1)}, u32[]{:S(2)}, u32[]{:S(2)}) collective-permute-start(bf16[160,1536]{1,0:T(8,128)(2,1)S(1)} %stack_rows.6.refs_0_), channel_id=1, source_target_pairs={{0,4},{2,6},{4,0},{6,2},{1,5},{3,7},{5,1},{7,3},{8,12},{10,14},{12... | collective-permute-start | bytes 1474568 | tf_op jit(solution)/shard_map/ppermute | solution.py:340
  28.0 12.3 %collective-permute-start.3 = (bf16[160,1536]{1,0:T(8,128)(2,1)S(1)}, bf16[160,1536]{1,0:T(8,128)(2,1)}, u32[]{:S(2)}, u32[]{:S(2)}) collective-permute-start(bf16[160,1536]{1,0:T(8,128)(2,1)S(1)} %stack_rows.6.refs_0_), channel_id=1, source_target_pairs={{0,2},{2,0},{4,6},{6,4},{1,3},{3,1},{5,7},{7,5},{8,10},{10,8},{12,... | collective-permute-start | bytes 1474568 | tf_op jit(solution)/shard_map/ppermute | solution.py:340
  29.0 16.9 %collective-permute-start.8 = (bf16[4,128,768]{2,1,0:T(8,128)(2,1)S(1)}, bf16[4,128,768]{2,1,0:T(8,128)(2,1)}, u32[]{:S(2)}, u32[]{:S(2)}) collective-permute-start(bf16[4,128,768]{2,1,0:T(8,128)(2,1)S(1)} %all-to-all-done.own_ref), channel_id=1, source_target_pairs={{0,1},{1,0},{2,3},{3,2},{4,5},{5,4},{6,7},{7,6},{8,9},{9,8},{10,11... | collective-permute-start | bytes 2359304 | tf_op jit(solution)/shard_map/ppermute | solution.py:340
  29.0 10.6 %collective-permute-start.6 = (bf16[48,1536]{1,0:T(8,128)(2,1)}, bf16[48,1536]{1,0:T(8,128)(2,1)S(1)}, u32[]{:S(2)}, u32[]{:S(2)}) collective-permute-start(bf16[48,1536]{1,0:T(8,128)(2,1)} %get-tuple-element.217), channel_id=1, source_target_pairs={{0,16},{8,24},{16,0},{24,8},{1,17},{9,25},{17,1},{25,9},{2,18},{10... | collective-permute-start | bytes 442376 | tf_op jit(solution)/shard_map/ppermute | solution.py:340
  41.1 16.9 %collective-permute-start.7 = (bf16[160,1536]{1,0:T(8,128)(2,1)}, bf16[160,1536]{1,0:T(8,128)(2,1)}, u32[]{:S(2)}, u32[]{:S(2)}) collective-permute-start(bf16[160,1536]{1,0:T(8,128)(2,1)} %collective-permute-done.3.refs_1_), channel_id=1, source_target_pairs={{0,4},{2,6},{4,0},{6,2},{1,5},{3,7},{5,1},{7,3},{8,12},{10,14},{12... | collective-permute-start | bytes 1474568 | tf_op jit(solution)/shard_map/ppermute | solution.py:340
  42.1 13.7 %collective-permute-start.11 = (bf16[48,1536]{1,0:T(8,128)(2,1)}, bf16[48,1536]{1,0:T(8,128)(2,1)S(1)}, u32[]{:S(2)}, u32[]{:S(2)}) collective-permute-start(bf16[48,1536]{1,0:T(8,128)(2,1)} %get-tuple-element.224), channel_id=1, source_target_pairs={{0,16},{8,24},{16,0},{24,8},{1,17},{9,25},{17,1},{25,9},{2,18},{10... | collective-permute-start | bytes 442376 | tf_op jit(solution)/shard_map/ppermute | solution.py:340
  42.9 12.9 %collective-permute-start.10 = (bf16[48,1536]{1,0:T(8,128)(2,1)}, bf16[48,1536]{1,0:T(8,128)(2,1)}, u32[]{:S(2)}, u32[]{:S(2)}) collective-permute-start(bf16[48,1536]{1,0:T(8,128)(2,1)} %get-tuple-element.224), channel_id=1, source_target_pairs={{0,8},{8,0},{16,24},{24,16},{1,9},{9,1},{17,25},{25,17},{2,10},{10... | collective-permute-start | bytes 442376 | tf_op jit(solution)/shard_map/ppermute | solution.py:340
  45.8 12.2 %collective-permute-start.9 = (bf16[48,1536]{1,0:T(8,128)(2,1)}, bf16[48,1536]{1,0:T(8,128)(2,1)}, u32[]{:S(2)}, u32[]{:S(2)}) collective-permute-start(bf16[48,1536]{1,0:T(8,128)(2,1)} %collective-permute-done.5.refs_0_), channel_id=1, source_target_pairs={{0,16},{8,24},{16,0},{24,8},{1,17},{9,25},{17,1},{25,9},{2,18},{10... | collective-permute-start | bytes 442376 | tf_op jit(solution)/shard_map/ppermute | solution.py:340
  59.0 21.2 %collective-permute-start.14 = (bf16[144,1536]{1,0:T(8,128)(2,1)S(1)}, bf16[144,1536]{1,0:T(8,128)(2,1)S(1)}, u32[]{:S(2)}, u32[]{:S(2)}) collective-permute-start(bf16[144,1536]{1,0:T(8,128)(2,1)S(1)} %stack_rows.7.refs_0_), channel_id=1, source_target_pairs={{0,6},{2,4},{4,2},{6,0},{1,7},{3,5},{5,3},{7,1},{8,14},{10,12},{12... | collective-permute-start | bytes 1327112 | tf_op jit(solution)/shard_map/ppermute | solution.py:340
  60.5 20.0 %collective-permute-start.13 = (bf16[144,1536]{1,0:T(8,128)(2,1)S(1)}, bf16[144,1536]{1,0:T(8,128)(2,1)S(1)}, u32[]{:S(2)}, u32[]{:S(2)}) collective-permute-start(bf16[144,1536]{1,0:T(8,128)(2,1)S(1)} %stack_rows.7.refs_0_), channel_id=1, source_target_pairs={{0,4},{2,6},{4,0},{6,2},{1,5},{3,7},{5,1},{7,3},{8,12},{10,14},{12... | collective-permute-start | bytes 1327112 | tf_op jit(solution)/shard_map/ppermute | solution.py:340
  61.1 19.5 %collective-permute-start.12 = (bf16[144,1536]{1,0:T(8,128)(2,1)S(1)}, bf16[144,1536]{1,0:T(8,128)(2,1)S(1)}, u32[]{:S(2)}, u32[]{:S(2)}) collective-permute-start(bf16[144,1536]{1,0:T(8,128)(2,1)S(1)} %stack_rows.7.refs_0_), channel_id=1, source_target_pairs={{0,2},{2,0},{4,6},{6,4},{1,3},{3,1},{5,7},{7,5},{8,10},{10,8},{12,... | collective-permute-start | bytes 1327112 | tf_op jit(solution)/shard_map/ppermute | solution.py:340
  62.6 17.6 %collective-permute-start.15 = (bf16[48,1536]{1,0:T(8,128)(2,1)}, bf16[48,1536]{1,0:T(8,128)(2,1)S(1)}, u32[]{:S(2)}, u32[]{:S(2)}) collective-permute-start(bf16[48,1536]{1,0:T(8,128)(2,1)} %collective-permute-done.10.refs_0_), channel_id=1, source_target_pairs={{0,16},{8,24},{16,0},{24,8},{1,17},{9,25},{17,1},{25,9},{2,18},{10... | collective-permute-start | bytes 442376 | tf_op jit(solution)/shard_map/ppermute | solution.py:340
  84.8 12.1 %collective-permute-start.18 = (bf16[144,768]{1,0:T(8,128)(2,1)S(1)}, bf16[144,768]{1,0:T(8,128)(2,1)S(1)}, u32[]{:S(2)}, u32[]{:S(2)}) collective-permute-start(bf16[144,768]{1,0:T(8,128)(2,1)S(1)} %slice.120), channel_id=1, source_target_pairs={{0,4},{2,6},{4,0},{6,2},{1,5},{3,7},{5,1},{7,3},{8,12},{10,14},{12... | collective-permute-start | bytes 663560 | tf_op jit(solution)/shard_map/ppermute | solution.py:340
  85.4 11.5 %collective-permute-start.17 = (bf16[144,768]{1,0:T(8,128)(2,1)S(1)}, bf16[144,768]{1,0:T(8,128)(2,1)S(1)}, u32[]{:S(2)}, u32[]{:S(2)}) collective-permute-start(bf16[144,768]{1,0:T(8,128)(2,1)S(1)} %slice.120), channel_id=1, source_target_pairs={{0,2},{2,0},{4,6},{6,4},{1,3},{3,1},{5,7},{7,5},{8,10},{10,8},{12,... | collective-permute-start | bytes 663560 | tf_op jit(solution)/shard_map/ppermute | solution.py:340
  98.3 11.6 %collective-permute-start.21 = (bf16[144,768]{1,0:T(8,128)(2,1)S(1)}, bf16[144,768]{1,0:T(8,128)(2,1)S(1)}, u32[]{:S(2)}, u32[]{:S(2)}) collective-permute-start(bf16[144,768]{1,0:T(8,128)(2,1)S(1)} %slice.98), channel_id=1, source_target_pairs={{0,4},{2,6},{4,0},{6,2},{1,5},{3,7},{5,1},{7,3},{8,12},{10,14},{12... | collective-permute-start | bytes 663560 | tf_op jit(solution)/shard_map/ppermute | solution.py:340
  98.9 11.0 %collective-permute-start.20 = (bf16[144,768]{1,0:T(8,128)(2,1)S(1)}, bf16[144,768]{1,0:T(8,128)(2,1)S(1)}, u32[]{:S(2)}, u32[]{:S(2)}) collective-permute-start(bf16[144,768]{1,0:T(8,128)(2,1)S(1)} %slice.98), channel_id=1, source_target_pairs={{0,2},{2,0},{4,6},{6,4},{1,3},{3,1},{5,7},{7,5},{8,10},{10,8},{12,... | collective-permute-start | bytes 663560 | tf_op jit(solution)/shard_map/ppermute | solution.py:340
  114.0 14.3 %collective-permute-start.23 = (bf16[1024,768]{1,0:T(8,128)(2,1)S(1)}, bf16[1024,768]{1,0:T(8,128)(2,1)S(1)}, u32[]{:S(2)}, u32[]{:S(2)}) collective-permute-start(bf16[1024,768]{1,0:T(8,128)(2,1)S(1)} %get-tuple-element.263.mine_ref), channel_id=1, source_target_pairs={{0,1},{1,0},{2,3},{3,2},{4,5},{5,4},{6,7},{7,6},{8,9},{9,8},{10,11... | collective-permute-start | bytes 4718600 | tf_op jit(solution)/shard_map/ppermute | solution.py:340
  133.5 14.8 %collective-permute-start.30 = (bf16[128,768]{1,0:T(8,128)(2,1)S(1)}, bf16[128,768]{1,0:T(8,128)(2,1)S(1)}, u32[]{:S(2)}, u32[]{:S(2)}) collective-permute-start(bf16[128,768]{1,0:T(8,128)(2,1)S(1)} %get-tuple-element.453), channel_id=1, source_target_pairs={{0,6},{2,4},{4,2},{6,0},{1,7},{3,5},{5,3},{7,1},{8,14},{10,12},{12... | collective-permute-start | bytes 589832 | tf_op jit(solution)/shard_map/ppermute | solution.py:340
  135.2 13.0 %collective-permute-start.29 = (bf16[128,768]{1,0:T(8,128)(2,1)S(1)}, bf16[128,768]{1,0:T(8,128)(2,1)S(1)}, u32[]{:S(2)}, u32[]{:S(2)}) collective-permute-start(bf16[128,768]{1,0:T(8,128)(2,1)S(1)} %get-tuple-element.454), channel_id=1, source_target_pairs={{0,4},{2,6},{4,0},{6,2},{1,5},{3,7},{5,1},{7,3},{8,12},{10,14},{12... | collective-permute-start | bytes 589832 | tf_op jit(solution)/shard_map/ppermute | solution.py:340
  136.5 11.8 %collective-permute-start.28 = (bf16[128,768]{1,0:T(8,128)(2,1)S(1)}, bf16[128,768]{1,0:T(8,128)(2,1)S(1)}, u32[]{:S(2)}, u32[]{:S(2)}) collective-permute-start(bf16[128,768]{1,0:T(8,128)(2,1)S(1)} %get-tuple-element.455), channel_id=1, source_target_pairs={{0,2},{2,0},{4,6},{6,4},{1,3},{3,1},{5,7},{7,5},{8,10},{10,8},{12,... | collective-permute-start | bytes 589832 | tf_op jit(solution)/shard_map/ppermute | solution.py:340
  148.3 35.4 %collective-permute-start.35 = (bf16[384,1536]{1,0:T(8,128)(2,1)S(1)}, bf16[384,1536]{1,0:T(8,128)(2,1)S(1)}, u32[]{:S(2)}, u32[]{:S(2)}) collective-permute-start(bf16[384,1536]{1,0:T(8,128)(2,1)S(1)} %get-tuple-element.290), channel_id=1, source_target_pairs={{0,8},{8,0},{16,24},{24,16},{1,9},{9,1},{17,25},{25,17},{2,10},{10... | collective-permute-start | bytes 3538952 | tf_op jit(solution)/shard_map/ppermute | solution.py:340
  154.5 25.4 %collective-permute-start.32 = (bf16[192,1536]{1,0:T(8,128)(2,1)S(1)}, bf16[192,1536]{1,0:T(8,128)(2,1)S(1)}, u32[]{:S(2)}, u32[]{:S(2)}) collective-permute-start(bf16[192,1536]{1,0:T(8,128)(2,1)S(1)} %get-tuple-element.287), channel_id=1, source_target_pairs={{0,2},{2,0},{4,6},{6,4},{1,3},{3,1},{5,7},{7,5},{8,10},{10,8},{12,... | collective-permute-start | bytes 1769480 | tf_op jit(solution)/shard_map/ppermute | solution.py:340
  156.0 27.8 %collective-permute-start.33 = (bf16[192,1536]{1,0:T(8,128)(2,1)S(1)}, bf16[192,1536]{1,0:T(8,128)(2,1)S(1)}, u32[]{:S(2)}, u32[]{:S(2)}) collective-permute-start(bf16[192,1536]{1,0:T(8,128)(2,1)S(1)} %get-tuple-element.288), channel_id=1, source_target_pairs={{0,4},{2,6},{4,0},{6,2},{1,5},{3,7},{5,1},{7,3},{8,12},{10,14},{12... | collective-permute-start | bytes 1769480 | tf_op jit(solution)/shard_map/ppermute | solution.py:340
  156.7 27.0 %collective-permute-start.34 = (bf16[192,1536]{1,0:T(8,128)(2,1)S(1)}, bf16[192,1536]{1,0:T(8,128)(2,1)S(1)}, u32[]{:S(2)}, u32[]{:S(2)}) collective-permute-start(bf16[192,1536]{1,0:T(8,128)(2,1)S(1)} %get-tuple-element.289), channel_id=1, source_target_pairs={{0,6},{2,4},{4,2},{6,0},{1,7},{3,5},{5,3},{7,1},{8,14},{10,12},{12... | collective-permute-start | bytes 1769480 | tf_op jit(solution)/shard_map/ppermute | solution.py:340
  164.4 19.3 %collective-permute-start.36 = (bf16[384,384]{1,0:T(8,128)(2,1)S(1)}, bf16[384,384]{1,0:T(8,128)(2,1)S(1)}, u32[]{:S(2)}, u32[]{:S(2)}) collective-permute-start(bf16[384,384]{1,0:T(8,128)(2,1)S(1)} %get-tuple-element.291), channel_id=1, source_target_pairs={{0,8},{8,0},{16,24},{24,16},{1,9},{9,1},{17,25},{25,17},{2,10},{10... | collective-permute-start | bytes 884744 | tf_op jit(solution)/shard_map/ppermute | solution.py:340
  188.4 34.6 %collective-permute-start.40 = (bf16[192,1536]{1,0:T(8,128)(2,1)S(1)}, bf16[192,1536]{1,0:T(8,128)(2,1)S(1)}, u32[]{:S(2)}, u32[]{:S(2)}) collective-permute-start(bf16[192,1536]{1,0:T(8,128)(2,1)S(1)} %get-tuple-element.318), channel_id=1, source_target_pairs={{0,16},{8,24},{16,0},{24,8},{1,17},{9,25},{17,1},{25,9},{2,18},{10... | collective-permute-start | bytes 1769480 | tf_op jit(solution)/shard_map/ppermute | solution.py:340
  190.4 32.6 %collective-permute-start.37 = (bf16[192,1152]{1,0:T(8,128)(2,1)S(1)}, bf16[192,1152]{1,0:T(8,128)(2,1)S(1)}, u32[]{:S(2)}, u32[]{:S(2)}) collective-permute-start(bf16[192,1152]{1,0:T(8,128)(2,1)S(1)} %get-tuple-element.312), channel_id=1, source_target_pairs={{0,2},{2,0},{4,6},{6,4},{1,3},{3,1},{5,7},{7,5},{8,10},{10,8},{12,... | collective-permute-start | bytes 1327112 | tf_op jit(solution)/shard_map/ppermute | solution.py:340
  191.8 31.2 %collective-permute-start.38 = (bf16[192,1152]{1,0:T(8,128)(2,1)S(1)}, bf16[192,1152]{1,0:T(8,128)(2,1)S(1)}, u32[]{:S(2)}, u32[]{:S(2)}) collective-permute-start(bf16[192,1152]{1,0:T(8,128)(2,1)S(1)} %get-tuple-element.313), channel_id=1, source_target_pairs={{0,4},{2,6},{4,0},{6,2},{1,5},{3,7},{5,1},{7,3},{8,12},{10,14},{12... | collective-permute-start | bytes 1327112 | tf_op jit(solution)/shard_map/ppermute | solution.py:340
  192.5 30.5 %collective-permute-start.39 = (bf16[192,1152]{1,0:T(8,128)(2,1)S(1)}, bf16[192,1152]{1,0:T(8,128)(2,1)S(1)}, u32[]{:S(2)}, u32[]{:S(2)}) collective-permute-start(bf16[192,1152]{1,0:T(8,128)(2,1)S(1)} %get-tuple-element.314), channel_id=1, source_target_pairs={{0,6},{2,4},{4,2},{6,0},{1,7},{3,5},{5,3},{7,1},{8,14},{10,12},{12... | collective-permute-start | bytes 1327112 | tf_op jit(solution)/shard_map/ppermute | solution.py:340
  193.9 29.1 %collective-permute-start.41 = (bf16[192,384]{1,0:T(8,128)(2,1)S(1)}, bf16[192,384]{1,0:T(8,128)(2,1)S(1)}, u32[]{:S(2)}, u32[]{:S(2)}) collective-permute-start(bf16[192,384]{1,0:T(8,128)(2,1)S(1)} %get-tuple-element.319), channel_id=1, source_target_pairs={{0,16},{8,24},{16,0},{24,8},{1,17},{9,25},{17,1},{25,9},{2,18},{10... | collective-permute-start | bytes 442376 | tf_op jit(solution)/shard_map/ppermute | solution.py:340
  223.4 14.2 %collective-permute-start.44 = (bf16[4,128,768]{2,1,0:T(8,128)(2,1)S(1)}, bf16[4,128,768]{2,1,0:T(8,128)(2,1)S(1)}, u32[]{:S(2)}, u32[]{:S(2)}) collective-permute-start(bf16[4,128,768]{2,1,0:T(8,128)(2,1)S(1)} %get-tuple-element.348), channel_id=1, source_target_pairs={{0,1},{1,0},{2,3},{3,2},{4,5},{5,4},{6,7},{7,6},{8,9},{9,8},{10,11... | collective-permute-start | bytes 2359304 | tf_op jit(solution)/shard_map/ppermute | solution.py:340
  223.9 13.7 %collective-permute-start.43 = (bf16[96,1536]{1,0:T(8,128)(2,1)S(1)}, bf16[96,1536]{1,0:T(8,128)(2,1)S(1)}, u32[]{:S(2)}, u32[]{:S(2)}) collective-permute-start(bf16[96,1536]{1,0:T(8,128)(2,1)S(1)} %get-tuple-element.347), channel_id=1, source_target_pairs={{0,8},{8,0},{16,24},{24,16},{1,9},{9,1},{17,25},{25,17},{2,10},{10... | collective-permute-start | bytes 884744 | tf_op jit(solution)/shard_map/ppermute | solution.py:340
  226.1 21.0 %collective-permute-start.48 = (bf16[192,1536]{1,0:T(8,128)(2,1)S(1)}, bf16[192,1536]{1,0:T(8,128)(2,1)S(1)}, u32[]{:S(2)}, u32[]{:S(2)}) collective-permute-start(bf16[192,1536]{1,0:T(8,128)(2,1)S(1)} %add_convert_fusion.2), channel_id=1, source_target_pairs={{0,2},{2,0},{4,6},{6,4},{1,3},{3,1},{5,7},{7,5},{8,10},{10,8},{12,... | collective-permute-start | bytes 1769480 | tf_op jit(solution)/shard_map/ppermute | solution.py:340
  239.1 11.0 %collective-permute-start.46 = (bf16[48,1152]{1,0:T(8,128)(2,1)S(1)}, bf16[48,1152]{1,0:T(8,128)(2,1)S(1)}, u32[]{:S(2)}, u32[]{:S(2)}) collective-permute-start(bf16[48,1152]{1,0:T(8,128)(2,1)S(1)} %get-tuple-element.364), channel_id=1, source_target_pairs={{0,16},{8,24},{16,0},{24,8},{1,17},{9,25},{17,1},{25,9},{2,18},{10... | collective-permute-start | bytes 331784 | tf_op jit(solution)/shard_map/ppermute | solution.py:340
  240.3 12.3 %collective-permute-start.47 = (bf16[48,1536]{1,0:T(8,128)(2,1)S(1)}, bf16[48,1536]{1,0:T(8,128)(2,1)S(1)}, u32[]{:S(2)}, u32[]{:S(2)}) collective-permute-start(bf16[48,1536]{1,0:T(8,128)(2,1)S(1)} %get-tuple-element.367), channel_id=1, source_target_pairs={{0,16},{8,24},{16,0},{24,8},{1,17},{9,25},{17,1},{25,9},{2,18},{10... | collective-permute-start | bytes 442376 | tf_op jit(solution)/shard_map/ppermute | solution.py:340
  252.8 16.5 %collective-permute-start.53 = (bf16[48,2688]{1,0:T(8,128)(2,1)S(1)}, bf16[48,2688]{1,0:T(8,128)(2,1)S(1)}, u32[]{:S(2)}, u32[]{:S(2)}) collective-permute-start(bf16[48,2688]{1,0:T(8,128)(2,1)S(1)} %stack_columns.1.refs_2_), channel_id=1, source_target_pairs={{0,4},{2,6},{4,0},{6,2},{1,5},{3,7},{5,1},{7,3},{8,12},{10,14},{12... | collective-permute-start | bytes 774152 | tf_op jit(solution)/shard_map/ppermute | solution.py:340
  253.5 15.8 %collective-permute-start.52 = (bf16[48,2688]{1,0:T(8,128)(2,1)S(1)}, bf16[48,2688]{1,0:T(8,128)(2,1)S(1)}, u32[]{:S(2)}, u32[]{:S(2)}) collective-permute-start(bf16[48,2688]{1,0:T(8,128)(2,1)S(1)} %stack_columns.1.refs_2_), channel_id=1, source_target_pairs={{0,2},{2,0},{4,6},{6,4},{1,3},{3,1},{5,7},{7,5},{8,10},{10,8},{12,... | collective-permute-start | bytes 774152 | tf_op jit(solution)/shard_map/ppermute | solution.py:340
  255.0 12.7 %collective-permute-start.56 = (bf16[128,768]{1,0:T(8,128)(2,1)S(1)}, bf16[128,768]{1,0:T(8,128)(2,1)S(1)}, u32[]{:S(2)}, u32[]{:S(2)}) collective-permute-start(bf16[128,768]{1,0:T(8,128)(2,1)S(1)} %get-tuple-element.450), channel_id=1, source_target_pairs={{0,6},{2,4},{4,2},{6,0},{1,7},{3,5},{5,3},{7,1},{8,14},{10,12},{12... | collective-permute-start | bytes 589832 | tf_op jit(solution)/shard_map/ppermute | solution.py:340
  256.4 12.4 %collective-permute-start.55 = (bf16[128,768]{1,0:T(8,128)(2,1)S(1)}, bf16[128,768]{1,0:T(8,128)(2,1)S(1)}, u32[]{:S(2)}, u32[]{:S(2)}) collective-permute-start(bf16[128,768]{1,0:T(8,128)(2,1)S(1)} %get-tuple-element.451), channel_id=1, source_target_pairs={{0,4},{2,6},{4,0},{6,2},{1,5},{3,7},{5,1},{7,3},{8,12},{10,14},{12... | collective-permute-start | bytes 589832 | tf_op jit(solution)/shard_map/ppermute | solution.py:340
  257.1 12.2 %collective-permute-start.54 = (bf16[128,768]{1,0:T(8,128)(2,1)S(1)}, bf16[128,768]{1,0:T(8,128)(2,1)S(1)}, u32[]{:S(2)}, u32[]{:S(2)}) collective-permute-start(bf16[128,768]{1,0:T(8,128)(2,1)S(1)} %get-tuple-element.452), channel_id=1, source_target_pairs={{0,2},{2,0},{4,6},{6,4},{1,3},{3,1},{5,7},{7,5},{8,10},{10,8},{12,... | collective-permute-start | bytes 589832 | tf_op jit(solution)/shard_map/ppermute | solution.py:340
  269.4 12.4 %collective-permute-start.62 = (bf16[4,128,768]{2,1,0:T(8,128)(2,1)S(1)}, bf16[4,128,768]{2,1,0:T(8,128)(2,1)S(1)}, u32[]{:S(2)}, u32[]{:S(2)}) collective-permute-start(bf16[4,128,768]{2,1,0:T(8,128)(2,1)S(1)} %bitcast.54), channel_id=1, source_target_pairs={{0,1},{1,0},{2,3},{3,2},{4,5},{5,4},{6,7},{7,6},{8,9},{9,8},{10,11... | collective-permute-start | bytes 2359304 | tf_op jit(solution)/shard_map/ppermute | solution.py:340
  269.6 24.5 %collective-permute-start.58 = (bf16[192,1536]{1,0:T(8,128)(2,1)S(1)}, bf16[192,1536]{1,0:T(8,128)(2,1)}, u32[]{:S(2)}, u32[]{:S(2)}) collective-permute-start(bf16[192,1536]{1,0:T(8,128)(2,1)S(1)} %add_convert_fusion.1), channel_id=1, source_target_pairs={{0,4},{2,6},{4,0},{6,2},{1,5},{3,7},{5,1},{7,3},{8,12},{10,14},{12... | collective-permute-start | bytes 1769480 | tf_op jit(solution)/shard_map/ppermute | solution.py:340
  274.6 14.4 %collective-permute-start.59 = (bf16[192,384]{1,0:T(8,128)(2,1)S(1)}, bf16[192,384]{1,0:T(8,128)(2,1)}, u32[]{:S(2)}, u32[]{:S(2)}) collective-permute-start(bf16[192,384]{1,0:T(8,128)(2,1)S(1)} %add_convert_fusion.3), channel_id=1, source_target_pairs={{0,4},{2,6},{4,0},{6,2},{1,5},{3,7},{5,1},{7,3},{8,12},{10,14},{12... | collective-permute-start | bytes 442376 | tf_op jit(solution)/shard_map/ppermute | solution.py:340
  276.1 17.9 %collective-permute-start.57 = (bf16[48,2688]{1,0:T(8,128)(2,1)S(1)}, bf16[48,2688]{1,0:T(8,128)(2,1)S(1)}, u32[]{:S(2)}, u32[]{:S(2)}) collective-permute-start(bf16[48,2688]{1,0:T(8,128)(2,1)S(1)} %collective-permute-done.52.refs_3_), channel_id=1, source_target_pairs={{0,4},{2,6},{4,0},{6,2},{1,5},{3,7},{5,1},{7,3},{8,12},{10,14},{12... | collective-permute-start | bytes 774152 | tf_op jit(solution)/shard_map/ppermute | solution.py:340
  (41 other events, 281.1 us)

commit v4 on v3

--- a/solution.py
+++ b/solution.py
@@ -278,21 +278,12 @@
     slope_ref[...] = (below + pre * bell).astype(slope_ref.dtype)
 
 
-def down_kernel(places, left_ref, own_ref, part_ref, *refs):
+def down_kernel(places, left_ref, own_ref, *refs):
     part_refs, (out_ref, full_ref) = refs[:-2], refs[-2:]
-    count = len(part_refs) // 2
-    cut = part_refs[0].shape[1]
 
     @pl.when(pl.program_id(0) == 0)
     def _():
-        for index in range(2):
-            span = slice(index * cut, (index + 1) * cut)
-            fill_rows(
-                places,
-                own_ref.at[:, span],
-                [part_ref.at[:, span]] + list(part_refs[index * count : (index + 1) * count]),
-                full_ref.at[:, span],
-            )
+        fill_rows(places, own_ref, part_refs, full_ref)
 
     out_ref[...] = rows_by_rows(left_ref[...], full_ref[...]).astype(out_ref.dtype)
 
@@ -755,57 +746,37 @@
 
 
 def place_kernel(places, ratio_ref, *refs, kinds):
-    part_refs, (first_ref, second_ref) = refs[:-2], refs[-2:]
-    rows = part_refs[0].shape[0]
-    width = first_ref.shape[1]
-    pairs = width // (kinds * LANES)
+    part_refs, out_ref = refs[:-1], refs[-1]
+    rows, columns = part_refs[0].shape
+    pairs = columns // (kinds * LANES)
     ratio = ratio_ref[0]
     for s in range(len(part_refs)):
         start = lax.bitwise_xor(places[0], jnp.int32(s)) * rows
         start = pl.multiple_of(start, rows)
-        second_ref[pl.ds(start, rows), :] = part_refs[s][:, width:].astype(jnp.float32) * ratio
         for kind in range(kinds):
             for pair in range(pairs):
                 source = (pair * kinds + kind) * LANES
                 target = (kind * pairs + pair) * LANES
-                out = part_refs[s][:, source : source + LANES].astype(jnp.float32) * ratio
-                first_ref[pl.ds(start, rows), target : target + LANES] = out
-
-
-def place_rows(places, parts, ratio, width, kinds):
+                out_ref[pl.ds(start, rows), target : target + LANES] = (
+                    part_refs[s][:, source : source + LANES].astype(jnp.float32) * ratio
+                )
+
+
+def place_rows(places, parts, ratio, kinds=1):
     rows, columns = parts[0].shape
-    whole = lambda shape: pl.BlockSpec(shape, lambda step, places: (0, 0))
-    shapes = [(rows * len(parts), width), (rows * len(parts), columns - width)]
+    block = pl.BlockSpec((rows, columns), lambda step, places: (0, 0))
     return pl.pallas_call(
         lambda *refs: place_kernel(*refs, kinds=kinds),
         grid_spec=pltpu.PrefetchScalarGridSpec(
             num_scalar_prefetch=1,
             grid=(1,),
-            in_specs=[pl.BlockSpec(memory_space=pltpu.SMEM)]
-            + [whole(item.shape) for item in parts],
-            out_specs=[whole(shape) for shape in shapes],
+            in_specs=[pl.BlockSpec(memory_space=pltpu.SMEM)] + [block] * len(parts),
+            out_specs=pl.BlockSpec((rows * len(parts), columns), lambda step, places: (0, 0)),
         ),
-        out_shape=[jax.ShapeDtypeStruct(shape, jnp.float32) for shape in shapes],
+        out_shape=jax.ShapeDtypeStruct((rows * len(parts), columns), jnp.float32),
         name="place_rows",
-        compiler_params=pltpu.CompilerParams(vmem_limit_bytes=10 << 20),
+        compiler_params=pltpu.CompilerParams(vmem_limit_bytes=6 << 20),
     )(places, ratio.reshape(1), *parts)
-
-
-def columns_kernel(first_ref, second_ref, out_ref):
-    width = first_ref.shape[1]
-    out_ref[:, :width] = first_ref[...]
-    out_ref[:, width:] = second_ref[...]
-
-
-def stack_columns(first, second):
-    return pl.pallas_call(
-        columns_kernel,
-        out_shape=jax.ShapeDtypeStruct(
-            (first.shape[0], first.shape[1] + second.shape[1]), first.dtype
-        ),
-        name="stack_columns",
-        compiler_params=pltpu.CompilerParams(vmem_limit_bytes=4 << 20),
-    )(first, second)
 
 
 def whole_local(
@@ -862,19 +833,15 @@
         full_bias,
     )
     weight_part = stack_rows(weight_rows + [count_rows])
-    weight_parts = [weight_part, swap(weight_part, "ctx", 1), swap(weight_part, "ctx", 2)]
-    up_rows = [swap(up_own, "fsdp", 1), swap(up_own, "fsdp", 2)]
-    weight_parts, up_rows = together(weight_parts, up_rows)
-    weight_parts = weight_parts + [swap(weight_parts[1], "ctx", 2)]
-    up_rows = up_rows + [swap(up_rows[0], "fsdp", 2)]
-    down_rows = [swap(down_own, "fsdp", 1), swap(down_own, "fsdp", 2)]
+    weight_parts = [weight_part] + swap_all(weight_part, "ctx")
+    up_rows = relay_all(up_own, "fsdp")
     flat_in = join_halves(hidden_half).reshape(row_count, model_width)
-    weight_parts, flat_in, up_rows, down_rows = together(
-        weight_parts, flat_in, up_rows, down_rows
+    weight_parts, flat_in, up_rows, down_own = together(
+        weight_parts, flat_in, up_rows, down_own
     )
     up_part = stack_rows(up_rows)
     up_parts = [up_part] + swap_all(up_part, "ctx")
-    down_rows = down_rows + [swap(down_rows[0], "fsdp", 2)]
+    down_rows = relay_all(down_own, "fsdp")
     counts = sum(wide(item[-16, :LANES]) for item in weight_parts)
     valid_count = lax.dynamic_index_in_dim(counts, place, 0, keepdims=False).astype(jnp.int32)
     facts = jnp.stack([valid_count, core, place])
@@ -894,8 +861,7 @@
     attended, log_total = attend(facts, projected, block_len)
     attended, up_parts, down_rows = together(attended, up_parts, down_rows)
     down_part = stack_rows(down_rows)
-    cut = hidden_width // 2
-    down_parts = [down_part] + swap_all(down_part[:, :cut], "ctx")
+    down_parts = [down_part] + swap_all(down_part, "ctx")
     branch = rows_times(attended, full_out, block_len, True)
     normal1, scale1, normed1_low = by_rows(
         first_norm_kernel,
@@ -908,8 +874,6 @@
             struct((row_count, model_width), jnp.bfloat16),
         ],
     )
-    normed1_low, down_parts = together(normed1_low, down_parts)
-    down_others = swap_all(down_parts[0][:, cut:], "ctx")
     active, slope, full_up = gathered_layer(
         up_kernel,
         "up",
@@ -922,7 +886,7 @@
         [hidden_width, hidden_width],
         fsdp_count,
     )
-    active, down_parts, down_others = together(active, down_parts, down_others)
+    active, down_parts = together(active, down_parts)
     teacher_half = stack_rows(
         [teacher_own[0]] + swap_each(teacher_own, "ctx")
     ).reshape(ctx_count, block_len // 2, model_width)
@@ -934,7 +898,7 @@
         active,
         [],
         down_weight,
-        down_parts[:1] + down_parts[1:] + down_others,
+        down_parts,
         [model_width],
         fsdp_count,
     )
@@ -991,82 +955,85 @@
     out_kept, out_sent, grad_attended = together(out_kept, out_sent, grad_attended)
     out_brought = swap(out_sent, "fsdp", 1)
     grad_qkv, stats_qkv = attend_back(facts, projected, grad_attended, log_total, block_len)
-    grad_qkv, up_brought, down_brought, out_brought = together(
-        grad_qkv, up_brought, down_brought, out_brought
-    )
+    grad_qkv, down_brought, out_brought = together(grad_qkv, down_brought, out_brought)
     last_pieces = weight_grad(places, [(flat_in, grad_qkv)])
     down_kept, down_sent = sum_and_cut([down_kept, down_brought])
     out_kept, out_sent = sum_and_cut([out_kept, out_brought])
-    last_pieces, grad_qkv, up_brought, down_sent, out_sent, layer_pieces, stats_qkv = together(
-        last_pieces, grad_qkv, up_brought, down_sent, out_sent, layer_pieces, stats_qkv
+    last_pieces, grad_qkv, down_sent, out_sent, layer_pieces, stats_qkv = together(
+        last_pieces, grad_qkv, down_sent, out_sent, layer_pieces, stats_qkv
     )
     last_brought = swap_each(last_pieces, "ctx")
     down_brought = swap(down_sent, "fsdp", 2)
-    out_brought = swap(out_sent, "fsdp", 2)
     mine, other = input_back(facts, grad_qkv, full_qkv_out, block_len)
     up_kept, up_sent = sum_and_cut([up_pieces[0]] + up_brought)
     local_count = jnp.broadcast_to(jnp.sum(local_counts), (1, LANES))
     small = pack(stats2, stats1, stats_up, stats_qkv, local_count)
-    last_brought, mine, other, down_brought, out_brought, up_sent, small, layer_pieces = together(
-        last_brought, mine, other, down_brought, out_brought, up_sent, small, layer_pieces
+    last_brought, mine, other, up_sent, out_sent, small, layer_pieces = together(
+        last_brought, mine, other, up_sent, out_sent, small, layer_pieces
     )
     last_kept, last_sent = sum_and_cut([last_pieces[0]] + last_brought)
-    last_sent, other, down_brought, out_brought, up_sent, small, layer_pieces = together(
-        last_sent, other, down_brought, out_brought, up_sent, small, layer_pieces
+    last_sent, other, down_brought, up_sent, out_sent, small, layer_pieces = together(
+        last_sent, other, down_brought, up_sent, out_sent, small, layer_pieces
     )
     last_brought = swap(last_sent, "fsdp", 1)
-    up_brought = swap(up_sent, "fsdp", 1)
     other = swap(other, "tp", 1)
     owned_down = low(wide(down_kept) + wide(down_brought))
     down_other = swap(owned_down, "ctx", 1)
-    layer_stack = stack_rows(layer_pieces).reshape(layer_half.shape)
-    layer_out = join_halves(layer_stack, place=place)
-    last_brought, up_brought, other, small, layer_out, out_brought = together(
-        last_brought, up_brought, other, small, layer_out, out_brought
+    last_brought, other, up_sent, out_sent, small, layer_pieces = together(
+        last_brought, other, up_sent, out_sent, small, layer_pieces
     )
     last_kept, last_sent = sum_and_cut([last_kept, last_brought])
-    last_sent, up_brought, other, small, out_brought = together(
-        last_sent, up_brought, other, small, out_brought
+    half = low(grad_half + (wide(mine) + wide(other)))
+    last_sent, half, up_sent, out_sent, small, layer_pieces = together(
+        last_sent, half, up_sent, out_sent, small, layer_pieces
     )
     last_brought = swap(last_sent, "fsdp", 2)
-    up_kept, up_sent = sum_and_cut([up_kept, up_brought])
-    up_brought = swap(up_sent, "fsdp", 2)
-    owned_out = low(wide(out_kept) + wide(out_brought))
-    out_other = swap(owned_out, "ctx", 1)
-    half = low(grad_half + (wide(mine) + wide(other)))
-    small = sum_over(small, "ctx")
-    last_brought, up_brought, half, down_other, out_other, small = together(
-        last_brought, up_brought, half, down_other, out_other, small
-    )
-    part = low(wide(last_kept) + wide(last_brought))
-    up_part = low(wide(up_kept) + wide(up_brought))
-    shared = stack_columns(part, up_part)
-    shared, half, down_other, out_other, small = together(
-        shared, half, down_other, out_other, small
-    )
-    shared = [shared, swap(shared, "ctx", 1), swap(shared, "ctx", 2)]
+    up_brought = swap(up_sent, "fsdp", 1)
     half_pieces = [half[s] for s in range(ctx_count)]
     half_brought = swap_each(half_pieces, "ctx")
-    shared, half_brought, down_other, out_other, small = together(
-        shared, half_brought, down_other, out_other, small
-    )
+    layer_stack = stack_rows(layer_pieces).reshape(layer_half.shape)
+    last_brought, up_brought, down_other, out_sent, small, layer_stack = together(
+        last_brought, up_brought, down_other, out_sent, small, layer_stack
+    )
+    part = low(wide(last_kept) + wide(last_brought))
+    up_kept, up_sent = sum_and_cut([up_kept, up_brought])
+    owned_down = low(wide(owned_down) + wide(down_other))
+    part, up_sent, owned_down, out_sent, small, layer_stack = together(
+        part, up_sent, owned_down, out_sent, small, layer_stack
+    )
+    shared = [part, swap(part, "ctx", 1), swap(part, "ctx", 2)]
+    up_brought = swap(up_sent, "fsdp", 2)
+    out_brought = swap(out_sent, "fsdp", 2)
+    down_other = swap(owned_down, "ctx", 2)
+    layer_out = join_halves(layer_stack, place=place)
+    shared, up_brought, half_brought, out_brought, small, layer_out = together(
+        shared, up_brought, half_brought, out_brought, small, layer_out
+    )
+    up_part = low(wide(up_kept) + wide(up_brought))
+    owned_out = low(wide(out_kept) + wide(out_brought))
+    up_part, owned_out, shared, small = together(up_part, owned_out, shared, small)
     shared = shared + [swap(shared[1], "ctx", 2)]
-    owned_down = low(wide(owned_down) + wide(down_other))
+    up_shared = [up_part, swap(up_part, "ctx", 1), swap(up_part, "ctx", 2)]
+    out_other = swap(owned_out, "ctx", 1)
+    input_half = stack_rows(half_pieces[:1] + half_brought).reshape(half.shape)
+    small = sum_over(small, "ctx")
+    up_shared, input_half, out_other, small = together(up_shared, input_half, out_other, small)
+    up_shared = up_shared + [swap(up_shared[1], "ctx", 2)]
     owned_out = low(wide(owned_out) + wide(out_other))
-    down_other, out_other = swap(owned_down, "ctx", 2), swap(owned_out, "ctx", 2)
+    out_other = swap(owned_out, "ctx", 2)
     small = sum_over(small, "fsdp")
-    input_half = stack_rows(half_pieces[:1] + half_brought).reshape(half.shape)
     at = 7 + -(-hidden_width // model_width)
     counted = small[at + -(-3 * inner_width // model_width), 0]
     ratio = float(row_count * ctx_count * fsdp_count) / counted
     loss = jnp.sum(small[3]) / (counted * model_width)
     scaled = small * ratio
     input_grad = join_halves(input_half, ratio, jnp.float32, place)
-    shared, down_other, out_other, input_grad, scaled = together(
-        shared, down_other, out_other, input_grad, scaled
-    )
-    owned_qkv, owned_up = place_rows(places, shared, ratio, 3 * inner_width, 3)
+    owned_qkv = place_rows(places, shared, ratio, 3)
+    owned_qkv, up_shared, down_other, out_other, input_grad, scaled = together(
+        owned_qkv, up_shared, down_other, out_other, input_grad, scaled
+    )
     owned_qkv = owned_qkv.reshape(qkv_weight.shape)
+    owned_up = place_rows(places, up_shared, ratio)
     owned_down = (wide(owned_down) + wide(down_other)) * ratio
     owned_out = (wide(owned_out) + wide(out_other)) * ratio
     grad_up_bias = scaled[7:at].reshape(-1)[:hidden_width]

time: 304 us -> 300 us (0.987)
  waiting for transfers between devices: 112 us -> 107 us
  Pallas kernels: 91 us -> 86.7 us
  local copies, waits for them, and re-layouts: 16.1 us -> 20.4 us
    ppermute x63, waiting for transfers between devices: 111 us -> 105 us  [swap(): return lax.ppermute(values, axis, pairs)]
    unnamed x51 -> x63, local copies, waits for them, and re-layouts: 4.69 us -> 8.63 us
  transfers between devices with their start and end apart: 64 -> 64, of which waited for: 29 -> 30; matrix products, arithmetic and copies ran while one was open for 3% -> 3% of each run, Pallas kernels for 24% -> 25%
where the time goes in v4:
time: 300 us; the launch traced here: 299 us
  waiting for transfers between devices  107 us (36%)
  Pallas kernels  86.7 us (29%)
  starting transfers between devices  71.2 us (24%)
  local copies, waits for them, and re-layouts  20.4 us (7%)
  other arithmetic  9.12 us (3%)
  between operations  4.61 us (2%)
    ppermute x63, waiting for transfers between devices, swap(): return lax.ppermute(values, axis, pairs)  105 us
    ppermute x63, starting transfers between devices, swap(): return lax.ppermute(values, axis, pairs)  67.2 us
    pallas_call x1, Pallas kernels, attend_back(): pl.pallas_call(lambda *refs: attend_back_kernel(*refs, block=block), grid...  15.5 us
    pallas_call x4, Pallas kernels, weight_grad(): pl.pallas_call(lambda *refs: weight_grad_kernel(*refs, chunks=chunks, fsd...  13.9 us
    pallas_call x3, Pallas kernels, gathered_layer(): pl.pallas_call(kernel, grid_spec=pltpu.PrefetchScalarGridSpec(num_scalar_...  13 us
    pallas_call x1, Pallas kernels, attend(): pl.pallas_call(lambda *refs: attend_kernel(*refs, block=block), grid_spec...  10.8 us
    pallas_call x3, Pallas kernels, by_rows(): pl.pallas_call(kernel, grid_spec=pltpu.PrefetchScalarGridSpec(num_scalar_...  10.1 us
    unnamed x63, local copies, waits for them, and re-layouts  8.63 us
  transfers between devices with their start and end apart: 64, of which 30 were waited for; matrix products, arithmetic and copies ran while one was open for 3% of the time, Pallas kernels for 25%

profile of v4, /device:TPU:0, one launch (start us, length us, event | category | flops | bytes accessed | tf_op | source)
XLA Modules:
  0.0 299.1 jit_solution(8119916898446774872)
XLA Ops:
  4.3 5.0 %collective-permute-start.2 = (bf16[48,1536]{1,0:T(8,128)(2,1)S(1)}, bf16[48,1536]{1,0:T(8,128)(2,1)S(1)}, u32[]{:S(2)}, u32[]{:S(2)}) collective-permute-start(bf16[48,1536]{1,0:T(8,128)(2,1)S(1)} %constant_dynamic-slice_fusion.3), channel_id=1, source_target_pairs={{0,24},{8,16},{16,8},{24,0},{1,25},{9,17},{17,9},{25,1},{2,26},{10... | collective-permute-start | bytes 442376 | tf_op jit(solution)/shard_map/ppermute | solution.py:331
  9.9 3.9 %all-to-all-start = ((bf16[4,128,768]{2,1,0:T(8,128)(2,1)}), bf16[4,128,768]{2,1,0:T(8,128)(2,1)S(1)}, u32[]{:S(2)}, u32[]{:S(2)}) async-start(bf16[4,128,768]{2,1,0:T(8,128)(2,1)} %constant_dynamic-slice_fusion.4), calls=%async_computation | async-start | bytes 1572864 | tf_op jit(solution)/shard_map/all_to_all | solution.py:382
  16.4 2.2 dynamic-slice_bitcast_fusion
  18.7 3.2 %collective-permute-done.1.refs_1_ = bf16[48,1536]{1,0:T(8,128)(2,1)S(1)} collective-permute-done((bf16[48,1536]{1,0:T(8,128)(2,1)S(1)}, bf16[48,1536]{1,0:T(8,128)(2,1)S(1)}, u32[]{:S(2)}, u32[]{:S(2)}) %collective-permute-start.1) | collective-permute-done | bytes 147488 | tf_op jit(solution)/shard_map/ppermute | solution.py:331
  21.9 2.1 all-to-all-done.own_ref
  29.0 4.2 %collective-permute-done.7.refs_0_ = bf16[48,1536]{1,0:T(8,128)(2,1)S(1)} collective-permute-done((bf16[48,1536]{1,0:T(8,128)(2,1)}, bf16[48,1536]{1,0:T(8,128)(2,1)S(1)}, u32[]{:S(2)}, u32[]{:S(2)}) %collective-permute-start.7) | collective-permute-done | bytes 147488 | tf_op jit(solution)/shard_map/ppermute | solution.py:331
  33.2 2.4 collective-permute-start.8
  37.1 9.1 %collective-permute-done.8.refs_1_ = bf16[48,1536]{1,0:T(8,128)(2,1)S(1)} collective-permute-done((bf16[48,1536]{1,0:T(8,128)(2,1)}, bf16[48,1536]{1,0:T(8,128)(2,1)S(1)}, u32[]{:S(2)}, u32[]{:S(2)}) %collective-permute-start.8) | collective-permute-done | bytes 147488 | tf_op jit(solution)/shard_map/ppermute | solution.py:331
  57.9 2.8 collective-permute-start.14
  64.7 3.5 %project.1 = (bf16[1024,1152]{1,0:T(8,128)(2,1)S(1)}, bf16[768,1536]{1,0:T(8,128)(2,1)S(1)}) custom-call(s32[2]{0:T(128)S(1)} %pad_add_fusion.places.refs_0_, bf16[1024,768]{1,0:T(8,128)(2,1)S(1)} %bitcast.51, f32[1,1152]{1,0:T(1,128)S(1)} %reshape_reshape.3.bias_ref, bf16[192,1536]{1,0:T(8,128)(2,1)S(1)} %constant_dynamic-update-slice_fusion.own_ref, ...), custom_call_target="tpu_custom_call" | custom-call | tf_op jit(solution)/shard_map/project/pallas_call | solution.py:296
  69.6 10.8 %attend.1 = (bf16[1024,384]{1,0:T(8,128)(2,1)S(1)}, f32[3,2,1024]{2,1,0:T(2,128)S(1)}) custom-call(s32[3]{0:T(128)S(1)} %pad_add_fusion.2.refs_0_.facts, bf16[1024,1152]{1,0:T(8,128)(2,1)S(1)} %get-tuple-element.225.refs_1_.refs_2_.refs_3_, bf16[1024,1152]{1,0:T(8,128)(2,1)S(1)} %get-tuple-element.225.refs_1_.refs_2_.refs_3_, ...), custom_call_target="tpu_custom_call" | custom-call | tf_op jit(solution)/shard_map/attend/pallas_call | solution.py:174
  87.5 5.6 %up.1 = (bf16[1024,1536]{1,0:T(8,128)(2,1)S(1)}, bf16[1024,1536]{1,0:T(8,128)(2,1)S(1)}, bf16[768,1536]{1,0:T(8,128)(2,1)S(1)}) custom-call(s32[2]{0:T(128)S(1)} %pad_add_fusion.places.refs_0_, bf16[1024,768]{1,0:T(8,128)(2,1)S(1)} %get-tuple-element.234.left_ref.refs_1_, f32[1,1536]{1,0:T(1,128)S(1)} %reshape.115.bias_ref, bf16[192,1536]{1,0:T(8,128)(2,1)S(1)} %copy-done.2, ...), custom_call_target="tpu_custom_call" | custom-call | tf_op jit(solution)/shard_map/up/pallas_call | solution.py:296
  93.1 3.1 %collective-permute-done.19.refs_3_ = bf16[144,1536]{1,0:T(8,128)(2,1)S(1)} collective-permute-done((bf16[144,1536]{1,0:T(8,128)(2,1)S(1)}, bf16[144,1536]{1,0:T(8,128)(2,1)S(1)}, u32[]{:S(2)}, u32[]{:S(2)}) %collective-permute-start.19) | collective-permute-done | bytes 442400 | tf_op jit(solution)/shard_map/ppermute | solution.py:331
  96.2 9.0 %collective-permute-done.18.refs_2_ = bf16[144,1536]{1,0:T(8,128)(2,1)S(1)} collective-permute-done((bf16[144,1536]{1,0:T(8,128)(2,1)S(1)}, bf16[144,1536]{1,0:T(8,128)(2,1)S(1)}, u32[]{:S(2)}, u32[]{:S(2)}) %collective-permute-start.18) | collective-permute-done | bytes 442400 | tf_op jit(solution)/shard_map/ppermute | solution.py:331
  105.3 4.0 %down.1 = (bf16[1024,768]{1,0:T(8,128)(2,1)S(1)}, bf16[768,1536]{1,0:T(8,128)(2,1)S(1)}) custom-call(s32[2]{0:T(128)S(1)} %pad_add_fusion.places.refs_0_, bf16[1024,1536]{1,0:T(8,128)(2,1)S(1)} %get-tuple-element.243.left_ref.refs_2_, bf16[192,1536]{1,0:T(8,128)(2,1)S(1)} %copy-done.3, bf16[144,1536]{1,0:T(8,128)(2,1)S(1)} %stack_rows.8.refs_0_, ...), custom_call_target="tpu_custom_call" | custom-call | tf_op jit(solution)/shard_map/down/pallas_call | solution.py:296
  112.9 4.2 %collective-permute-done.21.refs_1_ = bf16[128,768]{1,0:T(8,128)(2,1)S(1)} collective-permute-done((bf16[128,768]{1,0:T(8,128)(2,1)S(1)}, bf16[128,768]{1,0:T(8,128)(2,1)S(1)}, u32[]{:S(2)}, u32[]{:S(2)}) %collective-permute-start.21) | collective-permute-done | bytes 196640 | tf_op jit(solution)/shard_map/ppermute | solution.py:331
  117.2 4.9 %collective-permute-done.22.refs_2_ = bf16[128,768]{1,0:T(8,128)(2,1)S(1)} collective-permute-done((bf16[128,768]{1,0:T(8,128)(2,1)S(1)}, bf16[128,768]{1,0:T(8,128)(2,1)S(1)}, u32[]{:S(2)}, u32[]{:S(2)}) %collective-permute-start.22) | collective-permute-done | bytes 196640 | tf_op jit(solution)/shard_map/ppermute | solution.py:331
  122.2 2.2 collective-permute-done.24.other_teacher_ref
  124.4 5.0 %second_norm.1 = (bf16[4,128,768]{2,1,0:T(8,128)(2,1)S(1)}, f32[1024,768]{1,0:T(8,128)S(1)}, bf16[1024,768]{1,0:T(8,128)(2,1)S(1)}, f32[8,768]{1,0:T(8,128)S(1)}) custom-call(s32[3]{0:T(128)S(1)} %pad_add_fusion.2.refs_0_.facts, f32[1024,768]{1,0:T(8,128)S(1)} %get-tuple-element.233.normal_ref, f32[1,768]{1,0:T(1,128)S(1)} %reshape.113.gain_ref.gain1_ref, ...), custom_call_target="tpu_custom_call" | custom-call | tf_op jit(solution)/shard_map/second_norm/pallas_call | solution.py:497
  133.1 4.0 %weight_grad.4 = (bf16[384,1536]{1,0:T(8,128)(2,1)S(1)}, bf16[384,1536]{1,0:T(8,128)(2,1)S(1)}) custom-call(s32[2]{0:T(128)S(1)} %pad_add_fusion.places.refs_0_, bf16[1024,768]{1,0:T(8,128)(2,1)S(1)} %get-tuple-element.257.refs_1_.low_ref, bf16[1024,1536]{1,0:T(8,128)(2,1)S(1)} %get-tuple-element.243.left_ref.refs_2_), custom_call_target="tpu_custom_call" | custom-call | tf_op jit(solution)/shard_map/weight_grad/pallas_call | solution.py:701
  137.1 3.8 %grad_pre.1 = (bf16[1024,1536]{1,0:T(8,128)(2,1)S(1)}, f32[8,1536]{1,0:T(8,128)S(1)}) custom-call(bf16[1024,768]{1,0:T(8,128)(2,1)S(1)} %get-tuple-element.257.refs_1_.low_ref, bf16[768,1536]{1,0:T(8,128)(2,1)S(1)} %get-tuple-element.258.weight_ref, bf16[1024,1536]{1,0:T(8,128)(2,1)S(1)} %get-tuple-element.259.slope_ref), custom_call_target="tpu_custom_call" | custom-call | tf_op jit(solution)/shard_map/grad_pre/pallas_call | solution.py:531
  141.0 3.3 %rows_times.4.mine_ref = bf16[1024,768]{1,0:T(8,128)(2,1)S(1)} custom-call(bf16[1024,1536]{1,0:T(8,128)(2,1)S(1)} %get-tuple-element.296.refs_0_.refs_2_, bf16[768,1536]{1,0:T(8,128)(2,1)S(1)} %get-tuple-element.261.refs_1_), custom_call_target="tpu_custom_call" | custom-call | tf_op jit(solution)/shard_map/rows_times/pallas_call | solution.py:551
  145.4 4.0 %weight_grad.7 = (bf16[192,1536]{1,0:T(8,128)(2,1)S(1)}, bf16[192,1536]{1,0:T(8,128)(2,1)S(1)}, bf16[192,1536]{1,0:T(8,128)(2,1)S(1)}, bf16[192,1536]{1,0:T(8,128)(2,1)S(1)}) custom-call(s32[2]{0:T(128)S(1)} %pad_add_fusion.places.refs_0_, bf16[1024,768]{1,0:T(8,128)(2,1)S(1)} %get-tuple-element.234.left_ref.refs_1_, ...), custom_call_target="tpu_custom_call" | custom-call | tf_op jit(solution)/shard_map/weight_grad/pallas_call | solution.py:701
  151.6 3.4 %first_norm_back.1 = (bf16[1024,768]{1,0:T(8,128)(2,1)S(1)}, f32[4,128,768]{2,1,0:T(8,128)S(1)}, f32[8,768]{1,0:T(8,128)S(1)}) custom-call(s32[3]{0:T(128)S(1)} %pad_add_fusion.2.refs_0_.facts, f32[1024,768]{1,0:T(8,128)S(1)} %get-tuple-element.253.grad_ref, bf16[1024,768]{1,0:T(8,128)(2,1)S(1)} %rows_times.4.mine_ref, ...), custom_call_target="tpu_custom_call" | custom-call | tf_op jit(solution)/shard_map/first_norm_back/pallas_call | solution.py:497
  160.6 15.5 %attend_back.1 = (bf16[1024,1152]{1,0:T(8,128)(2,1)S(1)}, f32[8,1152]{1,0:T(8,128)S(1)}) custom-call(s32[3]{0:T(128)S(1)} %pad_add_fusion.2.refs_0_.facts, bf16[1024,1152]{1,0:T(8,128)(2,1)S(1)} %get-tuple-element.225.refs_1_.refs_2_.refs_3_, bf16[1024,1152]{1,0:T(8,128)(2,1)S(1)} %get-tuple-element.225.refs_1_.refs_2_.refs_3_, ...), custom_call_target="tpu_custom_call" | custom-call | tf_op jit(solution)/shard_map/attend_back/pallas_call | solution.py:198
  176.1 2.9 collective-permute-done.30.refs_1_
  179.0 4.3 %weight_grad.6 = (bf16[192,1152]{1,0:T(8,128)(2,1)S(1)}, bf16[192,1152]{1,0:T(8,128)(2,1)S(1)}, bf16[192,1152]{1,0:T(8,128)(2,1)S(1)}, bf16[192,1152]{1,0:T(8,128)(2,1)S(1)}) custom-call(s32[2]{0:T(128)S(1)} %pad_add_fusion.places.refs_0_, bf16[1024,768]{1,0:T(8,128)(2,1)S(1)} %bitcast.53, bf16[1024,1152]{1,0:T(8,128)(2,1)S(1)} %get-tuple-element.293.refs_2_.grad_ref), custom_call_target="tpu_custom_call" | custom-call | tf_op jit(solution)/shard_map/weight_grad/pallas_call | solution.py:701
  183.7 2.9 collective-permute-start.37
  190.3 3.9 %input_back.1 = (bf16[4,128,768]{2,1,0:T(8,128)(2,1)S(1)}, bf16[4,128,768]{2,1,0:T(8,128)(2,1)S(1)}) custom-call(s32[3]{0:T(128)S(1)} %pad_add_fusion.2.refs_0_.facts, bf16[1024,1152]{1,0:T(8,128)(2,1)S(1)} %get-tuple-element.293.refs_2_.grad_ref, bf16[768,1536]{1,0:T(8,128)(2,1)S(1)} %get-tuple-element.232.weight_ref), custom_call_target="tpu_custom_call" | custom-call | tf_op jit(solution)/shard_map/input_back/pallas_call | solution.py:576
  194.9 4.8 %collective-permute-done.31.refs_1_ = bf16[192,1152]{1,0:T(8,128)(2,1)S(1)} collective-permute-done((bf16[192,1152]{1,0:T(8,128)(2,1)S(1)}, bf16[192,1152]{1,0:T(8,128)(2,1)S(1)}, u32[]{:S(2)}, u32[]{:S(2)}) %collective-permute-start.31) | collective-permute-done | bytes 442400 | tf_op jit(solution)/shard_map/ppermute | solution.py:331
  199.6 8.2 %collective-permute-done.32.refs_2_ = bf16[192,1152]{1,0:T(8,128)(2,1)S(1)} collective-permute-done((bf16[192,1152]{1,0:T(8,128)(2,1)S(1)}, bf16[192,1152]{1,0:T(8,128)(2,1)S(1)}, u32[]{:S(2)}, u32[]{:S(2)}) %collective-permute-start.32) | collective-permute-done | bytes 442400 | tf_op jit(solution)/shard_map/ppermute | solution.py:331
  208.1 4.3 %collective-permute-done.37 = bf16[192,1536]{1,0:T(8,128)(2,1)S(1)} collective-permute-done((bf16[192,1536]{1,0:T(8,128)(2,1)S(1)}, bf16[192,1536]{1,0:T(8,128)(2,1)S(1)}, u32[]{:S(2)}, u32[]{:S(2)}) %collective-permute-start.37) | collective-permute-done | bytes 589856 | tf_op jit(solution)/shard_map/ppermute | solution.py:331
  213.2 7.0 %collective-permute-done.38.refs_1_ = bf16[96,1152]{1,0:T(8,128)(2,1)S(1)} collective-permute-done((bf16[96,1152]{1,0:T(8,128)(2,1)S(1)}, bf16[96,1152]{1,0:T(8,128)(2,1)S(1)}, u32[]{:S(2)}, u32[]{:S(2)}) %collective-permute-start.38) | collective-permute-done | bytes 221216 | tf_op jit(solution)/shard_map/ppermute | solution.py:331
  220.9 2.8 collective-permute-start.40
  223.7 4.5 %collective-permute-done.42 = bf16[192,1536]{1,0:T(8,128)(2,1)S(1)} collective-permute-done((bf16[192,1536]{1,0:T(8,128)(2,1)S(1)}, bf16[192,1536]{1,0:T(8,128)(2,1)S(1)}, u32[]{:S(2)}, u32[]{:S(2)}) %collective-permute-start.42) | collective-permute-done | bytes 589856 | tf_op jit(solution)/shard_map/ppermute | solution.py:331
  229.6 2.0 collective-permute-done.41.refs_1_
  237.0 3.8 %collective-permute-done.48.refs_3_ = bf16[128,768]{1,0:T(8,128)(2,1)S(1)} collective-permute-done((bf16[128,768]{1,0:T(8,128)(2,1)S(1)}, bf16[128,768]{1,0:T(8,128)(2,1)S(1)}, u32[]{:S(2)}, u32[]{:S(2)}) %collective-permute-start.48) | collective-permute-done | bytes 196640 | tf_op jit(solution)/shard_map/ppermute | solution.py:331
  242.1 2.4 collective-permute-done.47.refs_2_
  246.7 2.3 join_halves.4
  255.6 4.9 %collective-permute-done.54 = f32[16,768]{1,0:T(8,128)S(1)} collective-permute-done((f32[16,768]{1,0:T(8,128)S(1)}, f32[16,768]{1,0:T(8,128)S(1)}, u32[]{:S(2)}, u32[]{:S(2)}) %collective-permute-start.54) | collective-permute-done | bytes 49184 | tf_op jit(solution)/shard_map/ppermute | solution.py:331
  261.2 3.4 %collective-permute-done.55 = f32[16,768]{1,0:T(8,128)S(1)} collective-permute-done((f32[16,768]{1,0:T(8,128)S(1)}, f32[16,768]{1,0:T(8,128)S(1)}, u32[]{:S(2)}, u32[]{:S(2)}) %collective-permute-start.55) | collective-permute-done | bytes 49184 | tf_op jit(solution)/shard_map/ppermute | solution.py:331
  268.9 2.2 collective-permute-start.57
  272.4 2.1 collective-permute-done.57
  278.2 5.6 %collective-permute-done.58.refs_5_ = bf16[48,1152]{1,0:T(8,128)(2,1)S(1)} collective-permute-done((bf16[48,1152]{1,0:T(8,128)(2,1)S(1)}, bf16[48,1152]{1,0:T(8,128)(2,1)S(1)}, u32[]{:S(2)}, u32[]{:S(2)}) %collective-permute-start.58) | collective-permute-done | bytes 110624 | tf_op jit(solution)/shard_map/ppermute | solution.py:331
  284.5 2.7 join_halves.5
  287.2 2.2 collective-permute-done.59.refs_5_
  292.3 1.9 add_multiply_fusion.1
  294.1 2.2 add_multiply_fusion
  (233 shorter events, 90.3 us)
Async XLA Ops:
  4.3 14.3 %collective-permute-start.2 = (bf16[48,1536]{1,0:T(8,128)(2,1)S(1)}, bf16[48,1536]{1,0:T(8,128)(2,1)S(1)}, u32[]{:S(2)}, u32[]{:S(2)}) collective-permute-start(bf16[48,1536]{1,0:T(8,128)(2,1)S(1)} %constant_dynamic-slice_fusion.3), channel_id=1, source_target_pairs={{0,24},{8,16},{16,8},{24,0},{1,25},{9,17},{17,9},{25,1},{2,26},{10... | collective-permute-start | bytes 442376 | tf_op jit(solution)/shard_map/ppermute | solution.py:331
  9.4 12.5 %collective-permute-start.1 = (bf16[48,1536]{1,0:T(8,128)(2,1)S(1)}, bf16[48,1536]{1,0:T(8,128)(2,1)S(1)}, u32[]{:S(2)}, u32[]{:S(2)}) collective-permute-start(bf16[48,1536]{1,0:T(8,128)(2,1)S(1)} %constant_dynamic-slice_fusion.3), channel_id=1, source_target_pairs={{0,16},{8,24},{16,0},{24,8},{1,17},{9,25},{17,1},{25,9},{2,18},{10... | collective-permute-start | bytes 442376 | tf_op jit(solution)/shard_map/ppermute | solution.py:331
  9.4 12.5 %collective-permute-start = (bf16[48,1536]{1,0:T(8,128)(2,1)S(1)}, bf16[48,1536]{1,0:T(8,128)(2,1)S(1)}, u32[]{:S(2)}, u32[]{:S(2)}) collective-permute-start(bf16[48,1536]{1,0:T(8,128)(2,1)S(1)} %constant_dynamic-slice_fusion.3), channel_id=1, source_target_pairs={{0,8},{8,0},{16,24},{24,16},{1,9},{9,1},{17,25},{25,17},{2,10},{10... | collective-permute-start | bytes 442376 | tf_op jit(solution)/shard_map/ppermute | solution.py:331
  9.9 14.0 %all-to-all-start = ((bf16[4,128,768]{2,1,0:T(8,128)(2,1)}), bf16[4,128,768]{2,1,0:T(8,128)(2,1)S(1)}, u32[]{:S(2)}, u32[]{:S(2)}) async-start(bf16[4,128,768]{2,1,0:T(8,128)(2,1)} %constant_dynamic-slice_fusion.4), calls=%async_computation | async-start | bytes 1572864 | tf_op jit(solution)/shard_map/all_to_all | solution.py:382
  24.0 11.6 %collective-permute-start.6 = (bf16[4,128,768]{2,1,0:T(8,128)(2,1)S(1)}, bf16[4,128,768]{2,1,0:T(8,128)(2,1)S(1)}, u32[]{:S(2)}, u32[]{:S(2)}) collective-permute-start(bf16[4,128,768]{2,1,0:T(8,128)(2,1)S(1)} %all-to-all-done.own_ref), channel_id=1, source_target_pairs={{0,1},{1,0},{2,3},{3,2},{4,5},{5,4},{6,7},{7,6},{8,9},{9,8},{10,11... | collective-permute-start | bytes 2359304 | tf_op jit(solution)/shard_map/ppermute | solution.py:331
  24.0 24.9 %collective-permute-start.5 = (bf16[160,1536]{1,0:T(8,128)(2,1)S(1)}, bf16[160,1536]{1,0:T(8,128)(2,1)S(1)}, u32[]{:S(2)}, u32[]{:S(2)}) collective-permute-start(bf16[160,1536]{1,0:T(8,128)(2,1)S(1)} %stack_rows.6.refs_0_), channel_id=1, source_target_pairs={{0,6},{2,4},{4,2},{6,0},{1,7},{3,5},{5,3},{7,1},{8,14},{10,12},{12... | collective-permute-start | bytes 1474568 | tf_op jit(solution)/shard_map/ppermute | solution.py:331
  25.5 23.6 %collective-permute-start.4 = (bf16[160,1536]{1,0:T(8,128)(2,1)S(1)}, bf16[160,1536]{1,0:T(8,128)(2,1)S(1)}, u32[]{:S(2)}, u32[]{:S(2)}) collective-permute-start(bf16[160,1536]{1,0:T(8,128)(2,1)S(1)} %stack_rows.6.refs_0_), channel_id=1, source_target_pairs={{0,4},{2,6},{4,0},{6,2},{1,5},{3,7},{5,1},{7,3},{8,12},{10,14},{12... | collective-permute-start | bytes 1474568 | tf_op jit(solution)/shard_map/ppermute | solution.py:331
  27.0 22.2 %collective-permute-start.3 = (bf16[160,1536]{1,0:T(8,128)(2,1)S(1)}, bf16[160,1536]{1,0:T(8,128)(2,1)S(1)}, u32[]{:S(2)}, u32[]{:S(2)}) collective-permute-start(bf16[160,1536]{1,0:T(8,128)(2,1)S(1)} %stack_rows.6.refs_0_), channel_id=1, source_target_pairs={{0,2},{2,0},{4,6},{6,4},{1,3},{3,1},{5,7},{7,5},{8,10},{10,8},{12,... | collective-permute-start | bytes 1474568 | tf_op jit(solution)/shard_map/ppermute | solution.py:331
  33.2 13.0 %collective-permute-start.8 = (bf16[48,1536]{1,0:T(8,128)(2,1)}, bf16[48,1536]{1,0:T(8,128)(2,1)S(1)}, u32[]{:S(2)}, u32[]{:S(2)}) collective-permute-start(bf16[48,1536]{1,0:T(8,128)(2,1)} %get-tuple-element.217), channel_id=1, source_target_pairs={{0,16},{8,24},{16,0},{24,8},{1,17},{9,25},{17,1},{25,9},{2,18},{10... | collective-permute-start | bytes 442376 | tf_op jit(solution)/shard_map/ppermute | solution.py:331
  35.6 12.7 %collective-permute-start.9 = (bf16[48,1536]{1,0:T(8,128)(2,1)S(1)}, bf16[48,1536]{1,0:T(8,128)(2,1)S(1)}, u32[]{:S(2)}, u32[]{:S(2)}) collective-permute-start(bf16[48,1536]{1,0:T(8,128)(2,1)S(1)} %collective-permute-done.7.refs_0_), channel_id=1, source_target_pairs={{0,16},{8,24},{16,0},{24,8},{1,17},{9,25},{17,1},{25,9},{2,18},{10... | collective-permute-start | bytes 442376 | tf_op jit(solution)/shard_map/ppermute | solution.py:331
  54.3 26.1 %collective-permute-start.12 = (bf16[144,1536]{1,0:T(8,128)(2,1)S(1)}, bf16[144,1536]{1,0:T(8,128)(2,1)S(1)}, u32[]{:S(2)}, u32[]{:S(2)}) collective-permute-start(bf16[144,1536]{1,0:T(8,128)(2,1)S(1)} %stack_rows.7.refs_0_), channel_id=1, source_target_pairs={{0,6},{2,4},{4,2},{6,0},{1,7},{3,5},{5,3},{7,1},{8,14},{10,12},{12... | collective-permute-start | bytes 1327112 | tf_op jit(solution)/shard_map/ppermute | solution.py:331
  55.8 24.6 %collective-permute-start.11 = (bf16[144,1536]{1,0:T(8,128)(2,1)S(1)}, bf16[144,1536]{1,0:T(8,128)(2,1)S(1)}, u32[]{:S(2)}, u32[]{:S(2)}) collective-permute-start(bf16[144,1536]{1,0:T(8,128)(2,1)S(1)} %stack_rows.7.refs_0_), channel_id=1, source_target_pairs={{0,4},{2,6},{4,0},{6,2},{1,5},{3,7},{5,1},{7,3},{8,12},{10,14},{12... | collective-permute-start | bytes 1327112 | tf_op jit(solution)/shard_map/ppermute | solution.py:331
  57.3 23.1 %collective-permute-start.10 = (bf16[144,1536]{1,0:T(8,128)(2,1)S(1)}, bf16[144,1536]{1,0:T(8,128)(2,1)S(1)}, u32[]{:S(2)}, u32[]{:S(2)}) collective-permute-start(bf16[144,1536]{1,0:T(8,128)(2,1)S(1)} %stack_rows.7.refs_0_), channel_id=1, source_target_pairs={{0,2},{2,0},{4,6},{6,4},{1,3},{3,1},{5,7},{7,5},{8,10},{10,8},{12,... | collective-permute-start | bytes 1327112 | tf_op jit(solution)/shard_map/ppermute | solution.py:331
  57.9 22.4 %collective-permute-start.14 = (bf16[48,1536]{1,0:T(8,128)(2,1)}, bf16[48,1536]{1,0:T(8,128)(2,1)S(1)}, u32[]{:S(2)}, u32[]{:S(2)}) collective-permute-start(bf16[48,1536]{1,0:T(8,128)(2,1)} %get-tuple-element.230), channel_id=1, source_target_pairs={{0,16},{8,24},{16,0},{24,8},{1,17},{9,25},{17,1},{25,9},{2,18},{10... | collective-permute-start | bytes 442376 | tf_op jit(solution)/shard_map/ppermute | solution.py:331
  60.7 19.6 %collective-permute-start.15 = (bf16[48,1536]{1,0:T(8,128)(2,1)S(1)}, bf16[48,1536]{1,0:T(8,128)(2,1)S(1)}, u32[]{:S(2)}, u32[]{:S(2)}) collective-permute-start(bf16[48,1536]{1,0:T(8,128)(2,1)S(1)} %collective-permute-done.13.refs_0_), channel_id=1, source_target_pairs={{0,16},{8,24},{16,0},{24,8},{1,17},{9,25},{17,1},{25,9},{2,18},{10... | collective-permute-start | bytes 442376 | tf_op jit(solution)/shard_map/ppermute | solution.py:331
  82.2 14.0 %collective-permute-start.19 = (bf16[144,1536]{1,0:T(8,128)(2,1)S(1)}, bf16[144,1536]{1,0:T(8,128)(2,1)S(1)}, u32[]{:S(2)}, u32[]{:S(2)}) collective-permute-start(bf16[144,1536]{1,0:T(8,128)(2,1)S(1)} %stack_rows.8.refs_0_), channel_id=1, source_target_pairs={{0,6},{2,4},{4,2},{6,0},{1,7},{3,5},{5,3},{7,1},{8,14},{10,12},{12... | collective-permute-start | bytes 1327112 | tf_op jit(solution)/shard_map/ppermute | solution.py:331
  83.7 21.5 %collective-permute-start.18 = (bf16[144,1536]{1,0:T(8,128)(2,1)S(1)}, bf16[144,1536]{1,0:T(8,128)(2,1)S(1)}, u32[]{:S(2)}, u32[]{:S(2)}) collective-permute-start(bf16[144,1536]{1,0:T(8,128)(2,1)S(1)} %stack_rows.8.refs_0_), channel_id=1, source_target_pairs={{0,4},{2,6},{4,0},{6,2},{1,5},{3,7},{5,1},{7,3},{8,12},{10,14},{12... | collective-permute-start | bytes 1327112 | tf_op jit(solution)/shard_map/ppermute | solution.py:331
  85.1 20.1 %collective-permute-start.17 = (bf16[144,1536]{1,0:T(8,128)(2,1)S(1)}, bf16[144,1536]{1,0:T(8,128)(2,1)S(1)}, u32[]{:S(2)}, u32[]{:S(2)}) collective-permute-start(bf16[144,1536]{1,0:T(8,128)(2,1)S(1)} %stack_rows.8.refs_0_), channel_id=1, source_target_pairs={{0,2},{2,0},{4,6},{6,4},{1,3},{3,1},{5,7},{7,5},{8,10},{10,8},{12,... | collective-permute-start | bytes 1327112 | tf_op jit(solution)/shard_map/ppermute | solution.py:331
  109.3 15.1 %collective-permute-start.20 = (bf16[1024,768]{1,0:T(8,128)(2,1)S(1)}, bf16[1024,768]{1,0:T(8,128)(2,1)S(1)}, u32[]{:S(2)}, u32[]{:S(2)}) collective-permute-start(bf16[1024,768]{1,0:T(8,128)(2,1)S(1)} %get-tuple-element.248.mine_ref), channel_id=1, source_target_pairs={{0,1},{1,0},{2,3},{3,2},{4,5},{5,4},{6,7},{7,6},{8,9},{9,8},{10,11... | collective-permute-start | bytes 4718600 | tf_op jit(solution)/shard_map/ppermute | solution.py:331
  110.8 11.2 %collective-permute-start.22 = (bf16[128,768]{1,0:T(8,128)(2,1)S(1)}, bf16[128,768]{1,0:T(8,128)(2,1)S(1)}, u32[]{:S(2)}, u32[]{:S(2)}) collective-permute-start(bf16[128,768]{1,0:T(8,128)(2,1)S(1)} %copy-done.18), channel_id=1, source_target_pairs={{0,4},{2,6},{4,0},{6,2},{1,5},{3,7},{5,1},{7,3},{8,12},{10,14},{12... | collective-permute-start | bytes 589832 | tf_op jit(solution)/shard_map/ppermute | solution.py:331
  111.4 10.6 %collective-permute-start.23 = (bf16[128,768]{1,0:T(8,128)(2,1)S(1)}, bf16[128,768]{1,0:T(8,128)(2,1)S(1)}, u32[]{:S(2)}, u32[]{:S(2)}) collective-permute-start(bf16[128,768]{1,0:T(8,128)(2,1)S(1)} %copy-done.17), channel_id=1, source_target_pairs={{0,6},{2,4},{4,2},{6,0},{1,7},{3,5},{5,3},{7,1},{8,14},{10,12},{12... | collective-permute-start | bytes 589832 | tf_op jit(solution)/shard_map/ppermute | solution.py:331
  129.5 14.7 %collective-permute-start.27 = (bf16[128,768]{1,0:T(8,128)(2,1)S(1)}, bf16[128,768]{1,0:T(8,128)(2,1)S(1)}, u32[]{:S(2)}, u32[]{:S(2)}) collective-permute-start(bf16[128,768]{1,0:T(8,128)(2,1)S(1)} %get-tuple-element.451), channel_id=1, source_target_pairs={{0,6},{2,4},{4,2},{6,0},{1,7},{3,5},{5,3},{7,1},{8,14},{10,12},{12... | collective-permute-start | bytes 589832 | tf_op jit(solution)/shard_map/ppermute | solution.py:331
  131.1 13.1 %collective-permute-start.26 = (bf16[128,768]{1,0:T(8,128)(2,1)S(1)}, bf16[128,768]{1,0:T(8,128)(2,1)S(1)}, u32[]{:S(2)}, u32[]{:S(2)}) collective-permute-start(bf16[128,768]{1,0:T(8,128)(2,1)S(1)} %get-tuple-element.452), channel_id=1, source_target_pairs={{0,4},{2,6},{4,0},{6,2},{1,5},{3,7},{5,1},{7,3},{8,12},{10,14},{12... | collective-permute-start | bytes 589832 | tf_op jit(solution)/shard_map/ppermute | solution.py:331
  131.7 12.5 %collective-permute-start.25 = (bf16[128,768]{1,0:T(8,128)(2,1)S(1)}, bf16[128,768]{1,0:T(8,128)(2,1)S(1)}, u32[]{:S(2)}, u32[]{:S(2)}) collective-permute-start(bf16[128,768]{1,0:T(8,128)(2,1)S(1)} %get-tuple-element.453), channel_id=1, source_target_pairs={{0,2},{2,0},{4,6},{6,4},{1,3},{3,1},{5,7},{7,5},{8,10},{10,8},{12,... | collective-permute-start | bytes 589832 | tf_op jit(solution)/shard_map/ppermute | solution.py:331
  144.3 31.8 %collective-permute-start.29 = (bf16[384,1536]{1,0:T(8,128)(2,1)S(1)}, bf16[384,1536]{1,0:T(8,128)(2,1)S(1)}, u32[]{:S(2)}, u32[]{:S(2)}) collective-permute-start(bf16[384,1536]{1,0:T(8,128)(2,1)S(1)} %get-tuple-element.271), channel_id=1, source_target_pairs={{0,8},{8,0},{16,24},{24,16},{1,9},{9,1},{17,25},{25,17},{2,10},{10... | collective-permute-start | bytes 3538952 | tf_op jit(solution)/shard_map/ppermute | solution.py:331
  149.4 37.7 %collective-permute-start.34 = (bf16[192,1536]{1,0:T(8,128)(2,1)S(1)}, bf16[192,1536]{1,0:T(8,128)(2,1)S(1)}, u32[]{:S(2)}, u32[]{:S(2)}) collective-permute-start(bf16[192,1536]{1,0:T(8,128)(2,1)S(1)} %get-tuple-element.298), channel_id=1, source_target_pairs={{0,2},{2,0},{4,6},{6,4},{1,3},{3,1},{5,7},{7,5},{8,10},{10,8},{12,... | collective-permute-start | bytes 1769480 | tf_op jit(solution)/shard_map/ppermute | solution.py:331
  150.2 38.5 %collective-permute-start.35 = (bf16[192,1536]{1,0:T(8,128)(2,1)S(1)}, bf16[192,1536]{1,0:T(8,128)(2,1)S(1)}, u32[]{:S(2)}, u32[]{:S(2)}) collective-permute-start(bf16[192,1536]{1,0:T(8,128)(2,1)S(1)} %get-tuple-element.299), channel_id=1, source_target_pairs={{0,4},{2,6},{4,0},{6,2},{1,5},{3,7},{5,1},{7,3},{8,12},{10,14},{12... | collective-permute-start | bytes 1769480 | tf_op jit(solution)/shard_map/ppermute | solution.py:331
  158.1 20.9 %collective-permute-start.30 = (bf16[384,384]{1,0:T(8,128)(2,1)S(1)}, bf16[384,384]{1,0:T(8,128)(2,1)S(1)}, u32[]{:S(2)}, u32[]{:S(2)}) collective-permute-start(bf16[384,384]{1,0:T(8,128)(2,1)S(1)} %get-tuple-element.272), channel_id=1, source_target_pairs={{0,8},{8,0},{16,24},{24,16},{1,9},{9,1},{17,25},{25,17},{2,10},{10... | collective-permute-start | bytes 884744 | tf_op jit(solution)/shard_map/ppermute | solution.py:331
  159.2 30.8 %collective-permute-start.36 = (bf16[192,1536]{1,0:T(8,128)(2,1)S(1)}, bf16[192,1536]{1,0:T(8,128)(2,1)S(1)}, u32[]{:S(2)}, u32[]{:S(2)}) collective-permute-start(bf16[192,1536]{1,0:T(8,128)(2,1)S(1)} %get-tuple-element.300), channel_id=1, source_target_pairs={{0,6},{2,4},{4,2},{6,0},{1,7},{3,5},{5,3},{7,1},{8,14},{10,12},{12... | collective-permute-start | bytes 1769480 | tf_op jit(solution)/shard_map/ppermute | solution.py:331
  183.7 28.7 %collective-permute-start.37 = (bf16[192,1536]{1,0:T(8,128)(2,1)S(1)}, bf16[192,1536]{1,0:T(8,128)(2,1)S(1)}, u32[]{:S(2)}, u32[]{:S(2)}) collective-permute-start(bf16[192,1536]{1,0:T(8,128)(2,1)S(1)} %get-tuple-element.317), channel_id=1, source_target_pairs={{0,16},{8,24},{16,0},{24,8},{1,17},{9,25},{17,1},{25,9},{2,18},{10... | collective-permute-start | bytes 1769480 | tf_op jit(solution)/shard_map/ppermute | solution.py:331
  186.5 13.1 %collective-permute-start.31 = (bf16[192,1152]{1,0:T(8,128)(2,1)S(1)}, bf16[192,1152]{1,0:T(8,128)(2,1)S(1)}, u32[]{:S(2)}, u32[]{:S(2)}) collective-permute-start(bf16[192,1152]{1,0:T(8,128)(2,1)S(1)} %get-tuple-element.290), channel_id=1, source_target_pairs={{0,2},{2,0},{4,6},{6,4},{1,3},{3,1},{5,7},{7,5},{8,10},{10,8},{12,... | collective-permute-start | bytes 1327112 | tf_op jit(solution)/shard_map/ppermute | solution.py:331
  187.2 20.7 %collective-permute-start.32 = (bf16[192,1152]{1,0:T(8,128)(2,1)S(1)}, bf16[192,1152]{1,0:T(8,128)(2,1)S(1)}, u32[]{:S(2)}, u32[]{:S(2)}) collective-permute-start(bf16[192,1152]{1,0:T(8,128)(2,1)S(1)} %get-tuple-element.291), channel_id=1, source_target_pairs={{0,4},{2,6},{4,0},{6,2},{1,5},{3,7},{5,1},{7,3},{8,12},{10,14},{12... | collective-permute-start | bytes 1327112 | tf_op jit(solution)/shard_map/ppermute | solution.py:331
  188.6 19.2 %collective-permute-start.33 = (bf16[192,1152]{1,0:T(8,128)(2,1)S(1)}, bf16[192,1152]{1,0:T(8,128)(2,1)S(1)}, u32[]{:S(2)}, u32[]{:S(2)}) collective-permute-start(bf16[192,1152]{1,0:T(8,128)(2,1)S(1)} %get-tuple-element.292), channel_id=1, source_target_pairs={{0,6},{2,4},{4,2},{6,0},{1,7},{3,5},{5,3},{7,1},{8,14},{10,12},{12... | collective-permute-start | bytes 1327112 | tf_op jit(solution)/shard_map/ppermute | solution.py:331
  212.5 15.8 %collective-permute-start.42 = (bf16[192,1536]{1,0:T(8,128)(2,1)S(1)}, bf16[192,1536]{1,0:T(8,128)(2,1)S(1)}, u32[]{:S(2)}, u32[]{:S(2)}) collective-permute-start(bf16[192,1536]{1,0:T(8,128)(2,1)S(1)} %add_convert_fusion.2), channel_id=1, source_target_pairs={{0,2},{2,0},{4,6},{6,4},{1,3},{3,1},{5,7},{7,5},{8,10},{10,8},{12,... | collective-permute-start | bytes 1769480 | tf_op jit(solution)/shard_map/ppermute | solution.py:331
  220.6 11.1 %collective-permute-start.41 = (bf16[96,1536]{1,0:T(8,128)(2,1)S(1)}, bf16[96,1536]{1,0:T(8,128)(2,1)S(1)}, u32[]{:S(2)}, u32[]{:S(2)}) collective-permute-start(bf16[96,1536]{1,0:T(8,128)(2,1)S(1)} %get-tuple-element.348), channel_id=1, source_target_pairs={{0,8},{8,0},{16,24},{24,16},{1,9},{9,1},{17,25},{25,17},{2,10},{10... | collective-permute-start | bytes 884744 | tf_op jit(solution)/shard_map/ppermute | solution.py:331
  231.9 13.2 %collective-permute-start.50 = (bf16[4,128,768]{2,1,0:T(8,128)(2,1)S(1)}, bf16[4,128,768]{2,1,0:T(8,128)(2,1)S(1)}, u32[]{:S(2)}, u32[]{:S(2)}) collective-permute-start(bf16[4,128,768]{2,1,0:T(8,128)(2,1)S(1)} %bitcast.57), channel_id=1, source_target_pairs={{0,1},{1,0},{2,3},{3,2},{4,5},{5,4},{6,7},{7,6},{8,9},{9,8},{10,11... | collective-permute-start | bytes 2359304 | tf_op jit(solution)/shard_map/ppermute | solution.py:331
  233.6 10.9 %collective-permute-start.47 = (bf16[128,768]{1,0:T(8,128)(2,1)S(1)}, bf16[128,768]{1,0:T(8,128)(2,1)S(1)}, u32[]{:S(2)}, u32[]{:S(2)}) collective-permute-start(bf16[128,768]{1,0:T(8,128)(2,1)S(1)} %get-tuple-element.449), channel_id=1, source_target_pairs={{0,4},{2,6},{4,0},{6,2},{1,5},{3,7},{5,1},{7,3},{8,12},{10,14},{12... | collective-permute-start | bytes 589832 | tf_op jit(solution)/shard_map/ppermute | solution.py:331
  234.2 14.8 %collective-permute-start.46 = (bf16[128,768]{1,0:T(8,128)(2,1)S(1)}, bf16[128,768]{1,0:T(8,128)(2,1)S(1)}, u32[]{:S(2)}, u32[]{:S(2)}) collective-permute-start(bf16[128,768]{1,0:T(8,128)(2,1)S(1)} %get-tuple-element.450), channel_id=1, source_target_pairs={{0,2},{2,0},{4,6},{6,4},{1,3},{3,1},{5,7},{7,5},{8,10},{10,8},{12,... | collective-permute-start | bytes 589832 | tf_op jit(solution)/shard_map/ppermute | solution.py:331
  235.6 14.3 %collective-permute-start.45 = (bf16[48,1536]{1,0:T(8,128)(2,1)S(1)}, bf16[48,1536]{1,0:T(8,128)(2,1)S(1)}, u32[]{:S(2)}, u32[]{:S(2)}) collective-permute-start(bf16[48,1536]{1,0:T(8,128)(2,1)S(1)} %get-tuple-element.366), channel_id=1, source_target_pairs={{0,16},{8,24},{16,0},{24,8},{1,17},{9,25},{17,1},{25,9},{2,18},{10... | collective-permute-start | bytes 442376 | tf_op jit(solution)/shard_map/ppermute | solution.py:331
  240.7 10.6 %collective-permute-start.49 = (bf16[192,384]{1,0:T(8,128)(2,1)S(1)}, bf16[192,384]{1,0:T(8,128)(2,1)S(1)}, u32[]{:S(2)}, u32[]{:S(2)}) collective-permute-start(bf16[192,384]{1,0:T(8,128)(2,1)S(1)} %get-tuple-element.368), channel_id=1, source_target_pairs={{0,16},{8,24},{16,0},{24,8},{1,17},{9,25},{17,1},{25,9},{2,18},{10... | collective-permute-start | bytes 442376 | tf_op jit(solution)/shard_map/ppermute | solution.py:331
  251.5 13.2 %collective-permute-start.53 = (bf16[192,384]{1,0:T(8,128)(2,1)S(1)}, bf16[192,384]{1,0:T(8,128)(2,1)S(1)}, u32[]{:S(2)}, u32[]{:S(2)}) collective-permute-start(bf16[192,384]{1,0:T(8,128)(2,1)S(1)} %add_convert_fusion.4), channel_id=1, source_target_pairs={{0,2},{2,0},{4,6},{6,4},{1,3},{3,1},{5,7},{7,5},{8,10},{10,8},{12,... | collective-permute-start | bytes 442376 | tf_op jit(solution)/shard_map/ppermute | solution.py:331
  252.2 12.5 %collective-permute-start.52 = (bf16[48,1536]{1,0:T(8,128)(2,1)S(1)}, bf16[48,1536]{1,0:T(8,128)(2,1)S(1)}, u32[]{:S(2)}, u32[]{:S(2)}) collective-permute-start(bf16[48,1536]{1,0:T(8,128)(2,1)S(1)} %add_convert_fusion.5.refs_2_), channel_id=1, source_target_pairs={{0,4},{2,6},{4,0},{6,2},{1,5},{3,7},{5,1},{7,3},{8,12},{10,14},{12... | collective-permute-start | bytes 442376 | tf_op jit(solution)/shard_map/ppermute | solution.py:331
  253.6 11.1 %collective-permute-start.51 = (bf16[48,1536]{1,0:T(8,128)(2,1)S(1)}, bf16[48,1536]{1,0:T(8,128)(2,1)S(1)}, u32[]{:S(2)}, u32[]{:S(2)}) collective-permute-start(bf16[48,1536]{1,0:T(8,128)(2,1)S(1)} %add_convert_fusion.5.refs_2_), channel_id=1, source_target_pairs={{0,2},{2,0},{4,6},{6,4},{1,3},{3,1},{5,7},{7,5},{8,10},{10,8},{12,... | collective-permute-start | bytes 442376 | tf_op jit(solution)/shard_map/ppermute | solution.py:331
  264.7 19.8 %collective-permute-start.62 = (bf16[4,128,768]{2,1,0:T(8,128)(2,1)S(1)}, bf16[4,128,768]{2,1,0:T(8,128)(2,1)S(1)}, u32[]{:S(2)}, u32[]{:S(2)}) collective-permute-start(bf16[4,128,768]{2,1,0:T(8,128)(2,1)S(1)} %bitcast.55), channel_id=1, source_target_pairs={{0,1},{1,0},{2,3},{3,2},{4,5},{5,4},{6,7},{7,6},{8,9},{9,8},{10,11... | collective-permute-start | bytes 2359304 | tf_op jit(solution)/shard_map/ppermute | solution.py:331
  265.3 21.9 %collective-permute-start.60 = (bf16[192,1536]{1,0:T(8,128)(2,1)S(1)}, bf16[192,1536]{1,0:T(8,128)(2,1)}, u32[]{:S(2)}, u32[]{:S(2)}) collective-permute-start(bf16[192,1536]{1,0:T(8,128)(2,1)S(1)} %add_convert_fusion.1), channel_id=1, source_target_pairs={{0,4},{2,6},{4,0},{6,2},{1,5},{3,7},{5,1},{7,3},{8,12},{10,14},{12... | collective-permute-start | bytes 1769480 | tf_op jit(solution)/shard_map/ppermute | solution.py:331
  266.2 17.7 %collective-permute-start.58 = (bf16[48,1152]{1,0:T(8,128)(2,1)S(1)}, bf16[48,1152]{1,0:T(8,128)(2,1)S(1)}, u32[]{:S(2)}, u32[]{:S(2)}) collective-permute-start(bf16[48,1152]{1,0:T(8,128)(2,1)S(1)} %collective-permute-done.43.refs_3_), channel_id=1, source_target_pairs={{0,4},{2,6},{4,0},{6,2},{1,5},{3,7},{5,1},{7,3},{8,12},{10,14},{12... | collective-permute-start | bytes 331784 | tf_op jit(solution)/shard_map/ppermute | solution.py:331
  271.8 15.4 %collective-permute-start.61 = (bf16[192,384]{1,0:T(8,128)(2,1)}, bf16[192,384]{1,0:T(8,128)(2,1)S(1)}, u32[]{:S(2)}, u32[]{:S(2)}) collective-permute-start(bf16[192,384]{1,0:T(8,128)(2,1)} %add_convert_fusion.3), channel_id=1, source_target_pairs={{0,4},{2,6},{4,0},{6,2},{1,5},{3,7},{5,1},{7,3},{8,12},{10,14},{12... | collective-permute-start | bytes 442376 | tf_op jit(solution)/shard_map/ppermute | solution.py:331
  274.5 14.9 %collective-permute-start.59 = (bf16[48,1536]{1,0:T(8,128)(2,1)S(1)}, bf16[48,1536]{1,0:T(8,128)(2,1)S(1)}, u32[]{:S(2)}, u32[]{:S(2)}) collective-permute-start(bf16[48,1536]{1,0:T(8,128)(2,1)S(1)} %collective-permute-done.51.refs_3_), channel_id=1, source_target_pairs={{0,4},{2,6},{4,0},{6,2},{1,5},{3,7},{5,1},{7,3},{8,12},{10,14},{12... | collective-permute-start | bytes 442376 | tf_op jit(solution)/shard_map/ppermute | solution.py:331
  (47 other events, 262.0 us)

commit v5 on v4

--- a/solution.py
+++ b/solution.py
@@ -562,6 +562,27 @@
     )(left, right)
 
 
+def pick_kernel(seat, in_ref, out_ref):
+    out_ref[...] = in_ref[...]
+
+
+def pick_halves(seat, blocks):
+    count, rows, width = blocks.shape
+    half = (1, rows // 2, width)
+    return pl.pallas_call(
+        pick_kernel,
+        grid_spec=pltpu.PrefetchScalarGridSpec(
+            num_scalar_prefetch=1,
+            grid=(count,),
+            in_specs=[pl.BlockSpec(half, lambda step, seat: (step ^ seat[1], seat[0], 0))],
+            out_specs=pl.BlockSpec(half, lambda step, seat: (step, 0, 0)),
+        ),
+        out_shape=jax.ShapeDtypeStruct((count,) + half[1:], blocks.dtype),
+        name="pick_halves",
+        compiler_params=pltpu.CompilerParams(vmem_limit_bytes=4 << 20),
+    )(seat, blocks)
+
+
 def input_back_kernel(facts, grad_ref, weight_ref, mine_ref, other_ref):
     total = rows_by_rows(grad_ref[...], weight_ref[...]).astype(mine_ref.dtype)
     rows = mine_ref.shape[1]
@@ -621,7 +642,7 @@
         out_ref[0, pl.ds(pl.multiple_of(half * rows, rows), rows), :] = values.astype(out_ref.dtype)
 
 
-def join_halves(half, ratio=None, dtype=jnp.bfloat16, place=0):
+def join_halves(seat, half, ratio=None, dtype=jnp.bfloat16):
     count, rows, width = half.shape
     ratio = jnp.ones((1,), jnp.float32) if ratio is None else ratio.reshape(1)
     return pl.pallas_call(
@@ -638,12 +659,7 @@
         out_shape=jax.ShapeDtypeStruct((count, 2 * rows, width), dtype),
         name="join_halves",
         compiler_params=pltpu.CompilerParams(vmem_limit_bytes=4 << 20),
-    )(
-        jnp.stack([lax.axis_index("tp"), jnp.asarray(place, jnp.int32)]),
-        ratio,
-        half,
-        swap(half, "tp", 1),
-    )
+    )(seat, ratio, half, swap(half, "tp", 1))
 
 
 def weight_grad_kernel(places, *refs, chunks, fsdp, count, order):
@@ -804,6 +820,10 @@
     row_count = seq_count * block_len
     shape = hidden_in.shape
     places = jnp.stack([place, depth])
+    seat = jnp.stack([core, place])
+    lane = jnp.arange(LANES, dtype=jnp.int32)
+    chosen = wide(lane == place)
+    seat_rows = wide(jnp.where(lane == 0, seat[:, None], 0))
     fsdp_count = lax.axis_size("fsdp")
     row = lambda values: values.reshape(1, -1)
     struct = jax.ShapeDtypeStruct
@@ -818,12 +838,24 @@
         jnp.pad(low(local_counts), (0, qkv_out.shape[1] - seq_count)), (16, qkv_out.shape[1])
     )
     full_bias = row(by_pairs(jnp.stack([qv_bias[0], jnp.zeros_like(qv_bias[0]), qv_bias[1]])))
-    teacher_own = own_half(teacher)
-    teacher_own = [
-        lax.dynamic_index_in_dim(teacher_own, place ^ s, 0, keepdims=False)
-        for s in range(ctx_count)
-    ]
-    weight_rows, hidden_half, count_rows, up_own, down_own, teacher_own, full_bias = together(
+    teacher_own = pick_halves(seat, teacher)
+    (
+        places,
+        seat,
+        chosen,
+        seat_rows,
+        weight_rows,
+        hidden_half,
+        count_rows,
+        up_own,
+        down_own,
+        teacher_own,
+        full_bias,
+    ) = together(
+        places,
+        seat,
+        chosen,
+        seat_rows,
         weight_rows,
         hidden_half,
         count_rows,
@@ -835,16 +867,16 @@
     weight_part = stack_rows(weight_rows + [count_rows])
     weight_parts = [weight_part] + swap_all(weight_part, "ctx")
     up_rows = relay_all(up_own, "fsdp")
-    flat_in = join_halves(hidden_half).reshape(row_count, model_width)
+    flat_in = join_halves(seat * jnp.array([1, 0], jnp.int32), hidden_half).reshape(row_count, model_width)
     weight_parts, flat_in, up_rows, down_own = together(
         weight_parts, flat_in, up_rows, down_own
     )
     up_part = stack_rows(up_rows)
     up_parts = [up_part] + swap_all(up_part, "ctx")
-    down_rows = relay_all(down_own, "fsdp")
+    down_rows = [swap(down_own, "fsdp", 1), swap(down_own, "fsdp", 2)]
     counts = sum(wide(item[-16, :LANES]) for item in weight_parts)
-    valid_count = lax.dynamic_index_in_dim(counts, place, 0, keepdims=False).astype(jnp.int32)
-    facts = jnp.stack([valid_count, core, place])
+    facts = jnp.sum(jnp.concatenate([(counts * chosen)[None], seat_rows]), axis=1)
+    facts = facts.astype(jnp.int32)
     projected, full_qkv_out = gathered_layer(
         project_kernel,
         "project",
@@ -857,6 +889,8 @@
         [3 * inner_width],
         fsdp_count,
     )
+    projected, down_first = together(projected, down_rows[0])
+    down_rows = [down_first, down_rows[1], swap(down_first, "fsdp", 2)]
     full_out = full_qkv_out[:, 3 * inner_width :]
     attended, log_total = attend(facts, projected, block_len)
     attended, up_parts, down_rows = together(attended, up_parts, down_rows)
@@ -888,7 +922,7 @@
     )
     active, down_parts = together(active, down_parts)
     teacher_half = stack_rows(
-        [teacher_own[0]] + swap_each(teacher_own, "ctx")
+        [teacher_own[0]] + swap_each([teacher_own[s] for s in range(ctx_count)], "ctx")
     ).reshape(ctx_count, block_len // 2, model_width)
     branch, full_down = gathered_layer(
         down_kernel,
@@ -936,6 +970,7 @@
     )
     branch = rows_times(grad_pre, full_up, block_len, True)
     branch, grad_pre, layer_pieces = together(branch, grad_pre, layer_pieces)
+    layer_out = join_halves(seat, stack_rows(layer_pieces).reshape(layer_half.shape))
     up_pieces = weight_grad(places, [(normed1_low, grad_pre)])
     up_brought = swap_each(up_pieces, "ctx")
     grad_resid1_low, grad_half, stats1 = by_rows(
@@ -952,82 +987,93 @@
     )
     out_kept, out_sent = weight_grad(places, [(grad_resid1_low, attended)], "fsdp")
     grad_attended = rows_times(grad_resid1_low, full_out, block_len, False)
-    out_kept, out_sent, grad_attended = together(out_kept, out_sent, grad_attended)
+    out_kept, out_sent, grad_attended, layer_out = together(
+        out_kept, out_sent, grad_attended, layer_out
+    )
     out_brought = swap(out_sent, "fsdp", 1)
     grad_qkv, stats_qkv = attend_back(facts, projected, grad_attended, log_total, block_len)
     grad_qkv, down_brought, out_brought = together(grad_qkv, down_brought, out_brought)
+    local_count = jnp.broadcast_to(jnp.sum(local_counts), (1, LANES))
+    small = pack(stats2, stats1, stats_up, stats_qkv, local_count)
+    small_other = swap(small, "ctx", 1)
     last_pieces = weight_grad(places, [(flat_in, grad_qkv)])
     down_kept, down_sent = sum_and_cut([down_kept, down_brought])
     out_kept, out_sent = sum_and_cut([out_kept, out_brought])
-    last_pieces, grad_qkv, down_sent, out_sent, layer_pieces, stats_qkv = together(
-        last_pieces, grad_qkv, down_sent, out_sent, layer_pieces, stats_qkv
+    last_pieces, grad_qkv, down_sent, out_sent, small_other = together(
+        last_pieces, grad_qkv, down_sent, out_sent, small_other
     )
     last_brought = swap_each(last_pieces, "ctx")
     down_brought = swap(down_sent, "fsdp", 2)
     mine, other = input_back(facts, grad_qkv, full_qkv_out, block_len)
     up_kept, up_sent = sum_and_cut([up_pieces[0]] + up_brought)
-    local_count = jnp.broadcast_to(jnp.sum(local_counts), (1, LANES))
-    small = pack(stats2, stats1, stats_up, stats_qkv, local_count)
-    last_brought, mine, other, up_sent, out_sent, small, layer_pieces = together(
-        last_brought, mine, other, up_sent, out_sent, small, layer_pieces
+    small = small + small_other
+    small_other = swap(small, "ctx", 2)
+    last_brought, mine, other, up_sent, out_sent, small, small_other = together(
+        last_brought, mine, other, up_sent, out_sent, small, small_other
     )
     last_kept, last_sent = sum_and_cut([last_pieces[0]] + last_brought)
-    last_sent, other, down_brought, up_sent, out_sent, small, layer_pieces = together(
-        last_sent, other, down_brought, up_sent, out_sent, small, layer_pieces
+    last_sent, other, down_brought, up_sent, out_sent, small, small_other = together(
+        last_sent, other, down_brought, up_sent, out_sent, small, small_other
     )
     last_brought = swap(last_sent, "fsdp", 1)
     other = swap(other, "tp", 1)
     owned_down = low(wide(down_kept) + wide(down_brought))
     down_other = swap(owned_down, "ctx", 1)
-    last_brought, other, up_sent, out_sent, small, layer_pieces = together(
-        last_brought, other, up_sent, out_sent, small, layer_pieces
+    small = small + small_other
+    small_other = swap(small, "fsdp", 1)
+    last_brought, other, up_sent, out_sent, small, small_other = together(
+        last_brought, other, up_sent, out_sent, small, small_other
     )
     last_kept, last_sent = sum_and_cut([last_kept, last_brought])
     half = low(grad_half + (wide(mine) + wide(other)))
-    last_sent, half, up_sent, out_sent, small, layer_pieces = together(
-        last_sent, half, up_sent, out_sent, small, layer_pieces
+    small = small + small_other
+    last_sent, half, up_sent, out_sent, small = together(
+        last_sent, half, up_sent, out_sent, small
     )
     last_brought = swap(last_sent, "fsdp", 2)
     up_brought = swap(up_sent, "fsdp", 1)
     half_pieces = [half[s] for s in range(ctx_count)]
-    half_brought = swap_each(half_pieces, "ctx")
-    layer_stack = stack_rows(layer_pieces).reshape(layer_half.shape)
-    last_brought, up_brought, down_other, out_sent, small, layer_stack = together(
-        last_brought, up_brought, down_other, out_sent, small, layer_stack
+    half_brought = [half_pieces[0], swap(half_pieces[1], "ctx", 1)]
+    small_other = swap(small, "fsdp", 2)
+    last_brought, up_brought, down_other, out_sent, small_other, half_pieces = together(
+        last_brought, up_brought, down_other, out_sent, small_other, half_pieces
     )
     part = low(wide(last_kept) + wide(last_brought))
     up_kept, up_sent = sum_and_cut([up_kept, up_brought])
     owned_down = low(wide(owned_down) + wide(down_other))
-    part, up_sent, owned_down, out_sent, small, layer_stack = together(
-        part, up_sent, owned_down, out_sent, small, layer_stack
+    small = small + small_other
+    part, up_sent, owned_down, out_sent, small, half_pieces = together(
+        part, up_sent, owned_down, out_sent, small, half_pieces
     )
     shared = [part, swap(part, "ctx", 1), swap(part, "ctx", 2)]
     up_brought = swap(up_sent, "fsdp", 2)
     out_brought = swap(out_sent, "fsdp", 2)
     down_other = swap(owned_down, "ctx", 2)
-    layer_out = join_halves(layer_stack, place=place)
-    shared, up_brought, half_brought, out_brought, small, layer_out = together(
-        shared, up_brought, half_brought, out_brought, small, layer_out
+    shared, up_brought, out_brought, half_pieces, down_other = together(
+        shared, up_brought, out_brought, half_pieces, down_other
     )
     up_part = low(wide(up_kept) + wide(up_brought))
     owned_out = low(wide(out_kept) + wide(out_brought))
-    up_part, owned_out, shared, small = together(up_part, owned_out, shared, small)
+    up_part, owned_out, shared, half_pieces = together(up_part, owned_out, shared, half_pieces)
     shared = shared + [swap(shared[1], "ctx", 2)]
     up_shared = [up_part, swap(up_part, "ctx", 1), swap(up_part, "ctx", 2)]
+    half_brought = half_brought + [swap(half_pieces[s], "ctx", s) for s in range(2, ctx_count)]
+    up_shared, half_brought, owned_out = together(up_shared, half_brought, owned_out)
+    up_shared = up_shared + [swap(up_shared[1], "ctx", 2)]
+    input_half = stack_rows(half_brought).reshape(half.shape)
     out_other = swap(owned_out, "ctx", 1)
-    input_half = stack_rows(half_pieces[:1] + half_brought).reshape(half.shape)
-    small = sum_over(small, "ctx")
-    up_shared, input_half, out_other, small = together(up_shared, input_half, out_other, small)
-    up_shared = up_shared + [swap(up_shared[1], "ctx", 2)]
+    owned_out, out_other, input_half, up_shared = together(
+        owned_out, out_other, input_half, up_shared
+    )
     owned_out = low(wide(owned_out) + wide(out_other))
     out_other = swap(owned_out, "ctx", 2)
-    small = sum_over(small, "fsdp")
     at = 7 + -(-hidden_width // model_width)
-    counted = small[at + -(-3 * inner_width // model_width), 0]
+    last_row = at + -(-3 * inner_width // model_width)
+    counted = small[last_row : last_row + 1, :1]
     ratio = float(row_count * ctx_count * fsdp_count) / counted
-    loss = jnp.sum(small[3]) / (counted * model_width)
+    loss = jnp.sum(small[3:4], axis=1, keepdims=True) / (counted * model_width)
     scaled = small * ratio
-    input_grad = join_halves(input_half, ratio, jnp.float32, place)
+    input_grad = join_halves(seat, input_half, ratio, jnp.float32)
     owned_qkv = place_rows(places, shared, ratio, 3)
     owned_qkv, up_shared, down_other, out_other, input_grad, scaled = together(
         owned_qkv, up_shared, down_other, out_other, input_grad, scaled
@@ -1043,7 +1089,7 @@
     return (
         layer_out,
         input_grad,
-        loss,
+        loss.reshape(()),
         owned_qkv,
         grad_qv_bias,
         owned_out,

time: 300 us -> 288 us (0.960)
  local copies, waits for them, and re-layouts: 20.4 us -> 10.8 us
  other arithmetic: 9.12 us -> 5.35 us
    unnamed x63 -> x39, local copies, waits for them, and re-layouts: 8.63 us -> 1.54 us
  transfers between devices with their start and end apart: 64 -> 64, of which waited for: 30 -> 25; matrix products, arithmetic and copies ran while one was open for 3% -> 2% of each run, Pallas kernels for 25% -> 26%
where the time goes in v5:
time: 288 us; the launch traced here: 287 us
  waiting for transfers between devices  106 us (37%)
  Pallas kernels  88.2 us (31%)
  starting transfers between devices  72.7 us (25%)
  local copies, waits for them, and re-layouts  10.8 us (4%)
  other arithmetic  5.35 us (2%)
  between operations  4.57 us (2%)
    ppermute x63, waiting for transfers between devices, swap(): return lax.ppermute(values, axis, pairs)  104 us
    ppermute x63, starting transfers between devices, swap(): return lax.ppermute(values, axis, pairs)  68.7 us
    pallas_call x1, Pallas kernels, attend_back(): pl.pallas_call(lambda *refs: attend_back_kernel(*refs, block=block), grid...  15.5 us
    pallas_call x4, Pallas kernels, weight_grad(): pl.pallas_call(lambda *refs: weight_grad_kernel(*refs, chunks=chunks, fsd...  13.9 us
    pallas_call x3, Pallas kernels, gathered_layer(): pl.pallas_call(kernel, grid_spec=pltpu.PrefetchScalarGridSpec(num_scalar_...  13 us
    pallas_call x1, Pallas kernels, attend(): pl.pallas_call(lambda *refs: attend_kernel(*refs, block=block), grid_spec...  10.8 us
    pallas_call x3, Pallas kernels, by_rows(): pl.pallas_call(kernel, grid_spec=pltpu.PrefetchScalarGridSpec(num_scalar_...  9.85 us
    pallas_call x3, Pallas kernels, rows_times(): pl.pallas_call(lambda *refs: rows_kernel(*refs, transposed=transposed), g...  6.4 us
  transfers between devices with their start and end apart: 64, of which 25 were waited for; matrix products, arithmetic and copies ran while one was open for 2% of the time, Pallas kernels for 26%

profile of v5, /device:TPU:0, one launch (start us, length us, event | category | flops | bytes accessed | tf_op | source)
XLA Modules:
  0.0 287.4 jit_solution(14819211458144082076)
XLA Ops:
  5.0 5.0 %collective-permute-start.2 = (bf16[48,1536]{1,0:T(8,128)(2,1)}, bf16[48,1536]{1,0:T(8,128)(2,1)S(1)}, u32[]{:S(2)}, u32[]{:S(2)}) collective-permute-start(bf16[48,1536]{1,0:T(8,128)(2,1)} %constant_dynamic-slice_fusion.2), channel_id=1, source_target_pairs={{0,24},{8,16},{16,8},{24,0},{1,25},{9,17},{17,9},{25,1},{2,26},{10... | collective-permute-start | bytes 442376 | tf_op jit(solution)/shard_map/ppermute | solution.py:331
  10.6 3.9 %all-to-all-start = ((bf16[4,128,768]{2,1,0:T(8,128)(2,1)}), bf16[4,128,768]{2,1,0:T(8,128)(2,1)S(1)}, u32[]{:S(2)}, u32[]{:S(2)}) async-start(bf16[4,128,768]{2,1,0:T(8,128)(2,1)} %constant_dynamic-slice_fusion.3), calls=%async_computation | async-start | bytes 1572864 | tf_op jit(solution)/shard_map/all_to_all | solution.py:382
  18.4 4.4 %collective-permute-done.1.refs_1_ = bf16[48,1536]{1,0:T(8,128)(2,1)} collective-permute-done((bf16[48,1536]{1,0:T(8,128)(2,1)}, bf16[48,1536]{1,0:T(8,128)(2,1)}, u32[]{:S(2)}, u32[]{:S(2)}) %collective-permute-start.1) | collective-permute-done | bytes 147488 | tf_op jit(solution)/shard_map/ppermute | solution.py:331
  22.8 1.8 all-to-all-done.own_ref
  30.7 4.2 %collective-permute-done.7.refs_0_ = bf16[48,1536]{1,0:T(8,128)(2,1)S(1)} collective-permute-done((bf16[48,1536]{1,0:T(8,128)(2,1)}, bf16[48,1536]{1,0:T(8,128)(2,1)S(1)}, u32[]{:S(2)}, u32[]{:S(2)}) %collective-permute-start.7) | collective-permute-done | bytes 147488 | tf_op jit(solution)/shard_map/ppermute | solution.py:331
  34.8 2.4 collective-permute-start.8
  38.6 9.2 %collective-permute-done.8.refs_1_ = bf16[48,1536]{1,0:T(8,128)(2,1)S(1)} collective-permute-done((bf16[48,1536]{1,0:T(8,128)(2,1)}, bf16[48,1536]{1,0:T(8,128)(2,1)S(1)}, u32[]{:S(2)}, u32[]{:S(2)}) %collective-permute-start.8) | collective-permute-done | bytes 147488 | tf_op jit(solution)/shard_map/ppermute | solution.py:331
  47.8 2.1 collective-permute-done.9.refs_2_
  55.9 2.6 collective-permute-start.14
  58.5 3.5 %project.1 = (bf16[1024,1152]{1,0:T(8,128)(2,1)S(1)}, bf16[768,1536]{1,0:T(8,128)(2,1)S(1)}) custom-call(s32[2]{0:T(128)S(1)} %get-tuple-element.209.places.refs_0_, bf16[1024,768]{1,0:T(8,128)(2,1)S(1)} %bitcast.57, f32[1,1152]{1,0:T(1,128)S(1)} %reshape_reshape.3.bias_ref, bf16[192,1536]{1,0:T(8,128)(2,1)S(1)} %constant_dynamic-update-slice_fusion.own_ref, ...), custom_call_target="tpu_custom_call" | custom-call | tf_op jit(solution)/shard_map/project/pallas_call | solution.py:296
  63.5 10.8 %attend.1 = (bf16[1024,384]{1,0:T(8,128)(2,1)S(1)}, f32[3,2,1024]{2,1,0:T(2,128)S(1)}) custom-call(s32[3]{0:T(128)S(1)} %convert_element_type.116.refs_0_.facts, bf16[1024,1152]{1,0:T(8,128)(2,1)S(1)} %get-tuple-element.228.refs_1_.refs_2_.refs_3_, bf16[1024,1152]{1,0:T(8,128)(2,1)S(1)} %get-tuple-element.228.refs_1_.refs_2_.refs_3_, ...), custom_call_target="tpu_custom_call" | custom-call | tf_op jit(solution)/shard_map/attend/pallas_call | solution.py:174
  81.4 5.5 %up.1 = (bf16[1024,1536]{1,0:T(8,128)(2,1)S(1)}, bf16[1024,1536]{1,0:T(8,128)(2,1)S(1)}, bf16[768,1536]{1,0:T(8,128)(2,1)S(1)}) custom-call(s32[2]{0:T(128)S(1)} %get-tuple-element.209.places.refs_0_, bf16[1024,768]{1,0:T(8,128)(2,1)S(1)} %get-tuple-element.237.left_ref.refs_1_, f32[1,1536]{1,0:T(1,128)S(1)} %reshape.113.bias_ref, ...), custom_call_target="tpu_custom_call" | custom-call | tf_op jit(solution)/shard_map/up/pallas_call | solution.py:296
  86.9 3.1 %collective-permute-done.19.refs_3_ = bf16[144,1536]{1,0:T(8,128)(2,1)S(1)} collective-permute-done((bf16[144,1536]{1,0:T(8,128)(2,1)S(1)}, bf16[144,1536]{1,0:T(8,128)(2,1)S(1)}, u32[]{:S(2)}, u32[]{:S(2)}) %collective-permute-start.19) | collective-permute-done | bytes 442400 | tf_op jit(solution)/shard_map/ppermute | solution.py:331
  90.0 9.0 %collective-permute-done.18.refs_2_ = bf16[144,1536]{1,0:T(8,128)(2,1)S(1)} collective-permute-done((bf16[144,1536]{1,0:T(8,128)(2,1)S(1)}, bf16[144,1536]{1,0:T(8,128)(2,1)S(1)}, u32[]{:S(2)}, u32[]{:S(2)}) %collective-permute-start.18) | collective-permute-done | bytes 442400 | tf_op jit(solution)/shard_map/ppermute | solution.py:331
  99.1 4.0 %down.1 = (bf16[1024,768]{1,0:T(8,128)(2,1)S(1)}, bf16[768,1536]{1,0:T(8,128)(2,1)S(1)}) custom-call(s32[2]{0:T(128)S(1)} %get-tuple-element.209.places.refs_0_, bf16[1024,1536]{1,0:T(8,128)(2,1)S(1)} %get-tuple-element.246.left_ref.refs_2_, bf16[192,1536]{1,0:T(8,128)(2,1)S(1)} %copy-done.4, bf16[144,1536]{1,0:T(8,128)(2,1)S(1)} %stack_rows.8.refs_0_, ...), custom_call_target="tpu_custom_call" | custom-call | tf_op jit(solution)/shard_map/down/pallas_call | solution.py:296
  106.8 5.2 %collective-permute-done.23.refs_3_ = bf16[128,768]{1,0:T(8,128)(2,1)S(1)} collective-permute-done((bf16[128,768]{1,0:T(8,128)(2,1)S(1)}, bf16[128,768]{1,0:T(8,128)(2,1)S(1)}, u32[]{:S(2)}, u32[]{:S(2)}) %collective-permute-start.23) | collective-permute-done | bytes 196640 | tf_op jit(solution)/shard_map/ppermute | solution.py:331
  112.0 3.8 %collective-permute-done.22.refs_2_ = bf16[128,768]{1,0:T(8,128)(2,1)S(1)} collective-permute-done((bf16[128,768]{1,0:T(8,128)(2,1)S(1)}, bf16[128,768]{1,0:T(8,128)(2,1)S(1)}, u32[]{:S(2)}, u32[]{:S(2)}) %collective-permute-start.22) | collective-permute-done | bytes 196640 | tf_op jit(solution)/shard_map/ppermute | solution.py:331
  116.0 2.2 collective-permute-done.24.other_teacher_ref
  118.2 5.0 %second_norm.1 = (bf16[4,128,768]{2,1,0:T(8,128)(2,1)S(1)}, f32[1024,768]{1,0:T(8,128)S(1)}, bf16[1024,768]{1,0:T(8,128)(2,1)S(1)}, f32[8,768]{1,0:T(8,128)S(1)}) custom-call(s32[3]{0:T(128)S(1)} %convert_element_type.116.refs_0_.facts, f32[1024,768]{1,0:T(8,128)S(1)} %get-tuple-element.236.normal_ref, f32[1,768]{1,0:T(1,128)S(1)} %reshape.111.gain_ref.gain1_ref, ...), custom_call_target="tpu_custom_call" | custom-call | tf_op jit(solution)/shard_map/second_norm/pallas_call | solution.py:497
  126.9 4.0 %weight_grad.4 = (bf16[384,1536]{1,0:T(8,128)(2,1)S(1)}, bf16[384,1536]{1,0:T(8,128)(2,1)S(1)}) custom-call(s32[2]{0:T(128)S(1)} %get-tuple-element.209.places.refs_0_, bf16[1024,768]{1,0:T(8,128)(2,1)S(1)} %get-tuple-element.257.refs_1_.low_ref, bf16[1024,1536]{1,0:T(8,128)(2,1)S(1)} %get-tuple-element.246.left_ref.refs_2_), custom_call_target="tpu_custom_call" | custom-call | tf_op jit(solution)/shard_map/weight_grad/pallas_call | solution.py:717
  130.9 3.8 %grad_pre.1 = (bf16[1024,1536]{1,0:T(8,128)(2,1)S(1)}, f32[8,1536]{1,0:T(8,128)S(1)}) custom-call(bf16[1024,768]{1,0:T(8,128)(2,1)S(1)} %get-tuple-element.257.refs_1_.low_ref, bf16[768,1536]{1,0:T(8,128)(2,1)S(1)} %get-tuple-element.258.weight_ref, bf16[1024,1536]{1,0:T(8,128)(2,1)S(1)} %get-tuple-element.259.slope_ref), custom_call_target="tpu_custom_call" | custom-call | tf_op jit(solution)/shard_map/grad_pre/pallas_call | solution.py:531
  134.7 3.3 %rows_times.4.mine_ref = bf16[1024,768]{1,0:T(8,128)(2,1)S(1)} custom-call(bf16[1024,1536]{1,0:T(8,128)(2,1)S(1)} %get-tuple-element.300.refs_0_.refs_2_, bf16[768,1536]{1,0:T(8,128)(2,1)S(1)} %get-tuple-element.261.refs_1_), custom_call_target="tpu_custom_call" | custom-call | tf_op jit(solution)/shard_map/rows_times/pallas_call | solution.py:551
  138.1 2.4 collective-permute-start.30
  140.8 4.0 %weight_grad.7 = (bf16[192,1536]{1,0:T(8,128)(2,1)S(1)}, bf16[192,1536]{1,0:T(8,128)(2,1)S(1)}, bf16[192,1536]{1,0:T(8,128)(2,1)S(1)}, bf16[192,1536]{1,0:T(8,128)(2,1)S(1)}) custom-call(s32[2]{0:T(128)S(1)} %get-tuple-element.209.places.refs_0_, bf16[1024,768]{1,0:T(8,128)(2,1)S(1)} %get-tuple-element.237.left_ref.refs_1_, ...), custom_call_target="tpu_custom_call" | custom-call | tf_op jit(solution)/shard_map/weight_grad/pallas_call | solution.py:717
  146.8 2.3 join_halves.4
  149.2 3.2 %first_norm_back.1 = (bf16[1024,768]{1,0:T(8,128)(2,1)S(1)}, f32[4,128,768]{2,1,0:T(8,128)S(1)}, f32[8,768]{1,0:T(8,128)S(1)}) custom-call(s32[3]{0:T(128)S(1)} %convert_element_type.116.refs_0_.facts, f32[1024,768]{1,0:T(8,128)S(1)} %get-tuple-element.253.grad_ref, bf16[1024,768]{1,0:T(8,128)(2,1)S(1)} %rows_times.4.mine_ref, ...), custom_call_target="tpu_custom_call" | custom-call | tf_op jit(solution)/shard_map/first_norm_back/pallas_call | solution.py:497
  157.3 15.5 %attend_back.1 = (bf16[1024,1152]{1,0:T(8,128)(2,1)S(1)}, f32[8,1152]{1,0:T(8,128)S(1)}) custom-call(s32[3]{0:T(128)S(1)} %convert_element_type.116.refs_0_.facts, bf16[1024,1152]{1,0:T(8,128)(2,1)S(1)} %get-tuple-element.228.refs_1_.refs_2_.refs_3_, bf16[1024,1152]{1,0:T(8,128)(2,1)S(1)} %get-tuple-element.228.refs_1_.refs_2_.refs_3_, ...), custom_call_target="tpu_custom_call" | custom-call | tf_op jit(solution)/shard_map/attend_back/pallas_call | solution.py:198
  174.9 4.3 %weight_grad.6 = (bf16[192,1152]{1,0:T(8,128)(2,1)S(1)}, bf16[192,1152]{1,0:T(8,128)(2,1)S(1)}, bf16[192,1152]{1,0:T(8,128)(2,1)S(1)}, bf16[192,1152]{1,0:T(8,128)(2,1)S(1)}) custom-call(s32[2]{0:T(128)S(1)} %get-tuple-element.209.places.refs_0_, bf16[1024,768]{1,0:T(8,128)(2,1)S(1)} %bitcast.59, bf16[1024,1152]{1,0:T(8,128)(2,1)S(1)} %get-tuple-element.297.refs_2_.grad_ref), custom_call_target="tpu_custom_call" | custom-call | tf_op jit(solution)/shard_map/weight_grad/pallas_call | solution.py:717
  185.3 3.9 %input_back.1 = (bf16[4,128,768]{2,1,0:T(8,128)(2,1)S(1)}, bf16[4,128,768]{2,1,0:T(8,128)(2,1)S(1)}) custom-call(s32[3]{0:T(128)S(1)} %convert_element_type.116.refs_0_.facts, bf16[1024,1152]{1,0:T(8,128)(2,1)S(1)} %get-tuple-element.297.refs_2_.grad_ref, bf16[768,1536]{1,0:T(8,128)(2,1)S(1)} %get-tuple-element.235.weight_ref), custom_call_target="tpu_custom_call" | custom-call | tf_op jit(solution)/shard_map/input_back/pallas_call | solution.py:597
  189.2 13.3 %collective-permute-done.39 = f32[16,768]{1,0:T(8,128)S(1)} collective-permute-done((f32[16,768]{1,0:T(8,128)S(1)}, f32[16,768]{1,0:T(8,128)S(1)}, u32[]{:S(2)}, u32[]{:S(2)}) %collective-permute-start.39) | collective-permute-done | bytes 49184 | tf_op jit(solution)/shard_map/ppermute | solution.py:331
  202.7 4.7 %collective-permute-done.40 = bf16[192,1536]{1,0:T(8,128)(2,1)S(1)} collective-permute-done((bf16[192,1536]{1,0:T(8,128)(2,1)S(1)}, bf16[192,1536]{1,0:T(8,128)(2,1)S(1)}, u32[]{:S(2)}, u32[]{:S(2)}) %collective-permute-start.40) | collective-permute-done | bytes 589856 | tf_op jit(solution)/shard_map/ppermute | solution.py:331
  207.5 2.0 collective-permute-start.41
  210.4 1.7 collective-permute-done.43
  212.1 4.3 %collective-permute-done.41.refs_1_ = bf16[96,1152]{1,0:T(8,128)(2,1)S(1)} collective-permute-done((bf16[96,1152]{1,0:T(8,128)(2,1)S(1)}, bf16[96,1152]{1,0:T(8,128)(2,1)S(1)}, u32[]{:S(2)}, u32[]{:S(2)}) %collective-permute-start.41) | collective-permute-done | bytes 221216 | tf_op jit(solution)/shard_map/ppermute | solution.py:331
  217.5 1.8 collective-permute-start.47
  220.5 4.4 %collective-permute-done.46 = bf16[192,1536]{1,0:T(8,128)(2,1)S(1)} collective-permute-done((bf16[192,1536]{1,0:T(8,128)(2,1)S(1)}, bf16[192,1536]{1,0:T(8,128)(2,1)S(1)}, u32[]{:S(2)}, u32[]{:S(2)}) %collective-permute-start.46) | collective-permute-done | bytes 589856 | tf_op jit(solution)/shard_map/ppermute | solution.py:331
  226.7 2.1 collective-permute-done.45.refs_1_
  231.0 1.6 collective-permute-start.51
  234.7 11.0 %collective-permute-done.49.refs_4_ = bf16[48,1152]{1,0:T(8,128)(2,1)S(1)} collective-permute-done((bf16[48,1152]{1,0:T(8,128)(2,1)S(1)}, bf16[48,1152]{1,0:T(8,128)(2,1)S(1)}, u32[]{:S(2)}, u32[]{:S(2)}) %collective-permute-start.49) | collective-permute-done | bytes 110624 | tf_op jit(solution)/shard_map/ppermute | solution.py:331
  251.4 2.1 collective-permute-done.56.refs_1_
  253.5 4.9 %collective-permute-done.55.refs_4_ = bf16[48,1536]{1,0:T(8,128)(2,1)S(1)} collective-permute-done((bf16[48,1536]{1,0:T(8,128)(2,1)S(1)}, bf16[48,1536]{1,0:T(8,128)(2,1)S(1)}, u32[]{:S(2)}, u32[]{:S(2)}) %collective-permute-start.55) | collective-permute-done | bytes 147488 | tf_op jit(solution)/shard_map/ppermute | solution.py:331
  258.5 1.8 collective-permute-start.59
  260.6 3.1 %collective-permute-done.59 = bf16[192,384]{1,0:T(8,128)(2,1)S(1)} collective-permute-done((bf16[192,384]{1,0:T(8,128)(2,1)S(1)}, bf16[192,384]{1,0:T(8,128)(2,1)S(1)}, u32[]{:S(2)}, u32[]{:S(2)}) %collective-permute-start.59) | collective-permute-done | bytes 147488 | tf_op jit(solution)/shard_map/ppermute | solution.py:331
  263.7 1.8 collective-permute-done.60.refs_5_
  267.7 1.8 collective-permute-start.53
  270.8 4.6 %collective-permute-done.53.refs_5_ = bf16[48,1152]{1,0:T(8,128)(2,1)S(1)} collective-permute-done((bf16[48,1152]{1,0:T(8,128)(2,1)S(1)}, bf16[48,1152]{1,0:T(8,128)(2,1)S(1)}, u32[]{:S(2)}, u32[]{:S(2)}) %collective-permute-start.53) | collective-permute-done | bytes 110624 | tf_op jit(solution)/shard_map/ppermute | solution.py:331
  276.0 2.7 join_halves.5
  281.6 1.8 add_multiply_fusion.1
  (212 shorter events, 76.9 us)
Async XLA Ops:
  5.0 13.4 %collective-permute-start.2 = (bf16[48,1536]{1,0:T(8,128)(2,1)}, bf16[48,1536]{1,0:T(8,128)(2,1)S(1)}, u32[]{:S(2)}, u32[]{:S(2)}) collective-permute-start(bf16[48,1536]{1,0:T(8,128)(2,1)} %constant_dynamic-slice_fusion.2), channel_id=1, source_target_pairs={{0,24},{8,16},{16,8},{24,0},{1,25},{9,17},{17,9},{25,1},{2,26},{10... | collective-permute-start | bytes 442376 | tf_op jit(solution)/shard_map/ppermute | solution.py:331
  10.0 12.8 %collective-permute-start.1 = (bf16[48,1536]{1,0:T(8,128)(2,1)}, bf16[48,1536]{1,0:T(8,128)(2,1)}, u32[]{:S(2)}, u32[]{:S(2)}) collective-permute-start(bf16[48,1536]{1,0:T(8,128)(2,1)} %constant_dynamic-slice_fusion.2), channel_id=1, source_target_pairs={{0,16},{8,24},{16,0},{24,8},{1,17},{9,25},{17,1},{25,9},{2,18},{10... | collective-permute-start | bytes 442376 | tf_op jit(solution)/shard_map/ppermute | solution.py:331
  10.0 12.8 %collective-permute-start = (bf16[48,1536]{1,0:T(8,128)(2,1)}, bf16[48,1536]{1,0:T(8,128)(2,1)}, u32[]{:S(2)}, u32[]{:S(2)}) collective-permute-start(bf16[48,1536]{1,0:T(8,128)(2,1)} %constant_dynamic-slice_fusion.2), channel_id=1, source_target_pairs={{0,8},{8,0},{16,24},{24,16},{1,9},{9,1},{17,25},{25,17},{2,10},{10... | collective-permute-start | bytes 442376 | tf_op jit(solution)/shard_map/ppermute | solution.py:331
  10.6 14.0 %all-to-all-start = ((bf16[4,128,768]{2,1,0:T(8,128)(2,1)}), bf16[4,128,768]{2,1,0:T(8,128)(2,1)S(1)}, u32[]{:S(2)}, u32[]{:S(2)}) async-start(bf16[4,128,768]{2,1,0:T(8,128)(2,1)} %constant_dynamic-slice_fusion.3), calls=%async_computation | async-start | bytes 1572864 | tf_op jit(solution)/shard_map/all_to_all | solution.py:382
  24.6 12.6 %collective-permute-start.6 = (bf16[4,128,768]{2,1,0:T(8,128)(2,1)S(1)}, bf16[4,128,768]{2,1,0:T(8,128)(2,1)S(1)}, u32[]{:S(2)}, u32[]{:S(2)}) collective-permute-start(bf16[4,128,768]{2,1,0:T(8,128)(2,1)S(1)} %all-to-all-done.own_ref), channel_id=1, source_target_pairs={{0,1},{1,0},{2,3},{3,2},{4,5},{5,4},{6,7},{7,6},{8,9},{9,8},{10,11... | collective-permute-start | bytes 2359304 | tf_op jit(solution)/shard_map/ppermute | solution.py:331
  25.6 24.3 %collective-permute-start.5 = (bf16[160,1536]{1,0:T(8,128)(2,1)S(1)}, bf16[160,1536]{1,0:T(8,128)(2,1)S(1)}, u32[]{:S(2)}, u32[]{:S(2)}) collective-permute-start(bf16[160,1536]{1,0:T(8,128)(2,1)S(1)} %stack_rows.6.refs_0_), channel_id=1, source_target_pairs={{0,6},{2,4},{4,2},{6,0},{1,7},{3,5},{5,3},{7,1},{8,14},{10,12},{12... | collective-permute-start | bytes 1474568 | tf_op jit(solution)/shard_map/ppermute | solution.py:331
  27.1 23.6 %collective-permute-start.4 = (bf16[160,1536]{1,0:T(8,128)(2,1)S(1)}, bf16[160,1536]{1,0:T(8,128)(2,1)S(1)}, u32[]{:S(2)}, u32[]{:S(2)}) collective-permute-start(bf16[160,1536]{1,0:T(8,128)(2,1)S(1)} %stack_rows.6.refs_0_), channel_id=1, source_target_pairs={{0,4},{2,6},{4,0},{6,2},{1,5},{3,7},{5,1},{7,3},{8,12},{10,14},{12... | collective-permute-start | bytes 1474568 | tf_op jit(solution)/shard_map/ppermute | solution.py:331
  28.6 22.2 %collective-permute-start.3 = (bf16[160,1536]{1,0:T(8,128)(2,1)S(1)}, bf16[160,1536]{1,0:T(8,128)(2,1)S(1)}, u32[]{:S(2)}, u32[]{:S(2)}) collective-permute-start(bf16[160,1536]{1,0:T(8,128)(2,1)S(1)} %stack_rows.6.refs_0_), channel_id=1, source_target_pairs={{0,2},{2,0},{4,6},{6,4},{1,3},{3,1},{5,7},{7,5},{8,10},{10,8},{12,... | collective-permute-start | bytes 1474568 | tf_op jit(solution)/shard_map/ppermute | solution.py:331
  34.8 13.0 %collective-permute-start.8 = (bf16[48,1536]{1,0:T(8,128)(2,1)}, bf16[48,1536]{1,0:T(8,128)(2,1)S(1)}, u32[]{:S(2)}, u32[]{:S(2)}) collective-permute-start(bf16[48,1536]{1,0:T(8,128)(2,1)} %get-tuple-element.216), channel_id=1, source_target_pairs={{0,16},{8,24},{16,0},{24,8},{1,17},{9,25},{17,1},{25,9},{2,18},{10... | collective-permute-start | bytes 442376 | tf_op jit(solution)/shard_map/ppermute | solution.py:331
  37.2 12.7 %collective-permute-start.9 = (bf16[48,1536]{1,0:T(8,128)(2,1)S(1)}, bf16[48,1536]{1,0:T(8,128)(2,1)S(1)}, u32[]{:S(2)}, u32[]{:S(2)}) collective-permute-start(bf16[48,1536]{1,0:T(8,128)(2,1)S(1)} %collective-permute-done.7.refs_0_), channel_id=1, source_target_pairs={{0,16},{8,24},{16,0},{24,8},{1,17},{9,25},{17,1},{25,9},{2,18},{10... | collective-permute-start | bytes 442376 | tf_op jit(solution)/shard_map/ppermute | solution.py:331
  50.8 23.4 %collective-permute-start.13 = (bf16[144,1536]{1,0:T(8,128)(2,1)S(1)}, bf16[144,1536]{1,0:T(8,128)(2,1)S(1)}, u32[]{:S(2)}, u32[]{:S(2)}) collective-permute-start(bf16[144,1536]{1,0:T(8,128)(2,1)S(1)} %stack_rows.7.refs_0_), channel_id=1, source_target_pairs={{0,6},{2,4},{4,2},{6,0},{1,7},{3,5},{5,3},{7,1},{8,14},{10,12},{12... | collective-permute-start | bytes 1327112 | tf_op jit(solution)/shard_map/ppermute | solution.py:331
  52.3 21.9 %collective-permute-start.12 = (bf16[144,1536]{1,0:T(8,128)(2,1)S(1)}, bf16[144,1536]{1,0:T(8,128)(2,1)S(1)}, u32[]{:S(2)}, u32[]{:S(2)}) collective-permute-start(bf16[144,1536]{1,0:T(8,128)(2,1)S(1)} %stack_rows.7.refs_0_), channel_id=1, source_target_pairs={{0,4},{2,6},{4,0},{6,2},{1,5},{3,7},{5,1},{7,3},{8,12},{10,14},{12... | collective-permute-start | bytes 1327112 | tf_op jit(solution)/shard_map/ppermute | solution.py:331
  53.7 20.5 %collective-permute-start.11 = (bf16[144,1536]{1,0:T(8,128)(2,1)S(1)}, bf16[144,1536]{1,0:T(8,128)(2,1)S(1)}, u32[]{:S(2)}, u32[]{:S(2)}) collective-permute-start(bf16[144,1536]{1,0:T(8,128)(2,1)S(1)} %stack_rows.7.refs_0_), channel_id=1, source_target_pairs={{0,2},{2,0},{4,6},{6,4},{1,3},{3,1},{5,7},{7,5},{8,10},{10,8},{12,... | collective-permute-start | bytes 1327112 | tf_op jit(solution)/shard_map/ppermute | solution.py:331
  55.9 18.4 %collective-permute-start.14 = (bf16[48,1536]{1,0:T(8,128)(2,1)S(1)}, bf16[48,1536]{1,0:T(8,128)(2,1)S(1)}, u32[]{:S(2)}, u32[]{:S(2)}) collective-permute-start(bf16[48,1536]{1,0:T(8,128)(2,1)S(1)} %copy-done.8), channel_id=1, source_target_pairs={{0,16},{8,24},{16,0},{24,8},{1,17},{9,25},{17,1},{25,9},{2,18},{10... | collective-permute-start | bytes 442376 | tf_op jit(solution)/shard_map/ppermute | solution.py:331
  62.0 12.2 %collective-permute-start.15 = (bf16[48,1536]{1,0:T(8,128)(2,1)S(1)}, bf16[48,1536]{1,0:T(8,128)(2,1)S(1)}, u32[]{:S(2)}, u32[]{:S(2)}) collective-permute-start(bf16[48,1536]{1,0:T(8,128)(2,1)S(1)} %collective-permute-done.10.refs_0_), channel_id=1, source_target_pairs={{0,16},{8,24},{16,0},{24,8},{1,17},{9,25},{17,1},{25,9},{2,18},{10... | collective-permute-start | bytes 442376 | tf_op jit(solution)/shard_map/ppermute | solution.py:331
  76.1 14.0 %collective-permute-start.19 = (bf16[144,1536]{1,0:T(8,128)(2,1)S(1)}, bf16[144,1536]{1,0:T(8,128)(2,1)S(1)}, u32[]{:S(2)}, u32[]{:S(2)}) collective-permute-start(bf16[144,1536]{1,0:T(8,128)(2,1)S(1)} %stack_rows.8.refs_0_), channel_id=1, source_target_pairs={{0,6},{2,4},{4,2},{6,0},{1,7},{3,5},{5,3},{7,1},{8,14},{10,12},{12... | collective-permute-start | bytes 1327112 | tf_op jit(solution)/shard_map/ppermute | solution.py:331
  77.6 21.5 %collective-permute-start.18 = (bf16[144,1536]{1,0:T(8,128)(2,1)S(1)}, bf16[144,1536]{1,0:T(8,128)(2,1)S(1)}, u32[]{:S(2)}, u32[]{:S(2)}) collective-permute-start(bf16[144,1536]{1,0:T(8,128)(2,1)S(1)} %stack_rows.8.refs_0_), channel_id=1, source_target_pairs={{0,4},{2,6},{4,0},{6,2},{1,5},{3,7},{5,1},{7,3},{8,12},{10,14},{12... | collective-permute-start | bytes 1327112 | tf_op jit(solution)/shard_map/ppermute | solution.py:331
  79.0 20.1 %collective-permute-start.17 = (bf16[144,1536]{1,0:T(8,128)(2,1)S(1)}, bf16[144,1536]{1,0:T(8,128)(2,1)S(1)}, u32[]{:S(2)}, u32[]{:S(2)}) collective-permute-start(bf16[144,1536]{1,0:T(8,128)(2,1)S(1)} %stack_rows.8.refs_0_), channel_id=1, source_target_pairs={{0,2},{2,0},{4,6},{6,4},{1,3},{3,1},{5,7},{7,5},{8,10},{10,8},{12,... | collective-permute-start | bytes 1327112 | tf_op jit(solution)/shard_map/ppermute | solution.py:331
  103.2 15.0 %collective-permute-start.20 = (bf16[1024,768]{1,0:T(8,128)(2,1)S(1)}, bf16[1024,768]{1,0:T(8,128)(2,1)S(1)}, u32[]{:S(2)}, u32[]{:S(2)}) collective-permute-start(bf16[1024,768]{1,0:T(8,128)(2,1)S(1)} %get-tuple-element.251.mine_ref), channel_id=1, source_target_pairs={{0,1},{1,0},{2,3},{3,2},{4,5},{5,4},{6,7},{7,6},{8,9},{9,8},{10,11... | collective-permute-start | bytes 4718600 | tf_op jit(solution)/shard_map/ppermute | solution.py:331
  104.8 11.0 %collective-permute-start.22 = (bf16[128,768]{1,0:T(8,128)(2,1)S(1)}, bf16[128,768]{1,0:T(8,128)(2,1)S(1)}, u32[]{:S(2)}, u32[]{:S(2)}) collective-permute-start(bf16[128,768]{1,0:T(8,128)(2,1)S(1)} %get-tuple-element.461), channel_id=1, source_target_pairs={{0,4},{2,6},{4,0},{6,2},{1,5},{3,7},{5,1},{7,3},{8,12},{10,14},{12... | collective-permute-start | bytes 589832 | tf_op jit(solution)/shard_map/ppermute | solution.py:331
  106.2 9.6 %collective-permute-start.21 = (bf16[128,768]{1,0:T(8,128)(2,1)S(1)}, bf16[128,768]{1,0:T(8,128)(2,1)S(1)}, u32[]{:S(2)}, u32[]{:S(2)}) collective-permute-start(bf16[128,768]{1,0:T(8,128)(2,1)S(1)} %get-tuple-element.462), channel_id=1, source_target_pairs={{0,2},{2,0},{4,6},{6,4},{1,3},{3,1},{5,7},{7,5},{8,10},{10,8},{12,... | collective-permute-start | bytes 589832 | tf_op jit(solution)/shard_map/ppermute | solution.py:331
  123.3 14.7 %collective-permute-start.27 = (bf16[128,768]{1,0:T(8,128)(2,1)S(1)}, bf16[128,768]{1,0:T(8,128)(2,1)S(1)}, u32[]{:S(2)}, u32[]{:S(2)}) collective-permute-start(bf16[128,768]{1,0:T(8,128)(2,1)S(1)} %get-tuple-element.456), channel_id=1, source_target_pairs={{0,6},{2,4},{4,2},{6,0},{1,7},{3,5},{5,3},{7,1},{8,14},{10,12},{12... | collective-permute-start | bytes 589832 | tf_op jit(solution)/shard_map/ppermute | solution.py:331
  124.8 13.2 %collective-permute-start.26 = (bf16[128,768]{1,0:T(8,128)(2,1)S(1)}, bf16[128,768]{1,0:T(8,128)(2,1)S(1)}, u32[]{:S(2)}, u32[]{:S(2)}) collective-permute-start(bf16[128,768]{1,0:T(8,128)(2,1)S(1)} %get-tuple-element.457), channel_id=1, source_target_pairs={{0,4},{2,6},{4,0},{6,2},{1,5},{3,7},{5,1},{7,3},{8,12},{10,14},{12... | collective-permute-start | bytes 589832 | tf_op jit(solution)/shard_map/ppermute | solution.py:331
  126.2 11.8 %collective-permute-start.25 = (bf16[128,768]{1,0:T(8,128)(2,1)S(1)}, bf16[128,768]{1,0:T(8,128)(2,1)S(1)}, u32[]{:S(2)}, u32[]{:S(2)}) collective-permute-start(bf16[128,768]{1,0:T(8,128)(2,1)S(1)} %get-tuple-element.458), channel_id=1, source_target_pairs={{0,2},{2,0},{4,6},{6,4},{1,3},{3,1},{5,7},{7,5},{8,10},{10,8},{12,... | collective-permute-start | bytes 589832 | tf_op jit(solution)/shard_map/ppermute | solution.py:331
  138.0 11.1 %collective-permute-start.28 = (bf16[1024,768]{1,0:T(8,128)(2,1)S(1)}, bf16[1024,768]{1,0:T(8,128)(2,1)S(1)}, u32[]{:S(2)}, u32[]{:S(2)}) collective-permute-start(bf16[1024,768]{1,0:T(8,128)(2,1)S(1)} %rows_times.4.mine_ref), channel_id=1, source_target_pairs={{0,1},{1,0},{2,3},{3,2},{4,5},{5,4},{6,7},{7,6},{8,9},{9,8},{10,11... | collective-permute-start | bytes 4718600 | tf_op jit(solution)/shard_map/ppermute | solution.py:331
  138.1 35.4 %collective-permute-start.30 = (bf16[384,1536]{1,0:T(8,128)(2,1)S(1)}, bf16[384,1536]{1,0:T(8,128)(2,1)S(1)}, u32[]{:S(2)}, u32[]{:S(2)}) collective-permute-start(bf16[384,1536]{1,0:T(8,128)(2,1)S(1)} %get-tuple-element.276), channel_id=1, source_target_pairs={{0,8},{8,0},{16,24},{24,16},{1,9},{9,1},{17,25},{25,17},{2,10},{10... | collective-permute-start | bytes 3538952 | tf_op jit(solution)/shard_map/ppermute | solution.py:331
  144.8 36.7 %collective-permute-start.36 = (bf16[192,1536]{1,0:T(8,128)(2,1)S(1)}, bf16[192,1536]{1,0:T(8,128)(2,1)S(1)}, u32[]{:S(2)}, u32[]{:S(2)}) collective-permute-start(bf16[192,1536]{1,0:T(8,128)(2,1)S(1)} %get-tuple-element.302), channel_id=1, source_target_pairs={{0,2},{2,0},{4,6},{6,4},{1,3},{3,1},{5,7},{7,5},{8,10},{10,8},{12,... | collective-permute-start | bytes 1769480 | tf_op jit(solution)/shard_map/ppermute | solution.py:331
  146.2 36.7 %collective-permute-start.37 = (bf16[192,1536]{1,0:T(8,128)(2,1)S(1)}, bf16[192,1536]{1,0:T(8,128)(2,1)S(1)}, u32[]{:S(2)}, u32[]{:S(2)}) collective-permute-start(bf16[192,1536]{1,0:T(8,128)(2,1)S(1)} %get-tuple-element.303), channel_id=1, source_target_pairs={{0,4},{2,6},{4,0},{6,2},{1,5},{3,7},{5,1},{7,3},{8,12},{10,14},{12... | collective-permute-start | bytes 1769480 | tf_op jit(solution)/shard_map/ppermute | solution.py:331
  155.5 19.4 %collective-permute-start.31 = (bf16[384,384]{1,0:T(8,128)(2,1)S(1)}, bf16[384,384]{1,0:T(8,128)(2,1)S(1)}, u32[]{:S(2)}, u32[]{:S(2)}) collective-permute-start(bf16[384,384]{1,0:T(8,128)(2,1)S(1)} %get-tuple-element.277), channel_id=1, source_target_pairs={{0,8},{8,0},{16,24},{24,16},{1,9},{9,1},{17,25},{25,17},{2,10},{10... | collective-permute-start | bytes 884744 | tf_op jit(solution)/shard_map/ppermute | solution.py:331
  155.8 28.5 %collective-permute-start.38 = (bf16[192,1536]{1,0:T(8,128)(2,1)S(1)}, bf16[192,1536]{1,0:T(8,128)(2,1)S(1)}, u32[]{:S(2)}, u32[]{:S(2)}) collective-permute-start(bf16[192,1536]{1,0:T(8,128)(2,1)S(1)} %get-tuple-element.304), channel_id=1, source_target_pairs={{0,6},{2,4},{4,2},{6,0},{1,7},{3,5},{5,3},{7,1},{8,14},{10,12},{12... | collective-permute-start | bytes 1769480 | tf_op jit(solution)/shard_map/ppermute | solution.py:331
  179.6 27.9 %collective-permute-start.40 = (bf16[192,1536]{1,0:T(8,128)(2,1)S(1)}, bf16[192,1536]{1,0:T(8,128)(2,1)S(1)}, u32[]{:S(2)}, u32[]{:S(2)}) collective-permute-start(bf16[192,1536]{1,0:T(8,128)(2,1)S(1)} %get-tuple-element.314), channel_id=1, source_target_pairs={{0,16},{8,24},{16,0},{24,8},{1,17},{9,25},{17,1},{25,9},{2,18},{10... | collective-permute-start | bytes 1769480 | tf_op jit(solution)/shard_map/ppermute | solution.py:331
  180.8 21.7 %collective-permute-start.33 = (bf16[192,1152]{1,0:T(8,128)(2,1)S(1)}, bf16[192,1152]{1,0:T(8,128)(2,1)S(1)}, u32[]{:S(2)}, u32[]{:S(2)}) collective-permute-start(bf16[192,1152]{1,0:T(8,128)(2,1)S(1)} %get-tuple-element.294), channel_id=1, source_target_pairs={{0,2},{2,0},{4,6},{6,4},{1,3},{3,1},{5,7},{7,5},{8,10},{10,8},{12,... | collective-permute-start | bytes 1327112 | tf_op jit(solution)/shard_map/ppermute | solution.py:331
  181.5 21.0 %collective-permute-start.34 = (bf16[192,1152]{1,0:T(8,128)(2,1)S(1)}, bf16[192,1152]{1,0:T(8,128)(2,1)S(1)}, u32[]{:S(2)}, u32[]{:S(2)}) collective-permute-start(bf16[192,1152]{1,0:T(8,128)(2,1)S(1)} %get-tuple-element.295), channel_id=1, source_target_pairs={{0,4},{2,6},{4,0},{6,2},{1,5},{3,7},{5,1},{7,3},{8,12},{10,14},{12... | collective-permute-start | bytes 1327112 | tf_op jit(solution)/shard_map/ppermute | solution.py:331
  182.9 19.6 %collective-permute-start.35 = (bf16[192,1152]{1,0:T(8,128)(2,1)S(1)}, bf16[192,1152]{1,0:T(8,128)(2,1)S(1)}, u32[]{:S(2)}, u32[]{:S(2)}) collective-permute-start(bf16[192,1152]{1,0:T(8,128)(2,1)S(1)} %get-tuple-element.296), channel_id=1, source_target_pairs={{0,6},{2,4},{4,2},{6,0},{1,7},{3,5},{5,3},{7,1},{8,14},{10,12},{12... | collective-permute-start | bytes 1327112 | tf_op jit(solution)/shard_map/ppermute | solution.py:331
  184.3 18.1 %collective-permute-start.39 = (f32[16,768]{1,0:T(8,128)S(1)}, f32[16,768]{1,0:T(8,128)S(1)}, u32[]{:S(2)}, u32[]{:S(2)}) collective-permute-start(f32[16,768]{1,0:T(8,128)S(1)} %add.72), channel_id=1, source_target_pairs={{0,4},{2,6},{4,0},{6,2},{1,5},{3,7},{5,1},{7,3},{8,12},{10,14},{12... | collective-permute-start | bytes 147464 | tf_op jit(solution)/shard_map/ppermute | solution.py:331
  207.5 8.9 %collective-permute-start.42 = (bf16[4,128,768]{2,1,0:T(8,128)(2,1)S(1)}, bf16[4,128,768]{2,1,0:T(8,128)(2,1)S(1)}, u32[]{:S(2)}, u32[]{:S(2)}) collective-permute-start(bf16[4,128,768]{2,1,0:T(8,128)(2,1)S(1)} %get-tuple-element.320), channel_id=1, source_target_pairs={{0,1},{1,0},{2,3},{3,2},{4,5},{5,4},{6,7},{7,6},{8,9},{9,8},{10,11... | collective-permute-start | bytes 2359304 | tf_op jit(solution)/shard_map/ppermute | solution.py:331
  209.7 15.2 %collective-permute-start.46 = (bf16[192,1536]{1,0:T(8,128)(2,1)S(1)}, bf16[192,1536]{1,0:T(8,128)(2,1)S(1)}, u32[]{:S(2)}, u32[]{:S(2)}) collective-permute-start(bf16[192,1536]{1,0:T(8,128)(2,1)S(1)} %add_convert_fusion.2), channel_id=1, source_target_pairs={{0,2},{2,0},{4,6},{6,4},{1,3},{3,1},{5,7},{7,5},{8,10},{10,8},{12,... | collective-permute-start | bytes 1769480 | tf_op jit(solution)/shard_map/ppermute | solution.py:331
  216.7 12.1 %collective-permute-start.45 = (bf16[96,1536]{1,0:T(8,128)(2,1)S(1)}, bf16[96,1536]{1,0:T(8,128)(2,1)S(1)}, u32[]{:S(2)}, u32[]{:S(2)}) collective-permute-start(bf16[96,1536]{1,0:T(8,128)(2,1)S(1)} %get-tuple-element.336), channel_id=1, source_target_pairs={{0,8},{8,0},{16,24},{24,16},{1,9},{9,1},{17,25},{25,17},{2,10},{10... | collective-permute-start | bytes 884744 | tf_op jit(solution)/shard_map/ppermute | solution.py:331
  229.0 17.3 %collective-permute-start.52 = (bf16[192,1536]{1,0:T(8,128)(2,1)S(1)}, bf16[192,1536]{1,0:T(8,128)(2,1)S(1)}, u32[]{:S(2)}, u32[]{:S(2)}) collective-permute-start(bf16[192,1536]{1,0:T(8,128)(2,1)S(1)} %add_convert_fusion.1), channel_id=1, source_target_pairs={{0,4},{2,6},{4,0},{6,2},{1,5},{3,7},{5,1},{7,3},{8,12},{10,14},{12... | collective-permute-start | bytes 1769480 | tf_op jit(solution)/shard_map/ppermute | solution.py:331
  229.8 16.6 %collective-permute-start.50 = (bf16[48,1536]{1,0:T(8,128)(2,1)S(1)}, bf16[48,1536]{1,0:T(8,128)(2,1)S(1)}, u32[]{:S(2)}, u32[]{:S(2)}) collective-permute-start(bf16[48,1536]{1,0:T(8,128)(2,1)S(1)} %get-tuple-element.354), channel_id=1, source_target_pairs={{0,16},{8,24},{16,0},{24,8},{1,17},{9,25},{17,1},{25,9},{2,18},{10... | collective-permute-start | bytes 442376 | tf_op jit(solution)/shard_map/ppermute | solution.py:331
  231.0 15.3 %collective-permute-start.51 = (bf16[192,384]{1,0:T(8,128)(2,1)S(1)}, bf16[192,384]{1,0:T(8,128)(2,1)S(1)}, u32[]{:S(2)}, u32[]{:S(2)}) collective-permute-start(bf16[192,384]{1,0:T(8,128)(2,1)S(1)} %get-tuple-element.355), channel_id=1, source_target_pairs={{0,16},{8,24},{16,0},{24,8},{1,17},{9,25},{17,1},{25,9},{2,18},{10... | collective-permute-start | bytes 442376 | tf_op jit(solution)/shard_map/ppermute | solution.py:331
  232.7 13.0 %collective-permute-start.49 = (bf16[48,1152]{1,0:T(8,128)(2,1)S(1)}, bf16[48,1152]{1,0:T(8,128)(2,1)S(1)}, u32[]{:S(2)}, u32[]{:S(2)}) collective-permute-start(bf16[48,1152]{1,0:T(8,128)(2,1)S(1)} %add_convert_fusion.6.refs_2_), channel_id=1, source_target_pairs={{0,4},{2,6},{4,0},{6,2},{1,5},{3,7},{5,1},{7,3},{8,12},{10,14},{12... | collective-permute-start | bytes 331784 | tf_op jit(solution)/shard_map/ppermute | solution.py:331
  234.1 12.3 %collective-permute-start.48 = (bf16[48,1152]{1,0:T(8,128)(2,1)S(1)}, bf16[48,1152]{1,0:T(8,128)(2,1)S(1)}, u32[]{:S(2)}, u32[]{:S(2)}) collective-permute-start(bf16[48,1152]{1,0:T(8,128)(2,1)S(1)} %add_convert_fusion.6.refs_2_), channel_id=1, source_target_pairs={{0,2},{2,0},{4,6},{6,4},{1,3},{3,1},{5,7},{7,5},{8,10},{10,8},{12,... | collective-permute-start | bytes 331784 | tf_op jit(solution)/shard_map/ppermute | solution.py:331
  246.5 12.0 %collective-permute-start.57 = (bf16[128,768]{1,0:T(8,128)(2,1)S(1)}, bf16[128,768]{1,0:T(8,128)(2,1)S(1)}, u32[]{:S(2)}, u32[]{:S(2)}) collective-permute-start(bf16[128,768]{1,0:T(8,128)(2,1)S(1)} %get-tuple-element.371), channel_id=1, source_target_pairs={{0,4},{2,6},{4,0},{6,2},{1,5},{3,7},{5,1},{7,3},{8,12},{10,14},{12... | collective-permute-start | bytes 589832 | tf_op jit(solution)/shard_map/ppermute | solution.py:331
  247.9 10.5 %collective-permute-start.58 = (bf16[128,768]{1,0:T(8,128)(2,1)S(1)}, bf16[128,768]{1,0:T(8,128)(2,1)S(1)}, u32[]{:S(2)}, u32[]{:S(2)}) collective-permute-start(bf16[128,768]{1,0:T(8,128)(2,1)S(1)} %get-tuple-element.372), channel_id=1, source_target_pairs={{0,6},{2,4},{4,2},{6,0},{1,7},{3,5},{5,3},{7,1},{8,14},{10,12},{12... | collective-permute-start | bytes 589832 | tf_op jit(solution)/shard_map/ppermute | solution.py:331
  249.4 9.1 %collective-permute-start.55 = (bf16[48,1536]{1,0:T(8,128)(2,1)S(1)}, bf16[48,1536]{1,0:T(8,128)(2,1)S(1)}, u32[]{:S(2)}, u32[]{:S(2)}) collective-permute-start(bf16[48,1536]{1,0:T(8,128)(2,1)S(1)} %add_convert_fusion.5.refs_2_), channel_id=1, source_target_pairs={{0,4},{2,6},{4,0},{6,2},{1,5},{3,7},{5,1},{7,3},{8,12},{10,14},{12... | collective-permute-start | bytes 442376 | tf_op jit(solution)/shard_map/ppermute | solution.py:331
  265.5 10.6 %collective-permute-start.62 = (bf16[4,128,768]{2,1,0:T(8,128)(2,1)S(1)}, bf16[4,128,768]{2,1,0:T(8,128)(2,1)S(1)}, u32[]{:S(2)}, u32[]{:S(2)}) collective-permute-start(bf16[4,128,768]{2,1,0:T(8,128)(2,1)S(1)} %bitcast.61), channel_id=1, source_target_pairs={{0,1},{1,0},{2,3},{3,2},{4,5},{5,4},{6,7},{7,6},{8,9},{9,8},{10,11... | collective-permute-start | bytes 2359304 | tf_op jit(solution)/shard_map/ppermute | solution.py:331
  266.7 12.0 %collective-permute-start.61 = (bf16[192,384]{1,0:T(8,128)(2,1)S(1)}, bf16[192,384]{1,0:T(8,128)(2,1)}, u32[]{:S(2)}, u32[]{:S(2)}) collective-permute-start(bf16[192,384]{1,0:T(8,128)(2,1)S(1)} %add_convert_fusion.3), channel_id=1, source_target_pairs={{0,4},{2,6},{4,0},{6,2},{1,5},{3,7},{5,1},{7,3},{8,12},{10,14},{12... | collective-permute-start | bytes 442376 | tf_op jit(solution)/shard_map/ppermute | solution.py:331
  (35 other events, 269.2 us)

commit v6 on v5

--- a/solution.py
+++ b/solution.py
@@ -761,6 +761,28 @@
     )(*parts)
 
 
+def join_rows_kernel(ratio_ref, *refs):
+    out_ref, start = refs[-1], 0
+    for first, second in zip(refs[0:-1:2], refs[1:-1:2]):
+        total = first[...].astype(jnp.float32) + second[...].astype(jnp.float32)
+        out_ref[start : start + first.shape[0], :] = total * ratio_ref[0]
+        start += first.shape[0]
+
+
+def join_rows(pairs, ratio):
+    rows = sum(first.shape[0] for first, _ in pairs)
+    operands = [item for pair in pairs for item in pair]
+    vmem = pl.BlockSpec(memory_space=pltpu.VMEM)
+    return pl.pallas_call(
+        join_rows_kernel,
+        in_specs=[pl.BlockSpec(memory_space=pltpu.SMEM)] + [vmem] * len(operands),
+        out_specs=vmem,
+        out_shape=jax.ShapeDtypeStruct((rows, operands[0].shape[1]), jnp.float32),
+        name="join_rows",
+        compiler_params=pltpu.CompilerParams(vmem_limit_bytes=8 << 20),
+    )(ratio.reshape(1), *operands)
+
+
 def place_kernel(places, ratio_ref, *refs, kinds):
     part_refs, out_ref = refs[:-1], refs[-1]
     rows, columns = part_refs[0].shape
@@ -1017,8 +1039,12 @@
     )
     last_brought = swap(last_sent, "fsdp", 1)
     other = swap(other, "tp", 1)
-    owned_down = low(wide(down_kept) + wide(down_brought))
-    down_other = swap(owned_down, "ctx", 1)
+    cut = down_kept.shape[0] // 2
+    owned_down = [
+        low(wide(down_kept[span]) + wide(down_brought[span]))
+        for span in (slice(0, cut), slice(cut, 2 * cut))
+    ]
+    down_other = [swap(owned_down[0], "ctx", 1), swap(owned_down[1], "ctx", 2)]
     small = small + small_other
     small_other = swap(small, "fsdp", 1)
     last_brought, other, up_sent, out_sent, small, small_other = together(
@@ -1035,20 +1061,20 @@
     half_pieces = [half[s] for s in range(ctx_count)]
     half_brought = [half_pieces[0], swap(half_pieces[1], "ctx", 1)]
     small_other = swap(small, "fsdp", 2)
-    last_brought, up_brought, down_other, out_sent, small_other, half_pieces = together(
-        last_brought, up_brought, down_other, out_sent, small_other, half_pieces
+    out_brought = swap(out_sent, "fsdp", 2)
+    last_brought, up_brought, down_other, out_brought, small_other, half_pieces = together(
+        last_brought, up_brought, down_other, out_brought, small_other, half_pieces
     )
     part = low(wide(last_kept) + wide(last_brought))
     up_kept, up_sent = sum_and_cut([up_kept, up_brought])
-    owned_down = low(wide(owned_down) + wide(down_other))
+    owned_down = [low(wide(mine) + wide(other)) for mine, other in zip(owned_down, down_other)]
     small = small + small_other
-    part, up_sent, owned_down, out_sent, small, half_pieces = together(
-        part, up_sent, owned_down, out_sent, small, half_pieces
+    part, up_sent, owned_down, out_brought, small, half_pieces = together(
+        part, up_sent, owned_down, out_brought, small, half_pieces
     )
     shared = [part, swap(part, "ctx", 1), swap(part, "ctx", 2)]
     up_brought = swap(up_sent, "fsdp", 2)
-    out_brought = swap(out_sent, "fsdp", 2)
-    down_other = swap(owned_down, "ctx", 2)
+    down_other = [swap(owned_down[0], "ctx", 2), swap(owned_down[1], "ctx", 1)]
     shared, up_brought, out_brought, half_pieces, down_other = together(
         shared, up_brought, out_brought, half_pieces, down_other
     )
@@ -1058,7 +1084,9 @@
     shared = shared + [swap(shared[1], "ctx", 2)]
     up_shared = [up_part, swap(up_part, "ctx", 1), swap(up_part, "ctx", 2)]
     half_brought = half_brought + [swap(half_pieces[s], "ctx", s) for s in range(2, ctx_count)]
-    up_shared, half_brought, owned_out = together(up_shared, half_brought, owned_out)
+    up_shared, shared, half_brought, owned_out = together(
+        up_shared, shared, half_brought, owned_out
+    )
     up_shared = up_shared + [swap(up_shared[1], "ctx", 2)]
     input_half = stack_rows(half_brought).reshape(half.shape)
     out_other = swap(owned_out, "ctx", 1)
@@ -1075,12 +1103,12 @@
     scaled = small * ratio
     input_grad = join_halves(seat, input_half, ratio, jnp.float32)
     owned_qkv = place_rows(places, shared, ratio, 3)
-    owned_qkv, up_shared, down_other, out_other, input_grad, scaled = together(
-        owned_qkv, up_shared, down_other, out_other, input_grad, scaled
+    owned_down = join_rows(list(zip(owned_down, down_other)), ratio)
+    owned_up = place_rows(places, up_shared, ratio)
+    owned_qkv, owned_up, owned_down, out_other, input_grad, scaled = together(
+        owned_qkv, owned_up, owned_down, out_other, input_grad, scaled
     )
     owned_qkv = owned_qkv.reshape(qkv_weight.shape)
-    owned_up = place_rows(places, up_shared, ratio)
-    owned_down = (wide(owned_down) + wide(down_other)) * ratio
     owned_out = (wide(owned_out) + wide(out_other)) * ratio
     grad_up_bias = scaled[7:at].reshape(-1)[:hidden_width]
     grad_qv_bias = by_kinds(

time: 288 us -> 282 us (0.979)
  waiting for transfers between devices: 106 us -> 99.4 us
    ppermute x63 -> x65, waiting for transfers between devices: 104 us -> 97.6 us  [swap(): return lax.ppermute(values, axis, pairs)]
    ppermute x63 -> x65, starting transfers between devices: 68.7 us -> 70.2 us  [swap(): return lax.ppermute(values, axis, pairs)]
  transfers between devices with their start and end apart: 64 -> 66, of which waited for: 25 -> 23; matrix products, arithmetic and copies ran while one was open for 2% -> 2% of each run, Pallas kernels for 26% -> 28%
where the time goes in v6:
time: 282 us
  waiting for transfers between devices  99.4 us (35%)
  Pallas kernels  89.4 us (32%)
  starting transfers between devices  74.2 us (26%)
  local copies, waits for them, and re-layouts  10.8 us (4%)
  between operations  4.57 us (2%)
  other arithmetic  3.15 us (1%)
    ppermute x65, waiting for transfers between devices, swap(): return lax.ppermute(values, axis, pairs)  97.6 us
    ppermute x65, starting transfers between devices, swap(): return lax.ppermute(values, axis, pairs)  70.2 us
    pallas_call x1, Pallas kernels, attend_back(): pl.pallas_call(lambda *refs: attend_back_kernel(*refs, block=block), grid...  15.5 us
    pallas_call x4, Pallas kernels, weight_grad(): pl.pallas_call(lambda *refs: weight_grad_kernel(*refs, chunks=chunks, fsd...  13.9 us
    pallas_call x3, Pallas kernels, gathered_layer(): pl.pallas_call(kernel, grid_spec=pltpu.PrefetchScalarGridSpec(num_scalar_...  13 us
    pallas_call x1, Pallas kernels, attend(): pl.pallas_call(lambda *refs: attend_kernel(*refs, block=block), grid_spec...  10.8 us
    pallas_call x3, Pallas kernels, by_rows(): pl.pallas_call(kernel, grid_spec=pltpu.PrefetchScalarGridSpec(num_scalar_...  9.85 us
    pallas_call x3, Pallas kernels, rows_times(): pl.pallas_call(lambda *refs: rows_kernel(*refs, transposed=transposed), g...  6.4 us
  transfers between devices with their start and end apart: 66, of which 23 were waited for; matrix products, arithmetic and copies ran while one was open for 2% of the time, Pallas kernels for 28%

profile of v6, /device:TPU:0, one launch (start us, length us, event | category | flops | bytes accessed | tf_op | source)
XLA Modules:
  0.0 281.5 jit_solution(7563329504710416431)
XLA Ops:
  5.0 5.0 %collective-permute-start.2 = (bf16[48,1536]{1,0:T(8,128)(2,1)}, bf16[48,1536]{1,0:T(8,128)(2,1)S(1)}, u32[]{:S(2)}, u32[]{:S(2)}) collective-permute-start(bf16[48,1536]{1,0:T(8,128)(2,1)} %constant_dynamic-slice_fusion.2), channel_id=1, source_target_pairs={{0,24},{8,16},{16,8},{24,0},{1,25},{9,17},{17,9},{25,1},{2,26},{10... | collective-permute-start | bytes 442376 | tf_op jit(solution)/shard_map/ppermute | solution.py:331
  10.6 3.9 %all-to-all-start = ((bf16[4,128,768]{2,1,0:T(8,128)(2,1)}), bf16[4,128,768]{2,1,0:T(8,128)(2,1)S(1)}, u32[]{:S(2)}, u32[]{:S(2)}) async-start(bf16[4,128,768]{2,1,0:T(8,128)(2,1)} %constant_dynamic-slice_fusion.3), calls=%async_computation | async-start | bytes 1572864 | tf_op jit(solution)/shard_map/all_to_all | solution.py:382
  18.4 4.4 %collective-permute-done.1.refs_1_ = bf16[48,1536]{1,0:T(8,128)(2,1)} collective-permute-done((bf16[48,1536]{1,0:T(8,128)(2,1)}, bf16[48,1536]{1,0:T(8,128)(2,1)}, u32[]{:S(2)}, u32[]{:S(2)}) %collective-permute-start.1) | collective-permute-done | bytes 147488 | tf_op jit(solution)/shard_map/ppermute | solution.py:331
  22.8 1.8 all-to-all-done.own_ref
  30.7 4.2 %collective-permute-done.7.refs_0_ = bf16[48,1536]{1,0:T(8,128)(2,1)S(1)} collective-permute-done((bf16[48,1536]{1,0:T(8,128)(2,1)}, bf16[48,1536]{1,0:T(8,128)(2,1)S(1)}, u32[]{:S(2)}, u32[]{:S(2)}) %collective-permute-start.7) | collective-permute-done | bytes 147488 | tf_op jit(solution)/shard_map/ppermute | solution.py:331
  34.8 2.4 collective-permute-start.8
  38.6 9.2 %collective-permute-done.8.refs_1_ = bf16[48,1536]{1,0:T(8,128)(2,1)S(1)} collective-permute-done((bf16[48,1536]{1,0:T(8,128)(2,1)}, bf16[48,1536]{1,0:T(8,128)(2,1)S(1)}, u32[]{:S(2)}, u32[]{:S(2)}) %collective-permute-start.8) | collective-permute-done | bytes 147488 | tf_op jit(solution)/shard_map/ppermute | solution.py:331
  47.8 2.1 collective-permute-done.9.refs_2_
  55.9 2.6 collective-permute-start.14
  58.5 3.5 %project.1 = (bf16[1024,1152]{1,0:T(8,128)(2,1)S(1)}, bf16[768,1536]{1,0:T(8,128)(2,1)S(1)}) custom-call(s32[2]{0:T(128)S(1)} %get-tuple-element.213.places.refs_0_, bf16[1024,768]{1,0:T(8,128)(2,1)S(1)} %bitcast.57, f32[1,1152]{1,0:T(1,128)S(1)} %reshape_reshape.3.bias_ref, bf16[192,1536]{1,0:T(8,128)(2,1)S(1)} %constant_dynamic-update-slice_fusion.own_ref, ...), custom_call_target="tpu_custom_call" | custom-call | tf_op jit(solution)/shard_map/project/pallas_call | solution.py:296
  63.5 10.8 %attend.1 = (bf16[1024,384]{1,0:T(8,128)(2,1)S(1)}, f32[3,2,1024]{2,1,0:T(2,128)S(1)}) custom-call(s32[3]{0:T(128)S(1)} %convert_element_type.128.refs_0_.facts, bf16[1024,1152]{1,0:T(8,128)(2,1)S(1)} %get-tuple-element.232.refs_1_.refs_2_.refs_3_, bf16[1024,1152]{1,0:T(8,128)(2,1)S(1)} %get-tuple-element.232.refs_1_.refs_2_.refs_3_, ...), custom_call_target="tpu_custom_call" | custom-call | tf_op jit(solution)/shard_map/attend/pallas_call | solution.py:174
  79.7 1.6 first_norm.1
  81.4 5.5 %up.1 = (bf16[1024,1536]{1,0:T(8,128)(2,1)S(1)}, bf16[1024,1536]{1,0:T(8,128)(2,1)S(1)}, bf16[768,1536]{1,0:T(8,128)(2,1)S(1)}) custom-call(s32[2]{0:T(128)S(1)} %get-tuple-element.213.places.refs_0_, bf16[1024,768]{1,0:T(8,128)(2,1)S(1)} %get-tuple-element.241.left_ref.refs_1_, f32[1,1536]{1,0:T(1,128)S(1)} %reshape.114.bias_ref, ...), custom_call_target="tpu_custom_call" | custom-call | tf_op jit(solution)/shard_map/up/pallas_call | solution.py:296
  86.9 3.1 %collective-permute-done.19.refs_3_ = bf16[144,1536]{1,0:T(8,128)(2,1)S(1)} collective-permute-done((bf16[144,1536]{1,0:T(8,128)(2,1)S(1)}, bf16[144,1536]{1,0:T(8,128)(2,1)S(1)}, u32[]{:S(2)}, u32[]{:S(2)}) %collective-permute-start.19) | collective-permute-done | bytes 442400 | tf_op jit(solution)/shard_map/ppermute | solution.py:331
  90.0 9.0 %collective-permute-done.18.refs_2_ = bf16[144,1536]{1,0:T(8,128)(2,1)S(1)} collective-permute-done((bf16[144,1536]{1,0:T(8,128)(2,1)S(1)}, bf16[144,1536]{1,0:T(8,128)(2,1)S(1)}, u32[]{:S(2)}, u32[]{:S(2)}) %collective-permute-start.18) | collective-permute-done | bytes 442400 | tf_op jit(solution)/shard_map/ppermute | solution.py:331
  99.1 4.0 %down.1 = (bf16[1024,768]{1,0:T(8,128)(2,1)S(1)}, bf16[768,1536]{1,0:T(8,128)(2,1)S(1)}) custom-call(s32[2]{0:T(128)S(1)} %get-tuple-element.213.places.refs_0_, bf16[1024,1536]{1,0:T(8,128)(2,1)S(1)} %get-tuple-element.250.left_ref.refs_2_, bf16[192,1536]{1,0:T(8,128)(2,1)S(1)} %copy-done.4, bf16[144,1536]{1,0:T(8,128)(2,1)S(1)} %stack_rows.8.refs_0_, ...), custom_call_target="tpu_custom_call" | custom-call | tf_op jit(solution)/shard_map/down/pallas_call | solution.py:296
  106.8 5.2 %collective-permute-done.23.refs_3_ = bf16[128,768]{1,0:T(8,128)(2,1)S(1)} collective-permute-done((bf16[128,768]{1,0:T(8,128)(2,1)S(1)}, bf16[128,768]{1,0:T(8,128)(2,1)S(1)}, u32[]{:S(2)}, u32[]{:S(2)}) %collective-permute-start.23) | collective-permute-done | bytes 196640 | tf_op jit(solution)/shard_map/ppermute | solution.py:331
  112.0 3.8 %collective-permute-done.22.refs_2_ = bf16[128,768]{1,0:T(8,128)(2,1)S(1)} collective-permute-done((bf16[128,768]{1,0:T(8,128)(2,1)S(1)}, bf16[128,768]{1,0:T(8,128)(2,1)S(1)}, u32[]{:S(2)}, u32[]{:S(2)}) %collective-permute-start.22) | collective-permute-done | bytes 196640 | tf_op jit(solution)/shard_map/ppermute | solution.py:331
  116.0 2.2 collective-permute-done.24.other_teacher_ref
  118.2 5.0 %second_norm.1 = (bf16[4,128,768]{2,1,0:T(8,128)(2,1)S(1)}, f32[1024,768]{1,0:T(8,128)S(1)}, bf16[1024,768]{1,0:T(8,128)(2,1)S(1)}, f32[8,768]{1,0:T(8,128)S(1)}) custom-call(s32[3]{0:T(128)S(1)} %convert_element_type.128.refs_0_.facts, f32[1024,768]{1,0:T(8,128)S(1)} %get-tuple-element.240.normal_ref, f32[1,768]{1,0:T(1,128)S(1)} %reshape.112.gain_ref.gain1_ref, ...), custom_call_target="tpu_custom_call" | custom-call | tf_op jit(solution)/shard_map/second_norm/pallas_call | solution.py:497
  126.9 4.0 %weight_grad.4 = (bf16[384,1536]{1,0:T(8,128)(2,1)S(1)}, bf16[384,1536]{1,0:T(8,128)(2,1)S(1)}) custom-call(s32[2]{0:T(128)S(1)} %get-tuple-element.213.places.refs_0_, bf16[1024,768]{1,0:T(8,128)(2,1)S(1)} %get-tuple-element.261.refs_1_.low_ref, bf16[1024,1536]{1,0:T(8,128)(2,1)S(1)} %get-tuple-element.250.left_ref.refs_2_), custom_call_target="tpu_custom_call" | custom-call | tf_op jit(solution)/shard_map/weight_grad/pallas_call | solution.py:717
  130.9 3.8 %grad_pre.1 = (bf16[1024,1536]{1,0:T(8,128)(2,1)S(1)}, f32[8,1536]{1,0:T(8,128)S(1)}) custom-call(bf16[1024,768]{1,0:T(8,128)(2,1)S(1)} %get-tuple-element.261.refs_1_.low_ref, bf16[768,1536]{1,0:T(8,128)(2,1)S(1)} %get-tuple-element.262.weight_ref, bf16[1024,1536]{1,0:T(8,128)(2,1)S(1)} %get-tuple-element.263.slope_ref), custom_call_target="tpu_custom_call" | custom-call | tf_op jit(solution)/shard_map/grad_pre/pallas_call | solution.py:531
  134.7 3.3 %rows_times.4.mine_ref = bf16[1024,768]{1,0:T(8,128)(2,1)S(1)} custom-call(bf16[1024,1536]{1,0:T(8,128)(2,1)S(1)} %get-tuple-element.304.refs_0_.refs_2_, bf16[768,1536]{1,0:T(8,128)(2,1)S(1)} %get-tuple-element.265.refs_1_), custom_call_target="tpu_custom_call" | custom-call | tf_op jit(solution)/shard_map/rows_times/pallas_call | solution.py:551
  138.1 2.4 collective-permute-start.30
  140.8 4.0 %weight_grad.7 = (bf16[192,1536]{1,0:T(8,128)(2,1)S(1)}, bf16[192,1536]{1,0:T(8,128)(2,1)S(1)}, bf16[192,1536]{1,0:T(8,128)(2,1)S(1)}, bf16[192,1536]{1,0:T(8,128)(2,1)S(1)}) custom-call(s32[2]{0:T(128)S(1)} %get-tuple-element.213.places.refs_0_, bf16[1024,768]{1,0:T(8,128)(2,1)S(1)} %get-tuple-element.241.left_ref.refs_1_, ...), custom_call_target="tpu_custom_call" | custom-call | tf_op jit(solution)/shard_map/weight_grad/pallas_call | solution.py:717
  146.8 2.3 join_halves.4
  149.2 3.2 %first_norm_back.1 = (bf16[1024,768]{1,0:T(8,128)(2,1)S(1)}, f32[4,128,768]{2,1,0:T(8,128)S(1)}, f32[8,768]{1,0:T(8,128)S(1)}) custom-call(s32[3]{0:T(128)S(1)} %convert_element_type.128.refs_0_.facts, f32[1024,768]{1,0:T(8,128)S(1)} %get-tuple-element.257.grad_ref, bf16[1024,768]{1,0:T(8,128)(2,1)S(1)} %rows_times.4.mine_ref, ...), custom_call_target="tpu_custom_call" | custom-call | tf_op jit(solution)/shard_map/first_norm_back/pallas_call | solution.py:497
  152.3 1.6 weight_grad.5
  157.3 15.5 %attend_back.1 = (bf16[1024,1152]{1,0:T(8,128)(2,1)S(1)}, f32[8,1152]{1,0:T(8,128)S(1)}) custom-call(s32[3]{0:T(128)S(1)} %convert_element_type.128.refs_0_.facts, bf16[1024,1152]{1,0:T(8,128)(2,1)S(1)} %get-tuple-element.232.refs_1_.refs_2_.refs_3_, bf16[1024,1152]{1,0:T(8,128)(2,1)S(1)} %get-tuple-element.232.refs_1_.refs_2_.refs_3_, ...), custom_call_target="tpu_custom_call" | custom-call | tf_op jit(solution)/shard_map/attend_back/pallas_call | solution.py:198
  174.9 4.3 %weight_grad.6 = (bf16[192,1152]{1,0:T(8,128)(2,1)S(1)}, bf16[192,1152]{1,0:T(8,128)(2,1)S(1)}, bf16[192,1152]{1,0:T(8,128)(2,1)S(1)}, bf16[192,1152]{1,0:T(8,128)(2,1)S(1)}) custom-call(s32[2]{0:T(128)S(1)} %get-tuple-element.213.places.refs_0_, bf16[1024,768]{1,0:T(8,128)(2,1)S(1)} %bitcast.59, bf16[1024,1152]{1,0:T(8,128)(2,1)S(1)} %get-tuple-element.301.refs_2_.grad_ref), custom_call_target="tpu_custom_call" | custom-call | tf_op jit(solution)/shard_map/weight_grad/pallas_call | solution.py:717
  185.3 3.9 %input_back.1 = (bf16[4,128,768]{2,1,0:T(8,128)(2,1)S(1)}, bf16[4,128,768]{2,1,0:T(8,128)(2,1)S(1)}) custom-call(s32[3]{0:T(128)S(1)} %convert_element_type.128.refs_0_.facts, bf16[1024,1152]{1,0:T(8,128)(2,1)S(1)} %get-tuple-element.301.refs_2_.grad_ref, bf16[768,1536]{1,0:T(8,128)(2,1)S(1)} %get-tuple-element.239.weight_ref), custom_call_target="tpu_custom_call" | custom-call | tf_op jit(solution)/shard_map/input_back/pallas_call | solution.py:597
  189.2 13.3 %collective-permute-done.39 = f32[16,768]{1,0:T(8,128)S(1)} collective-permute-done((f32[16,768]{1,0:T(8,128)S(1)}, f32[16,768]{1,0:T(8,128)S(1)}, u32[]{:S(2)}, u32[]{:S(2)}) %collective-permute-start.39) | collective-permute-done | bytes 49184 | tf_op jit(solution)/shard_map/ppermute | solution.py:331
  202.7 4.7 %collective-permute-done.40 = bf16[192,1536]{1,0:T(8,128)(2,1)S(1)} collective-permute-done((bf16[192,1536]{1,0:T(8,128)(2,1)S(1)}, bf16[192,1536]{1,0:T(8,128)(2,1)S(1)}, u32[]{:S(2)}, u32[]{:S(2)}) %collective-permute-start.40) | collective-permute-done | bytes 589856 | tf_op jit(solution)/shard_map/ppermute | solution.py:331
  207.5 2.0 collective-permute-start.41
  212.1 4.3 %collective-permute-done.41.refs_1_ = bf16[96,1152]{1,0:T(8,128)(2,1)S(1)} collective-permute-done((bf16[96,1152]{1,0:T(8,128)(2,1)S(1)}, bf16[96,1152]{1,0:T(8,128)(2,1)S(1)}, u32[]{:S(2)}, u32[]{:S(2)}) %collective-permute-start.41) | collective-permute-done | bytes 221216 | tf_op jit(solution)/shard_map/ppermute | solution.py:331
  217.5 1.8 collective-permute-start.49
  220.4 1.8 collective-permute-start.48
  222.4 3.7 %collective-permute-done.49 = f32[16,768]{1,0:T(8,128)S(1)} collective-permute-done((f32[16,768]{1,0:T(8,128)S(1)}, f32[16,768]{1,0:T(8,128)S(1)}, u32[]{:S(2)}, u32[]{:S(2)}) %collective-permute-start.49) | collective-permute-done | bytes 49184 | tf_op jit(solution)/shard_map/ppermute | solution.py:331
  226.1 6.8 %collective-permute-done.44 = bf16[48,1152]{1,0:T(8,128)(2,1)S(1)} collective-permute-done((bf16[48,1152]{1,0:T(8,128)(2,1)S(1)}, bf16[48,1152]{1,0:T(8,128)(2,1)S(1)}, u32[]{:S(2)}, u32[]{:S(2)}) %collective-permute-start.44) | collective-permute-done | bytes 110624 | tf_op jit(solution)/shard_map/ppermute | solution.py:331
  232.8 1.8 collective-permute-done.48
  239.0 6.0 %collective-permute-done.51.refs_4_ = bf16[48,1152]{1,0:T(8,128)(2,1)S(1)} collective-permute-done((bf16[48,1152]{1,0:T(8,128)(2,1)S(1)}, bf16[48,1152]{1,0:T(8,128)(2,1)S(1)}, u32[]{:S(2)}, u32[]{:S(2)}) %collective-permute-start.51) | collective-permute-done | bytes 110624 | tf_op jit(solution)/shard_map/ppermute | solution.py:331
  245.8 1.8 collective-permute-start.59
  249.3 1.8 collective-permute-start.55
  251.1 1.8 collective-permute-done.58.refs_1_
  253.5 6.6 %collective-permute-done.57.refs_5_ = bf16[48,1152]{1,0:T(8,128)(2,1)S(1)} collective-permute-done((bf16[48,1152]{1,0:T(8,128)(2,1)S(1)}, bf16[48,1152]{1,0:T(8,128)(2,1)S(1)}, u32[]{:S(2)}, u32[]{:S(2)}) %collective-permute-start.57) | collective-permute-done | bytes 110624 | tf_op jit(solution)/shard_map/ppermute | solution.py:331
  262.3 3.0 %collective-permute-done.61 = bf16[192,384]{1,0:T(8,128)(2,1)S(1)} collective-permute-done((bf16[192,384]{1,0:T(8,128)(2,1)S(1)}, bf16[192,384]{1,0:T(8,128)(2,1)S(1)}, u32[]{:S(2)}, u32[]{:S(2)}) %collective-permute-start.61) | collective-permute-done | bytes 147488 | tf_op jit(solution)/shard_map/ppermute | solution.py:331
  272.4 1.6 place_rows.3
  274.1 2.7 join_halves.5
  (213 shorter events, 73.8 us)
Async XLA Ops:
  5.0 13.4 %collective-permute-start.2 = (bf16[48,1536]{1,0:T(8,128)(2,1)}, bf16[48,1536]{1,0:T(8,128)(2,1)S(1)}, u32[]{:S(2)}, u32[]{:S(2)}) collective-permute-start(bf16[48,1536]{1,0:T(8,128)(2,1)} %constant_dynamic-slice_fusion.2), channel_id=1, source_target_pairs={{0,24},{8,16},{16,8},{24,0},{1,25},{9,17},{17,9},{25,1},{2,26},{10... | collective-permute-start | bytes 442376 | tf_op jit(solution)/shard_map/ppermute | solution.py:331
  10.0 12.8 %collective-permute-start.1 = (bf16[48,1536]{1,0:T(8,128)(2,1)}, bf16[48,1536]{1,0:T(8,128)(2,1)}, u32[]{:S(2)}, u32[]{:S(2)}) collective-permute-start(bf16[48,1536]{1,0:T(8,128)(2,1)} %constant_dynamic-slice_fusion.2), channel_id=1, source_target_pairs={{0,16},{8,24},{16,0},{24,8},{1,17},{9,25},{17,1},{25,9},{2,18},{10... | collective-permute-start | bytes 442376 | tf_op jit(solution)/shard_map/ppermute | solution.py:331
  10.0 12.8 %collective-permute-start = (bf16[48,1536]{1,0:T(8,128)(2,1)}, bf16[48,1536]{1,0:T(8,128)(2,1)}, u32[]{:S(2)}, u32[]{:S(2)}) collective-permute-start(bf16[48,1536]{1,0:T(8,128)(2,1)} %constant_dynamic-slice_fusion.2), channel_id=1, source_target_pairs={{0,8},{8,0},{16,24},{24,16},{1,9},{9,1},{17,25},{25,17},{2,10},{10... | collective-permute-start | bytes 442376 | tf_op jit(solution)/shard_map/ppermute | solution.py:331
  10.6 14.0 %all-to-all-start = ((bf16[4,128,768]{2,1,0:T(8,128)(2,1)}), bf16[4,128,768]{2,1,0:T(8,128)(2,1)S(1)}, u32[]{:S(2)}, u32[]{:S(2)}) async-start(bf16[4,128,768]{2,1,0:T(8,128)(2,1)} %constant_dynamic-slice_fusion.3), calls=%async_computation | async-start | bytes 1572864 | tf_op jit(solution)/shard_map/all_to_all | solution.py:382
  24.6 12.6 %collective-permute-start.6 = (bf16[4,128,768]{2,1,0:T(8,128)(2,1)S(1)}, bf16[4,128,768]{2,1,0:T(8,128)(2,1)S(1)}, u32[]{:S(2)}, u32[]{:S(2)}) collective-permute-start(bf16[4,128,768]{2,1,0:T(8,128)(2,1)S(1)} %all-to-all-done.own_ref), channel_id=1, source_target_pairs={{0,1},{1,0},{2,3},{3,2},{4,5},{5,4},{6,7},{7,6},{8,9},{9,8},{10,11... | collective-permute-start | bytes 2359304 | tf_op jit(solution)/shard_map/ppermute | solution.py:331
  25.6 24.3 %collective-permute-start.5 = (bf16[160,1536]{1,0:T(8,128)(2,1)S(1)}, bf16[160,1536]{1,0:T(8,128)(2,1)S(1)}, u32[]{:S(2)}, u32[]{:S(2)}) collective-permute-start(bf16[160,1536]{1,0:T(8,128)(2,1)S(1)} %stack_rows.6.refs_0_), channel_id=1, source_target_pairs={{0,6},{2,4},{4,2},{6,0},{1,7},{3,5},{5,3},{7,1},{8,14},{10,12},{12... | collective-permute-start | bytes 1474568 | tf_op jit(solution)/shard_map/ppermute | solution.py:331
  27.1 23.6 %collective-permute-start.4 = (bf16[160,1536]{1,0:T(8,128)(2,1)S(1)}, bf16[160,1536]{1,0:T(8,128)(2,1)S(1)}, u32[]{:S(2)}, u32[]{:S(2)}) collective-permute-start(bf16[160,1536]{1,0:T(8,128)(2,1)S(1)} %stack_rows.6.refs_0_), channel_id=1, source_target_pairs={{0,4},{2,6},{4,0},{6,2},{1,5},{3,7},{5,1},{7,3},{8,12},{10,14},{12... | collective-permute-start | bytes 1474568 | tf_op jit(solution)/shard_map/ppermute | solution.py:331
  28.6 22.2 %collective-permute-start.3 = (bf16[160,1536]{1,0:T(8,128)(2,1)S(1)}, bf16[160,1536]{1,0:T(8,128)(2,1)S(1)}, u32[]{:S(2)}, u32[]{:S(2)}) collective-permute-start(bf16[160,1536]{1,0:T(8,128)(2,1)S(1)} %stack_rows.6.refs_0_), channel_id=1, source_target_pairs={{0,2},{2,0},{4,6},{6,4},{1,3},{3,1},{5,7},{7,5},{8,10},{10,8},{12,... | collective-permute-start | bytes 1474568 | tf_op jit(solution)/shard_map/ppermute | solution.py:331
  34.8 13.0 %collective-permute-start.8 = (bf16[48,1536]{1,0:T(8,128)(2,1)}, bf16[48,1536]{1,0:T(8,128)(2,1)S(1)}, u32[]{:S(2)}, u32[]{:S(2)}) collective-permute-start(bf16[48,1536]{1,0:T(8,128)(2,1)} %get-tuple-element.220), channel_id=1, source_target_pairs={{0,16},{8,24},{16,0},{24,8},{1,17},{9,25},{17,1},{25,9},{2,18},{10... | collective-permute-start | bytes 442376 | tf_op jit(solution)/shard_map/ppermute | solution.py:331
  37.2 12.7 %collective-permute-start.9 = (bf16[48,1536]{1,0:T(8,128)(2,1)S(1)}, bf16[48,1536]{1,0:T(8,128)(2,1)S(1)}, u32[]{:S(2)}, u32[]{:S(2)}) collective-permute-start(bf16[48,1536]{1,0:T(8,128)(2,1)S(1)} %collective-permute-done.7.refs_0_), channel_id=1, source_target_pairs={{0,16},{8,24},{16,0},{24,8},{1,17},{9,25},{17,1},{25,9},{2,18},{10... | collective-permute-start | bytes 442376 | tf_op jit(solution)/shard_map/ppermute | solution.py:331
  50.8 23.4 %collective-permute-start.13 = (bf16[144,1536]{1,0:T(8,128)(2,1)S(1)}, bf16[144,1536]{1,0:T(8,128)(2,1)S(1)}, u32[]{:S(2)}, u32[]{:S(2)}) collective-permute-start(bf16[144,1536]{1,0:T(8,128)(2,1)S(1)} %stack_rows.7.refs_0_), channel_id=1, source_target_pairs={{0,6},{2,4},{4,2},{6,0},{1,7},{3,5},{5,3},{7,1},{8,14},{10,12},{12... | collective-permute-start | bytes 1327112 | tf_op jit(solution)/shard_map/ppermute | solution.py:331
  52.3 21.9 %collective-permute-start.12 = (bf16[144,1536]{1,0:T(8,128)(2,1)S(1)}, bf16[144,1536]{1,0:T(8,128)(2,1)S(1)}, u32[]{:S(2)}, u32[]{:S(2)}) collective-permute-start(bf16[144,1536]{1,0:T(8,128)(2,1)S(1)} %stack_rows.7.refs_0_), channel_id=1, source_target_pairs={{0,4},{2,6},{4,0},{6,2},{1,5},{3,7},{5,1},{7,3},{8,12},{10,14},{12... | collective-permute-start | bytes 1327112 | tf_op jit(solution)/shard_map/ppermute | solution.py:331
  53.7 20.5 %collective-permute-start.11 = (bf16[144,1536]{1,0:T(8,128)(2,1)S(1)}, bf16[144,1536]{1,0:T(8,128)(2,1)S(1)}, u32[]{:S(2)}, u32[]{:S(2)}) collective-permute-start(bf16[144,1536]{1,0:T(8,128)(2,1)S(1)} %stack_rows.7.refs_0_), channel_id=1, source_target_pairs={{0,2},{2,0},{4,6},{6,4},{1,3},{3,1},{5,7},{7,5},{8,10},{10,8},{12,... | collective-permute-start | bytes 1327112 | tf_op jit(solution)/shard_map/ppermute | solution.py:331
  55.9 18.4 %collective-permute-start.14 = (bf16[48,1536]{1,0:T(8,128)(2,1)S(1)}, bf16[48,1536]{1,0:T(8,128)(2,1)S(1)}, u32[]{:S(2)}, u32[]{:S(2)}) collective-permute-start(bf16[48,1536]{1,0:T(8,128)(2,1)S(1)} %copy-done.6), channel_id=1, source_target_pairs={{0,16},{8,24},{16,0},{24,8},{1,17},{9,25},{17,1},{25,9},{2,18},{10... | collective-permute-start | bytes 442376 | tf_op jit(solution)/shard_map/ppermute | solution.py:331
  62.0 12.2 %collective-permute-start.15 = (bf16[48,1536]{1,0:T(8,128)(2,1)S(1)}, bf16[48,1536]{1,0:T(8,128)(2,1)S(1)}, u32[]{:S(2)}, u32[]{:S(2)}) collective-permute-start(bf16[48,1536]{1,0:T(8,128)(2,1)S(1)} %collective-permute-done.10.refs_0_), channel_id=1, source_target_pairs={{0,16},{8,24},{16,0},{24,8},{1,17},{9,25},{17,1},{25,9},{2,18},{10... | collective-permute-start | bytes 442376 | tf_op jit(solution)/shard_map/ppermute | solution.py:331
  76.1 14.0 %collective-permute-start.19 = (bf16[144,1536]{1,0:T(8,128)(2,1)S(1)}, bf16[144,1536]{1,0:T(8,128)(2,1)S(1)}, u32[]{:S(2)}, u32[]{:S(2)}) collective-permute-start(bf16[144,1536]{1,0:T(8,128)(2,1)S(1)} %stack_rows.8.refs_0_), channel_id=1, source_target_pairs={{0,6},{2,4},{4,2},{6,0},{1,7},{3,5},{5,3},{7,1},{8,14},{10,12},{12... | collective-permute-start | bytes 1327112 | tf_op jit(solution)/shard_map/ppermute | solution.py:331
  77.6 21.5 %collective-permute-start.18 = (bf16[144,1536]{1,0:T(8,128)(2,1)S(1)}, bf16[144,1536]{1,0:T(8,128)(2,1)S(1)}, u32[]{:S(2)}, u32[]{:S(2)}) collective-permute-start(bf16[144,1536]{1,0:T(8,128)(2,1)S(1)} %stack_rows.8.refs_0_), channel_id=1, source_target_pairs={{0,4},{2,6},{4,0},{6,2},{1,5},{3,7},{5,1},{7,3},{8,12},{10,14},{12... | collective-permute-start | bytes 1327112 | tf_op jit(solution)/shard_map/ppermute | solution.py:331
  79.0 20.1 %collective-permute-start.17 = (bf16[144,1536]{1,0:T(8,128)(2,1)S(1)}, bf16[144,1536]{1,0:T(8,128)(2,1)S(1)}, u32[]{:S(2)}, u32[]{:S(2)}) collective-permute-start(bf16[144,1536]{1,0:T(8,128)(2,1)S(1)} %stack_rows.8.refs_0_), channel_id=1, source_target_pairs={{0,2},{2,0},{4,6},{6,4},{1,3},{3,1},{5,7},{7,5},{8,10},{10,8},{12,... | collective-permute-start | bytes 1327112 | tf_op jit(solution)/shard_map/ppermute | solution.py:331
  103.2 15.0 %collective-permute-start.20 = (bf16[1024,768]{1,0:T(8,128)(2,1)S(1)}, bf16[1024,768]{1,0:T(8,128)(2,1)S(1)}, u32[]{:S(2)}, u32[]{:S(2)}) collective-permute-start(bf16[1024,768]{1,0:T(8,128)(2,1)S(1)} %get-tuple-element.255.mine_ref), channel_id=1, source_target_pairs={{0,1},{1,0},{2,3},{3,2},{4,5},{5,4},{6,7},{7,6},{8,9},{9,8},{10,11... | collective-permute-start | bytes 4718600 | tf_op jit(solution)/shard_map/ppermute | solution.py:331
  104.8 11.0 %collective-permute-start.22 = (bf16[128,768]{1,0:T(8,128)(2,1)S(1)}, bf16[128,768]{1,0:T(8,128)(2,1)S(1)}, u32[]{:S(2)}, u32[]{:S(2)}) collective-permute-start(bf16[128,768]{1,0:T(8,128)(2,1)S(1)} %get-tuple-element.471), channel_id=1, source_target_pairs={{0,4},{2,6},{4,0},{6,2},{1,5},{3,7},{5,1},{7,3},{8,12},{10,14},{12... | collective-permute-start | bytes 589832 | tf_op jit(solution)/shard_map/ppermute | solution.py:331
  106.2 9.6 %collective-permute-start.21 = (bf16[128,768]{1,0:T(8,128)(2,1)S(1)}, bf16[128,768]{1,0:T(8,128)(2,1)S(1)}, u32[]{:S(2)}, u32[]{:S(2)}) collective-permute-start(bf16[128,768]{1,0:T(8,128)(2,1)S(1)} %get-tuple-element.472), channel_id=1, source_target_pairs={{0,2},{2,0},{4,6},{6,4},{1,3},{3,1},{5,7},{7,5},{8,10},{10,8},{12,... | collective-permute-start | bytes 589832 | tf_op jit(solution)/shard_map/ppermute | solution.py:331
  123.3 14.7 %collective-permute-start.27 = (bf16[128,768]{1,0:T(8,128)(2,1)S(1)}, bf16[128,768]{1,0:T(8,128)(2,1)S(1)}, u32[]{:S(2)}, u32[]{:S(2)}) collective-permute-start(bf16[128,768]{1,0:T(8,128)(2,1)S(1)} %get-tuple-element.466), channel_id=1, source_target_pairs={{0,6},{2,4},{4,2},{6,0},{1,7},{3,5},{5,3},{7,1},{8,14},{10,12},{12... | collective-permute-start | bytes 589832 | tf_op jit(solution)/shard_map/ppermute | solution.py:331
  124.8 13.2 %collective-permute-start.26 = (bf16[128,768]{1,0:T(8,128)(2,1)S(1)}, bf16[128,768]{1,0:T(8,128)(2,1)S(1)}, u32[]{:S(2)}, u32[]{:S(2)}) collective-permute-start(bf16[128,768]{1,0:T(8,128)(2,1)S(1)} %get-tuple-element.467), channel_id=1, source_target_pairs={{0,4},{2,6},{4,0},{6,2},{1,5},{3,7},{5,1},{7,3},{8,12},{10,14},{12... | collective-permute-start | bytes 589832 | tf_op jit(solution)/shard_map/ppermute | solution.py:331
  126.2 11.8 %collective-permute-start.25 = (bf16[128,768]{1,0:T(8,128)(2,1)S(1)}, bf16[128,768]{1,0:T(8,128)(2,1)S(1)}, u32[]{:S(2)}, u32[]{:S(2)}) collective-permute-start(bf16[128,768]{1,0:T(8,128)(2,1)S(1)} %get-tuple-element.468), channel_id=1, source_target_pairs={{0,2},{2,0},{4,6},{6,4},{1,3},{3,1},{5,7},{7,5},{8,10},{10,8},{12,... | collective-permute-start | bytes 589832 | tf_op jit(solution)/shard_map/ppermute | solution.py:331
  138.0 11.1 %collective-permute-start.28 = (bf16[1024,768]{1,0:T(8,128)(2,1)S(1)}, bf16[1024,768]{1,0:T(8,128)(2,1)S(1)}, u32[]{:S(2)}, u32[]{:S(2)}) collective-permute-start(bf16[1024,768]{1,0:T(8,128)(2,1)S(1)} %rows_times.4.mine_ref), channel_id=1, source_target_pairs={{0,1},{1,0},{2,3},{3,2},{4,5},{5,4},{6,7},{7,6},{8,9},{9,8},{10,11... | collective-permute-start | bytes 4718600 | tf_op jit(solution)/shard_map/ppermute | solution.py:331
  138.1 35.4 %collective-permute-start.30 = (bf16[384,1536]{1,0:T(8,128)(2,1)S(1)}, bf16[384,1536]{1,0:T(8,128)(2,1)S(1)}, u32[]{:S(2)}, u32[]{:S(2)}) collective-permute-start(bf16[384,1536]{1,0:T(8,128)(2,1)S(1)} %get-tuple-element.280), channel_id=1, source_target_pairs={{0,8},{8,0},{16,24},{24,16},{1,9},{9,1},{17,25},{25,17},{2,10},{10... | collective-permute-start | bytes 3538952 | tf_op jit(solution)/shard_map/ppermute | solution.py:331
  144.8 36.7 %collective-permute-start.36 = (bf16[192,1536]{1,0:T(8,128)(2,1)S(1)}, bf16[192,1536]{1,0:T(8,128)(2,1)S(1)}, u32[]{:S(2)}, u32[]{:S(2)}) collective-permute-start(bf16[192,1536]{1,0:T(8,128)(2,1)S(1)} %get-tuple-element.306), channel_id=1, source_target_pairs={{0,2},{2,0},{4,6},{6,4},{1,3},{3,1},{5,7},{7,5},{8,10},{10,8},{12,... | collective-permute-start | bytes 1769480 | tf_op jit(solution)/shard_map/ppermute | solution.py:331
  146.2 36.7 %collective-permute-start.37 = (bf16[192,1536]{1,0:T(8,128)(2,1)S(1)}, bf16[192,1536]{1,0:T(8,128)(2,1)S(1)}, u32[]{:S(2)}, u32[]{:S(2)}) collective-permute-start(bf16[192,1536]{1,0:T(8,128)(2,1)S(1)} %get-tuple-element.307), channel_id=1, source_target_pairs={{0,4},{2,6},{4,0},{6,2},{1,5},{3,7},{5,1},{7,3},{8,12},{10,14},{12... | collective-permute-start | bytes 1769480 | tf_op jit(solution)/shard_map/ppermute | solution.py:331
  155.5 19.4 %collective-permute-start.31 = (bf16[384,384]{1,0:T(8,128)(2,1)S(1)}, bf16[384,384]{1,0:T(8,128)(2,1)S(1)}, u32[]{:S(2)}, u32[]{:S(2)}) collective-permute-start(bf16[384,384]{1,0:T(8,128)(2,1)S(1)} %get-tuple-element.281), channel_id=1, source_target_pairs={{0,8},{8,0},{16,24},{24,16},{1,9},{9,1},{17,25},{25,17},{2,10},{10... | collective-permute-start | bytes 884744 | tf_op jit(solution)/shard_map/ppermute | solution.py:331
  155.8 28.5 %collective-permute-start.38 = (bf16[192,1536]{1,0:T(8,128)(2,1)S(1)}, bf16[192,1536]{1,0:T(8,128)(2,1)S(1)}, u32[]{:S(2)}, u32[]{:S(2)}) collective-permute-start(bf16[192,1536]{1,0:T(8,128)(2,1)S(1)} %get-tuple-element.308), channel_id=1, source_target_pairs={{0,6},{2,4},{4,2},{6,0},{1,7},{3,5},{5,3},{7,1},{8,14},{10,12},{12... | collective-permute-start | bytes 1769480 | tf_op jit(solution)/shard_map/ppermute | solution.py:331
  179.6 27.9 %collective-permute-start.40 = (bf16[192,1536]{1,0:T(8,128)(2,1)S(1)}, bf16[192,1536]{1,0:T(8,128)(2,1)S(1)}, u32[]{:S(2)}, u32[]{:S(2)}) collective-permute-start(bf16[192,1536]{1,0:T(8,128)(2,1)S(1)} %get-tuple-element.318), channel_id=1, source_target_pairs={{0,16},{8,24},{16,0},{24,8},{1,17},{9,25},{17,1},{25,9},{2,18},{10... | collective-permute-start | bytes 1769480 | tf_op jit(solution)/shard_map/ppermute | solution.py:331
  180.8 21.7 %collective-permute-start.33 = (bf16[192,1152]{1,0:T(8,128)(2,1)S(1)}, bf16[192,1152]{1,0:T(8,128)(2,1)S(1)}, u32[]{:S(2)}, u32[]{:S(2)}) collective-permute-start(bf16[192,1152]{1,0:T(8,128)(2,1)S(1)} %get-tuple-element.298), channel_id=1, source_target_pairs={{0,2},{2,0},{4,6},{6,4},{1,3},{3,1},{5,7},{7,5},{8,10},{10,8},{12,... | collective-permute-start | bytes 1327112 | tf_op jit(solution)/shard_map/ppermute | solution.py:331
  181.5 21.0 %collective-permute-start.34 = (bf16[192,1152]{1,0:T(8,128)(2,1)S(1)}, bf16[192,1152]{1,0:T(8,128)(2,1)S(1)}, u32[]{:S(2)}, u32[]{:S(2)}) collective-permute-start(bf16[192,1152]{1,0:T(8,128)(2,1)S(1)} %get-tuple-element.299), channel_id=1, source_target_pairs={{0,4},{2,6},{4,0},{6,2},{1,5},{3,7},{5,1},{7,3},{8,12},{10,14},{12... | collective-permute-start | bytes 1327112 | tf_op jit(solution)/shard_map/ppermute | solution.py:331
  182.9 19.6 %collective-permute-start.35 = (bf16[192,1152]{1,0:T(8,128)(2,1)S(1)}, bf16[192,1152]{1,0:T(8,128)(2,1)S(1)}, u32[]{:S(2)}, u32[]{:S(2)}) collective-permute-start(bf16[192,1152]{1,0:T(8,128)(2,1)S(1)} %get-tuple-element.300), channel_id=1, source_target_pairs={{0,6},{2,4},{4,2},{6,0},{1,7},{3,5},{5,3},{7,1},{8,14},{10,12},{12... | collective-permute-start | bytes 1327112 | tf_op jit(solution)/shard_map/ppermute | solution.py:331
  184.3 18.1 %collective-permute-start.39 = (f32[16,768]{1,0:T(8,128)S(1)}, f32[16,768]{1,0:T(8,128)S(1)}, u32[]{:S(2)}, u32[]{:S(2)}) collective-permute-start(f32[16,768]{1,0:T(8,128)S(1)} %add.75), channel_id=1, source_target_pairs={{0,4},{2,6},{4,0},{6,2},{1,5},{3,7},{5,1},{7,3},{8,12},{10,14},{12... | collective-permute-start | bytes 147464 | tf_op jit(solution)/shard_map/ppermute | solution.py:331
  207.5 8.9 %collective-permute-start.42 = (bf16[4,128,768]{2,1,0:T(8,128)(2,1)S(1)}, bf16[4,128,768]{2,1,0:T(8,128)(2,1)S(1)}, u32[]{:S(2)}, u32[]{:S(2)}) collective-permute-start(bf16[4,128,768]{2,1,0:T(8,128)(2,1)S(1)} %get-tuple-element.324), channel_id=1, source_target_pairs={{0,1},{1,0},{2,3},{3,2},{4,5},{5,4},{6,7},{7,6},{8,9},{9,8},{10,11... | collective-permute-start | bytes 2359304 | tf_op jit(solution)/shard_map/ppermute | solution.py:331
  207.5 8.8 %collective-permute-start.41 = (bf16[96,1152]{1,0:T(8,128)(2,1)S(1)}, bf16[96,1152]{1,0:T(8,128)(2,1)S(1)}, u32[]{:S(2)}, u32[]{:S(2)}) collective-permute-start(bf16[96,1152]{1,0:T(8,128)(2,1)S(1)} %get-tuple-element.323), channel_id=1, source_target_pairs={{0,8},{8,0},{16,24},{24,16},{1,9},{9,1},{17,25},{25,17},{2,10},{10... | collective-permute-start | bytes 663560 | tf_op jit(solution)/shard_map/ppermute | solution.py:331
  209.7 10.7 %collective-permute-start.47 = (bf16[96,1536]{1,0:T(8,128)(2,1)S(1)}, bf16[96,1536]{1,0:T(8,128)(2,1)S(1)}, u32[]{:S(2)}, u32[]{:S(2)}) collective-permute-start(bf16[96,1536]{1,0:T(8,128)(2,1)S(1)} %get-tuple-element.460), channel_id=1, source_target_pairs={{0,4},{2,6},{4,0},{6,2},{1,5},{3,7},{5,1},{7,3},{8,12},{10,14},{12... | collective-permute-start | bytes 884744 | tf_op jit(solution)/shard_map/ppermute | solution.py:331
  210.4 11.9 %collective-permute-start.46 = (bf16[96,1536]{1,0:T(8,128)(2,1)S(1)}, bf16[96,1536]{1,0:T(8,128)(2,1)S(1)}, u32[]{:S(2)}, u32[]{:S(2)}) collective-permute-start(bf16[96,1536]{1,0:T(8,128)(2,1)S(1)} %get-tuple-element.461), channel_id=1, source_target_pairs={{0,2},{2,0},{4,6},{6,4},{1,3},{3,1},{5,7},{7,5},{8,10},{10,8},{12,... | collective-permute-start | bytes 884744 | tf_op jit(solution)/shard_map/ppermute | solution.py:331
  216.8 17.9 %collective-permute-start.45 = (bf16[96,1536]{1,0:T(8,128)(2,1)S(1)}, bf16[96,1536]{1,0:T(8,128)(2,1)S(1)}, u32[]{:S(2)}, u32[]{:S(2)}) collective-permute-start(bf16[96,1536]{1,0:T(8,128)(2,1)S(1)} %get-tuple-element.340), channel_id=1, source_target_pairs={{0,8},{8,0},{16,24},{24,16},{1,9},{9,1},{17,25},{25,17},{2,10},{10... | collective-permute-start | bytes 884744 | tf_op jit(solution)/shard_map/ppermute | solution.py:331
  219.4 13.5 %collective-permute-start.44 = (bf16[48,1152]{1,0:T(8,128)(2,1)S(1)}, bf16[48,1152]{1,0:T(8,128)(2,1)S(1)}, u32[]{:S(2)}, u32[]{:S(2)}) collective-permute-start(bf16[48,1152]{1,0:T(8,128)(2,1)S(1)} %get-tuple-element.339), channel_id=1, source_target_pairs={{0,16},{8,24},{16,0},{24,8},{1,17},{9,25},{17,1},{25,9},{2,18},{10... | collective-permute-start | bytes 331784 | tf_op jit(solution)/shard_map/ppermute | solution.py:331
  220.4 14.2 %collective-permute-start.48 = (bf16[192,384]{1,0:T(8,128)(2,1)S(1)}, bf16[192,384]{1,0:T(8,128)(2,1)S(1)}, u32[]{:S(2)}, u32[]{:S(2)}) collective-permute-start(bf16[192,384]{1,0:T(8,128)(2,1)S(1)} %get-tuple-element.343), channel_id=1, source_target_pairs={{0,16},{8,24},{16,0},{24,8},{1,17},{9,25},{17,1},{25,9},{2,18},{10... | collective-permute-start | bytes 442376 | tf_op jit(solution)/shard_map/ppermute | solution.py:331
  234.9 10.7 %collective-permute-start.53 = (bf16[96,1536]{1,0:T(8,128)(2,1)S(1)}, bf16[96,1536]{1,0:T(8,128)(2,1)S(1)}, u32[]{:S(2)}, u32[]{:S(2)}) collective-permute-start(bf16[96,1536]{1,0:T(8,128)(2,1)S(1)} %add_convert_fusion.2.refs_0_), channel_id=1, source_target_pairs={{0,4},{2,6},{4,0},{6,2},{1,5},{3,7},{5,1},{7,3},{8,12},{10,14},{12... | collective-permute-start | bytes 884744 | tf_op jit(solution)/shard_map/ppermute | solution.py:331
  235.6 10.1 %collective-permute-start.54 = (bf16[96,1536]{1,0:T(8,128)(2,1)S(1)}, bf16[96,1536]{1,0:T(8,128)(2,1)S(1)}, u32[]{:S(2)}, u32[]{:S(2)}) collective-permute-start(bf16[96,1536]{1,0:T(8,128)(2,1)S(1)} %add_convert_fusion.1.refs_2_), channel_id=1, source_target_pairs={{0,2},{2,0},{4,6},{6,4},{1,3},{3,1},{5,7},{7,5},{8,10},{10,8},{12,... | collective-permute-start | bytes 884744 | tf_op jit(solution)/shard_map/ppermute | solution.py:331
  245.8 14.3 %collective-permute-start.59 = (bf16[128,768]{1,0:T(8,128)(2,1)S(1)}, bf16[128,768]{1,0:T(8,128)(2,1)S(1)}, u32[]{:S(2)}, u32[]{:S(2)}) collective-permute-start(bf16[128,768]{1,0:T(8,128)(2,1)S(1)} %get-tuple-element.377), channel_id=1, source_target_pairs={{0,4},{2,6},{4,0},{6,2},{1,5},{3,7},{5,1},{7,3},{8,12},{10,14},{12... | collective-permute-start | bytes 589832 | tf_op jit(solution)/shard_map/ppermute | solution.py:331
  247.6 12.5 %collective-permute-start.60 = (bf16[128,768]{1,0:T(8,128)(2,1)S(1)}, bf16[128,768]{1,0:T(8,128)(2,1)S(1)}, u32[]{:S(2)}, u32[]{:S(2)}) collective-permute-start(bf16[128,768]{1,0:T(8,128)(2,1)S(1)} %get-tuple-element.378), channel_id=1, source_target_pairs={{0,6},{2,4},{4,2},{6,0},{1,7},{3,5},{5,3},{7,1},{8,14},{10,12},{12... | collective-permute-start | bytes 589832 | tf_op jit(solution)/shard_map/ppermute | solution.py:331
  249.1 11.0 %collective-permute-start.56 = (bf16[48,1536]{1,0:T(8,128)(2,1)S(1)}, bf16[48,1536]{1,0:T(8,128)(2,1)S(1)}, u32[]{:S(2)}, u32[]{:S(2)}) collective-permute-start(bf16[48,1536]{1,0:T(8,128)(2,1)S(1)} %add_convert_fusion.7.refs_2_), channel_id=1, source_target_pairs={{0,4},{2,6},{4,0},{6,2},{1,5},{3,7},{5,1},{7,3},{8,12},{10,14},{12... | collective-permute-start | bytes 442376 | tf_op jit(solution)/shard_map/ppermute | solution.py:331
  249.3 10.8 %collective-permute-start.55 = (bf16[48,1536]{1,0:T(8,128)(2,1)S(1)}, bf16[48,1536]{1,0:T(8,128)(2,1)S(1)}, u32[]{:S(2)}, u32[]{:S(2)}) collective-permute-start(bf16[48,1536]{1,0:T(8,128)(2,1)S(1)} %add_convert_fusion.7.refs_2_), channel_id=1, source_target_pairs={{0,2},{2,0},{4,6},{6,4},{1,3},{3,1},{5,7},{7,5},{8,10},{10,8},{12,... | collective-permute-start | bytes 442376 | tf_op jit(solution)/shard_map/ppermute | solution.py:331
  (35 other events, 270.6 us)

commit v7 on v6

--- a/solution.py
+++ b/solution.py
@@ -943,9 +943,8 @@
         fsdp_count,
     )
     active, down_parts = together(active, down_parts)
-    teacher_half = stack_rows(
-        [teacher_own[0]] + swap_each([teacher_own[s] for s in range(ctx_count)], "ctx")
-    ).reshape(ctx_count, block_len // 2, model_width)
+    teacher_pieces = [teacher_own[s] for s in range(ctx_count)]
+    teacher_pieces = teacher_pieces[:1] + swap_each(teacher_pieces, "ctx")
     branch, full_down = gathered_layer(
         down_kernel,
         "down",
@@ -958,6 +957,8 @@
         [model_width],
         fsdp_count,
     )
+    branch, teacher_pieces = together(branch, teacher_pieces)
+    teacher_half = stack_rows(teacher_pieces).reshape(ctx_count, block_len // 2, model_width)
     layer_half, grad_resid2, grad_resid2_low, stats2 = by_rows(
         second_norm_kernel,
         "second_norm",

time: 282 us -> 276 us (0.979)
  waiting for transfers between devices: 99.4 us -> 93 us
    ppermute x65, waiting for transfers between devices: 97.6 us -> 91.2 us  [swap(): return lax.ppermute(values, axis, pairs)]
  transfers between devices with their start and end apart: 66 -> 66, of which waited for: 23 -> 24; matrix products, arithmetic and copies ran while one was open for 2% -> 2% of each run, Pallas kernels for 28% -> 30%
where the time goes in v7:
time: 276 us; the launch traced here: 275 us
  waiting for transfers between devices  93 us (34%)
  Pallas kernels  89.4 us (32%)
  starting transfers between devices  74.5 us (27%)
  local copies, waits for them, and re-layouts  10.8 us (4%)
  between operations  4.56 us (2%)
  other arithmetic  3.15 us (1%)
    ppermute x65, waiting for transfers between devices, swap(): return lax.ppermute(values, axis, pairs)  91.2 us
    ppermute x65, starting transfers between devices, swap(): return lax.ppermute(values, axis, pairs)  70.5 us
    pallas_call x1, Pallas kernels, attend_back(): pl.pallas_call(lambda *refs: attend_back_kernel(*refs, block=block), grid...  15.5 us
    pallas_call x4, Pallas kernels, weight_grad(): pl.pallas_call(lambda *refs: weight_grad_kernel(*refs, chunks=chunks, fsd...  13.9 us
    pallas_call x3, Pallas kernels, gathered_layer(): pl.pallas_call(kernel, grid_spec=pltpu.PrefetchScalarGridSpec(num_scalar_...  13 us
    pallas_call x1, Pallas kernels, attend(): pl.pallas_call(lambda *refs: attend_kernel(*refs, block=block), grid_spec...  10.8 us
    pallas_call x3, Pallas kernels, by_rows(): pl.pallas_call(kernel, grid_spec=pltpu.PrefetchScalarGridSpec(num_scalar_...  9.88 us
    pallas_call x3, Pallas kernels, rows_times(): pl.pallas_call(lambda *refs: rows_kernel(*refs, transposed=transposed), g...  6.4 us
  transfers between devices with their start and end apart: 66, of which 24 were waited for; matrix products, arithmetic and copies ran while one was open for 2% of the time, Pallas kernels for 30%

profile of v7, /device:TPU:0, one launch (start us, length us, event | category | flops | bytes accessed | tf_op | source)
XLA Modules:
  0.0 275.4 jit_solution(12374133831241969655)
XLA Ops:
  0.7 1.6 reshape.107
  5.0 5.0 %collective-permute-start.2 = (bf16[48,1536]{1,0:T(8,128)(2,1)}, bf16[48,1536]{1,0:T(8,128)(2,1)S(1)}, u32[]{:S(2)}, u32[]{:S(2)}) collective-permute-start(bf16[48,1536]{1,0:T(8,128)(2,1)} %constant_dynamic-slice_fusion.2), channel_id=1, source_target_pairs={{0,24},{8,16},{16,8},{24,0},{1,25},{9,17},{17,9},{25,1},{2,26},{10... | collective-permute-start | bytes 442376 | tf_op jit(solution)/shard_map/ppermute | solution.py:331
  10.6 3.9 %all-to-all-start = ((bf16[4,128,768]{2,1,0:T(8,128)(2,1)}), bf16[4,128,768]{2,1,0:T(8,128)(2,1)S(1)}, u32[]{:S(2)}, u32[]{:S(2)}) async-start(bf16[4,128,768]{2,1,0:T(8,128)(2,1)} %constant_dynamic-slice_fusion.3), calls=%async_computation | async-start | bytes 1572864 | tf_op jit(solution)/shard_map/all_to_all | solution.py:382
  18.4 4.4 %collective-permute-done.1.refs_1_ = bf16[48,1536]{1,0:T(8,128)(2,1)} collective-permute-done((bf16[48,1536]{1,0:T(8,128)(2,1)}, bf16[48,1536]{1,0:T(8,128)(2,1)}, u32[]{:S(2)}, u32[]{:S(2)}) %collective-permute-start.1) | collective-permute-done | bytes 147488 | tf_op jit(solution)/shard_map/ppermute | solution.py:331
  22.8 1.8 all-to-all-done.own_ref
  30.7 4.2 %collective-permute-done.7.refs_0_ = bf16[48,1536]{1,0:T(8,128)(2,1)S(1)} collective-permute-done((bf16[48,1536]{1,0:T(8,128)(2,1)}, bf16[48,1536]{1,0:T(8,128)(2,1)S(1)}, u32[]{:S(2)}, u32[]{:S(2)}) %collective-permute-start.7) | collective-permute-done | bytes 147488 | tf_op jit(solution)/shard_map/ppermute | solution.py:331
  34.8 2.4 collective-permute-start.8
  38.6 9.2 %collective-permute-done.8.refs_1_ = bf16[48,1536]{1,0:T(8,128)(2,1)S(1)} collective-permute-done((bf16[48,1536]{1,0:T(8,128)(2,1)}, bf16[48,1536]{1,0:T(8,128)(2,1)S(1)}, u32[]{:S(2)}, u32[]{:S(2)}) %collective-permute-start.8) | collective-permute-done | bytes 147488 | tf_op jit(solution)/shard_map/ppermute | solution.py:331
  47.8 2.1 collective-permute-done.9.refs_2_
  55.9 2.6 collective-permute-start.14
  58.5 3.5 %project.1 = (bf16[1024,1152]{1,0:T(8,128)(2,1)S(1)}, bf16[768,1536]{1,0:T(8,128)(2,1)S(1)}) custom-call(s32[2]{0:T(128)S(1)} %get-tuple-element.218.places.refs_0_, bf16[1024,768]{1,0:T(8,128)(2,1)S(1)} %bitcast.57, f32[1,1152]{1,0:T(1,128)S(1)} %reshape_reshape.3.bias_ref, bf16[192,1536]{1,0:T(8,128)(2,1)S(1)} %constant_dynamic-update-slice_fusion.own_ref, ...), custom_call_target="tpu_custom_call" | custom-call | tf_op jit(solution)/shard_map/project/pallas_call | solution.py:296
  63.5 10.8 %attend.1 = (bf16[1024,384]{1,0:T(8,128)(2,1)S(1)}, f32[3,2,1024]{2,1,0:T(2,128)S(1)}) custom-call(s32[3]{0:T(128)S(1)} %convert_element_type.128.refs_0_.facts, bf16[1024,1152]{1,0:T(8,128)(2,1)S(1)} %get-tuple-element.237.refs_1_.refs_2_.refs_3_, bf16[1024,1152]{1,0:T(8,128)(2,1)S(1)} %get-tuple-element.237.refs_1_.refs_2_.refs_3_, ...), custom_call_target="tpu_custom_call" | custom-call | tf_op jit(solution)/shard_map/attend/pallas_call | solution.py:174
  74.3 1.6 rows_times.3.mine_ref
  81.2 8.9 %collective-permute-done.19.refs_3_ = bf16[144,1536]{1,0:T(8,128)(2,1)S(1)} collective-permute-done((bf16[144,1536]{1,0:T(8,128)(2,1)S(1)}, bf16[144,1536]{1,0:T(8,128)(2,1)S(1)}, u32[]{:S(2)}, u32[]{:S(2)}) %collective-permute-start.19) | collective-permute-done | bytes 442400 | tf_op jit(solution)/shard_map/ppermute | solution.py:331
  92.1 1.6 first_norm.1
  93.7 5.5 %up.1 = (bf16[1024,1536]{1,0:T(8,128)(2,1)S(1)}, bf16[1024,1536]{1,0:T(8,128)(2,1)S(1)}, bf16[768,1536]{1,0:T(8,128)(2,1)S(1)}) custom-call(s32[2]{0:T(128)S(1)} %get-tuple-element.218.places.refs_0_, bf16[1024,768]{1,0:T(8,128)(2,1)S(1)} %get-tuple-element.246.left_ref.refs_1_, f32[1,1536]{1,0:T(1,128)S(1)} %reshape.114.bias_ref, ...), custom_call_target="tpu_custom_call" | custom-call | tf_op jit(solution)/shard_map/up/pallas_call | solution.py:296
  99.6 4.0 %down.1 = (bf16[1024,768]{1,0:T(8,128)(2,1)S(1)}, bf16[768,1536]{1,0:T(8,128)(2,1)S(1)}) custom-call(s32[2]{0:T(128)S(1)} %get-tuple-element.218.places.refs_0_, bf16[1024,1536]{1,0:T(8,128)(2,1)S(1)} %get-tuple-element.255.left_ref.refs_2_, bf16[192,1536]{1,0:T(8,128)(2,1)S(1)} %copy-done.4, bf16[144,1536]{1,0:T(8,128)(2,1)S(1)} %stack_rows.8.refs_0_, ...), custom_call_target="tpu_custom_call" | custom-call | tf_op jit(solution)/shard_map/down/pallas_call | solution.py:296
  103.8 3.7 %collective-permute-done.21.refs_2_ = bf16[128,768]{1,0:T(8,128)(2,1)S(1)} collective-permute-done((bf16[128,768]{1,0:T(8,128)(2,1)S(1)}, bf16[128,768]{1,0:T(8,128)(2,1)S(1)}, u32[]{:S(2)}, u32[]{:S(2)}) %collective-permute-start.21) | collective-permute-done | bytes 196640 | tf_op jit(solution)/shard_map/ppermute | solution.py:331
  108.3 3.9 %collective-permute-done.24.other_teacher_ref = bf16[4,128,768]{2,1,0:T(8,128)(2,1)S(1)} collective-permute-done((bf16[4,128,768]{2,1,0:T(8,128)(2,1)S(1)}, bf16[4,128,768]{2,1,0:T(8,128)(2,1)S(1)}, u32[]{:S(2)}, u32[]{:S(2)}) %collective-permute-start.24) | collective-permute-done | bytes 786464 | tf_op jit(solution)/shard_map/ppermute | solution.py:331
  112.1 5.1 %second_norm.1 = (bf16[4,128,768]{2,1,0:T(8,128)(2,1)S(1)}, f32[1024,768]{1,0:T(8,128)S(1)}, bf16[1024,768]{1,0:T(8,128)(2,1)S(1)}, f32[8,768]{1,0:T(8,128)S(1)}) custom-call(s32[3]{0:T(128)S(1)} %convert_element_type.128.refs_0_.facts, f32[1024,768]{1,0:T(8,128)S(1)} %get-tuple-element.245.normal_ref, f32[1,768]{1,0:T(1,128)S(1)} %reshape.112.gain_ref.gain1_ref, ...), custom_call_target="tpu_custom_call" | custom-call | tf_op jit(solution)/shard_map/second_norm/pallas_call | solution.py:497
  120.8 4.0 %weight_grad.4 = (bf16[384,1536]{1,0:T(8,128)(2,1)S(1)}, bf16[384,1536]{1,0:T(8,128)(2,1)S(1)}) custom-call(s32[2]{0:T(128)S(1)} %get-tuple-element.218.places.refs_0_, bf16[1024,768]{1,0:T(8,128)(2,1)S(1)} %get-tuple-element.271.refs_1_.low_ref, bf16[1024,1536]{1,0:T(8,128)(2,1)S(1)} %get-tuple-element.255.left_ref.refs_2_), custom_call_target="tpu_custom_call" | custom-call | tf_op jit(solution)/shard_map/weight_grad/pallas_call | solution.py:717
  124.9 3.9 %grad_pre.1 = (bf16[1024,1536]{1,0:T(8,128)(2,1)S(1)}, f32[8,1536]{1,0:T(8,128)S(1)}) custom-call(bf16[1024,768]{1,0:T(8,128)(2,1)S(1)} %get-tuple-element.271.refs_1_.low_ref, bf16[768,1536]{1,0:T(8,128)(2,1)S(1)} %get-tuple-element.272.weight_ref, bf16[1024,1536]{1,0:T(8,128)(2,1)S(1)} %get-tuple-element.273.slope_ref), custom_call_target="tpu_custom_call" | custom-call | tf_op jit(solution)/shard_map/grad_pre/pallas_call | solution.py:531
  128.7 3.3 %rows_times.4.mine_ref = bf16[1024,768]{1,0:T(8,128)(2,1)S(1)} custom-call(bf16[1024,1536]{1,0:T(8,128)(2,1)S(1)} %get-tuple-element.314.refs_0_.refs_2_, bf16[768,1536]{1,0:T(8,128)(2,1)S(1)} %get-tuple-element.275.refs_1_), custom_call_target="tpu_custom_call" | custom-call | tf_op jit(solution)/shard_map/rows_times/pallas_call | solution.py:551
  132.1 2.3 collective-permute-start.30
  134.7 4.0 %weight_grad.7 = (bf16[192,1536]{1,0:T(8,128)(2,1)S(1)}, bf16[192,1536]{1,0:T(8,128)(2,1)S(1)}, bf16[192,1536]{1,0:T(8,128)(2,1)S(1)}, bf16[192,1536]{1,0:T(8,128)(2,1)S(1)}) custom-call(s32[2]{0:T(128)S(1)} %get-tuple-element.218.places.refs_0_, bf16[1024,768]{1,0:T(8,128)(2,1)S(1)} %get-tuple-element.246.left_ref.refs_1_, ...), custom_call_target="tpu_custom_call" | custom-call | tf_op jit(solution)/shard_map/weight_grad/pallas_call | solution.py:717
  140.8 2.3 join_halves.4
  143.1 3.2 %first_norm_back.1 = (bf16[1024,768]{1,0:T(8,128)(2,1)S(1)}, f32[4,128,768]{2,1,0:T(8,128)S(1)}, f32[8,768]{1,0:T(8,128)S(1)}) custom-call(s32[3]{0:T(128)S(1)} %convert_element_type.128.refs_0_.facts, f32[1024,768]{1,0:T(8,128)S(1)} %get-tuple-element.267.grad_ref, bf16[1024,768]{1,0:T(8,128)(2,1)S(1)} %rows_times.4.mine_ref, ...), custom_call_target="tpu_custom_call" | custom-call | tf_op jit(solution)/shard_map/first_norm_back/pallas_call | solution.py:497
  146.3 1.6 weight_grad.5
  151.3 15.5 %attend_back.1 = (bf16[1024,1152]{1,0:T(8,128)(2,1)S(1)}, f32[8,1152]{1,0:T(8,128)S(1)}) custom-call(s32[3]{0:T(128)S(1)} %convert_element_type.128.refs_0_.facts, bf16[1024,1152]{1,0:T(8,128)(2,1)S(1)} %get-tuple-element.237.refs_1_.refs_2_.refs_3_, bf16[1024,1152]{1,0:T(8,128)(2,1)S(1)} %get-tuple-element.237.refs_1_.refs_2_.refs_3_, ...), custom_call_target="tpu_custom_call" | custom-call | tf_op jit(solution)/shard_map/attend_back/pallas_call | solution.py:198
  168.9 4.3 %weight_grad.6 = (bf16[192,1152]{1,0:T(8,128)(2,1)S(1)}, bf16[192,1152]{1,0:T(8,128)(2,1)S(1)}, bf16[192,1152]{1,0:T(8,128)(2,1)S(1)}, bf16[192,1152]{1,0:T(8,128)(2,1)S(1)}) custom-call(s32[2]{0:T(128)S(1)} %get-tuple-element.218.places.refs_0_, bf16[1024,768]{1,0:T(8,128)(2,1)S(1)} %bitcast.59, bf16[1024,1152]{1,0:T(8,128)(2,1)S(1)} %get-tuple-element.311.refs_2_.grad_ref), custom_call_target="tpu_custom_call" | custom-call | tf_op jit(solution)/shard_map/weight_grad/pallas_call | solution.py:717
  179.3 3.9 %input_back.1 = (bf16[4,128,768]{2,1,0:T(8,128)(2,1)S(1)}, bf16[4,128,768]{2,1,0:T(8,128)(2,1)S(1)}) custom-call(s32[3]{0:T(128)S(1)} %convert_element_type.128.refs_0_.facts, bf16[1024,1152]{1,0:T(8,128)(2,1)S(1)} %get-tuple-element.311.refs_2_.grad_ref, bf16[768,1536]{1,0:T(8,128)(2,1)S(1)} %get-tuple-element.244.weight_ref), custom_call_target="tpu_custom_call" | custom-call | tf_op jit(solution)/shard_map/input_back/pallas_call | solution.py:597
  183.2 13.3 %collective-permute-done.39 = f32[16,768]{1,0:T(8,128)S(1)} collective-permute-done((f32[16,768]{1,0:T(8,128)S(1)}, f32[16,768]{1,0:T(8,128)S(1)}, u32[]{:S(2)}, u32[]{:S(2)}) %collective-permute-start.39) | collective-permute-done | bytes 49184 | tf_op jit(solution)/shard_map/ppermute | solution.py:331
  196.7 4.7 %collective-permute-done.40 = bf16[192,1536]{1,0:T(8,128)(2,1)S(1)} collective-permute-done((bf16[192,1536]{1,0:T(8,128)(2,1)S(1)}, bf16[192,1536]{1,0:T(8,128)(2,1)S(1)}, u32[]{:S(2)}, u32[]{:S(2)}) %collective-permute-start.40) | collective-permute-done | bytes 589856 | tf_op jit(solution)/shard_map/ppermute | solution.py:331
  201.5 2.0 collective-permute-start.41
  206.0 4.3 %collective-permute-done.41.refs_1_ = bf16[96,1152]{1,0:T(8,128)(2,1)S(1)} collective-permute-done((bf16[96,1152]{1,0:T(8,128)(2,1)S(1)}, bf16[96,1152]{1,0:T(8,128)(2,1)S(1)}, u32[]{:S(2)}, u32[]{:S(2)}) %collective-permute-start.41) | collective-permute-done | bytes 221216 | tf_op jit(solution)/shard_map/ppermute | solution.py:331
  211.5 1.8 collective-permute-start.49
  214.4 1.8 collective-permute-start.48
  216.3 3.7 %collective-permute-done.49 = f32[16,768]{1,0:T(8,128)S(1)} collective-permute-done((f32[16,768]{1,0:T(8,128)S(1)}, f32[16,768]{1,0:T(8,128)S(1)}, u32[]{:S(2)}, u32[]{:S(2)}) %collective-permute-start.49) | collective-permute-done | bytes 49184 | tf_op jit(solution)/shard_map/ppermute | solution.py:331
  220.0 6.8 %collective-permute-done.44 = bf16[48,1152]{1,0:T(8,128)(2,1)S(1)} collective-permute-done((bf16[48,1152]{1,0:T(8,128)(2,1)S(1)}, bf16[48,1152]{1,0:T(8,128)(2,1)S(1)}, u32[]{:S(2)}, u32[]{:S(2)}) %collective-permute-start.44) | collective-permute-done | bytes 110624 | tf_op jit(solution)/shard_map/ppermute | solution.py:331
  226.8 1.8 collective-permute-done.48
  233.0 6.0 %collective-permute-done.51.refs_4_ = bf16[48,1152]{1,0:T(8,128)(2,1)S(1)} collective-permute-done((bf16[48,1152]{1,0:T(8,128)(2,1)S(1)}, bf16[48,1152]{1,0:T(8,128)(2,1)S(1)}, u32[]{:S(2)}, u32[]{:S(2)}) %collective-permute-start.51) | collective-permute-done | bytes 110624 | tf_op jit(solution)/shard_map/ppermute | solution.py:331
  239.7 1.7 collective-permute-start.59
  243.3 1.7 collective-permute-start.55
  244.9 1.8 collective-permute-done.58.refs_1_
  247.4 6.6 %collective-permute-done.57.refs_5_ = bf16[48,1152]{1,0:T(8,128)(2,1)S(1)} collective-permute-done((bf16[48,1152]{1,0:T(8,128)(2,1)S(1)}, bf16[48,1152]{1,0:T(8,128)(2,1)S(1)}, u32[]{:S(2)}, u32[]{:S(2)}) %collective-permute-start.57) | collective-permute-done | bytes 110624 | tf_op jit(solution)/shard_map/ppermute | solution.py:331
  256.2 3.0 %collective-permute-done.61 = bf16[192,384]{1,0:T(8,128)(2,1)S(1)} collective-permute-done((bf16[192,384]{1,0:T(8,128)(2,1)S(1)}, bf16[192,384]{1,0:T(8,128)(2,1)S(1)}, u32[]{:S(2)}, u32[]{:S(2)}) %collective-permute-start.61) | collective-permute-done | bytes 147488 | tf_op jit(solution)/shard_map/ppermute | solution.py:331
  266.4 1.6 place_rows.3
  268.0 2.7 join_halves.5
  (213 shorter events, 71.6 us)
Async XLA Ops:
  5.0 13.4 %collective-permute-start.2 = (bf16[48,1536]{1,0:T(8,128)(2,1)}, bf16[48,1536]{1,0:T(8,128)(2,1)S(1)}, u32[]{:S(2)}, u32[]{:S(2)}) collective-permute-start(bf16[48,1536]{1,0:T(8,128)(2,1)} %constant_dynamic-slice_fusion.2), channel_id=1, source_target_pairs={{0,24},{8,16},{16,8},{24,0},{1,25},{9,17},{17,9},{25,1},{2,26},{10... | collective-permute-start | bytes 442376 | tf_op jit(solution)/shard_map/ppermute | solution.py:331
  10.0 12.8 %collective-permute-start.1 = (bf16[48,1536]{1,0:T(8,128)(2,1)}, bf16[48,1536]{1,0:T(8,128)(2,1)}, u32[]{:S(2)}, u32[]{:S(2)}) collective-permute-start(bf16[48,1536]{1,0:T(8,128)(2,1)} %constant_dynamic-slice_fusion.2), channel_id=1, source_target_pairs={{0,16},{8,24},{16,0},{24,8},{1,17},{9,25},{17,1},{25,9},{2,18},{10... | collective-permute-start | bytes 442376 | tf_op jit(solution)/shard_map/ppermute | solution.py:331
  10.0 12.8 %collective-permute-start = (bf16[48,1536]{1,0:T(8,128)(2,1)}, bf16[48,1536]{1,0:T(8,128)(2,1)}, u32[]{:S(2)}, u32[]{:S(2)}) collective-permute-start(bf16[48,1536]{1,0:T(8,128)(2,1)} %constant_dynamic-slice_fusion.2), channel_id=1, source_target_pairs={{0,8},{8,0},{16,24},{24,16},{1,9},{9,1},{17,25},{25,17},{2,10},{10... | collective-permute-start | bytes 442376 | tf_op jit(solution)/shard_map/ppermute | solution.py:331
  10.6 14.0 %all-to-all-start = ((bf16[4,128,768]{2,1,0:T(8,128)(2,1)}), bf16[4,128,768]{2,1,0:T(8,128)(2,1)S(1)}, u32[]{:S(2)}, u32[]{:S(2)}) async-start(bf16[4,128,768]{2,1,0:T(8,128)(2,1)} %constant_dynamic-slice_fusion.3), calls=%async_computation | async-start | bytes 1572864 | tf_op jit(solution)/shard_map/all_to_all | solution.py:382
  24.6 12.6 %collective-permute-start.6 = (bf16[4,128,768]{2,1,0:T(8,128)(2,1)S(1)}, bf16[4,128,768]{2,1,0:T(8,128)(2,1)S(1)}, u32[]{:S(2)}, u32[]{:S(2)}) collective-permute-start(bf16[4,128,768]{2,1,0:T(8,128)(2,1)S(1)} %all-to-all-done.own_ref), channel_id=1, source_target_pairs={{0,1},{1,0},{2,3},{3,2},{4,5},{5,4},{6,7},{7,6},{8,9},{9,8},{10,11... | collective-permute-start | bytes 2359304 | tf_op jit(solution)/shard_map/ppermute | solution.py:331
  25.6 24.3 %collective-permute-start.5 = (bf16[160,1536]{1,0:T(8,128)(2,1)S(1)}, bf16[160,1536]{1,0:T(8,128)(2,1)S(1)}, u32[]{:S(2)}, u32[]{:S(2)}) collective-permute-start(bf16[160,1536]{1,0:T(8,128)(2,1)S(1)} %stack_rows.6.refs_0_), channel_id=1, source_target_pairs={{0,6},{2,4},{4,2},{6,0},{1,7},{3,5},{5,3},{7,1},{8,14},{10,12},{12... | collective-permute-start | bytes 1474568 | tf_op jit(solution)/shard_map/ppermute | solution.py:331
  27.1 23.6 %collective-permute-start.4 = (bf16[160,1536]{1,0:T(8,128)(2,1)S(1)}, bf16[160,1536]{1,0:T(8,128)(2,1)S(1)}, u32[]{:S(2)}, u32[]{:S(2)}) collective-permute-start(bf16[160,1536]{1,0:T(8,128)(2,1)S(1)} %stack_rows.6.refs_0_), channel_id=1, source_target_pairs={{0,4},{2,6},{4,0},{6,2},{1,5},{3,7},{5,1},{7,3},{8,12},{10,14},{12... | collective-permute-start | bytes 1474568 | tf_op jit(solution)/shard_map/ppermute | solution.py:331
  28.6 22.2 %collective-permute-start.3 = (bf16[160,1536]{1,0:T(8,128)(2,1)S(1)}, bf16[160,1536]{1,0:T(8,128)(2,1)S(1)}, u32[]{:S(2)}, u32[]{:S(2)}) collective-permute-start(bf16[160,1536]{1,0:T(8,128)(2,1)S(1)} %stack_rows.6.refs_0_), channel_id=1, source_target_pairs={{0,2},{2,0},{4,6},{6,4},{1,3},{3,1},{5,7},{7,5},{8,10},{10,8},{12,... | collective-permute-start | bytes 1474568 | tf_op jit(solution)/shard_map/ppermute | solution.py:331
  34.8 13.0 %collective-permute-start.8 = (bf16[48,1536]{1,0:T(8,128)(2,1)}, bf16[48,1536]{1,0:T(8,128)(2,1)S(1)}, u32[]{:S(2)}, u32[]{:S(2)}) collective-permute-start(bf16[48,1536]{1,0:T(8,128)(2,1)} %get-tuple-element.225), channel_id=1, source_target_pairs={{0,16},{8,24},{16,0},{24,8},{1,17},{9,25},{17,1},{25,9},{2,18},{10... | collective-permute-start | bytes 442376 | tf_op jit(solution)/shard_map/ppermute | solution.py:331
  37.2 12.7 %collective-permute-start.9 = (bf16[48,1536]{1,0:T(8,128)(2,1)S(1)}, bf16[48,1536]{1,0:T(8,128)(2,1)S(1)}, u32[]{:S(2)}, u32[]{:S(2)}) collective-permute-start(bf16[48,1536]{1,0:T(8,128)(2,1)S(1)} %collective-permute-done.7.refs_0_), channel_id=1, source_target_pairs={{0,16},{8,24},{16,0},{24,8},{1,17},{9,25},{17,1},{25,9},{2,18},{10... | collective-permute-start | bytes 442376 | tf_op jit(solution)/shard_map/ppermute | solution.py:331
  50.8 23.4 %collective-permute-start.13 = (bf16[144,1536]{1,0:T(8,128)(2,1)S(1)}, bf16[144,1536]{1,0:T(8,128)(2,1)S(1)}, u32[]{:S(2)}, u32[]{:S(2)}) collective-permute-start(bf16[144,1536]{1,0:T(8,128)(2,1)S(1)} %stack_rows.7.refs_0_), channel_id=1, source_target_pairs={{0,6},{2,4},{4,2},{6,0},{1,7},{3,5},{5,3},{7,1},{8,14},{10,12},{12... | collective-permute-start | bytes 1327112 | tf_op jit(solution)/shard_map/ppermute | solution.py:331
  52.3 21.9 %collective-permute-start.12 = (bf16[144,1536]{1,0:T(8,128)(2,1)S(1)}, bf16[144,1536]{1,0:T(8,128)(2,1)S(1)}, u32[]{:S(2)}, u32[]{:S(2)}) collective-permute-start(bf16[144,1536]{1,0:T(8,128)(2,1)S(1)} %stack_rows.7.refs_0_), channel_id=1, source_target_pairs={{0,4},{2,6},{4,0},{6,2},{1,5},{3,7},{5,1},{7,3},{8,12},{10,14},{12... | collective-permute-start | bytes 1327112 | tf_op jit(solution)/shard_map/ppermute | solution.py:331
  53.7 20.5 %collective-permute-start.11 = (bf16[144,1536]{1,0:T(8,128)(2,1)S(1)}, bf16[144,1536]{1,0:T(8,128)(2,1)S(1)}, u32[]{:S(2)}, u32[]{:S(2)}) collective-permute-start(bf16[144,1536]{1,0:T(8,128)(2,1)S(1)} %stack_rows.7.refs_0_), channel_id=1, source_target_pairs={{0,2},{2,0},{4,6},{6,4},{1,3},{3,1},{5,7},{7,5},{8,10},{10,8},{12,... | collective-permute-start | bytes 1327112 | tf_op jit(solution)/shard_map/ppermute | solution.py:331
  55.9 18.4 %collective-permute-start.14 = (bf16[48,1536]{1,0:T(8,128)(2,1)S(1)}, bf16[48,1536]{1,0:T(8,128)(2,1)S(1)}, u32[]{:S(2)}, u32[]{:S(2)}) collective-permute-start(bf16[48,1536]{1,0:T(8,128)(2,1)S(1)} %copy-done.6), channel_id=1, source_target_pairs={{0,16},{8,24},{16,0},{24,8},{1,17},{9,25},{17,1},{25,9},{2,18},{10... | collective-permute-start | bytes 442376 | tf_op jit(solution)/shard_map/ppermute | solution.py:331
  62.0 12.2 %collective-permute-start.15 = (bf16[48,1536]{1,0:T(8,128)(2,1)S(1)}, bf16[48,1536]{1,0:T(8,128)(2,1)S(1)}, u32[]{:S(2)}, u32[]{:S(2)}) collective-permute-start(bf16[48,1536]{1,0:T(8,128)(2,1)S(1)} %collective-permute-done.10.refs_0_), channel_id=1, source_target_pairs={{0,16},{8,24},{16,0},{24,8},{1,17},{9,25},{17,1},{25,9},{2,18},{10... | collective-permute-start | bytes 442376 | tf_op jit(solution)/shard_map/ppermute | solution.py:331
  76.0 15.6 %collective-permute-start.16 = (bf16[1024,768]{1,0:T(8,128)(2,1)S(1)}, bf16[1024,768]{1,0:T(8,128)(2,1)S(1)}, u32[]{:S(2)}, u32[]{:S(2)}) collective-permute-start(bf16[1024,768]{1,0:T(8,128)(2,1)S(1)} %rows_times.3.mine_ref), channel_id=1, source_target_pairs={{0,1},{1,0},{2,3},{3,2},{4,5},{5,4},{6,7},{7,6},{8,9},{9,8},{10,11... | collective-permute-start | bytes 4718600 | tf_op jit(solution)/shard_map/ppermute | solution.py:331
  76.1 14.0 %collective-permute-start.19 = (bf16[144,1536]{1,0:T(8,128)(2,1)S(1)}, bf16[144,1536]{1,0:T(8,128)(2,1)S(1)}, u32[]{:S(2)}, u32[]{:S(2)}) collective-permute-start(bf16[144,1536]{1,0:T(8,128)(2,1)S(1)} %stack_rows.8.refs_0_), channel_id=1, source_target_pairs={{0,6},{2,4},{4,2},{6,0},{1,7},{3,5},{5,3},{7,1},{8,14},{10,12},{12... | collective-permute-start | bytes 1327112 | tf_op jit(solution)/shard_map/ppermute | solution.py:331
  77.6 22.0 %collective-permute-start.18 = (bf16[144,1536]{1,0:T(8,128)(2,1)S(1)}, bf16[144,1536]{1,0:T(8,128)(2,1)S(1)}, u32[]{:S(2)}, u32[]{:S(2)}) collective-permute-start(bf16[144,1536]{1,0:T(8,128)(2,1)S(1)} %stack_rows.8.refs_0_), channel_id=1, source_target_pairs={{0,4},{2,6},{4,0},{6,2},{1,5},{3,7},{5,1},{7,3},{8,12},{10,14},{12... | collective-permute-start | bytes 1327112 | tf_op jit(solution)/shard_map/ppermute | solution.py:331
  79.0 20.5 %collective-permute-start.17 = (bf16[144,1536]{1,0:T(8,128)(2,1)S(1)}, bf16[144,1536]{1,0:T(8,128)(2,1)S(1)}, u32[]{:S(2)}, u32[]{:S(2)}) collective-permute-start(bf16[144,1536]{1,0:T(8,128)(2,1)S(1)} %stack_rows.8.refs_0_), channel_id=1, source_target_pairs={{0,2},{2,0},{4,6},{6,4},{1,3},{3,1},{5,7},{7,5},{8,10},{10,8},{12,... | collective-permute-start | bytes 1327112 | tf_op jit(solution)/shard_map/ppermute | solution.py:331
  79.7 24.1 %collective-permute-start.22 = (bf16[128,768]{1,0:T(8,128)(2,1)S(1)}, bf16[128,768]{1,0:T(8,128)(2,1)S(1)}, u32[]{:S(2)}, u32[]{:S(2)}) collective-permute-start(bf16[128,768]{1,0:T(8,128)(2,1)S(1)} %get-tuple-element.480), channel_id=1, source_target_pairs={{0,6},{2,4},{4,2},{6,0},{1,7},{3,5},{5,3},{7,1},{8,14},{10,12},{12... | collective-permute-start | bytes 589832 | tf_op jit(solution)/shard_map/ppermute | solution.py:331
  90.0 17.5 %collective-permute-start.21 = (bf16[128,768]{1,0:T(8,128)(2,1)S(1)}, bf16[128,768]{1,0:T(8,128)(2,1)S(1)}, u32[]{:S(2)}, u32[]{:S(2)}) collective-permute-start(bf16[128,768]{1,0:T(8,128)(2,1)S(1)} %get-tuple-element.481), channel_id=1, source_target_pairs={{0,4},{2,6},{4,0},{6,2},{1,5},{3,7},{5,1},{7,3},{8,12},{10,14},{12... | collective-permute-start | bytes 589832 | tf_op jit(solution)/shard_map/ppermute | solution.py:331
  91.5 16.1 %collective-permute-start.20 = (bf16[128,768]{1,0:T(8,128)(2,1)S(1)}, bf16[128,768]{1,0:T(8,128)(2,1)S(1)}, u32[]{:S(2)}, u32[]{:S(2)}) collective-permute-start(bf16[128,768]{1,0:T(8,128)(2,1)S(1)} %get-tuple-element.482), channel_id=1, source_target_pairs={{0,2},{2,0},{4,6},{6,4},{1,3},{3,1},{5,7},{7,5},{8,10},{10,8},{12,... | collective-permute-start | bytes 589832 | tf_op jit(solution)/shard_map/ppermute | solution.py:331
  117.3 14.7 %collective-permute-start.27 = (bf16[128,768]{1,0:T(8,128)(2,1)S(1)}, bf16[128,768]{1,0:T(8,128)(2,1)S(1)}, u32[]{:S(2)}, u32[]{:S(2)}) collective-permute-start(bf16[128,768]{1,0:T(8,128)(2,1)S(1)} %get-tuple-element.476), channel_id=1, source_target_pairs={{0,6},{2,4},{4,2},{6,0},{1,7},{3,5},{5,3},{7,1},{8,14},{10,12},{12... | collective-permute-start | bytes 589832 | tf_op jit(solution)/shard_map/ppermute | solution.py:331
  118.8 13.2 %collective-permute-start.26 = (bf16[128,768]{1,0:T(8,128)(2,1)S(1)}, bf16[128,768]{1,0:T(8,128)(2,1)S(1)}, u32[]{:S(2)}, u32[]{:S(2)}) collective-permute-start(bf16[128,768]{1,0:T(8,128)(2,1)S(1)} %get-tuple-element.477), channel_id=1, source_target_pairs={{0,4},{2,6},{4,0},{6,2},{1,5},{3,7},{5,1},{7,3},{8,12},{10,14},{12... | collective-permute-start | bytes 589832 | tf_op jit(solution)/shard_map/ppermute | solution.py:331
  120.1 11.9 %collective-permute-start.25 = (bf16[128,768]{1,0:T(8,128)(2,1)S(1)}, bf16[128,768]{1,0:T(8,128)(2,1)S(1)}, u32[]{:S(2)}, u32[]{:S(2)}) collective-permute-start(bf16[128,768]{1,0:T(8,128)(2,1)S(1)} %get-tuple-element.478), channel_id=1, source_target_pairs={{0,2},{2,0},{4,6},{6,4},{1,3},{3,1},{5,7},{7,5},{8,10},{10,8},{12,... | collective-permute-start | bytes 589832 | tf_op jit(solution)/shard_map/ppermute | solution.py:331
  132.0 11.1 %collective-permute-start.28 = (bf16[1024,768]{1,0:T(8,128)(2,1)S(1)}, bf16[1024,768]{1,0:T(8,128)(2,1)S(1)}, u32[]{:S(2)}, u32[]{:S(2)}) collective-permute-start(bf16[1024,768]{1,0:T(8,128)(2,1)S(1)} %rows_times.4.mine_ref), channel_id=1, source_target_pairs={{0,1},{1,0},{2,3},{3,2},{4,5},{5,4},{6,7},{7,6},{8,9},{9,8},{10,11... | collective-permute-start | bytes 4718600 | tf_op jit(solution)/shard_map/ppermute | solution.py:331
  132.1 35.4 %collective-permute-start.30 = (bf16[384,1536]{1,0:T(8,128)(2,1)S(1)}, bf16[384,1536]{1,0:T(8,128)(2,1)S(1)}, u32[]{:S(2)}, u32[]{:S(2)}) collective-permute-start(bf16[384,1536]{1,0:T(8,128)(2,1)S(1)} %get-tuple-element.290), channel_id=1, source_target_pairs={{0,8},{8,0},{16,24},{24,16},{1,9},{9,1},{17,25},{25,17},{2,10},{10... | collective-permute-start | bytes 3538952 | tf_op jit(solution)/shard_map/ppermute | solution.py:331
  138.8 36.7 %collective-permute-start.36 = (bf16[192,1536]{1,0:T(8,128)(2,1)S(1)}, bf16[192,1536]{1,0:T(8,128)(2,1)S(1)}, u32[]{:S(2)}, u32[]{:S(2)}) collective-permute-start(bf16[192,1536]{1,0:T(8,128)(2,1)S(1)} %get-tuple-element.316), channel_id=1, source_target_pairs={{0,2},{2,0},{4,6},{6,4},{1,3},{3,1},{5,7},{7,5},{8,10},{10,8},{12,... | collective-permute-start | bytes 1769480 | tf_op jit(solution)/shard_map/ppermute | solution.py:331
  140.2 36.7 %collective-permute-start.37 = (bf16[192,1536]{1,0:T(8,128)(2,1)S(1)}, bf16[192,1536]{1,0:T(8,128)(2,1)S(1)}, u32[]{:S(2)}, u32[]{:S(2)}) collective-permute-start(bf16[192,1536]{1,0:T(8,128)(2,1)S(1)} %get-tuple-element.317), channel_id=1, source_target_pairs={{0,4},{2,6},{4,0},{6,2},{1,5},{3,7},{5,1},{7,3},{8,12},{10,14},{12... | collective-permute-start | bytes 1769480 | tf_op jit(solution)/shard_map/ppermute | solution.py:331
  149.5 19.4 %collective-permute-start.31 = (bf16[384,384]{1,0:T(8,128)(2,1)S(1)}, bf16[384,384]{1,0:T(8,128)(2,1)S(1)}, u32[]{:S(2)}, u32[]{:S(2)}) collective-permute-start(bf16[384,384]{1,0:T(8,128)(2,1)S(1)} %get-tuple-element.291), channel_id=1, source_target_pairs={{0,8},{8,0},{16,24},{24,16},{1,9},{9,1},{17,25},{25,17},{2,10},{10... | collective-permute-start | bytes 884744 | tf_op jit(solution)/shard_map/ppermute | solution.py:331
  149.8 28.4 %collective-permute-start.38 = (bf16[192,1536]{1,0:T(8,128)(2,1)S(1)}, bf16[192,1536]{1,0:T(8,128)(2,1)S(1)}, u32[]{:S(2)}, u32[]{:S(2)}) collective-permute-start(bf16[192,1536]{1,0:T(8,128)(2,1)S(1)} %get-tuple-element.318), channel_id=1, source_target_pairs={{0,6},{2,4},{4,2},{6,0},{1,7},{3,5},{5,3},{7,1},{8,14},{10,12},{12... | collective-permute-start | bytes 1769480 | tf_op jit(solution)/shard_map/ppermute | solution.py:331
  173.5 27.9 %collective-permute-start.40 = (bf16[192,1536]{1,0:T(8,128)(2,1)S(1)}, bf16[192,1536]{1,0:T(8,128)(2,1)S(1)}, u32[]{:S(2)}, u32[]{:S(2)}) collective-permute-start(bf16[192,1536]{1,0:T(8,128)(2,1)S(1)} %get-tuple-element.328), channel_id=1, source_target_pairs={{0,16},{8,24},{16,0},{24,8},{1,17},{9,25},{17,1},{25,9},{2,18},{10... | collective-permute-start | bytes 1769480 | tf_op jit(solution)/shard_map/ppermute | solution.py:331
  174.8 21.7 %collective-permute-start.33 = (bf16[192,1152]{1,0:T(8,128)(2,1)S(1)}, bf16[192,1152]{1,0:T(8,128)(2,1)S(1)}, u32[]{:S(2)}, u32[]{:S(2)}) collective-permute-start(bf16[192,1152]{1,0:T(8,128)(2,1)S(1)} %get-tuple-element.308), channel_id=1, source_target_pairs={{0,2},{2,0},{4,6},{6,4},{1,3},{3,1},{5,7},{7,5},{8,10},{10,8},{12,... | collective-permute-start | bytes 1327112 | tf_op jit(solution)/shard_map/ppermute | solution.py:331
  175.5 21.0 %collective-permute-start.34 = (bf16[192,1152]{1,0:T(8,128)(2,1)S(1)}, bf16[192,1152]{1,0:T(8,128)(2,1)S(1)}, u32[]{:S(2)}, u32[]{:S(2)}) collective-permute-start(bf16[192,1152]{1,0:T(8,128)(2,1)S(1)} %get-tuple-element.309), channel_id=1, source_target_pairs={{0,4},{2,6},{4,0},{6,2},{1,5},{3,7},{5,1},{7,3},{8,12},{10,14},{12... | collective-permute-start | bytes 1327112 | tf_op jit(solution)/shard_map/ppermute | solution.py:331
  176.9 19.6 %collective-permute-start.35 = (bf16[192,1152]{1,0:T(8,128)(2,1)S(1)}, bf16[192,1152]{1,0:T(8,128)(2,1)S(1)}, u32[]{:S(2)}, u32[]{:S(2)}) collective-permute-start(bf16[192,1152]{1,0:T(8,128)(2,1)S(1)} %get-tuple-element.310), channel_id=1, source_target_pairs={{0,6},{2,4},{4,2},{6,0},{1,7},{3,5},{5,3},{7,1},{8,14},{10,12},{12... | collective-permute-start | bytes 1327112 | tf_op jit(solution)/shard_map/ppermute | solution.py:331
  178.3 18.2 %collective-permute-start.39 = (f32[16,768]{1,0:T(8,128)S(1)}, f32[16,768]{1,0:T(8,128)S(1)}, u32[]{:S(2)}, u32[]{:S(2)}) collective-permute-start(f32[16,768]{1,0:T(8,128)S(1)} %add.75), channel_id=1, source_target_pairs={{0,4},{2,6},{4,0},{6,2},{1,5},{3,7},{5,1},{7,3},{8,12},{10,14},{12... | collective-permute-start | bytes 147464 | tf_op jit(solution)/shard_map/ppermute | solution.py:331
  201.4 8.9 %collective-permute-start.42 = (bf16[4,128,768]{2,1,0:T(8,128)(2,1)S(1)}, bf16[4,128,768]{2,1,0:T(8,128)(2,1)S(1)}, u32[]{:S(2)}, u32[]{:S(2)}) collective-permute-start(bf16[4,128,768]{2,1,0:T(8,128)(2,1)S(1)} %get-tuple-element.334), channel_id=1, source_target_pairs={{0,1},{1,0},{2,3},{3,2},{4,5},{5,4},{6,7},{7,6},{8,9},{9,8},{10,11... | collective-permute-start | bytes 2359304 | tf_op jit(solution)/shard_map/ppermute | solution.py:331
  203.6 10.7 %collective-permute-start.47 = (bf16[96,1536]{1,0:T(8,128)(2,1)S(1)}, bf16[96,1536]{1,0:T(8,128)(2,1)S(1)}, u32[]{:S(2)}, u32[]{:S(2)}) collective-permute-start(bf16[96,1536]{1,0:T(8,128)(2,1)S(1)} %get-tuple-element.470), channel_id=1, source_target_pairs={{0,4},{2,6},{4,0},{6,2},{1,5},{3,7},{5,1},{7,3},{8,12},{10,14},{12... | collective-permute-start | bytes 884744 | tf_op jit(solution)/shard_map/ppermute | solution.py:331
  204.4 11.9 %collective-permute-start.46 = (bf16[96,1536]{1,0:T(8,128)(2,1)S(1)}, bf16[96,1536]{1,0:T(8,128)(2,1)S(1)}, u32[]{:S(2)}, u32[]{:S(2)}) collective-permute-start(bf16[96,1536]{1,0:T(8,128)(2,1)S(1)} %get-tuple-element.471), channel_id=1, source_target_pairs={{0,2},{2,0},{4,6},{6,4},{1,3},{3,1},{5,7},{7,5},{8,10},{10,8},{12,... | collective-permute-start | bytes 884744 | tf_op jit(solution)/shard_map/ppermute | solution.py:331
  210.7 17.9 %collective-permute-start.45 = (bf16[96,1536]{1,0:T(8,128)(2,1)S(1)}, bf16[96,1536]{1,0:T(8,128)(2,1)S(1)}, u32[]{:S(2)}, u32[]{:S(2)}) collective-permute-start(bf16[96,1536]{1,0:T(8,128)(2,1)S(1)} %get-tuple-element.350), channel_id=1, source_target_pairs={{0,8},{8,0},{16,24},{24,16},{1,9},{9,1},{17,25},{25,17},{2,10},{10... | collective-permute-start | bytes 884744 | tf_op jit(solution)/shard_map/ppermute | solution.py:331
  213.3 13.5 %collective-permute-start.44 = (bf16[48,1152]{1,0:T(8,128)(2,1)S(1)}, bf16[48,1152]{1,0:T(8,128)(2,1)S(1)}, u32[]{:S(2)}, u32[]{:S(2)}) collective-permute-start(bf16[48,1152]{1,0:T(8,128)(2,1)S(1)} %get-tuple-element.349), channel_id=1, source_target_pairs={{0,16},{8,24},{16,0},{24,8},{1,17},{9,25},{17,1},{25,9},{2,18},{10... | collective-permute-start | bytes 331784 | tf_op jit(solution)/shard_map/ppermute | solution.py:331
  214.4 14.2 %collective-permute-start.48 = (bf16[192,384]{1,0:T(8,128)(2,1)S(1)}, bf16[192,384]{1,0:T(8,128)(2,1)S(1)}, u32[]{:S(2)}, u32[]{:S(2)}) collective-permute-start(bf16[192,384]{1,0:T(8,128)(2,1)S(1)} %get-tuple-element.353), channel_id=1, source_target_pairs={{0,16},{8,24},{16,0},{24,8},{1,17},{9,25},{17,1},{25,9},{2,18},{10... | collective-permute-start | bytes 442376 | tf_op jit(solution)/shard_map/ppermute | solution.py:331
  228.9 10.8 %collective-permute-start.53 = (bf16[96,1536]{1,0:T(8,128)(2,1)S(1)}, bf16[96,1536]{1,0:T(8,128)(2,1)S(1)}, u32[]{:S(2)}, u32[]{:S(2)}) collective-permute-start(bf16[96,1536]{1,0:T(8,128)(2,1)S(1)} %add_convert_fusion.2.refs_0_), channel_id=1, source_target_pairs={{0,4},{2,6},{4,0},{6,2},{1,5},{3,7},{5,1},{7,3},{8,12},{10,14},{12... | collective-permute-start | bytes 884744 | tf_op jit(solution)/shard_map/ppermute | solution.py:331
  229.6 10.1 %collective-permute-start.54 = (bf16[96,1536]{1,0:T(8,128)(2,1)S(1)}, bf16[96,1536]{1,0:T(8,128)(2,1)S(1)}, u32[]{:S(2)}, u32[]{:S(2)}) collective-permute-start(bf16[96,1536]{1,0:T(8,128)(2,1)S(1)} %add_convert_fusion.1.refs_2_), channel_id=1, source_target_pairs={{0,2},{2,0},{4,6},{6,4},{1,3},{3,1},{5,7},{7,5},{8,10},{10,8},{12,... | collective-permute-start | bytes 884744 | tf_op jit(solution)/shard_map/ppermute | solution.py:331
  239.7 14.3 %collective-permute-start.59 = (bf16[128,768]{1,0:T(8,128)(2,1)S(1)}, bf16[128,768]{1,0:T(8,128)(2,1)S(1)}, u32[]{:S(2)}, u32[]{:S(2)}) collective-permute-start(bf16[128,768]{1,0:T(8,128)(2,1)S(1)} %get-tuple-element.387), channel_id=1, source_target_pairs={{0,4},{2,6},{4,0},{6,2},{1,5},{3,7},{5,1},{7,3},{8,12},{10,14},{12... | collective-permute-start | bytes 589832 | tf_op jit(solution)/shard_map/ppermute | solution.py:331
  241.4 12.6 %collective-permute-start.60 = (bf16[128,768]{1,0:T(8,128)(2,1)S(1)}, bf16[128,768]{1,0:T(8,128)(2,1)S(1)}, u32[]{:S(2)}, u32[]{:S(2)}) collective-permute-start(bf16[128,768]{1,0:T(8,128)(2,1)S(1)} %get-tuple-element.388), channel_id=1, source_target_pairs={{0,6},{2,4},{4,2},{6,0},{1,7},{3,5},{5,3},{7,1},{8,14},{10,12},{12... | collective-permute-start | bytes 589832 | tf_op jit(solution)/shard_map/ppermute | solution.py:331
  243.0 11.0 %collective-permute-start.56 = (bf16[48,1536]{1,0:T(8,128)(2,1)S(1)}, bf16[48,1536]{1,0:T(8,128)(2,1)S(1)}, u32[]{:S(2)}, u32[]{:S(2)}) collective-permute-start(bf16[48,1536]{1,0:T(8,128)(2,1)S(1)} %add_convert_fusion.7.refs_2_), channel_id=1, source_target_pairs={{0,4},{2,6},{4,0},{6,2},{1,5},{3,7},{5,1},{7,3},{8,12},{10,14},{12... | collective-permute-start | bytes 442376 | tf_op jit(solution)/shard_map/ppermute | solution.py:331
  243.3 10.8 %collective-permute-start.55 = (bf16[48,1536]{1,0:T(8,128)(2,1)S(1)}, bf16[48,1536]{1,0:T(8,128)(2,1)S(1)}, u32[]{:S(2)}, u32[]{:S(2)}) collective-permute-start(bf16[48,1536]{1,0:T(8,128)(2,1)S(1)} %add_convert_fusion.7.refs_2_), channel_id=1, source_target_pairs={{0,2},{2,0},{4,6},{6,4},{1,3},{3,1},{5,7},{7,5},{8,10},{10,8},{12,... | collective-permute-start | bytes 442376 | tf_op jit(solution)/shard_map/ppermute | solution.py:331
  (35 other events, 292.4 us)

commit v8 on v7

--- a/solution.py
+++ b/solution.py
@@ -1062,17 +1062,17 @@
     half_pieces = [half[s] for s in range(ctx_count)]
     half_brought = [half_pieces[0], swap(half_pieces[1], "ctx", 1)]
     small_other = swap(small, "fsdp", 2)
-    out_brought = swap(out_sent, "fsdp", 2)
-    last_brought, up_brought, down_other, out_brought, small_other, half_pieces = together(
-        last_brought, up_brought, down_other, out_brought, small_other, half_pieces
+    last_brought, up_brought, down_other, out_sent, small_other, half_pieces = together(
+        last_brought, up_brought, down_other, out_sent, small_other, half_pieces
     )
     part = low(wide(last_kept) + wide(last_brought))
     up_kept, up_sent = sum_and_cut([up_kept, up_brought])
     owned_down = [low(wide(mine) + wide(other)) for mine, other in zip(owned_down, down_other)]
     small = small + small_other
-    part, up_sent, owned_down, out_brought, small, half_pieces = together(
-        part, up_sent, owned_down, out_brought, small, half_pieces
-    )
+    part, up_sent, owned_down, out_sent, small, half_pieces = together(
+        part, up_sent, owned_down, out_sent, small, half_pieces
+    )
+    out_brought = swap(out_sent, "fsdp", 2)
     shared = [part, swap(part, "ctx", 1), swap(part, "ctx", 2)]
     up_brought = swap(up_sent, "fsdp", 2)
     down_other = [swap(owned_down[0], "ctx", 2), swap(owned_down[1], "ctx", 1)]

time: 276 us -> 278 us (level)
  transfers between devices with their start and end apart: 66 -> 66, of which waited for: 24 -> 25; matrix products, arithmetic and copies ran while one was open for 2% -> 2% of each run, Pallas kernels for 30% -> 30%
where the time goes in v8:
time: 278 us
  waiting for transfers between devices  95.3 us (34%)
  Pallas kernels  89.4 us (32%)
  starting transfers between devices  74.3 us (27%)
  local copies, waits for them, and re-layouts  10.8 us (4%)
  between operations  4.55 us (2%)
  other arithmetic  3.15 us (1%)
    ppermute x65, waiting for transfers between devices, swap(): return lax.ppermute(values, axis, pairs)  93.5 us
    ppermute x65, starting transfers between devices, swap(): return lax.ppermute(values, axis, pairs)  70.4 us
    pallas_call x1, Pallas kernels, attend_back(): pl.pallas_call(lambda *refs: attend_back_kernel(*refs, block=block), grid...  15.5 us
    pallas_call x4, Pallas kernels, weight_grad(): pl.pallas_call(lambda *refs: weight_grad_kernel(*refs, chunks=chunks, fsd...  13.9 us
    pallas_call x3, Pallas kernels, gathered_layer(): pl.pallas_call(kernel, grid_spec=pltpu.PrefetchScalarGridSpec(num_scalar_...  13 us
    pallas_call x1, Pallas kernels, attend(): pl.pallas_call(lambda *refs: attend_kernel(*refs, block=block), grid_spec...  10.8 us
    pallas_call x3, Pallas kernels, by_rows(): pl.pallas_call(kernel, grid_spec=pltpu.PrefetchScalarGridSpec(num_scalar_...  9.88 us
    pallas_call x3, Pallas kernels, rows_times(): pl.pallas_call(lambda *refs: rows_kernel(*refs, transposed=transposed), g...  6.4 us
  transfers between devices with their start and end apart: 66, of which 25 were waited for; matrix products, arithmetic and copies ran while one was open for 2% of the time, Pallas kernels for 30%

profile of v8, /device:TPU:0, one launch (start us, length us, event | category | flops | bytes accessed | tf_op | source)
XLA Modules:
  0.0 277.6 jit_solution(17686701741439683803)
XLA Ops:
  0.7 1.6 reshape.107
  5.0 5.0 %collective-permute-start.2 = (bf16[48,1536]{1,0:T(8,128)(2,1)}, bf16[48,1536]{1,0:T(8,128)(2,1)S(1)}, u32[]{:S(2)}, u32[]{:S(2)}) collective-permute-start(bf16[48,1536]{1,0:T(8,128)(2,1)} %constant_dynamic-slice_fusion.2), channel_id=1, source_target_pairs={{0,24},{8,16},{16,8},{24,0},{1,25},{9,17},{17,9},{25,1},{2,26},{10... | collective-permute-start | bytes 442376 | tf_op jit(solution)/shard_map/ppermute | solution.py:331
  10.6 3.9 %all-to-all-start = ((bf16[4,128,768]{2,1,0:T(8,128)(2,1)}), bf16[4,128,768]{2,1,0:T(8,128)(2,1)S(1)}, u32[]{:S(2)}, u32[]{:S(2)}) async-start(bf16[4,128,768]{2,1,0:T(8,128)(2,1)} %constant_dynamic-slice_fusion.3), calls=%async_computation | async-start | bytes 1572864 | tf_op jit(solution)/shard_map/all_to_all | solution.py:382
  18.4 4.4 %collective-permute-done.1.refs_1_ = bf16[48,1536]{1,0:T(8,128)(2,1)} collective-permute-done((bf16[48,1536]{1,0:T(8,128)(2,1)}, bf16[48,1536]{1,0:T(8,128)(2,1)}, u32[]{:S(2)}, u32[]{:S(2)}) %collective-permute-start.1) | collective-permute-done | bytes 147488 | tf_op jit(solution)/shard_map/ppermute | solution.py:331
  22.8 1.8 all-to-all-done.own_ref
  25.6 1.5 collective-permute-start.5
  30.7 4.2 %collective-permute-done.7.refs_0_ = bf16[48,1536]{1,0:T(8,128)(2,1)S(1)} collective-permute-done((bf16[48,1536]{1,0:T(8,128)(2,1)}, bf16[48,1536]{1,0:T(8,128)(2,1)S(1)}, u32[]{:S(2)}, u32[]{:S(2)}) %collective-permute-start.7) | collective-permute-done | bytes 147488 | tf_op jit(solution)/shard_map/ppermute | solution.py:331
  34.8 2.4 collective-permute-start.8
  38.6 9.2 %collective-permute-done.8.refs_1_ = bf16[48,1536]{1,0:T(8,128)(2,1)S(1)} collective-permute-done((bf16[48,1536]{1,0:T(8,128)(2,1)}, bf16[48,1536]{1,0:T(8,128)(2,1)S(1)}, u32[]{:S(2)}, u32[]{:S(2)}) %collective-permute-start.8) | collective-permute-done | bytes 147488 | tf_op jit(solution)/shard_map/ppermute | solution.py:331
  47.8 2.1 collective-permute-done.9.refs_2_
  55.9 2.6 collective-permute-start.14
  58.5 3.5 %project.1 = (bf16[1024,1152]{1,0:T(8,128)(2,1)S(1)}, bf16[768,1536]{1,0:T(8,128)(2,1)S(1)}) custom-call(s32[2]{0:T(128)S(1)} %get-tuple-element.218.places.refs_0_, bf16[1024,768]{1,0:T(8,128)(2,1)S(1)} %bitcast.57, f32[1,1152]{1,0:T(1,128)S(1)} %reshape_reshape.3.bias_ref, bf16[192,1536]{1,0:T(8,128)(2,1)S(1)} %constant_dynamic-update-slice_fusion.own_ref, ...), custom_call_target="tpu_custom_call" | custom-call | tf_op jit(solution)/shard_map/project/pallas_call | solution.py:296
  63.5 10.8 %attend.1 = (bf16[1024,384]{1,0:T(8,128)(2,1)S(1)}, f32[3,2,1024]{2,1,0:T(2,128)S(1)}) custom-call(s32[3]{0:T(128)S(1)} %convert_element_type.128.refs_0_.facts, bf16[1024,1152]{1,0:T(8,128)(2,1)S(1)} %get-tuple-element.237.refs_1_.refs_2_.refs_3_, bf16[1024,1152]{1,0:T(8,128)(2,1)S(1)} %get-tuple-element.237.refs_1_.refs_2_.refs_3_, ...), custom_call_target="tpu_custom_call" | custom-call | tf_op jit(solution)/shard_map/attend/pallas_call | solution.py:174
  74.3 1.6 rows_times.3.mine_ref
  76.1 1.5 collective-permute-start.19
  81.2 8.9 %collective-permute-done.19.refs_3_ = bf16[144,1536]{1,0:T(8,128)(2,1)S(1)} collective-permute-done((bf16[144,1536]{1,0:T(8,128)(2,1)S(1)}, bf16[144,1536]{1,0:T(8,128)(2,1)S(1)}, u32[]{:S(2)}, u32[]{:S(2)}) %collective-permute-start.19) | collective-permute-done | bytes 442400 | tf_op jit(solution)/shard_map/ppermute | solution.py:331
  92.1 1.6 first_norm.1
  93.7 5.5 %up.1 = (bf16[1024,1536]{1,0:T(8,128)(2,1)S(1)}, bf16[1024,1536]{1,0:T(8,128)(2,1)S(1)}, bf16[768,1536]{1,0:T(8,128)(2,1)S(1)}) custom-call(s32[2]{0:T(128)S(1)} %get-tuple-element.218.places.refs_0_, bf16[1024,768]{1,0:T(8,128)(2,1)S(1)} %get-tuple-element.246.left_ref.refs_1_, f32[1,1536]{1,0:T(1,128)S(1)} %reshape.114.bias_ref, ...), custom_call_target="tpu_custom_call" | custom-call | tf_op jit(solution)/shard_map/up/pallas_call | solution.py:296
  99.6 4.0 %down.1 = (bf16[1024,768]{1,0:T(8,128)(2,1)S(1)}, bf16[768,1536]{1,0:T(8,128)(2,1)S(1)}) custom-call(s32[2]{0:T(128)S(1)} %get-tuple-element.218.places.refs_0_, bf16[1024,1536]{1,0:T(8,128)(2,1)S(1)} %get-tuple-element.255.left_ref.refs_2_, bf16[192,1536]{1,0:T(8,128)(2,1)S(1)} %copy-done.4, bf16[144,1536]{1,0:T(8,128)(2,1)S(1)} %stack_rows.8.refs_0_, ...), custom_call_target="tpu_custom_call" | custom-call | tf_op jit(solution)/shard_map/down/pallas_call | solution.py:296
  103.8 3.7 %collective-permute-done.21.refs_2_ = bf16[128,768]{1,0:T(8,128)(2,1)S(1)} collective-permute-done((bf16[128,768]{1,0:T(8,128)(2,1)S(1)}, bf16[128,768]{1,0:T(8,128)(2,1)S(1)}, u32[]{:S(2)}, u32[]{:S(2)}) %collective-permute-start.21) | collective-permute-done | bytes 196640 | tf_op jit(solution)/shard_map/ppermute | solution.py:331
  108.3 3.9 %collective-permute-done.24.other_teacher_ref = bf16[4,128,768]{2,1,0:T(8,128)(2,1)S(1)} collective-permute-done((bf16[4,128,768]{2,1,0:T(8,128)(2,1)S(1)}, bf16[4,128,768]{2,1,0:T(8,128)(2,1)S(1)}, u32[]{:S(2)}, u32[]{:S(2)}) %collective-permute-start.24) | collective-permute-done | bytes 786464 | tf_op jit(solution)/shard_map/ppermute | solution.py:331
  112.1 5.1 %second_norm.1 = (bf16[4,128,768]{2,1,0:T(8,128)(2,1)S(1)}, f32[1024,768]{1,0:T(8,128)S(1)}, bf16[1024,768]{1,0:T(8,128)(2,1)S(1)}, f32[8,768]{1,0:T(8,128)S(1)}) custom-call(s32[3]{0:T(128)S(1)} %convert_element_type.128.refs_0_.facts, f32[1024,768]{1,0:T(8,128)S(1)} %get-tuple-element.245.normal_ref, f32[1,768]{1,0:T(1,128)S(1)} %reshape.112.gain_ref.gain1_ref, ...), custom_call_target="tpu_custom_call" | custom-call | tf_op jit(solution)/shard_map/second_norm/pallas_call | solution.py:497
  120.8 4.0 %weight_grad.4 = (bf16[384,1536]{1,0:T(8,128)(2,1)S(1)}, bf16[384,1536]{1,0:T(8,128)(2,1)S(1)}) custom-call(s32[2]{0:T(128)S(1)} %get-tuple-element.218.places.refs_0_, bf16[1024,768]{1,0:T(8,128)(2,1)S(1)} %get-tuple-element.271.refs_1_.low_ref, bf16[1024,1536]{1,0:T(8,128)(2,1)S(1)} %get-tuple-element.255.left_ref.refs_2_), custom_call_target="tpu_custom_call" | custom-call | tf_op jit(solution)/shard_map/weight_grad/pallas_call | solution.py:717
  124.9 3.9 %grad_pre.1 = (bf16[1024,1536]{1,0:T(8,128)(2,1)S(1)}, f32[8,1536]{1,0:T(8,128)S(1)}) custom-call(bf16[1024,768]{1,0:T(8,128)(2,1)S(1)} %get-tuple-element.271.refs_1_.low_ref, bf16[768,1536]{1,0:T(8,128)(2,1)S(1)} %get-tuple-element.272.weight_ref, bf16[1024,1536]{1,0:T(8,128)(2,1)S(1)} %get-tuple-element.273.slope_ref), custom_call_target="tpu_custom_call" | custom-call | tf_op jit(solution)/shard_map/grad_pre/pallas_call | solution.py:531
  128.7 3.3 %rows_times.4.mine_ref = bf16[1024,768]{1,0:T(8,128)(2,1)S(1)} custom-call(bf16[1024,1536]{1,0:T(8,128)(2,1)S(1)} %get-tuple-element.314.refs_0_.refs_2_, bf16[768,1536]{1,0:T(8,128)(2,1)S(1)} %get-tuple-element.275.refs_1_), custom_call_target="tpu_custom_call" | custom-call | tf_op jit(solution)/shard_map/rows_times/pallas_call | solution.py:551
  132.1 2.3 collective-permute-start.30
  134.7 4.0 %weight_grad.7 = (bf16[192,1536]{1,0:T(8,128)(2,1)S(1)}, bf16[192,1536]{1,0:T(8,128)(2,1)S(1)}, bf16[192,1536]{1,0:T(8,128)(2,1)S(1)}, bf16[192,1536]{1,0:T(8,128)(2,1)S(1)}) custom-call(s32[2]{0:T(128)S(1)} %get-tuple-element.218.places.refs_0_, bf16[1024,768]{1,0:T(8,128)(2,1)S(1)} %get-tuple-element.246.left_ref.refs_1_, ...), custom_call_target="tpu_custom_call" | custom-call | tf_op jit(solution)/shard_map/weight_grad/pallas_call | solution.py:717
  140.8 2.3 join_halves.4
  143.1 3.2 %first_norm_back.1 = (bf16[1024,768]{1,0:T(8,128)(2,1)S(1)}, f32[4,128,768]{2,1,0:T(8,128)S(1)}, f32[8,768]{1,0:T(8,128)S(1)}) custom-call(s32[3]{0:T(128)S(1)} %convert_element_type.128.refs_0_.facts, f32[1024,768]{1,0:T(8,128)S(1)} %get-tuple-element.267.grad_ref, bf16[1024,768]{1,0:T(8,128)(2,1)S(1)} %rows_times.4.mine_ref, ...), custom_call_target="tpu_custom_call" | custom-call | tf_op jit(solution)/shard_map/first_norm_back/pallas_call | solution.py:497
  146.3 1.6 weight_grad.5
  147.9 1.5 rows_times.5.refs_4_
  151.3 15.5 %attend_back.1 = (bf16[1024,1152]{1,0:T(8,128)(2,1)S(1)}, f32[8,1152]{1,0:T(8,128)S(1)}) custom-call(s32[3]{0:T(128)S(1)} %convert_element_type.128.refs_0_.facts, bf16[1024,1152]{1,0:T(8,128)(2,1)S(1)} %get-tuple-element.237.refs_1_.refs_2_.refs_3_, bf16[1024,1152]{1,0:T(8,128)(2,1)S(1)} %get-tuple-element.237.refs_1_.refs_2_.refs_3_, ...), custom_call_target="tpu_custom_call" | custom-call | tf_op jit(solution)/shard_map/attend_back/pallas_call | solution.py:198
  168.9 4.3 %weight_grad.6 = (bf16[192,1152]{1,0:T(8,128)(2,1)S(1)}, bf16[192,1152]{1,0:T(8,128)(2,1)S(1)}, bf16[192,1152]{1,0:T(8,128)(2,1)S(1)}, bf16[192,1152]{1,0:T(8,128)(2,1)S(1)}) custom-call(s32[2]{0:T(128)S(1)} %get-tuple-element.218.places.refs_0_, bf16[1024,768]{1,0:T(8,128)(2,1)S(1)} %bitcast.59, bf16[1024,1152]{1,0:T(8,128)(2,1)S(1)} %get-tuple-element.311.refs_2_.grad_ref), custom_call_target="tpu_custom_call" | custom-call | tf_op jit(solution)/shard_map/weight_grad/pallas_call | solution.py:717
  179.3 3.9 %input_back.1 = (bf16[4,128,768]{2,1,0:T(8,128)(2,1)S(1)}, bf16[4,128,768]{2,1,0:T(8,128)(2,1)S(1)}) custom-call(s32[3]{0:T(128)S(1)} %convert_element_type.128.refs_0_.facts, bf16[1024,1152]{1,0:T(8,128)(2,1)S(1)} %get-tuple-element.311.refs_2_.grad_ref, bf16[768,1536]{1,0:T(8,128)(2,1)S(1)} %get-tuple-element.244.weight_ref), custom_call_target="tpu_custom_call" | custom-call | tf_op jit(solution)/shard_map/input_back/pallas_call | solution.py:597
  183.2 13.3 %collective-permute-done.39 = f32[16,768]{1,0:T(8,128)S(1)} collective-permute-done((f32[16,768]{1,0:T(8,128)S(1)}, f32[16,768]{1,0:T(8,128)S(1)}, u32[]{:S(2)}, u32[]{:S(2)}) %collective-permute-start.39) | collective-permute-done | bytes 49184 | tf_op jit(solution)/shard_map/ppermute | solution.py:331
  196.7 4.7 %collective-permute-done.40 = bf16[192,1536]{1,0:T(8,128)(2,1)S(1)} collective-permute-done((bf16[192,1536]{1,0:T(8,128)(2,1)S(1)}, bf16[192,1536]{1,0:T(8,128)(2,1)S(1)}, u32[]{:S(2)}, u32[]{:S(2)}) %collective-permute-start.40) | collective-permute-done | bytes 589856 | tf_op jit(solution)/shard_map/ppermute | solution.py:331
  201.5 2.0 collective-permute-start.41
  206.0 4.3 %collective-permute-done.41.refs_1_ = bf16[96,1152]{1,0:T(8,128)(2,1)S(1)} collective-permute-done((bf16[96,1152]{1,0:T(8,128)(2,1)S(1)}, bf16[96,1152]{1,0:T(8,128)(2,1)S(1)}, u32[]{:S(2)}, u32[]{:S(2)}) %collective-permute-start.41) | collective-permute-done | bytes 221216 | tf_op jit(solution)/shard_map/ppermute | solution.py:331
  211.5 1.8 collective-permute-start.48
  214.5 5.0 %collective-permute-done.48 = f32[16,768]{1,0:T(8,128)S(1)} collective-permute-done((f32[16,768]{1,0:T(8,128)S(1)}, f32[16,768]{1,0:T(8,128)S(1)}, u32[]{:S(2)}, u32[]{:S(2)}) %collective-permute-start.48) | collective-permute-done | bytes 49184 | tf_op jit(solution)/shard_map/ppermute | solution.py:331
  220.6 2.1 collective-permute-done.45.refs_1_
  227.1 1.6 collective-permute-start.52
  228.7 4.6 %collective-permute-done.50.refs_4_ = bf16[48,1152]{1,0:T(8,128)(2,1)S(1)} collective-permute-done((bf16[48,1152]{1,0:T(8,128)(2,1)S(1)}, bf16[48,1152]{1,0:T(8,128)(2,1)S(1)}, u32[]{:S(2)}, u32[]{:S(2)}) %collective-permute-start.50) | collective-permute-done | bytes 110624 | tf_op jit(solution)/shard_map/ppermute | solution.py:331
  234.0 4.3 %collective-permute-done.49.refs_3_ = bf16[48,1152]{1,0:T(8,128)(2,1)S(1)} collective-permute-done((bf16[48,1152]{1,0:T(8,128)(2,1)S(1)}, bf16[48,1152]{1,0:T(8,128)(2,1)S(1)}, u32[]{:S(2)}, u32[]{:S(2)}) %collective-permute-start.49) | collective-permute-done | bytes 110624 | tf_op jit(solution)/shard_map/ppermute | solution.py:331
  245.5 10.7 %collective-permute-done.57.refs_5_ = bf16[48,1152]{1,0:T(8,128)(2,1)S(1)} collective-permute-done((bf16[48,1152]{1,0:T(8,128)(2,1)S(1)}, bf16[48,1152]{1,0:T(8,128)(2,1)S(1)}, u32[]{:S(2)}, u32[]{:S(2)}) %collective-permute-start.57) | collective-permute-done | bytes 110624 | tf_op jit(solution)/shard_map/ppermute | solution.py:331
  258.4 3.1 %collective-permute-done.61 = bf16[192,384]{1,0:T(8,128)(2,1)S(1)} collective-permute-done((bf16[192,384]{1,0:T(8,128)(2,1)S(1)}, bf16[192,384]{1,0:T(8,128)(2,1)S(1)}, u32[]{:S(2)}, u32[]{:S(2)}) %collective-permute-start.61) | collective-permute-done | bytes 147488 | tf_op jit(solution)/shard_map/ppermute | solution.py:331
  268.5 1.6 place_rows.3
  270.1 2.7 join_halves.5
  (213 shorter events, 72.7 us)
Async XLA Ops:
  5.0 13.4 %collective-permute-start.2 = (bf16[48,1536]{1,0:T(8,128)(2,1)}, bf16[48,1536]{1,0:T(8,128)(2,1)S(1)}, u32[]{:S(2)}, u32[]{:S(2)}) collective-permute-start(bf16[48,1536]{1,0:T(8,128)(2,1)} %constant_dynamic-slice_fusion.2), channel_id=1, source_target_pairs={{0,24},{8,16},{16,8},{24,0},{1,25},{9,17},{17,9},{25,1},{2,26},{10... | collective-permute-start | bytes 442376 | tf_op jit(solution)/shard_map/ppermute | solution.py:331
  10.0 12.8 %collective-permute-start.1 = (bf16[48,1536]{1,0:T(8,128)(2,1)}, bf16[48,1536]{1,0:T(8,128)(2,1)}, u32[]{:S(2)}, u32[]{:S(2)}) collective-permute-start(bf16[48,1536]{1,0:T(8,128)(2,1)} %constant_dynamic-slice_fusion.2), channel_id=1, source_target_pairs={{0,16},{8,24},{16,0},{24,8},{1,17},{9,25},{17,1},{25,9},{2,18},{10... | collective-permute-start | bytes 442376 | tf_op jit(solution)/shard_map/ppermute | solution.py:331
  10.0 12.8 %collective-permute-start = (bf16[48,1536]{1,0:T(8,128)(2,1)}, bf16[48,1536]{1,0:T(8,128)(2,1)}, u32[]{:S(2)}, u32[]{:S(2)}) collective-permute-start(bf16[48,1536]{1,0:T(8,128)(2,1)} %constant_dynamic-slice_fusion.2), channel_id=1, source_target_pairs={{0,8},{8,0},{16,24},{24,16},{1,9},{9,1},{17,25},{25,17},{2,10},{10... | collective-permute-start | bytes 442376 | tf_op jit(solution)/shard_map/ppermute | solution.py:331
  10.6 14.0 %all-to-all-start = ((bf16[4,128,768]{2,1,0:T(8,128)(2,1)}), bf16[4,128,768]{2,1,0:T(8,128)(2,1)S(1)}, u32[]{:S(2)}, u32[]{:S(2)}) async-start(bf16[4,128,768]{2,1,0:T(8,128)(2,1)} %constant_dynamic-slice_fusion.3), calls=%async_computation | async-start | bytes 1572864 | tf_op jit(solution)/shard_map/all_to_all | solution.py:382
  24.6 12.6 %collective-permute-start.6 = (bf16[4,128,768]{2,1,0:T(8,128)(2,1)S(1)}, bf16[4,128,768]{2,1,0:T(8,128)(2,1)S(1)}, u32[]{:S(2)}, u32[]{:S(2)}) collective-permute-start(bf16[4,128,768]{2,1,0:T(8,128)(2,1)S(1)} %all-to-all-done.own_ref), channel_id=1, source_target_pairs={{0,1},{1,0},{2,3},{3,2},{4,5},{5,4},{6,7},{7,6},{8,9},{9,8},{10,11... | collective-permute-start | bytes 2359304 | tf_op jit(solution)/shard_map/ppermute | solution.py:331
  25.6 24.3 %collective-permute-start.5 = (bf16[160,1536]{1,0:T(8,128)(2,1)S(1)}, bf16[160,1536]{1,0:T(8,128)(2,1)S(1)}, u32[]{:S(2)}, u32[]{:S(2)}) collective-permute-start(bf16[160,1536]{1,0:T(8,128)(2,1)S(1)} %stack_rows.6.refs_0_), channel_id=1, source_target_pairs={{0,6},{2,4},{4,2},{6,0},{1,7},{3,5},{5,3},{7,1},{8,14},{10,12},{12... | collective-permute-start | bytes 1474568 | tf_op jit(solution)/shard_map/ppermute | solution.py:331
  27.1 23.6 %collective-permute-start.4 = (bf16[160,1536]{1,0:T(8,128)(2,1)S(1)}, bf16[160,1536]{1,0:T(8,128)(2,1)S(1)}, u32[]{:S(2)}, u32[]{:S(2)}) collective-permute-start(bf16[160,1536]{1,0:T(8,128)(2,1)S(1)} %stack_rows.6.refs_0_), channel_id=1, source_target_pairs={{0,4},{2,6},{4,0},{6,2},{1,5},{3,7},{5,1},{7,3},{8,12},{10,14},{12... | collective-permute-start | bytes 1474568 | tf_op jit(solution)/shard_map/ppermute | solution.py:331
  28.6 22.2 %collective-permute-start.3 = (bf16[160,1536]{1,0:T(8,128)(2,1)S(1)}, bf16[160,1536]{1,0:T(8,128)(2,1)S(1)}, u32[]{:S(2)}, u32[]{:S(2)}) collective-permute-start(bf16[160,1536]{1,0:T(8,128)(2,1)S(1)} %stack_rows.6.refs_0_), channel_id=1, source_target_pairs={{0,2},{2,0},{4,6},{6,4},{1,3},{3,1},{5,7},{7,5},{8,10},{10,8},{12,... | collective-permute-start | bytes 1474568 | tf_op jit(solution)/shard_map/ppermute | solution.py:331
  34.8 13.0 %collective-permute-start.8 = (bf16[48,1536]{1,0:T(8,128)(2,1)}, bf16[48,1536]{1,0:T(8,128)(2,1)S(1)}, u32[]{:S(2)}, u32[]{:S(2)}) collective-permute-start(bf16[48,1536]{1,0:T(8,128)(2,1)} %get-tuple-element.225), channel_id=1, source_target_pairs={{0,16},{8,24},{16,0},{24,8},{1,17},{9,25},{17,1},{25,9},{2,18},{10... | collective-permute-start | bytes 442376 | tf_op jit(solution)/shard_map/ppermute | solution.py:331
  37.2 12.7 %collective-permute-start.9 = (bf16[48,1536]{1,0:T(8,128)(2,1)S(1)}, bf16[48,1536]{1,0:T(8,128)(2,1)S(1)}, u32[]{:S(2)}, u32[]{:S(2)}) collective-permute-start(bf16[48,1536]{1,0:T(8,128)(2,1)S(1)} %collective-permute-done.7.refs_0_), channel_id=1, source_target_pairs={{0,16},{8,24},{16,0},{24,8},{1,17},{9,25},{17,1},{25,9},{2,18},{10... | collective-permute-start | bytes 442376 | tf_op jit(solution)/shard_map/ppermute | solution.py:331
  50.8 23.4 %collective-permute-start.13 = (bf16[144,1536]{1,0:T(8,128)(2,1)S(1)}, bf16[144,1536]{1,0:T(8,128)(2,1)S(1)}, u32[]{:S(2)}, u32[]{:S(2)}) collective-permute-start(bf16[144,1536]{1,0:T(8,128)(2,1)S(1)} %stack_rows.7.refs_0_), channel_id=1, source_target_pairs={{0,6},{2,4},{4,2},{6,0},{1,7},{3,5},{5,3},{7,1},{8,14},{10,12},{12... | collective-permute-start | bytes 1327112 | tf_op jit(solution)/shard_map/ppermute | solution.py:331
  52.3 21.9 %collective-permute-start.12 = (bf16[144,1536]{1,0:T(8,128)(2,1)S(1)}, bf16[144,1536]{1,0:T(8,128)(2,1)S(1)}, u32[]{:S(2)}, u32[]{:S(2)}) collective-permute-start(bf16[144,1536]{1,0:T(8,128)(2,1)S(1)} %stack_rows.7.refs_0_), channel_id=1, source_target_pairs={{0,4},{2,6},{4,0},{6,2},{1,5},{3,7},{5,1},{7,3},{8,12},{10,14},{12... | collective-permute-start | bytes 1327112 | tf_op jit(solution)/shard_map/ppermute | solution.py:331
  53.7 20.5 %collective-permute-start.11 = (bf16[144,1536]{1,0:T(8,128)(2,1)S(1)}, bf16[144,1536]{1,0:T(8,128)(2,1)S(1)}, u32[]{:S(2)}, u32[]{:S(2)}) collective-permute-start(bf16[144,1536]{1,0:T(8,128)(2,1)S(1)} %stack_rows.7.refs_0_), channel_id=1, source_target_pairs={{0,2},{2,0},{4,6},{6,4},{1,3},{3,1},{5,7},{7,5},{8,10},{10,8},{12,... | collective-permute-start | bytes 1327112 | tf_op jit(solution)/shard_map/ppermute | solution.py:331
  55.9 18.4 %collective-permute-start.14 = (bf16[48,1536]{1,0:T(8,128)(2,1)S(1)}, bf16[48,1536]{1,0:T(8,128)(2,1)S(1)}, u32[]{:S(2)}, u32[]{:S(2)}) collective-permute-start(bf16[48,1536]{1,0:T(8,128)(2,1)S(1)} %copy-done.6), channel_id=1, source_target_pairs={{0,16},{8,24},{16,0},{24,8},{1,17},{9,25},{17,1},{25,9},{2,18},{10... | collective-permute-start | bytes 442376 | tf_op jit(solution)/shard_map/ppermute | solution.py:331
  62.0 12.2 %collective-permute-start.15 = (bf16[48,1536]{1,0:T(8,128)(2,1)S(1)}, bf16[48,1536]{1,0:T(8,128)(2,1)S(1)}, u32[]{:S(2)}, u32[]{:S(2)}) collective-permute-start(bf16[48,1536]{1,0:T(8,128)(2,1)S(1)} %collective-permute-done.10.refs_0_), channel_id=1, source_target_pairs={{0,16},{8,24},{16,0},{24,8},{1,17},{9,25},{17,1},{25,9},{2,18},{10... | collective-permute-start | bytes 442376 | tf_op jit(solution)/shard_map/ppermute | solution.py:331
  76.0 15.6 %collective-permute-start.16 = (bf16[1024,768]{1,0:T(8,128)(2,1)S(1)}, bf16[1024,768]{1,0:T(8,128)(2,1)S(1)}, u32[]{:S(2)}, u32[]{:S(2)}) collective-permute-start(bf16[1024,768]{1,0:T(8,128)(2,1)S(1)} %rows_times.3.mine_ref), channel_id=1, source_target_pairs={{0,1},{1,0},{2,3},{3,2},{4,5},{5,4},{6,7},{7,6},{8,9},{9,8},{10,11... | collective-permute-start | bytes 4718600 | tf_op jit(solution)/shard_map/ppermute | solution.py:331
  76.1 14.0 %collective-permute-start.19 = (bf16[144,1536]{1,0:T(8,128)(2,1)S(1)}, bf16[144,1536]{1,0:T(8,128)(2,1)S(1)}, u32[]{:S(2)}, u32[]{:S(2)}) collective-permute-start(bf16[144,1536]{1,0:T(8,128)(2,1)S(1)} %stack_rows.8.refs_0_), channel_id=1, source_target_pairs={{0,6},{2,4},{4,2},{6,0},{1,7},{3,5},{5,3},{7,1},{8,14},{10,12},{12... | collective-permute-start | bytes 1327112 | tf_op jit(solution)/shard_map/ppermute | solution.py:331
  77.6 22.0 %collective-permute-start.18 = (bf16[144,1536]{1,0:T(8,128)(2,1)S(1)}, bf16[144,1536]{1,0:T(8,128)(2,1)S(1)}, u32[]{:S(2)}, u32[]{:S(2)}) collective-permute-start(bf16[144,1536]{1,0:T(8,128)(2,1)S(1)} %stack_rows.8.refs_0_), channel_id=1, source_target_pairs={{0,4},{2,6},{4,0},{6,2},{1,5},{3,7},{5,1},{7,3},{8,12},{10,14},{12... | collective-permute-start | bytes 1327112 | tf_op jit(solution)/shard_map/ppermute | solution.py:331
  79.0 20.5 %collective-permute-start.17 = (bf16[144,1536]{1,0:T(8,128)(2,1)S(1)}, bf16[144,1536]{1,0:T(8,128)(2,1)S(1)}, u32[]{:S(2)}, u32[]{:S(2)}) collective-permute-start(bf16[144,1536]{1,0:T(8,128)(2,1)S(1)} %stack_rows.8.refs_0_), channel_id=1, source_target_pairs={{0,2},{2,0},{4,6},{6,4},{1,3},{3,1},{5,7},{7,5},{8,10},{10,8},{12,... | collective-permute-start | bytes 1327112 | tf_op jit(solution)/shard_map/ppermute | solution.py:331
  79.7 24.1 %collective-permute-start.22 = (bf16[128,768]{1,0:T(8,128)(2,1)S(1)}, bf16[128,768]{1,0:T(8,128)(2,1)S(1)}, u32[]{:S(2)}, u32[]{:S(2)}) collective-permute-start(bf16[128,768]{1,0:T(8,128)(2,1)S(1)} %get-tuple-element.480), channel_id=1, source_target_pairs={{0,6},{2,4},{4,2},{6,0},{1,7},{3,5},{5,3},{7,1},{8,14},{10,12},{12... | collective-permute-start | bytes 589832 | tf_op jit(solution)/shard_map/ppermute | solution.py:331
  90.0 17.5 %collective-permute-start.21 = (bf16[128,768]{1,0:T(8,128)(2,1)S(1)}, bf16[128,768]{1,0:T(8,128)(2,1)S(1)}, u32[]{:S(2)}, u32[]{:S(2)}) collective-permute-start(bf16[128,768]{1,0:T(8,128)(2,1)S(1)} %get-tuple-element.481), channel_id=1, source_target_pairs={{0,4},{2,6},{4,0},{6,2},{1,5},{3,7},{5,1},{7,3},{8,12},{10,14},{12... | collective-permute-start | bytes 589832 | tf_op jit(solution)/shard_map/ppermute | solution.py:331
  91.5 16.1 %collective-permute-start.20 = (bf16[128,768]{1,0:T(8,128)(2,1)S(1)}, bf16[128,768]{1,0:T(8,128)(2,1)S(1)}, u32[]{:S(2)}, u32[]{:S(2)}) collective-permute-start(bf16[128,768]{1,0:T(8,128)(2,1)S(1)} %get-tuple-element.482), channel_id=1, source_target_pairs={{0,2},{2,0},{4,6},{6,4},{1,3},{3,1},{5,7},{7,5},{8,10},{10,8},{12,... | collective-permute-start | bytes 589832 | tf_op jit(solution)/shard_map/ppermute | solution.py:331
  117.3 14.7 %collective-permute-start.27 = (bf16[128,768]{1,0:T(8,128)(2,1)S(1)}, bf16[128,768]{1,0:T(8,128)(2,1)S(1)}, u32[]{:S(2)}, u32[]{:S(2)}) collective-permute-start(bf16[128,768]{1,0:T(8,128)(2,1)S(1)} %get-tuple-element.476), channel_id=1, source_target_pairs={{0,6},{2,4},{4,2},{6,0},{1,7},{3,5},{5,3},{7,1},{8,14},{10,12},{12... | collective-permute-start | bytes 589832 | tf_op jit(solution)/shard_map/ppermute | solution.py:331
  118.8 13.2 %collective-permute-start.26 = (bf16[128,768]{1,0:T(8,128)(2,1)S(1)}, bf16[128,768]{1,0:T(8,128)(2,1)S(1)}, u32[]{:S(2)}, u32[]{:S(2)}) collective-permute-start(bf16[128,768]{1,0:T(8,128)(2,1)S(1)} %get-tuple-element.477), channel_id=1, source_target_pairs={{0,4},{2,6},{4,0},{6,2},{1,5},{3,7},{5,1},{7,3},{8,12},{10,14},{12... | collective-permute-start | bytes 589832 | tf_op jit(solution)/shard_map/ppermute | solution.py:331
  120.1 11.9 %collective-permute-start.25 = (bf16[128,768]{1,0:T(8,128)(2,1)S(1)}, bf16[128,768]{1,0:T(8,128)(2,1)S(1)}, u32[]{:S(2)}, u32[]{:S(2)}) collective-permute-start(bf16[128,768]{1,0:T(8,128)(2,1)S(1)} %get-tuple-element.478), channel_id=1, source_target_pairs={{0,2},{2,0},{4,6},{6,4},{1,3},{3,1},{5,7},{7,5},{8,10},{10,8},{12,... | collective-permute-start | bytes 589832 | tf_op jit(solution)/shard_map/ppermute | solution.py:331
  132.0 11.1 %collective-permute-start.28 = (bf16[1024,768]{1,0:T(8,128)(2,1)S(1)}, bf16[1024,768]{1,0:T(8,128)(2,1)S(1)}, u32[]{:S(2)}, u32[]{:S(2)}) collective-permute-start(bf16[1024,768]{1,0:T(8,128)(2,1)S(1)} %rows_times.4.mine_ref), channel_id=1, source_target_pairs={{0,1},{1,0},{2,3},{3,2},{4,5},{5,4},{6,7},{7,6},{8,9},{9,8},{10,11... | collective-permute-start | bytes 4718600 | tf_op jit(solution)/shard_map/ppermute | solution.py:331
  132.1 35.4 %collective-permute-start.30 = (bf16[384,1536]{1,0:T(8,128)(2,1)S(1)}, bf16[384,1536]{1,0:T(8,128)(2,1)S(1)}, u32[]{:S(2)}, u32[]{:S(2)}) collective-permute-start(bf16[384,1536]{1,0:T(8,128)(2,1)S(1)} %get-tuple-element.290), channel_id=1, source_target_pairs={{0,8},{8,0},{16,24},{24,16},{1,9},{9,1},{17,25},{25,17},{2,10},{10... | collective-permute-start | bytes 3538952 | tf_op jit(solution)/shard_map/ppermute | solution.py:331
  138.8 36.7 %collective-permute-start.36 = (bf16[192,1536]{1,0:T(8,128)(2,1)S(1)}, bf16[192,1536]{1,0:T(8,128)(2,1)S(1)}, u32[]{:S(2)}, u32[]{:S(2)}) collective-permute-start(bf16[192,1536]{1,0:T(8,128)(2,1)S(1)} %get-tuple-element.316), channel_id=1, source_target_pairs={{0,2},{2,0},{4,6},{6,4},{1,3},{3,1},{5,7},{7,5},{8,10},{10,8},{12,... | collective-permute-start | bytes 1769480 | tf_op jit(solution)/shard_map/ppermute | solution.py:331
  140.2 36.7 %collective-permute-start.37 = (bf16[192,1536]{1,0:T(8,128)(2,1)S(1)}, bf16[192,1536]{1,0:T(8,128)(2,1)S(1)}, u32[]{:S(2)}, u32[]{:S(2)}) collective-permute-start(bf16[192,1536]{1,0:T(8,128)(2,1)S(1)} %get-tuple-element.317), channel_id=1, source_target_pairs={{0,4},{2,6},{4,0},{6,2},{1,5},{3,7},{5,1},{7,3},{8,12},{10,14},{12... | collective-permute-start | bytes 1769480 | tf_op jit(solution)/shard_map/ppermute | solution.py:331
  149.5 19.4 %collective-permute-start.31 = (bf16[384,384]{1,0:T(8,128)(2,1)S(1)}, bf16[384,384]{1,0:T(8,128)(2,1)S(1)}, u32[]{:S(2)}, u32[]{:S(2)}) collective-permute-start(bf16[384,384]{1,0:T(8,128)(2,1)S(1)} %get-tuple-element.291), channel_id=1, source_target_pairs={{0,8},{8,0},{16,24},{24,16},{1,9},{9,1},{17,25},{25,17},{2,10},{10... | collective-permute-start | bytes 884744 | tf_op jit(solution)/shard_map/ppermute | solution.py:331
  149.8 28.4 %collective-permute-start.38 = (bf16[192,1536]{1,0:T(8,128)(2,1)S(1)}, bf16[192,1536]{1,0:T(8,128)(2,1)S(1)}, u32[]{:S(2)}, u32[]{:S(2)}) collective-permute-start(bf16[192,1536]{1,0:T(8,128)(2,1)S(1)} %get-tuple-element.318), channel_id=1, source_target_pairs={{0,6},{2,4},{4,2},{6,0},{1,7},{3,5},{5,3},{7,1},{8,14},{10,12},{12... | collective-permute-start | bytes 1769480 | tf_op jit(solution)/shard_map/ppermute | solution.py:331
  173.5 27.9 %collective-permute-start.40 = (bf16[192,1536]{1,0:T(8,128)(2,1)S(1)}, bf16[192,1536]{1,0:T(8,128)(2,1)S(1)}, u32[]{:S(2)}, u32[]{:S(2)}) collective-permute-start(bf16[192,1536]{1,0:T(8,128)(2,1)S(1)} %get-tuple-element.328), channel_id=1, source_target_pairs={{0,16},{8,24},{16,0},{24,8},{1,17},{9,25},{17,1},{25,9},{2,18},{10... | collective-permute-start | bytes 1769480 | tf_op jit(solution)/shard_map/ppermute | solution.py:331
  174.8 21.7 %collective-permute-start.33 = (bf16[192,1152]{1,0:T(8,128)(2,1)S(1)}, bf16[192,1152]{1,0:T(8,128)(2,1)S(1)}, u32[]{:S(2)}, u32[]{:S(2)}) collective-permute-start(bf16[192,1152]{1,0:T(8,128)(2,1)S(1)} %get-tuple-element.308), channel_id=1, source_target_pairs={{0,2},{2,0},{4,6},{6,4},{1,3},{3,1},{5,7},{7,5},{8,10},{10,8},{12,... | collective-permute-start | bytes 1327112 | tf_op jit(solution)/shard_map/ppermute | solution.py:331
  175.5 21.0 %collective-permute-start.34 = (bf16[192,1152]{1,0:T(8,128)(2,1)S(1)}, bf16[192,1152]{1,0:T(8,128)(2,1)S(1)}, u32[]{:S(2)}, u32[]{:S(2)}) collective-permute-start(bf16[192,1152]{1,0:T(8,128)(2,1)S(1)} %get-tuple-element.309), channel_id=1, source_target_pairs={{0,4},{2,6},{4,0},{6,2},{1,5},{3,7},{5,1},{7,3},{8,12},{10,14},{12... | collective-permute-start | bytes 1327112 | tf_op jit(solution)/shard_map/ppermute | solution.py:331
  176.9 19.6 %collective-permute-start.35 = (bf16[192,1152]{1,0:T(8,128)(2,1)S(1)}, bf16[192,1152]{1,0:T(8,128)(2,1)S(1)}, u32[]{:S(2)}, u32[]{:S(2)}) collective-permute-start(bf16[192,1152]{1,0:T(8,128)(2,1)S(1)} %get-tuple-element.310), channel_id=1, source_target_pairs={{0,6},{2,4},{4,2},{6,0},{1,7},{3,5},{5,3},{7,1},{8,14},{10,12},{12... | collective-permute-start | bytes 1327112 | tf_op jit(solution)/shard_map/ppermute | solution.py:331
  178.3 18.2 %collective-permute-start.39 = (f32[16,768]{1,0:T(8,128)S(1)}, f32[16,768]{1,0:T(8,128)S(1)}, u32[]{:S(2)}, u32[]{:S(2)}) collective-permute-start(f32[16,768]{1,0:T(8,128)S(1)} %add.75), channel_id=1, source_target_pairs={{0,4},{2,6},{4,0},{6,2},{1,5},{3,7},{5,1},{7,3},{8,12},{10,14},{12... | collective-permute-start | bytes 147464 | tf_op jit(solution)/shard_map/ppermute | solution.py:331
  203.6 10.8 %collective-permute-start.47 = (bf16[96,1536]{1,0:T(8,128)(2,1)S(1)}, bf16[96,1536]{1,0:T(8,128)(2,1)S(1)}, u32[]{:S(2)}, u32[]{:S(2)}) collective-permute-start(bf16[96,1536]{1,0:T(8,128)(2,1)S(1)} %get-tuple-element.470), channel_id=1, source_target_pairs={{0,4},{2,6},{4,0},{6,2},{1,5},{3,7},{5,1},{7,3},{8,12},{10,14},{12... | collective-permute-start | bytes 884744 | tf_op jit(solution)/shard_map/ppermute | solution.py:331
  204.4 10.1 %collective-permute-start.46 = (bf16[96,1536]{1,0:T(8,128)(2,1)S(1)}, bf16[96,1536]{1,0:T(8,128)(2,1)S(1)}, u32[]{:S(2)}, u32[]{:S(2)}) collective-permute-start(bf16[96,1536]{1,0:T(8,128)(2,1)S(1)} %get-tuple-element.471), channel_id=1, source_target_pairs={{0,2},{2,0},{4,6},{6,4},{1,3},{3,1},{5,7},{7,5},{8,10},{10,8},{12,... | collective-permute-start | bytes 884744 | tf_op jit(solution)/shard_map/ppermute | solution.py:331
  210.7 12.1 %collective-permute-start.45 = (bf16[96,1536]{1,0:T(8,128)(2,1)S(1)}, bf16[96,1536]{1,0:T(8,128)(2,1)S(1)}, u32[]{:S(2)}, u32[]{:S(2)}) collective-permute-start(bf16[96,1536]{1,0:T(8,128)(2,1)S(1)} %get-tuple-element.350), channel_id=1, source_target_pairs={{0,8},{8,0},{16,24},{24,16},{1,9},{9,1},{17,25},{25,17},{2,10},{10... | collective-permute-start | bytes 884744 | tf_op jit(solution)/shard_map/ppermute | solution.py:331
  223.0 16.8 %collective-permute-start.53 = (bf16[96,1536]{1,0:T(8,128)(2,1)S(1)}, bf16[96,1536]{1,0:T(8,128)(2,1)S(1)}, u32[]{:S(2)}, u32[]{:S(2)}) collective-permute-start(bf16[96,1536]{1,0:T(8,128)(2,1)S(1)} %add_convert_fusion.2.refs_0_), channel_id=1, source_target_pairs={{0,4},{2,6},{4,0},{6,2},{1,5},{3,7},{5,1},{7,3},{8,12},{10,14},{12... | collective-permute-start | bytes 884744 | tf_op jit(solution)/shard_map/ppermute | solution.py:331
  223.8 16.1 %collective-permute-start.54 = (bf16[96,1536]{1,0:T(8,128)(2,1)S(1)}, bf16[96,1536]{1,0:T(8,128)(2,1)S(1)}, u32[]{:S(2)}, u32[]{:S(2)}) collective-permute-start(bf16[96,1536]{1,0:T(8,128)(2,1)S(1)} %add_convert_fusion.1.refs_2_), channel_id=1, source_target_pairs={{0,2},{2,0},{4,6},{6,4},{1,3},{3,1},{5,7},{7,5},{8,10},{10,8},{12,... | collective-permute-start | bytes 884744 | tf_op jit(solution)/shard_map/ppermute | solution.py:331
  225.8 13.2 %collective-permute-start.51 = (bf16[48,1536]{1,0:T(8,128)(2,1)S(1)}, bf16[48,1536]{1,0:T(8,128)(2,1)S(1)}, u32[]{:S(2)}, u32[]{:S(2)}) collective-permute-start(bf16[48,1536]{1,0:T(8,128)(2,1)S(1)} %get-tuple-element.369), channel_id=1, source_target_pairs={{0,16},{8,24},{16,0},{24,8},{1,17},{9,25},{17,1},{25,9},{2,18},{10... | collective-permute-start | bytes 442376 | tf_op jit(solution)/shard_map/ppermute | solution.py:331
  227.1 12.8 %collective-permute-start.52 = (bf16[192,384]{1,0:T(8,128)(2,1)S(1)}, bf16[192,384]{1,0:T(8,128)(2,1)S(1)}, u32[]{:S(2)}, u32[]{:S(2)}) collective-permute-start(bf16[192,384]{1,0:T(8,128)(2,1)S(1)} %get-tuple-element.370), channel_id=1, source_target_pairs={{0,16},{8,24},{16,0},{24,8},{1,17},{9,25},{17,1},{25,9},{2,18},{10... | collective-permute-start | bytes 442376 | tf_op jit(solution)/shard_map/ppermute | solution.py:331
  239.9 16.3 %collective-permute-start.59 = (bf16[128,768]{1,0:T(8,128)(2,1)S(1)}, bf16[128,768]{1,0:T(8,128)(2,1)S(1)}, u32[]{:S(2)}, u32[]{:S(2)}) collective-permute-start(bf16[128,768]{1,0:T(8,128)(2,1)S(1)} %get-tuple-element.387), channel_id=1, source_target_pairs={{0,4},{2,6},{4,0},{6,2},{1,5},{3,7},{5,1},{7,3},{8,12},{10,14},{12... | collective-permute-start | bytes 589832 | tf_op jit(solution)/shard_map/ppermute | solution.py:331
  241.4 14.9 %collective-permute-start.60 = (bf16[128,768]{1,0:T(8,128)(2,1)S(1)}, bf16[128,768]{1,0:T(8,128)(2,1)S(1)}, u32[]{:S(2)}, u32[]{:S(2)}) collective-permute-start(bf16[128,768]{1,0:T(8,128)(2,1)S(1)} %get-tuple-element.388), channel_id=1, source_target_pairs={{0,6},{2,4},{4,2},{6,0},{1,7},{3,5},{5,3},{7,1},{8,14},{10,12},{12... | collective-permute-start | bytes 589832 | tf_op jit(solution)/shard_map/ppermute | solution.py:331
  242.8 13.5 %collective-permute-start.56 = (bf16[48,1536]{1,0:T(8,128)(2,1)S(1)}, bf16[48,1536]{1,0:T(8,128)(2,1)S(1)}, u32[]{:S(2)}, u32[]{:S(2)}) collective-permute-start(bf16[48,1536]{1,0:T(8,128)(2,1)S(1)} %add_convert_fusion.7.refs_2_), channel_id=1, source_target_pairs={{0,4},{2,6},{4,0},{6,2},{1,5},{3,7},{5,1},{7,3},{8,12},{10,14},{12... | collective-permute-start | bytes 442376 | tf_op jit(solution)/shard_map/ppermute | solution.py:331
  243.5 12.8 %collective-permute-start.55 = (bf16[48,1536]{1,0:T(8,128)(2,1)S(1)}, bf16[48,1536]{1,0:T(8,128)(2,1)S(1)}, u32[]{:S(2)}, u32[]{:S(2)}) collective-permute-start(bf16[48,1536]{1,0:T(8,128)(2,1)S(1)} %add_convert_fusion.7.refs_2_), channel_id=1, source_target_pairs={{0,2},{2,0},{4,6},{6,4},{1,3},{3,1},{5,7},{7,5},{8,10},{10,8},{12,... | collective-permute-start | bytes 442376 | tf_op jit(solution)/shard_map/ppermute | solution.py:331
  244.9 11.4 %collective-permute-start.57 = (bf16[48,1152]{1,0:T(8,128)(2,1)S(1)}, bf16[48,1152]{1,0:T(8,128)(2,1)S(1)}, u32[]{:S(2)}, u32[]{:S(2)}) collective-permute-start(bf16[48,1152]{1,0:T(8,128)(2,1)S(1)} %collective-permute-done.49.refs_3_), channel_id=1, source_target_pairs={{0,4},{2,6},{4,0},{6,2},{1,5},{3,7},{5,1},{7,3},{8,12},{10,14},{12... | collective-permute-start | bytes 331784 | tf_op jit(solution)/shard_map/ppermute | solution.py:331
  (35 other events, 287.7 us)
